TPU v7x, 128 devices: a whole 4x4x4 slice. The times are simulated.
128 devices in a mesh: row: 2 (over x_lo), col: 2 (over x_hi), dp: 32 (over y, z, core).
Axes of the slice: x: 4 (x_hi: 2, x_lo: 2; x = x_hi * 2 + x_lo), y: 4, z: 4, core: 2. Of those that a mesh axis runs over, the one named last changes fastest.
Arguments:
- features: bfloat16 [32, 48, 48, 1024], P('dp', 'row', 'col'), may hold values from -6 to 6
- cotangent: bfloat16 [32, 48, 48, 256], P('dp', 'row', 'col'), may hold values from -0.09375 to 0.09375
- w_point: bfloat16 [1024, 256], replicated, may hold values from -0.1875 to 0.1875
- w_rate_a: bfloat16 [3, 3, 1024, 256], replicated, may hold values from -0.0625 to 0.0625
- w_rate_b: bfloat16 [3, 3, 1024, 256], replicated, may hold values from -0.0625 to 0.0625
- w_rate_c: bfloat16 [3, 3, 1024, 256], replicated, may hold values from -0.0625 to 0.0625
- w_proj: bfloat16 [1024, 256], replicated, may hold values from -0.1875 to 0.1875
- bucket_slot: int32 [176], replicated, may hold values from 0 to 191, as said below
Outputs:
- owned_grads: float32 [192, 16384], P('dp', ('row', 'col'))
Inputs may be any that keep to these rules, and one draw needn't show every extreme that they name: Distinct slot numbers, one for each of the 176 slices; slice s belongs to data replica bucket_slot[s] // 6. In every draw all 6 slots of some replica are taken. Rows of owned_grads that no slice names are zero.
All inputs are finite; a program needn't handle non-finite values.
Results may differ from a plain program's by a relative error of at most 0.0043.
Values may be sent and summed in bfloat16 or wider, within the bound.
No kernel may reach another device: no remote copies, remote signals or barrier semaphores. Data moves between devices by JAX's collectives and lax.ppermute only.
A program may use at most 192 MiB of HBM per device.

v0:
```python
import jax
import jax.numpy as jnp
from jax import lax
from jax.experimental import pallas as pl
from jax.experimental.pallas import tpu as pltpu
from jax.sharding import Mesh
from jax.sharding import PartitionSpec as P

RATE_A = 6
RATE_B = 12
RATE_C = 18
DP = ("dp_0", "dp_1", "dp_2")


BF = jnp.bfloat16
F32 = jnp.float32
VMEM_LIMIT = 56 * 1024 * 1024


def flip(x, mask):
    if mask == 1:
        return lax.ppermute(x, "col", [(0, 1), (1, 0)])
    if mask == 2:
        return lax.ppermute(x, "row", [(0, 1), (1, 0)])
    return lax.ppermute(x, ("row", "col"), [(0, 3), (3, 0), (1, 2), (2, 1)])


def smem():
    return pl.BlockSpec(memory_space=pltpu.SMEM)


def vmem():
    return pl.BlockSpec(memory_space=pltpu.VMEM)


def call(body, outs, n_smem, n_vmem, flops, nbytes, scratch=(), name=None):
    return pl.pallas_call(
        body,
        out_shape=outs,
        in_specs=[smem()] * n_smem + [vmem()] * n_vmem,
        out_specs=jax.tree.map(lambda _: vmem(), outs),
        scratch_shapes=list(scratch),
        compiler_params=pltpu.CompilerParams(vmem_limit_bytes=VMEM_LIMIT),
        cost_estimate=pl.CostEstimate(flops=flops, bytes_accessed=nbytes, transcendentals=0),
        name=name,
    )


def select_channels(pos_ref, x_ref, *o_refs):
    chans = x_ref.shape[1]
    width = o_refs[0].shape[1]
    source = lax.broadcasted_iota(jnp.int32, (chans, width), 0)
    col = lax.broadcasted_iota(jnp.int32, (chans, width), 1)
    wanted = 64 * (col // 16) + col % 16
    for k, o_ref in enumerate(o_refs):
        c = jnp.bitwise_xor(pos_ref[0], k)
        pick = (source == wanted + 16 * c).astype(F32).astype(BF)
        o_ref[...] = jnp.dot(x_ref[...], pick, preferred_element_type=F32).astype(BF)


def turn_pixels(pos_ref, x0, x1, x2, x3, o_ref, held):
    pixels, width = x0.shape
    for k, x in enumerate((x0, x1, x2, x3)):
        s = jnp.bitwise_xor(pos_ref[0], k)
        held[s % 2, pl.ds((s // 2) * pixels, pixels), :] = x[...]
    eye = (
        lax.broadcasted_iota(jnp.int32, (width, width), 0)
        == lax.broadcasted_iota(jnp.int32, (width, width), 1)
    ).astype(F32).astype(BF)
    for g in range(2):
        o_ref[g] = lax.dot_general(
            eye, held[g], (((1,), (1,)), ((), ())), preferred_element_type=F32
        ).astype(BF)


def roll_cols(x, shift):
    return jnp.concatenate([x[:, x.shape[1] - shift :], x[:, : x.shape[1] - shift]], axis=1)


def tap_grads(pos_ref, place_ref, d0, d1, d2, d3, xt_ref, gp_ref, keep_ref, send_ref, held, padded, buf):
    side = RATE_C
    pixels, width = d0.shape
    cols = 24
    rows = pixels // cols
    for k, d in enumerate((d0, d1, d2, d3)):
        s = jnp.bitwise_xor(pos_ref[0], k)
        held[s % 2, pl.ds((s // 2) * pixels, pixels), :] = d[...]
    buf[...] = jnp.zeros_like(buf)
    tall = 2 * pixels
    lead = side * cols
    zeros = jnp.zeros((2, lead, width), BF)
    halves = [held[g].astype(F32).reshape(2 * rows, cols, width) for g in range(2)]
    at = lax.broadcasted_iota(jnp.int32, (2 * rows, cols, width), 1)
    rest = cols - side
    for across in (-1, 0, 1):
        padded[:, pl.ds(0, lead), :] = zeros
        padded[:, pl.ds(lead + tall, lead), :] = zeros
        if across == 0:
            shifted = halves
        elif across == 1:
            rolled = [roll_cols(h, side) for h in halves]
            shifted = [
                jnp.where(at >= side, rolled[0], 0.0),
                jnp.where(at < side, rolled[0], rolled[1]),
            ]
        else:
            rolled = [roll_cols(h, rest) for h in halves]
            shifted = [
                jnp.where(at < rest, rolled[0], rolled[1]),
                jnp.where(at < rest, rolled[1], 0.0),
            ]
        for g in range(2):
            padded[g, pl.ds(lead, tall), :] = shifted[g].reshape(tall, width).astype(BF)
        for above in (-1, 0, 1):
            first, last = {-1: (0, 32), 0: (0, 48), 1: (16, 48)}[above]
            base = first - side * above + side
            total = None
            for g in range(2):
                part = jnp.dot(
                    xt_ref[g, :, first * cols : last * cols],
                    padded[g, base * cols : (base + last - first) * cols, :],
                    preferred_element_type=F32,
                )
                total = part if total is None else total + part
            tap = 3 * (above + 1) + across + 1
            groups = total.reshape(width // 16, 16, width)
            for m in range(width // 16):
                buf[place_ref[32 + 16 * tap + m]] = groups[m]
    for n in range(gp_ref.shape[0]):
        buf[place_ref[pos_ref[1] + n]] = gp_ref[n]
    half = buf.shape[0] // 2
    keep_ref[...] = buf[:half]
    send_ref[...] = buf[half:].astype(BF)


def exchange_sum(blocks, axis, dtype):
    count = lax.axis_size(axis)
    me = lax.axis_index(axis)
    total = lax.dynamic_index_in_dim(blocks, me, 0, keepdims=False)
    for step in range(1, count):
        out = lax.dynamic_index_in_dim(blocks, (me + step) % count, 0, keepdims=False).astype(dtype)
        got = lax.ppermute(out, axis, [(i, (i + step) % count) for i in range(count)])
        total = total + got.astype(F32)
    return total


def exchange_sum_image(blocks, me, dtype):
    total = lax.dynamic_index_in_dim(blocks, me, 0, keepdims=False)
    for mask in (1, 2, 3):
        out = lax.dynamic_index_in_dim(blocks, jnp.bitwise_xor(me, mask), 0, keepdims=False)
        total = total + flip(out.astype(dtype), mask).astype(F32)
    return total


def swap_core(x):
    return lax.ppermute(x, "dp_2", [(0, 1), (1, 0)])


def pick(pos, centre):
    pixels, chans = centre.shape
    block = jax.ShapeDtypeStruct((pixels, chans // 4), BF)
    return call(select_channels, [block] * 4, 1, 1, 2 * pixels * chans * chans, 4 * pixels * chans, name="pick")(
        pos, centre
    )


def turn(pos, got):
    pixels, width = got[0].shape
    return call(
        turn_pixels,
        jax.ShapeDtypeStruct((2, width, 2 * pixels), BF),
        1,
        4,
        8 * pixels * width * width,
        16 * pixels * width,
        [pltpu.VMEM((2, 2 * pixels, width), BF)],
        name="turn",
    )(pos, *got)


def reduce_pair(kept, sent, me):
    kept = kept + swap_core(sent).astype(F32)
    ys = lax.axis_size("dp_0")
    width = kept.shape[1]
    mine = exchange_sum(kept.reshape(ys, -1, width), "dp_0", BF)
    blocks = jnp.moveaxis(mine.reshape(-1, 4, 16, width), 1, 0)
    return exchange_sum_image(blocks, me, BF)


def place_slots(bucket_slot, core, slot_count):
    replicas = lax.axis_size(DP)
    capacity = slot_count // replicas
    owner = bucket_slot // capacity
    other = jnp.bitwise_xor(owner % 2, core)
    return other * (slot_count // 2) + (owner // 2) * capacity + bucket_slot % capacity


def reduce_slots(pos, place, deltas, turned, pair, slot_count):
    pixels, width = deltas[0].shape
    half = slot_count // 2
    kept, sent = call(
        tap_grads,
        [
            jax.ShapeDtypeStruct((half, 16, width), F32),
            jax.ShapeDtypeStruct((half, 16, width), BF),
        ],
        2,
        6,
        2 * 7 * 4 * pixels * width * width,
        8 * 1024 * 1024,
        [
            pltpu.VMEM((2, 2 * pixels, width), BF),
            pltpu.VMEM((2, 2 * pixels + 2 * RATE_C * 24, width), BF),
            pltpu.VMEM((slot_count, 16, width), F32),
        ],
        name="taps",
    )(pos, place, *deltas, turned, pair)
    total = kept + swap_core(sent).astype(F32)
    ys, zs = lax.axis_size("dp_0"), lax.axis_size("dp_1")
    total = exchange_sum(total.reshape(ys, half // ys * 16, width), "dp_0", BF)
    total = exchange_sum(total.reshape(zs, half // ys // zs * 16, width), "dp_1", BF)
    return total.reshape(half // ys // zs, 16 * width)


def silu_slope(value):
    sig = jax.nn.sigmoid(value)
    return sig * (1.0 + value * (1.0 - sig))


RATES = (RATE_A, RATE_B, RATE_C)
SIDE = 24


def turned_by(x, shift, far):
    return jnp.where(far == 0, roll_cols(x, shift), roll_cols(x, SIDE - shift))


def rank_of(shape, far):
    at = lax.broadcasted_iota(jnp.int32, shape, 1)
    return jnp.where(far == 0, at, SIDE - 1 - at)


def conv_parts(
    pos_ref, x_ref, wa_ref, wb_ref, wc_ref, wp_ref, pre0_ref, pre_ref, row_ref, col_ref, diag_ref, ext, held
):
    step = pl.program_id(0)
    across = step // 3
    low = pos_ref[2]
    far = pos_ref[3]
    width = x_ref.shape[1] // 4
    whole = SIDE * SIDE

    def blocks(x):
        return x.reshape(x.shape[0] // SIDE, SIDE, width)

    def flat(x):
        return x.reshape(x.shape[0] * SIDE, width)

    def rate_step(index, rate, w_ref):
        lead = rate * SIDE
        inside = (SIDE - rate) * SIDE
        own_at = pl.multiple_of(jnp.where(low == 0, 0, lead), 16)
        out_at = pl.multiple_of(jnp.where(low == 0, lead, 0), 16)
        next_at = pl.multiple_of(jnp.where(low == 0, whole, 0), 16)
        blank_at = pl.multiple_of(jnp.where(low == 0, 0, whole), 16)
        in_from = pl.multiple_of(jnp.where(low == 0, lead, 0), 16)
        in_at = pl.multiple_of(jnp.where(low == 0, 0, 2 * lead), 16)
        out_tap = jnp.where(low == 0, 0, 2)
        in_tap = jnp.where(low == 0, 2, 0)
        ext[pl.ds(blank_at, lead), :] = jnp.zeros((lead, width), F32)
        ext[pl.ds(out_at, whole), :] = jnp.dot(x_ref[...], w_ref[out_tap, 0], preferred_element_type=F32)
        ext[pl.ds(own_at, whole), :] += jnp.dot(x_ref[...], w_ref[1, 0], preferred_element_type=F32)
        ext[pl.ds(in_at, inside), :] += jnp.dot(
            x_ref[pl.ds(in_from, inside), :], w_ref[in_tap, 0], preferred_element_type=F32
        )
        own_rows = pl.ds(own_at, whole)
        next_rows = pl.ds(next_at, lead)
        first = {RATE_C: 0, RATE_B: RATE_C * SIDE, RATE_A: (RATE_C + RATE_B) * SIDE}[rate]
        to_row = slice(first, first + lead)

        @pl.when(across == 0)
        def _():
            pre_ref[index] = ext[own_rows, :]
            held[to_row, :] = ext[next_rows, :]

        @pl.when(across == 1)
        def _():
            own = blocks(ext[own_rows, :])
            ours = turned_by(own, rate, far)
            rank = rank_of(own.shape, far)
            pre_ref[index] += flat(jnp.where(rank >= rate, ours, 0.0))
            below = blocks(ext[next_rows, :])
            theirs = turned_by(below, rate, far)
            place = rank_of(below.shape, far)
            held[to_row, :] += flat(jnp.where(place >= rate, theirs, 0.0))
            if rate == RATE_C:
                col_ref[:whole, :] = flat(jnp.where(rank < rate, ours, 0.0)).astype(BF)
                diag_ref[:lead, :] = flat(jnp.where(place < rate, theirs, 0.0)).astype(BF)
            elif rate == RATE_B:
                half = rate // 2
                part = rank[:rate] < rate
                col_ref[whole:, :] = flat(jnp.where(part, ours[:rate], own[rate:])).astype(BF)
                part = place[:half] < rate
                diag_ref[RATE_C * SIDE :, :] = flat(jnp.where(part, theirs[:half], below[half:])).astype(BF)
            else:
                have = blocks(col_ref[:whole, :].astype(F32))
                col_ref[:whole, :] = flat(jnp.where(rank >= RATE_C, own, have)).astype(BF)
                have = blocks(diag_ref[:lead, :].astype(F32))
                diag_ref[:lead, :] = flat(jnp.where(place >= RATE_C, below, have)).astype(BF)

        @pl.when(across == 2)
        def _():
            own = blocks(ext[own_rows, :])
            rank = rank_of(own.shape, far)
            pre_ref[index] += flat(jnp.where(rank < SIDE - rate, turned_by(own, rate, 1 - far), 0.0))
            below = blocks(ext[next_rows, :])
            place = rank_of(below.shape, far)
            theirs = jnp.where(place < SIDE - rate, turned_by(below, rate, 1 - far), 0.0)
            row_ref[to_row, :] = (held[to_row, :] + flat(theirs)).astype(BF)

    @pl.when(step == 0)
    def _():
        pre0_ref[...] = jnp.dot(x_ref[...], wp_ref[...], preferred_element_type=F32)

    for turn, (index, rate, w_ref) in enumerate(((2, RATE_C, wc_ref), (1, RATE_B, wb_ref), (0, RATE_A, wa_ref))):

        @pl.when(step % 3 == turn)
        def _(index=index, rate=rate, w_ref=w_ref):
            rate_step(index, rate, w_ref)


def convolve(pos, centre, w_rate_a, w_rate_b, w_rate_c, w_point):
    pixels, chans = centre.shape
    width = w_point.shape[1]
    sends = (RATE_A + RATE_B + RATE_C) * SIDE
    corner = pixels

    def taps_spec(turn):
        def at(step, pos_ref):
            across = (step - turn + 2) // 3
            out = jnp.where(pos_ref[3] == 0, 0, 2)
            return (0, jnp.where(across == 0, 1, jnp.where(across == 1, out, 2 - out)), 0, 0)

        return pl.BlockSpec((3, 1, chans, width), at)

    def still(shape):
        return pl.BlockSpec(shape, lambda step, pos_ref: (0,) * len(shape))

    shapes = [
        ((pixels, width), F32),
        ((3, pixels, width), F32),
        ((sends, width), BF),
        ((sends, width), BF),
        ((corner, width), BF),
    ]
    return pl.pallas_call(
        conv_parts,
        out_shape=[jax.ShapeDtypeStruct(*s) for s in shapes],
        grid_spec=pltpu.PrefetchScalarGridSpec(
            num_scalar_prefetch=1,
            grid=(9,),
            in_specs=[
                still((pixels, chans)),
                taps_spec(2),
                taps_spec(1),
                taps_spec(0),
                still((chans, width)),
            ],
            out_specs=[still(s[0]) for s in shapes],
            scratch_shapes=[
                pltpu.VMEM(((SIDE + RATE_C) * SIDE, width), F32),
                pltpu.VMEM((sends, width), F32),
            ],
        ),
        compiler_params=pltpu.CompilerParams(vmem_limit_bytes=VMEM_LIMIT),
        cost_estimate=pl.CostEstimate(
            flops=2 * pixels * chans * width * 25, bytes_accessed=20 * 1024 * 1024, transcendentals=0
        ),
        name="convs",
    )(pos, centre, w_rate_a, w_rate_b, w_rate_c, w_point)


def merge_parts(
    pos_ref, pre0_ref, own_ref, row_ref, col_ref, diag_ref, cot_ref, wp_ref, joined_ref, g_ref, d0_ref, d3_ref, pre
):
    low = pos_ref[2]
    theirs = 1 - pos_ref[3]
    width = pre0_ref.shape[1]
    whole = SIDE * SIDE

    def blocks(x):
        return x.reshape(x.shape[0] // SIDE, SIDE, width)

    def flat(x):
        return x.reshape(x.shape[0] * SIDE, width)

    def rows_of(rate):
        return pl.multiple_of(jnp.where(low == 0, (SIDE - rate) * SIDE, 0), 16)

    pre[...] = own_ref[...]
    first = 0
    for index, rate in ((2, RATE_C), (1, RATE_B), (0, RATE_A)):
        lead = rate * SIDE
        pre[index, pl.ds(rows_of(rate), lead), :] += row_ref[first : first + lead, :].astype(F32)
        first += lead

    part = blocks(col_ref[:whole, :].astype(F32))
    rank = rank_of(part.shape, theirs)
    pre[2] += flat(jnp.where(rank < RATE_C, part, 0.0))
    pre[0] += flat(turned_by(jnp.where(rank >= RATE_C, part, 0.0), RATE_A, theirs))
    part = blocks(col_ref[whole:, :].astype(F32))
    rank = rank_of(part.shape, theirs)
    pre[1, : RATE_B * SIDE, :] += flat(jnp.where(rank < RATE_B, part, 0.0))
    pre[1, RATE_B * SIDE :, :] += flat(roll_cols(jnp.where(rank >= RATE_B, part, 0.0), RATE_B))

    part = blocks(diag_ref[: RATE_C * SIDE, :].astype(F32))
    rank = rank_of(part.shape, theirs)
    pre[2, pl.ds(rows_of(RATE_C), RATE_C * SIDE), :] += flat(jnp.where(rank < RATE_C, part, 0.0))
    few = part[:RATE_A]
    few = turned_by(jnp.where(rank[:RATE_A] >= RATE_C, few, 0.0), RATE_A, theirs)
    pre[0, pl.ds(rows_of(RATE_A), RATE_A * SIDE), :] += flat(few)
    part = blocks(diag_ref[RATE_C * SIDE :, :].astype(F32))
    rank = rank_of(part.shape, theirs)
    half = RATE_B // 2
    at = rows_of(RATE_B)
    pre[1, pl.ds(at, half * SIDE), :] += flat(jnp.where(rank < RATE_B, part, 0.0))
    last = pl.multiple_of(at + half * SIDE, 16)
    pre[1, pl.ds(last, half * SIDE), :] += flat(roll_cols(jnp.where(rank >= RATE_B, part, 0.0), RATE_B))

    slopes = {}
    for k in range(4):
        value = pre0_ref[...] if k == 0 else pre[k - 1]
        sig = jax.nn.sigmoid(value)
        joined_ref[:, k * width : (k + 1) * width] = (value * sig).astype(BF)
        if k in (0, 3):
            slopes[k] = sig * (1.0 + value * (1.0 - sig))
    proj_pre = jnp.dot(joined_ref[...], wp_ref[...], preferred_element_type=F32)
    g_proj = (cot_ref[...].astype(F32) * silu_slope(proj_pre)).astype(BF)
    g_ref[...] = g_proj
    for k, out in ((3, d3_ref), (0, d0_ref)):
        back = lax.dot_general(
            g_proj, wp_ref[k * width : (k + 1) * width, :], (((1,), (1,)), ((), ())), preferred_element_type=F32
        )
        out[...] = (back * slopes[k]).astype(BF)


def merge(pos, pre0, own, row, col, diag, cot, w_proj):
    pixels, width = pre0.shape
    block = jax.ShapeDtypeStruct((pixels, width), BF)
    return call(
        merge_parts,
        [jax.ShapeDtypeStruct((pixels, 4 * width), BF), block, block, block],
        1,
        7,
        2 * pixels * width * width * 6,
        6 * 1024 * 1024,
        [pltpu.VMEM((3, pixels, width), F32)],
        name="merge",
    )(pos, pre0, own, row, col, diag, cot, w_proj)


def pair_grads(pos_ref, joined_ref, g_ref, x_ref, d0_ref, keep_ref, send_ref):
    core = pos_ref[4]
    over = (((0,), (0,)), ((), ()))
    grad_proj = lax.dot_general(joined_ref[...], g_ref[...], over, preferred_element_type=F32)
    grad_point = lax.dot_general(x_ref[...], d0_ref[...], over, preferred_element_type=F32)
    keep_ref[...] = jnp.where(core == 0, grad_proj, grad_point)
    send_ref[...] = jnp.where(core == 0, grad_point, grad_proj).astype(BF)


def shards(features, cotangent, w_point, w_rate_a, w_rate_b, w_rate_c, w_proj, bucket_slot):
    image = features[0]
    rows_dev, cols_dev, chans = image.shape
    pixels = rows_dev * cols_dev
    width = w_point.shape[1]
    row, col, core = (lax.axis_index(n) for n in ("row", "col", "dp_2"))
    me = 2 * row + col
    pos = jnp.stack([me, 16 * core + 4 * lax.axis_index("dp_0"), row, col, core]).astype(jnp.int32)
    replicas = lax.axis_size(DP)
    slot_count = replicas * (bucket_slot.shape[0] // replicas + 1)
    place = place_slots(bucket_slot, core, slot_count)
    centre = image.reshape(pixels, chans)
    picked = pick(pos, centre)
    centre, *picked = lax.optimization_barrier((centre, *picked))
    got = [picked[0]] + [flip(picked[k], k) for k in (1, 2, 3)]
    pre0, own, *parts = convolve(pos, centre, w_rate_a, w_rate_b, w_rate_c, w_point)
    parts, got = lax.optimization_barrier((parts, got))
    to_row, to_col, to_diag = parts
    from_row, from_col, from_diag = flip(to_row, 2), flip(to_col, 1), flip(to_diag, 3)
    turned = turn(pos, got)
    joined, g_proj, delta0, delta3 = merge(
        pos, pre0, own, from_row, from_col, from_diag, cotangent[0].reshape(pixels, width), w_proj
    )
    shared = [delta3] + [flip(delta3, k) for k in (1, 2, 3)]
    block = (4 * width, width)
    kept, sent = call(
        pair_grads,
        [jax.ShapeDtypeStruct(block, F32), jax.ShapeDtypeStruct(block, BF)],
        1,
        4,
        4 * pixels * chans * width,
        4 * 1024 * 1024,
        name="pair",
    )(pos, joined, g_proj, centre, delta0)
    pair = reduce_pair(kept, sent, me)
    return reduce_slots(pos, place, shared, turned, pair, slot_count)


def solution(mesh):
    torus = Mesh(
        mesh.devices.reshape(mesh.shape["row"], mesh.shape["col"], 4, 4, 2),
        ("row", "col", "dp_0", "dp_1", "dp_2"),
    )
    in_specs = (P(DP, "row", "col", None), P(DP, "row", "col", None), P(), P(), P(), P(), P(), P())
    out_specs = P(DP, ("row", "col"))
    return jax.shard_map(
        shards, mesh=torus, in_specs=in_specs, out_specs=out_specs, check_vma=False
    )
```

profile of v0, /device:TPU:0, one launch (start us, length us, event | category | flops | bytes accessed | tf_op | source)
XLA Modules:
  0.0 126.6 jit_solution(5220673520155611314)
XLA Ops:
  0.6 3.5 %pick.1 = (bf16[576,256]{1,0:T(8,128)(2,1)}, bf16[576,256]{1,0:T(8,128)(2,1)}, bf16[576,256]{1,0:T(8,128)(2,1)}, bf16[576,256]{1,0:T(8,128)(2,1)}) custom-call(s32[5]{0:T(128)} %stack.23.pos_ref, bf16[576,1024]{1,0:T(8,128)(2,1)} %bitcast.75), custom_call_target="tpu_custom_call" | custom-call | flops 1207959552 | bytes 2359296 | tf_op jit(solution)/shard_map/pick/pallas_call | solution.py:162
  4.1 3.1 %collective-permute-start = (bf16[576,256]{1,0:T(8,128)(2,1)}, bf16[576,256]{1,0:T(8,128)(2,1)S(1)}, u32[]{:S(2)}, u32[]{:S(2)}) collective-permute-start(bf16[576,256]{1,0:T(8,128)(2,1)} %get-tuple-element.45), channel_id=1, source_target_pairs={{0,32},{32,0},{1,33},{33,1},{2,34},{34,2},{3,35},{35,3},{4,36},{36... | collective-permute-start | bytes 884744 | tf_op jit(solution)/shard_map/ppermute | solution.py:22
  8.4 17.5 %convs.1 = (f32[576,256]{1,0:T(8,128)}, f32[3,576,256]{2,1,0:T(8,128)}, bf16[864,256]{1,0:T(8,128)(2,1)}, bf16[864,256]{1,0:T(8,128)(2,1)}, bf16[576,256]{1,0:T(8,128)(2,1)}) custom-call(s32[5]{0:T(128)} %stack.23.pos_ref, bf16[576,1024]{1,0:T(8,128)(2,1)} %bitcast.76, bf16[3,3,1024,256]{3,2,1,0:T(8,128)(2,1)} %wa_ref.1, bf16[3,3,1024,256]{3,2,1,0:T(8,128)(2,1)} %wb_ref.1, ...), custom_call_target="tpu_custom_call" | custom-call | flops 7549747200 | bytes 20971520 | tf_op jit(solution)/shard_map/convs/pallas_call | solution.py:356
  25.9 1.5 %collective-permute-start.3 = (bf16[864,256]{1,0:T(8,128)(2,1)}, bf16[864,256]{1,0:T(8,128)(2,1)S(1)}, u32[]{:S(2)}, u32[]{:S(2)}) collective-permute-start(bf16[864,256]{1,0:T(8,128)(2,1)} %get-tuple-element.48), channel_id=1, source_target_pairs={{0,64},{64,0},{1,65},{65,1},{2,66},{66,2},{3,67},{67,3},{4,68},{68... | collective-permute-start | bytes 1327112 | tf_op jit(solution)/shard_map/ppermute | solution.py:24
  27.4 2.7 %collective-permute-start.4 = (bf16[864,256]{1,0:T(8,128)(2,1)}, bf16[864,256]{1,0:T(8,128)(2,1)S(1)}, u32[]{:S(2)}, u32[]{:S(2)}) collective-permute-start(bf16[864,256]{1,0:T(8,128)(2,1)} %get-tuple-element.49), channel_id=1, source_target_pairs={{0,32},{32,0},{1,33},{33,1},{2,34},{34,2},{3,35},{35,3},{4,36},{36... | collective-permute-start | bytes 1327112 | tf_op jit(solution)/shard_map/ppermute | solution.py:22
  30.6 9.8 %collective-permute-done.5.diag_ref = bf16[576,256]{1,0:T(8,128)(2,1)S(1)} collective-permute-done((bf16[576,256]{1,0:T(8,128)(2,1)}, bf16[576,256]{1,0:T(8,128)(2,1)S(1)}, u32[]{:S(2)}, u32[]{:S(2)}) %collective-permute-start.5) | collective-permute-done | bytes 294944 | tf_op jit(solution)/shard_map/ppermute | solution.py:25
  40.5 8.4 %collective-permute-done.4.col_ref = bf16[864,256]{1,0:T(8,128)(2,1)S(1)} collective-permute-done((bf16[864,256]{1,0:T(8,128)(2,1)}, bf16[864,256]{1,0:T(8,128)(2,1)S(1)}, u32[]{:S(2)}, u32[]{:S(2)}) %collective-permute-start.4) | collective-permute-done | bytes 442400 | tf_op jit(solution)/shard_map/ppermute | solution.py:22
  49.6 4.8 %merge.1 = (bf16[576,1024]{1,0:T(8,128)(2,1)}, bf16[576,256]{1,0:T(8,128)(2,1)}, bf16[576,256]{1,0:T(8,128)(2,1)}, bf16[576,256]{1,0:T(8,128)(2,1)}) custom-call(s32[5]{0:T(128)} %stack.23.pos_ref, f32[576,256]{1,0:T(8,128)} %get-tuple-element.39.pre0_ref, f32[3,576,256]{2,1,0:T(8,128)} %get-tuple-element.40.own_ref, bf16[864,256]{1,0:T(8,128)(2,1)} %copy-done, ...), custom_call_target="tpu_custom_call" | custom-call | flops 452984832 | bytes 6291456 | tf_op jit(solution)/shard_map/merge/pallas_call | solution.py:450
  54.5 4.0 %pair.1 = (f32[1024,256]{1,0:T(8,128)}, bf16[1024,256]{1,0:T(8,128)(2,1)}) custom-call(s32[5]{0:T(128)} %stack.23.pos_ref, bf16[576,1024]{1,0:T(8,128)(2,1)} %get-tuple-element.56.joined_ref, bf16[576,256]{1,0:T(8,128)(2,1)} %get-tuple-element.57.g_ref, bf16[576,1024]{1,0:T(8,128)(2,1)} %bitcast.77, bf16[576,256]{1,0:T(8,128)(2,1)} %get-tuple-element.58.d0_ref), custom_call_target="tpu_custom_call" | custom-call | flops 603979776 | bytes 4194304 | tf_op jit(solution)/shard_map/pair/pallas_call | solution.py:496
  58.5 2.1 %collective-permute-done.9 = bf16[1024,256]{1,0:T(8,128)(2,1)S(1)} collective-permute-done((bf16[1024,256]{1,0:T(8,128)(2,1)}, bf16[1024,256]{1,0:T(8,128)(2,1)S(1)}, u32[]{:S(2)}, u32[]{:S(2)}) %collective-permute-start.9) | collective-permute-done | bytes 524320 | tf_op jit(solution)/shard_map/ppermute | solution.py:156
  60.6 1.3 %convert_add_fusion.1 = f32[1024,256]{1,0:T(8,128)S(1)} fusion(f32[1024,256]{1,0:T(8,128)} %get-tuple-element.59, bf16[1024,256]{1,0:T(8,128)(2,1)S(1)} %collective-permute-done.9), kind=kLoop, calls=%fused_computation.1 | loop fusion | flops 524288 | bytes 2621440 | tf_op jit(solution)/shard_map/add | solution.py:182
  62.0 1.7 %collective-permute-start.10 = (bf16[256,256]{1,0:T(8,128)(2,1)S(1)}, bf16[256,256]{1,0:T(8,128)(2,1)S(1)}, u32[]{:S(2)}, u32[]{:S(2)}) collective-permute-start(bf16[256,256]{1,0:T(8,128)(2,1)S(1)} %get-tuple-element.66), channel_id=1, source_target_pairs={{0,8},{8,16},{16,24},{24,0},{1,9},{9,17},{17,25},{25,1},{2,10},{10... | collective-permute-start | bytes 393224 | tf_op jit(solution)/shard_map/ppermute | solution.py:142
  63.7 2.9 %collective-permute-start.11 = (bf16[256,256]{1,0:T(8,128)(2,1)S(1)}, bf16[256,256]{1,0:T(8,128)(2,1)S(1)}, u32[]{:S(2)}, u32[]{:S(2)}) collective-permute-start(bf16[256,256]{1,0:T(8,128)(2,1)S(1)} %get-tuple-element.68), channel_id=1, source_target_pairs={{0,16},{8,24},{16,0},{24,8},{1,17},{9,25},{17,1},{25,9},{2,18},{10... | collective-permute-start | bytes 393224 | tf_op jit(solution)/shard_map/ppermute | solution.py:142
  66.6 1.3 %collective-permute-start.12 = (bf16[256,256]{1,0:T(8,128)(2,1)S(1)}, bf16[256,256]{1,0:T(8,128)(2,1)S(1)}, u32[]{:S(2)}, u32[]{:S(2)}) collective-permute-start(bf16[256,256]{1,0:T(8,128)(2,1)S(1)} %get-tuple-element.67), channel_id=1, source_target_pairs={{0,24},{8,0},{16,8},{24,16},{1,25},{9,1},{17,9},{25,17},{2,26},{10... | collective-permute-start | bytes 393224 | tf_op jit(solution)/shard_map/ppermute | solution.py:142
  68.9 4.0 %collective-permute-done.11 = bf16[256,256]{1,0:T(8,128)(2,1)S(1)} collective-permute-done((bf16[256,256]{1,0:T(8,128)(2,1)S(1)}, bf16[256,256]{1,0:T(8,128)(2,1)S(1)}, u32[]{:S(2)}, u32[]{:S(2)}) %collective-permute-start.11) | collective-permute-done | bytes 131104 | tf_op jit(solution)/shard_map/ppermute | solution.py:142
  73.9 2.7 %collective-permute-start.6 = (bf16[576,256]{1,0:T(8,128)(2,1)S(1)}, bf16[576,256]{1,0:T(8,128)(2,1)S(1)}, u32[]{:S(2)}, u32[]{:S(2)}) collective-permute-start(bf16[576,256]{1,0:T(8,128)(2,1)S(1)} %copy-done.7), channel_id=1, source_target_pairs={{0,32},{32,0},{1,33},{33,1},{2,34},{34,2},{3,35},{35,3},{4,36},{36... | collective-permute-start | bytes 884744 | tf_op jit(solution)/shard_map/ppermute | solution.py:22
  76.8 1.2 collective-permute-start.8
  78.9 2.4 %collective-permute-start.15 = (bf16[4,16,256]{2,1,0:T(8,128)(2,1)S(1)}, bf16[4,16,256]{2,1,0:T(8,128)(2,1)S(1)}, u32[]{:S(2)}, u32[]{:S(2)}) collective-permute-start(bf16[4,16,256]{2,1,0:T(8,128)(2,1)S(1)} %get-tuple-element.74), channel_id=1, source_target_pairs={{0,96},{96,0},{32,64},{64,32},{1,97},{97,1},{33,65},{65,33},{2,98}... | collective-permute-start | bytes 98312 | tf_op jit(solution)/shard_map/ppermute | solution.py:25
  81.8 2.9 %turn.1.xt_ref = bf16[2,256,1152]{2,1,0:T(8,128)(2,1)} custom-call(s32[5]{0:T(128)} %stack.23.pos_ref, bf16[576,256]{1,0:T(8,128)(2,1)} %get-tuple-element.52.x0, bf16[576,256]{1,0:T(8,128)(2,1)} %copy-done.2, bf16[576,256]{1,0:T(8,128)(2,1)} %copy-done.3, bf16[576,256]{1,0:T(8,128)(2,1)} %copy-done.4), custom_call_target="tpu_custom_call" | custom-call | flops 301989888 | bytes 2359296 | tf_op jit(solution)/shard_map/turn/pallas_call | solution.py:169
  84.7 5.3 %collective-permute-done.14 = bf16[4,16,256]{2,1,0:T(8,128)(2,1)S(1)} collective-permute-done((bf16[4,16,256]{2,1,0:T(8,128)(2,1)S(1)}, bf16[4,16,256]{2,1,0:T(8,128)(2,1)S(1)}, u32[]{:S(2)}, u32[]{:S(2)}) %collective-permute-start.14) | collective-permute-done | bytes 32800 | tf_op jit(solution)/shard_map/ppermute | solution.py:24
  92.9 5.9 %taps.1 = (f32[96,16,256]{2,1,0:T(8,128)}, bf16[96,16,256]{2,1,0:T(8,128)(2,1)}) custom-call(s32[5]{0:T(128)} %stack.23.pos_ref, s32[176]{0:T(256)} %fusion.21.place_ref, bf16[576,256]{1,0:T(8,128)(2,1)} %get-tuple-element.51.d0, bf16[576,256]{1,0:T(8,128)(2,1)} %copy-done.8, bf16[576,256]{1,0:T(8,128)(2,1)} %copy-done.9, bf16[576,256]{1,0:T(8,128)(2,1)} %copy-done.10, ...), custom_call_target="tpu_custom_call" | custom-call | flops 2113929216 | bytes 8388608 | tf_op jit(solution)/shard_map/taps/pallas_call | solution.py:201
  98.8 2.5 %collective-permute-done.16 = bf16[96,16,256]{2,1,0:T(8,128)(2,1)S(1)} collective-permute-done((bf16[96,16,256]{2,1,0:T(8,128)(2,1)}, bf16[96,16,256]{2,1,0:T(8,128)(2,1)S(1)}, u32[]{:S(2)}, u32[]{:S(2)}) %collective-permute-start.16) | collective-permute-done | bytes 786464 | tf_op jit(solution)/shard_map/ppermute | solution.py:156
  101.3 1.7 %convert_add_fusion = f32[96,16,256]{2,1,0:T(8,128)S(1)} fusion(f32[96,16,256]{2,1,0:T(8,128)} %get-tuple-element.61, bf16[96,16,256]{2,1,0:T(8,128)(2,1)S(1)} %collective-permute-done.16), kind=kLoop, calls=%fused_computation | loop fusion | flops 786432 | bytes 3932160 | tf_op jit(solution)/shard_map/add | solution.py:218
  103.1 1.3 %collective-permute-start.17 = (bf16[384,256]{1,0:T(8,128)(2,1)S(1)}, bf16[384,256]{1,0:T(8,128)(2,1)S(1)}, u32[]{:S(2)}, u32[]{:S(2)}) collective-permute-start(bf16[384,256]{1,0:T(8,128)(2,1)S(1)} %get-tuple-element.63), channel_id=1, source_target_pairs={{0,8},{8,16},{16,24},{24,0},{1,9},{9,17},{17,25},{25,1},{2,10},{10... | collective-permute-start | bytes 589832 | tf_op jit(solution)/shard_map/ppermute | solution.py:142
  104.4 2.5 %collective-permute-start.18 = (bf16[384,256]{1,0:T(8,128)(2,1)S(1)}, bf16[384,256]{1,0:T(8,128)(2,1)S(1)}, u32[]{:S(2)}, u32[]{:S(2)}) collective-permute-start(bf16[384,256]{1,0:T(8,128)(2,1)S(1)} %get-tuple-element.65), channel_id=1, source_target_pairs={{0,16},{8,24},{16,0},{24,8},{1,17},{9,25},{17,1},{25,9},{2,18},{10... | collective-permute-start | bytes 589832 | tf_op jit(solution)/shard_map/ppermute | solution.py:142
  106.9 1.2 collective-permute-start.19
  108.1 3.5 %collective-permute-done.17 = bf16[384,256]{1,0:T(8,128)(2,1)S(1)} collective-permute-done((bf16[384,256]{1,0:T(8,128)(2,1)S(1)}, bf16[384,256]{1,0:T(8,128)(2,1)S(1)}, u32[]{:S(2)}, u32[]{:S(2)}) %collective-permute-start.17) | collective-permute-done | bytes 196640 | tf_op jit(solution)/shard_map/ppermute | solution.py:142
  111.6 4.4 %collective-permute-done.18 = bf16[384,256]{1,0:T(8,128)(2,1)S(1)} collective-permute-done((bf16[384,256]{1,0:T(8,128)(2,1)S(1)}, bf16[384,256]{1,0:T(8,128)(2,1)S(1)}, u32[]{:S(2)}, u32[]{:S(2)}) %collective-permute-start.18) | collective-permute-done | bytes 196640 | tf_op jit(solution)/shard_map/ppermute | solution.py:142
  116.3 2.0 %collective-permute-start.20 = (bf16[96,256]{1,0:T(8,128)(2,1)S(1)}, bf16[96,256]{1,0:T(8,128)(2,1)S(1)}, u32[]{:S(2)}, u32[]{:S(2)}) collective-permute-start(bf16[96,256]{1,0:T(8,128)(2,1)S(1)} %get-tuple-element.69), channel_id=1, source_target_pairs={{0,2},{2,4},{4,6},{6,0},{1,3},{3,5},{5,7},{7,1},{8,10},{10,12},{12... | collective-permute-start | bytes 147464 | tf_op jit(solution)/shard_map/ppermute | solution.py:142
  118.3 3.6 %collective-permute-start.21 = (bf16[96,256]{1,0:T(8,128)(2,1)S(1)}, bf16[96,256]{1,0:T(8,128)(2,1)S(1)}, u32[]{:S(2)}, u32[]{:S(2)}) collective-permute-start(bf16[96,256]{1,0:T(8,128)(2,1)S(1)} %get-tuple-element.71), channel_id=1, source_target_pairs={{0,4},{2,6},{4,0},{6,2},{1,5},{3,7},{5,1},{7,3},{8,12},{10,14},{12... | collective-permute-start | bytes 147464 | tf_op jit(solution)/shard_map/ppermute | solution.py:142
  123.0 1.5 %collective-permute-done.21 = bf16[96,256]{1,0:T(8,128)(2,1)S(1)} collective-permute-done((bf16[96,256]{1,0:T(8,128)(2,1)S(1)}, bf16[96,256]{1,0:T(8,128)(2,1)S(1)}, u32[]{:S(2)}, u32[]{:S(2)}) %collective-permute-start.21) | collective-permute-done | bytes 49184 | tf_op jit(solution)/shard_map/ppermute | solution.py:142
  124.4 1.5 %collective-permute-done.22 = bf16[96,256]{1,0:T(8,128)(2,1)S(1)} collective-permute-done((bf16[96,256]{1,0:T(8,128)(2,1)S(1)}, bf16[96,256]{1,0:T(8,128)(2,1)S(1)}, u32[]{:S(2)}, u32[]{:S(2)}) %collective-permute-start.22) | collective-permute-done | bytes 49184 | tf_op jit(solution)/shard_map/ppermute | solution.py:142
  (55 shorter events, 11.7 us)
Async XLA Ops:
  4.1 21.7 %collective-permute-start = (bf16[576,256]{1,0:T(8,128)(2,1)}, bf16[576,256]{1,0:T(8,128)(2,1)S(1)}, u32[]{:S(2)}, u32[]{:S(2)}) collective-permute-start(bf16[576,256]{1,0:T(8,128)(2,1)} %get-tuple-element.45), channel_id=1, source_target_pairs={{0,32},{32,0},{1,33},{33,1},{2,34},{34,2},{3,35},{35,3},{4,36},{36... | collective-permute-start | bytes 884744 | tf_op jit(solution)/shard_map/ppermute | solution.py:22
  7.2 18.6 %collective-permute-start.1 = (bf16[576,256]{1,0:T(8,128)(2,1)}, bf16[576,256]{1,0:T(8,128)(2,1)S(1)}, u32[]{:S(2)}, u32[]{:S(2)}) collective-permute-start(bf16[576,256]{1,0:T(8,128)(2,1)} %get-tuple-element.46), channel_id=1, source_target_pairs={{0,64},{64,0},{1,65},{65,1},{2,66},{66,2},{3,67},{67,3},{4,68},{68... | collective-permute-start | bytes 884744 | tf_op jit(solution)/shard_map/ppermute | solution.py:24
  7.8 18.0 %collective-permute-start.2 = (bf16[576,256]{1,0:T(8,128)(2,1)}, bf16[576,256]{1,0:T(8,128)(2,1)S(1)}, u32[]{:S(2)}, u32[]{:S(2)}) collective-permute-start(bf16[576,256]{1,0:T(8,128)(2,1)} %get-tuple-element.47), channel_id=1, source_target_pairs={{0,96},{96,0},{32,64},{64,32},{1,97},{97,1},{33,65},{65,33},{2,98}... | collective-permute-start | bytes 884744 | tf_op jit(solution)/shard_map/ppermute | solution.py:25
  25.8 36.1 %copy-start.2 = (bf16[576,256]{1,0:T(8,128)(2,1)}, bf16[576,256]{1,0:T(8,128)(2,1)S(1)}, u32[]{:S(2)}) copy-start(bf16[576,256]{1,0:T(8,128)(2,1)S(1)} %collective-permute-done.x1) | copy-start | bytes 884740
  25.8 36.1 %copy-start.3 = (bf16[576,256]{1,0:T(8,128)(2,1)}, bf16[576,256]{1,0:T(8,128)(2,1)S(1)}, u32[]{:S(2)}) copy-start(bf16[576,256]{1,0:T(8,128)(2,1)S(1)} %collective-permute-done.1.x2) | copy-start | bytes 884740
  25.8 36.1 %copy-start.4 = (bf16[576,256]{1,0:T(8,128)(2,1)}, bf16[576,256]{1,0:T(8,128)(2,1)S(1)}, u32[]{:S(2)}) copy-start(bf16[576,256]{1,0:T(8,128)(2,1)S(1)} %collective-permute-done.2.x3) | copy-start | bytes 884740
  25.9 14.6 %collective-permute-start.3 = (bf16[864,256]{1,0:T(8,128)(2,1)}, bf16[864,256]{1,0:T(8,128)(2,1)S(1)}, u32[]{:S(2)}, u32[]{:S(2)}) collective-permute-start(bf16[864,256]{1,0:T(8,128)(2,1)} %get-tuple-element.48), channel_id=1, source_target_pairs={{0,64},{64,0},{1,65},{65,1},{2,66},{66,2},{3,67},{67,3},{4,68},{68... | collective-permute-start | bytes 1327112 | tf_op jit(solution)/shard_map/ppermute | solution.py:24
  27.4 21.5 %collective-permute-start.4 = (bf16[864,256]{1,0:T(8,128)(2,1)}, bf16[864,256]{1,0:T(8,128)(2,1)S(1)}, u32[]{:S(2)}, u32[]{:S(2)}) collective-permute-start(bf16[864,256]{1,0:T(8,128)(2,1)} %get-tuple-element.49), channel_id=1, source_target_pairs={{0,32},{32,0},{1,33},{33,1},{2,34},{34,2},{3,35},{35,3},{4,36},{36... | collective-permute-start | bytes 1327112 | tf_op jit(solution)/shard_map/ppermute | solution.py:22
  30.1 10.3 %collective-permute-start.5 = (bf16[576,256]{1,0:T(8,128)(2,1)}, bf16[576,256]{1,0:T(8,128)(2,1)S(1)}, u32[]{:S(2)}, u32[]{:S(2)}) collective-permute-start(bf16[576,256]{1,0:T(8,128)(2,1)} %get-tuple-element.50), channel_id=1, source_target_pairs={{0,96},{96,0},{32,64},{64,32},{1,97},{97,1},{33,65},{65,33},{2,98}... | collective-permute-start | bytes 884744 | tf_op jit(solution)/shard_map/ppermute | solution.py:25
  40.4 8.4 %copy-start.5 = (bf16[576,256]{1,0:T(8,128)(2,1)}, bf16[576,256]{1,0:T(8,128)(2,1)S(1)}, u32[]{:S(2)}) copy-start(bf16[576,256]{1,0:T(8,128)(2,1)S(1)} %collective-permute-done.5.diag_ref) | copy-start | bytes 884740
  40.4 8.4 %copy-start = (bf16[864,256]{1,0:T(8,128)(2,1)}, bf16[864,256]{1,0:T(8,128)(2,1)S(1)}, u32[]{:S(2)}) copy-start(bf16[864,256]{1,0:T(8,128)(2,1)S(1)} %collective-permute-done.3.row_ref) | copy-start | bytes 1327108
  48.9 0.8 copy-start.1
  58.5 2.1 %collective-permute-start.9 = (bf16[1024,256]{1,0:T(8,128)(2,1)}, bf16[1024,256]{1,0:T(8,128)(2,1)S(1)}, u32[]{:S(2)}, u32[]{:S(2)}) collective-permute-start(bf16[1024,256]{1,0:T(8,128)(2,1)} %get-tuple-element.60), channel_id=1, source_target_pairs={{0,1},{1,0},{2,3},{3,2},{4,5},{5,4},{6,7},{7,6},{8,9},{9,8},{10,11... | collective-permute-start | bytes 1572872 | tf_op jit(solution)/shard_map/ppermute | solution.py:156
  62.0 11.9 %copy-start.7 = (bf16[576,256]{1,0:T(8,128)(2,1)S(1)}, bf16[576,256]{1,0:T(8,128)(2,1)}, u32[]{:S(2)}) copy-start(bf16[576,256]{1,0:T(8,128)(2,1)} %get-tuple-element.51.d0) | copy-start | bytes 884740
  62.0 19.3 %copy-start.6 = (s32[176]{0:T(256)S(1)}, s32[176]{0:T(256)}, u32[]{:S(2)}) copy-start(s32[176]{0:T(256)} %param.15) | copy-start | bytes 2116
  62.0 6.9 %collective-permute-start.10 = (bf16[256,256]{1,0:T(8,128)(2,1)S(1)}, bf16[256,256]{1,0:T(8,128)(2,1)S(1)}, u32[]{:S(2)}, u32[]{:S(2)}) collective-permute-start(bf16[256,256]{1,0:T(8,128)(2,1)S(1)} %get-tuple-element.66), channel_id=1, source_target_pairs={{0,8},{8,16},{16,24},{24,0},{1,9},{9,17},{17,25},{25,1},{2,10},{10... | collective-permute-start | bytes 393224 | tf_op jit(solution)/shard_map/ppermute | solution.py:142
  63.7 9.2 %collective-permute-start.11 = (bf16[256,256]{1,0:T(8,128)(2,1)S(1)}, bf16[256,256]{1,0:T(8,128)(2,1)S(1)}, u32[]{:S(2)}, u32[]{:S(2)}) collective-permute-start(bf16[256,256]{1,0:T(8,128)(2,1)S(1)} %get-tuple-element.68), channel_id=1, source_target_pairs={{0,16},{8,24},{16,0},{24,8},{1,17},{9,25},{17,1},{25,9},{2,18},{10... | collective-permute-start | bytes 393224 | tf_op jit(solution)/shard_map/ppermute | solution.py:142
  66.6 6.3 %collective-permute-start.12 = (bf16[256,256]{1,0:T(8,128)(2,1)S(1)}, bf16[256,256]{1,0:T(8,128)(2,1)S(1)}, u32[]{:S(2)}, u32[]{:S(2)}) collective-permute-start(bf16[256,256]{1,0:T(8,128)(2,1)S(1)} %get-tuple-element.67), channel_id=1, source_target_pairs={{0,24},{8,0},{16,8},{24,16},{1,25},{9,1},{17,9},{25,17},{2,26},{10... | collective-permute-start | bytes 393224 | tf_op jit(solution)/shard_map/ppermute | solution.py:142
  73.0 5.9 %collective-permute-start.13 = (bf16[4,16,256]{2,1,0:T(8,128)(2,1)S(1)}, bf16[4,16,256]{2,1,0:T(8,128)(2,1)S(1)}, u32[]{:S(2)}, u32[]{:S(2)}) collective-permute-start(bf16[4,16,256]{2,1,0:T(8,128)(2,1)S(1)} %get-tuple-element.72), channel_id=1, source_target_pairs={{0,32},{32,0},{1,33},{33,1},{2,34},{34,2},{3,35},{35,3},{4,36},{36... | collective-permute-start | bytes 98312 | tf_op jit(solution)/shard_map/ppermute | solution.py:22
  73.9 17.5 %collective-permute-start.6 = (bf16[576,256]{1,0:T(8,128)(2,1)S(1)}, bf16[576,256]{1,0:T(8,128)(2,1)S(1)}, u32[]{:S(2)}, u32[]{:S(2)}) collective-permute-start(bf16[576,256]{1,0:T(8,128)(2,1)S(1)} %copy-done.7), channel_id=1, source_target_pairs={{0,32},{32,0},{1,33},{33,1},{2,34},{34,2},{3,35},{35,3},{4,36},{36... | collective-permute-start | bytes 884744 | tf_op jit(solution)/shard_map/ppermute | solution.py:22
  76.6 14.7 %collective-permute-start.7 = (bf16[576,256]{1,0:T(8,128)(2,1)S(1)}, bf16[576,256]{1,0:T(8,128)(2,1)S(1)}, u32[]{:S(2)}, u32[]{:S(2)}) collective-permute-start(bf16[576,256]{1,0:T(8,128)(2,1)S(1)} %copy-done.7), channel_id=1, source_target_pairs={{0,64},{64,0},{1,65},{65,1},{2,66},{66,2},{3,67},{67,3},{4,68},{68... | collective-permute-start | bytes 884744 | tf_op jit(solution)/shard_map/ppermute | solution.py:24
  76.8 14.6 %collective-permute-start.8 = (bf16[576,256]{1,0:T(8,128)(2,1)S(1)}, bf16[576,256]{1,0:T(8,128)(2,1)S(1)}, u32[]{:S(2)}, u32[]{:S(2)}) collective-permute-start(bf16[576,256]{1,0:T(8,128)(2,1)S(1)} %copy-done.7), channel_id=1, source_target_pairs={{0,96},{96,0},{32,64},{64,32},{1,97},{97,1},{33,65},{65,33},{2,98}... | collective-permute-start | bytes 884744 | tf_op jit(solution)/shard_map/ppermute | solution.py:25
  78.0 12.0 %collective-permute-start.14 = (bf16[4,16,256]{2,1,0:T(8,128)(2,1)S(1)}, bf16[4,16,256]{2,1,0:T(8,128)(2,1)S(1)}, u32[]{:S(2)}, u32[]{:S(2)}) collective-permute-start(bf16[4,16,256]{2,1,0:T(8,128)(2,1)S(1)} %get-tuple-element.73), channel_id=1, source_target_pairs={{0,64},{64,0},{1,65},{65,1},{2,66},{66,2},{3,67},{67,3},{4,68},{68... | collective-permute-start | bytes 98312 | tf_op jit(solution)/shard_map/ppermute | solution.py:24
  78.9 11.8 %collective-permute-start.15 = (bf16[4,16,256]{2,1,0:T(8,128)(2,1)S(1)}, bf16[4,16,256]{2,1,0:T(8,128)(2,1)S(1)}, u32[]{:S(2)}, u32[]{:S(2)}) collective-permute-start(bf16[4,16,256]{2,1,0:T(8,128)(2,1)S(1)} %get-tuple-element.74), channel_id=1, source_target_pairs={{0,96},{96,0},{32,64},{64,32},{1,97},{97,1},{33,65},{65,33},{2,98}... | collective-permute-start | bytes 98312 | tf_op jit(solution)/shard_map/ppermute | solution.py:25
  91.4 0.8 copy-start.9
  98.8 2.5 %collective-permute-start.16 = (bf16[96,16,256]{2,1,0:T(8,128)(2,1)}, bf16[96,16,256]{2,1,0:T(8,128)(2,1)S(1)}, u32[]{:S(2)}, u32[]{:S(2)}) collective-permute-start(bf16[96,16,256]{2,1,0:T(8,128)(2,1)} %get-tuple-element.62), channel_id=1, source_target_pairs={{0,1},{1,0},{2,3},{3,2},{4,5},{5,4},{6,7},{7,6},{8,9},{9,8},{10,11... | collective-permute-start | bytes 2359304 | tf_op jit(solution)/shard_map/ppermute | solution.py:156
  103.1 8.5 %collective-permute-start.17 = (bf16[384,256]{1,0:T(8,128)(2,1)S(1)}, bf16[384,256]{1,0:T(8,128)(2,1)S(1)}, u32[]{:S(2)}, u32[]{:S(2)}) collective-permute-start(bf16[384,256]{1,0:T(8,128)(2,1)S(1)} %get-tuple-element.63), channel_id=1, source_target_pairs={{0,8},{8,16},{16,24},{24,0},{1,9},{9,17},{17,25},{25,1},{2,10},{10... | collective-permute-start | bytes 589832 | tf_op jit(solution)/shard_map/ppermute | solution.py:142
  104.4 11.7 %collective-permute-start.18 = (bf16[384,256]{1,0:T(8,128)(2,1)S(1)}, bf16[384,256]{1,0:T(8,128)(2,1)S(1)}, u32[]{:S(2)}, u32[]{:S(2)}) collective-permute-start(bf16[384,256]{1,0:T(8,128)(2,1)S(1)} %get-tuple-element.65), channel_id=1, source_target_pairs={{0,16},{8,24},{16,0},{24,8},{1,17},{9,25},{17,1},{25,9},{2,18},{10... | collective-permute-start | bytes 589832 | tf_op jit(solution)/shard_map/ppermute | solution.py:142
  106.9 9.3 %collective-permute-start.19 = (bf16[384,256]{1,0:T(8,128)(2,1)S(1)}, bf16[384,256]{1,0:T(8,128)(2,1)S(1)}, u32[]{:S(2)}, u32[]{:S(2)}) collective-permute-start(bf16[384,256]{1,0:T(8,128)(2,1)S(1)} %get-tuple-element.64), channel_id=1, source_target_pairs={{0,24},{8,0},{16,8},{24,16},{1,25},{9,1},{17,9},{25,17},{2,26},{10... | collective-permute-start | bytes 589832 | tf_op jit(solution)/shard_map/ppermute | solution.py:142
  116.3 6.7 %collective-permute-start.20 = (bf16[96,256]{1,0:T(8,128)(2,1)S(1)}, bf16[96,256]{1,0:T(8,128)(2,1)S(1)}, u32[]{:S(2)}, u32[]{:S(2)}) collective-permute-start(bf16[96,256]{1,0:T(8,128)(2,1)S(1)} %get-tuple-element.69), channel_id=1, source_target_pairs={{0,2},{2,4},{4,6},{6,0},{1,3},{3,5},{5,7},{7,1},{8,10},{10,12},{12... | collective-permute-start | bytes 147464 | tf_op jit(solution)/shard_map/ppermute | solution.py:142
  118.3 6.2 %collective-permute-start.21 = (bf16[96,256]{1,0:T(8,128)(2,1)S(1)}, bf16[96,256]{1,0:T(8,128)(2,1)S(1)}, u32[]{:S(2)}, u32[]{:S(2)}) collective-permute-start(bf16[96,256]{1,0:T(8,128)(2,1)S(1)} %get-tuple-element.71), channel_id=1, source_target_pairs={{0,4},{2,6},{4,0},{6,2},{1,5},{3,7},{5,1},{7,3},{8,12},{10,14},{12... | collective-permute-start | bytes 147464 | tf_op jit(solution)/shard_map/ppermute | solution.py:142
  121.8 4.1 %collective-permute-start.22 = (bf16[96,256]{1,0:T(8,128)(2,1)S(1)}, bf16[96,256]{1,0:T(8,128)(2,1)S(1)}, u32[]{:S(2)}, u32[]{:S(2)}) collective-permute-start(bf16[96,256]{1,0:T(8,128)(2,1)S(1)} %get-tuple-element.70), channel_id=1, source_target_pairs={{0,6},{2,0},{4,2},{6,4},{1,7},{3,1},{5,3},{7,5},{8,14},{10,8},{12,... | collective-permute-start | bytes 147464 | tf_op jit(solution)/shard_map/ppermute | solution.py:142
  (2 other events, 1.4 us)
where the time goes:
time: 127 us
  waiting for transfers between devices  44.9 us (35%)
  Pallas kernels  38.6 us (30%)
  starting transfers between devices  34.8 us (27%)
  other arithmetic  4.38 us (3%)
  local copies, waits for them, and re-layouts  3.78 us (3%)
    ppermute x9, starting transfers between devices, exchange_sum(): lax.ppermute(out, axis, [(i, (i + step) % count) for i in range(count)])  17.5 us
    pallas_call x1, Pallas kernels, convolve(): pl.pallas_call(conv_parts, out_shape=[jax.ShapeDtypeStruct(*s) for s in s...  17.5 us
    ppermute x9, waiting for transfers between devices, exchange_sum(): lax.ppermute(out, axis, [(i, (i + step) % count) for i in range(count)])  16.1 us
    ppermute x4, waiting for transfers between devices, flip(): return lax.ppermute(x, ('row', 'col'), [(0, 3), (3, 0), (1, 2), (2, 1)])  10.5 us
    ppermute x4, starting transfers between devices, flip(): return lax.ppermute(x, 'col', [(0, 1), (1, 0)])  9.45 us
    ppermute x4, waiting for transfers between devices, flip(): return lax.ppermute(x, 'col', [(0, 1), (1, 0)])  8.43 us
    pallas_call x1, Pallas kernels, reduce_slots(): call(tap_grads, [jax.ShapeDtypeStruct((half, 16, width), F32), jax.ShapeD...  5.91 us
    ppermute x4, waiting for transfers between devices, flip(): return lax.ppermute(x, 'row', [(0, 1), (1, 0)])  5.31 us
  transfers between devices with their start and end apart: 23, of which 14 were waited for; matrix products, arithmetic and copies ran while one was open for 1% of the time, Pallas kernels for 16%

commit v1 on v0

v1 whole, which is shorter than its diff:
```python
import jax
import jax.numpy as jnp
from jax import lax
from jax.experimental import pallas as pl
from jax.experimental.pallas import tpu as pltpu
from jax.sharding import Mesh
from jax.sharding import PartitionSpec as P

RATE_A = 6
RATE_B = 12
RATE_C = 18
DP = ("dp_0", "dp_1", "dp_2")


BF = jnp.bfloat16
F32 = jnp.float32
MIB = 1024 * 1024


def flip(x, mask):
    if mask == 1:
        return lax.ppermute(x, "col", [(0, 1), (1, 0)])
    if mask == 2:
        return lax.ppermute(x, "row", [(0, 1), (1, 0)])
    return lax.ppermute(x, ("row", "col"), [(0, 3), (3, 0), (1, 2), (2, 1)])


def smem():
    return pl.BlockSpec(memory_space=pltpu.SMEM)


def vmem():
    return pl.BlockSpec(memory_space=pltpu.VMEM)


def call(body, outs, n_smem, n_vmem, flops, nbytes, limit, scratch=(), name=None, n_any=0):
    return pl.pallas_call(
        body,
        out_shape=outs,
        in_specs=[smem()] * n_smem + [vmem()] * n_vmem + [pl.BlockSpec(memory_space=pltpu.HBM)] * n_any,
        out_specs=jax.tree.map(lambda _: vmem(), outs),
        scratch_shapes=list(scratch),
        compiler_params=pltpu.CompilerParams(vmem_limit_bytes=limit * MIB),
        cost_estimate=pl.CostEstimate(flops=flops, bytes_accessed=nbytes, transcendentals=0),
        name=name,
    )


def select_channels(pos_ref, x_ref, *o_refs):
    chans = x_ref.shape[1]
    width = o_refs[0].shape[1]
    source = lax.broadcasted_iota(jnp.int32, (chans, width), 0)
    col = lax.broadcasted_iota(jnp.int32, (1, width), 1)
    wanted = 64 * (col // 16) + col % 16
    for k, o_ref in enumerate(o_refs):
        c = jnp.bitwise_xor(pos_ref[0], k)
        pick = jnp.where(source == wanted + 16 * c, 1.0, 0.0).astype(BF)
        o_ref[...] = jnp.dot(x_ref[...], pick, preferred_element_type=F32).astype(BF)


def turn_pixels(pos_ref, x0, x1, x2, x3, o_ref, held):
    pixels, width = x0.shape
    for k, x in enumerate((x0, x1, x2, x3)):
        s = jnp.bitwise_xor(pos_ref[0], k)
        held[s % 2, pl.ds((s // 2) * pixels, pixels), :] = x[...]
    eye = (
        lax.broadcasted_iota(jnp.int32, (width, width), 0)
        == lax.broadcasted_iota(jnp.int32, (width, width), 1)
    ).astype(F32).astype(BF)
    for g in range(2):
        o_ref[g] = lax.dot_general(
            eye, held[g], (((1,), (1,)), ((), ())), preferred_element_type=F32
        ).astype(BF)


def roll_cols(x, shift):
    return jnp.concatenate([x[:, x.shape[1] - shift :], x[:, : x.shape[1] - shift]], axis=1)


def tap_grads(pos_ref, place_ref, d0, d1, d2, d3, xt_ref, keep_ref, send_ref, held, padded, buf):
    side = RATE_C
    pixels, width = d0.shape
    cols = 24
    rows = pixels // cols
    for k, d in enumerate((d0, d1, d2, d3)):
        s = jnp.bitwise_xor(pos_ref[0], k)
        held[s % 2, pl.ds((s // 2) * pixels, pixels), :] = d[...]
    buf[...] = jnp.zeros_like(buf)
    tall = 2 * pixels
    lead = side * cols
    zeros = jnp.zeros((2, lead, width), BF)
    halves = [held[g].astype(F32).reshape(2 * rows, cols, width) for g in range(2)]
    at = lax.broadcasted_iota(jnp.int32, (2 * rows, cols, width), 1)
    rest = cols - side
    for across in (-1, 0, 1):
        padded[:, pl.ds(0, lead), :] = zeros
        padded[:, pl.ds(lead + tall, lead), :] = zeros
        if across == 0:
            shifted = halves
        elif across == 1:
            rolled = [roll_cols(h, side) for h in halves]
            shifted = [
                jnp.where(at >= side, rolled[0], 0.0),
                jnp.where(at < side, rolled[0], rolled[1]),
            ]
        else:
            rolled = [roll_cols(h, rest) for h in halves]
            shifted = [
                jnp.where(at < rest, rolled[0], rolled[1]),
                jnp.where(at < rest, rolled[1], 0.0),
            ]
        for g in range(2):
            padded[g, pl.ds(lead, tall), :] = shifted[g].reshape(tall, width).astype(BF)
        for above in (-1, 0, 1):
            first, last = {-1: (0, 32), 0: (0, 48), 1: (16, 48)}[above]
            base = first - side * above + side
            total = None
            for g in range(2):
                part = jnp.dot(
                    xt_ref[g, :, first * cols : last * cols],
                    padded[g, base * cols : (base + last - first) * cols, :],
                    preferred_element_type=F32,
                )
                total = part if total is None else total + part
            tap = 3 * (above + 1) + across + 1
            groups = total.reshape(width // 16, 16, width)
            for m in range(width // 16):
                buf[place_ref[32 + 16 * tap + m]] = groups[m]
    half = buf.shape[0] // 2
    keep_ref[...] = buf[:half]
    send_ref[...] = buf[half:].astype(BF)


def hand_out(total, me, outs):
    outs[0][...] = total[me]
    for s in range(1, len(outs)):
        outs[s][...] = total[lax.rem(me + s, len(outs))].astype(BF)


def join_owners(pos_ref, place_ref, keep_ref, got_ref, mine_ref, other_ref, *rest):
    *outs, total = rest
    count, each = total.shape[0], total.shape[1]
    total[...] = (keep_ref[...] + got_ref[...].astype(F32)).reshape(total.shape)
    core = pos_ref[4]
    for n in range(mine_ref.shape[0]):
        for ref, first in ((mine_ref, 16 * core), (other_ref, 16 * (1 - core))):
            at = place_ref[first + n]

            @pl.when(at < count * each)
            def _(ref=ref, at=at, n=n):
                total[at // each, at % each] = ref[n].astype(F32)

    hand_out(total, pos_ref[1], outs)


def fold_next(pos_ref, *refs):
    total = refs[-1]
    value = refs[0][...]
    for got in refs[1:4]:
        value = value + got[...].astype(F32)
    total[...] = value.reshape(total.shape)
    hand_out(total, pos_ref[5], refs[4:-1])


def fold_last(r0, r1, r2, r3, o_ref):
    total = r0[...] + r1[...].astype(F32) + r2[...].astype(F32) + r3[...].astype(F32)
    width = total.shape[2]
    for i in range(total.shape[1]):
        o_ref[:, i * width : (i + 1) * width] = total[:, i, :]


def share_rows(pos_ref, kept_ref, got0, got1, *rest):
    *outs, total = rest
    half, each = got0.shape[0], total.shape[0] // 2
    for n, got in enumerate((got0, got1)):
        value = kept_ref[n * half : (n + 1) * half, :] + got[...].astype(F32)
        total[n * each : (n + 1) * each] = value.reshape(each, *total.shape[1:])
    for k, out in enumerate(outs):
        out[...] = total[:, jnp.bitwise_xor(pos_ref[0], k)].astype(out.dtype)


def along(blocks, axis):
    count = lax.axis_size(axis)
    return [blocks[0]] + [
        lax.ppermute(blocks[s], axis, [(i, (i + s) % count) for i in range(count)]) for s in range(1, count)
    ]


def swap_core(x):
    return lax.ppermute(x, "dp_2", [(0, 1), (1, 0)])


def pick(pos, centre):
    pixels, chans = centre.shape
    block = jax.ShapeDtypeStruct((pixels, chans // 4), BF)
    return call(select_channels, [block] * 4, 1, 1, 2 * pixels * chans * chans, 4 * pixels * chans, 14, name="pick")(
        pos, centre
    )


def turn(pos, got):
    pixels, width = got[0].shape
    return call(
        turn_pixels,
        jax.ShapeDtypeStruct((2, width, 2 * pixels), BF),
        1,
        4,
        8 * pixels * width * width,
        16 * pixels * width,
        12,
        [pltpu.VMEM((2, 2 * pixels, width), BF)],
        name="turn",
    )(pos, *got)


def split_pair(pos, kept, got):
    width = kept.shape[1]
    slices = kept.shape[0] // 64
    shape = (slices, 16, width)
    return call(
        share_rows,
        [jax.ShapeDtypeStruct(shape, F32)] + [jax.ShapeDtypeStruct(shape, BF)] * 3,
        1,
        3,
        kept.size,
        8 * kept.size,
        10,
        [pltpu.VMEM((slices, 4, 16, width), F32)],
        name="rows",
    )(pos, kept, *got)


def sum_pair(blocks):
    mine = blocks[0] + sum(block.astype(F32) for block in blocks[1:])
    return mine, swap_core(mine.astype(BF))


def place_slots(bucket_slot, core, slot_count):
    replicas = lax.axis_size(DP)
    capacity = slot_count // replicas
    owner = bucket_slot // capacity
    other = jnp.bitwise_xor(owner % 2, core)
    return other * (slot_count // 2) + (owner // 2) * capacity + bucket_slot % capacity


def tap_slots(pos, place, deltas, turned, slot_count):
    pixels, width = deltas[0].shape
    half = slot_count // 2
    return call(
        tap_grads,
        [jax.ShapeDtypeStruct((half, 16, width), F32), jax.ShapeDtypeStruct((half, 16, width), BF)],
        2,
        5,
        2 * 7 * 4 * pixels * width * width,
        8 * 1024 * 1024,
        26,
        [
            pltpu.VMEM((2, 2 * pixels, width), BF),
            pltpu.VMEM((2, 2 * pixels + 2 * RATE_C * SIDE, width), BF),
            pltpu.VMEM((slot_count, 16, width), F32),
        ],
        name="taps",
    )(pos, place, *deltas, turned)


def reduce_slots(pos, place, kept, sent, mine, other):
    half, rows, width = kept.shape
    ys, zs = lax.axis_size("dp_0"), lax.axis_size("dp_1")
    each = half // ys
    last = each // zs

    def blocks(count, n):
        shape = (n, rows, width)
        return [jax.ShapeDtypeStruct(shape, F32)] + [jax.ShapeDtypeStruct(shape, BF)] * (count - 1)

    total = call(
        join_owners,
        blocks(ys, each),
        2,
        4,
        kept.size,
        8 * kept.size,
        12,
        [pltpu.VMEM((ys, each, rows, width), F32)],
        name="owners",
    )(pos, place, kept, swap_core(sent), mine, other)
    total = call(
        fold_next,
        blocks(zs, last),
        1,
        4,
        kept.size // 4,
        2 * kept.size,
        6,
        [pltpu.VMEM((zs, last, rows, width), F32)],
        name="fold",
    )(pos, *along(total, "dp_0"))
    return call(
        fold_last,
        jax.ShapeDtypeStruct((last, rows * width), F32),
        0,
        4,
        kept.size // 16,
        kept.size // 2,
        4,
        name="last",
    )(*along(total, "dp_1"))


def silu_slope(value):
    sig = jax.nn.sigmoid(value)
    return sig * (1.0 + value * (1.0 - sig))


RATES = (RATE_A, RATE_B, RATE_C)
SIDE = 24


def turned_by(x, shift, far):
    return jnp.where(far == 0, roll_cols(x, shift), roll_cols(x, SIDE - shift))


def rank_of(shape, far):
    at = lax.broadcasted_iota(jnp.int32, shape, 1)
    return jnp.where(far == 0, at, SIDE - 1 - at)


def row_marks(low, rate):
    lead = rate * SIDE
    whole = SIDE * SIDE

    def either(upper, lower):
        return pl.multiple_of(jnp.where(low == 0, upper, lower), 16)

    return dict(
        own=either(0, lead),
        out=either(lead, 0),
        theirs=either(whole, 0),
        inward_from=either(lead, 0),
        inward=either(0, 2 * lead),
        kept=either(lead, 0),
        inner=either(0, lead),
    )


def blocks(x):
    return x.reshape(x.shape[0] // SIDE, SIDE, x.shape[1])


def flat(x):
    return x.reshape(x.shape[0] * SIDE, x.shape[2])


def tap_copies(pos_ref, refs, jobs, held, sems):
    copies = []
    for n, (branch, above, across) in enumerate(jobs):
        a = 1 if above == 1 else jnp.where(pos_ref[2] == 0, above, 2 - above)
        b = 1 if across == 1 else jnp.where(pos_ref[3] == 0, across, 2 - across)
        copies.append(pltpu.make_async_copy(refs[branch].at[a, b], held.at[n], sems.at[n]))
    return copies


OUTER = [(k, a, b) for k in (2, 1, 0) for a, b in ((0, 0), (1, 0), (2, 0), (0, 1), (0, 2))]
INNER = [(k, a, b) for k in (2, 1, 0) for a, b in ((1, 1), (2, 1), (1, 2), (2, 2))]


def outer_parts(pos_ref, x_ref, wa_ref, wb_ref, wc_ref, pre_ref, row_ref, col_ref, diag_ref, ext, acc, held, sems):
    low, far = pos_ref[2], pos_ref[3]
    whole = SIDE * SIDE
    width = pre_ref.shape[2]
    copies = tap_copies(pos_ref, (wa_ref, wb_ref, wc_ref), OUTER, held, sems)
    for copy in copies:
        copy.start()
    first = 0
    for turn, (index, rate) in enumerate(((2, RATE_C), (1, RATE_B), (0, RATE_A))):
        lead = rate * SIDE
        inside = whole - lead
        at = row_marks(low, rate)

        def times(n, rows=slice(None)):
            copies[5 * turn + n].wait()
            return jnp.dot(x_ref[rows, :], held[5 * turn + n], preferred_element_type=F32)

        own_rows = pl.ds(at["own"], whole)
        their_rows = pl.ds(at["theirs"], lead)
        kept_rows = pl.ds(at["kept"], inside)
        to_row = slice(first, first + lead)
        first += lead
        ext[pl.ds(pl.multiple_of(whole - at["theirs"], 16), lead), :] = jnp.zeros((lead, width), F32)
        ext[pl.ds(at["out"], whole), :] = times(0)
        ext[own_rows, :] += times(1)
        ext[pl.ds(at["inward"], inside), :] += times(2, pl.ds(at["inward_from"], inside))
        own = blocks(ext[own_rows, :])
        ours = turned_by(own, rate, far)
        rank = rank_of(own.shape, far)
        pre_ref[index] = flat(jnp.where(rank >= rate, ours, 0.0))
        below = blocks(ext[their_rows, :])
        theirs = turned_by(below, rate, far)
        place = rank_of(below.shape, far)
        acc[:lead, :] = flat(jnp.where(place >= rate, theirs, 0.0))
        if rate == RATE_C:
            col_ref[:whole, :] = flat(jnp.where(rank < rate, ours, 0.0)).astype(BF)
            diag_ref[:lead, :] = flat(jnp.where(place < rate, theirs, 0.0)).astype(BF)
        elif rate == RATE_B:
            half = rate // 2
            col_ref[whole:, :] = flat(jnp.where(rank[:rate] < rate, ours[:rate], own[rate:])).astype(BF)
            part = place[:half] < rate
            diag_ref[RATE_C * SIDE :, :] = flat(jnp.where(part, theirs[:half], below[half:])).astype(BF)
        else:
            have = blocks(col_ref[:whole, :].astype(F32))
            col_ref[:whole, :] = flat(jnp.where(rank >= RATE_C, own, have)).astype(BF)
            have = blocks(diag_ref[:lead, :].astype(F32))
            diag_ref[:lead, :] = flat(jnp.where(place >= RATE_C, below, have)).astype(BF)
        ext[pl.ds(at["out"], whole), :] = times(3)
        pre_ref[index, kept_rows, :] += ext[lead:whole, :]
        acc[:lead, :] += ext[their_rows, :]
        ext[pl.ds(at["out"], whole), :] = times(4)
        own = blocks(ext[lead:whole, :])
        rank = rank_of(own.shape, far)
        pre_ref[index, kept_rows, :] += flat(jnp.where(rank < SIDE - rate, turned_by(own, rate, 1 - far), 0.0))
        below = blocks(ext[their_rows, :])
        theirs = jnp.where(place < SIDE - rate, turned_by(below, rate, 1 - far), 0.0)
        row_ref[to_row, :] = (acc[:lead, :] + flat(theirs)).astype(BF)


def inner_parts(pos_ref, x_ref, part_ref, wp_ref, wa_ref, wb_ref, wc_ref, pre0_ref, pre_ref, acc, held, sems):
    low, far = pos_ref[2], pos_ref[3]
    whole = SIDE * SIDE
    copies = tap_copies(pos_ref, (wa_ref, wb_ref, wc_ref), INNER, held, sems)
    for copy in copies:
        copy.start()
    pre0_ref[...] = jnp.dot(x_ref[...], wp_ref[...], preferred_element_type=F32)
    for turn, (index, rate) in enumerate(((2, RATE_C), (1, RATE_B), (0, RATE_A))):
        lead = rate * SIDE
        inside = whole - lead
        at = row_marks(low, rate)
        from_rows = pl.ds(at["inward_from"], inside)
        to_rows = pl.ds(at["inner"], inside)

        def times(n, rows=slice(None)):
            copies[4 * turn + n].wait()
            return jnp.dot(x_ref[rows, :], held[4 * turn + n], preferred_element_type=F32)

        pre_ref[index] = part_ref[index] + times(0)
        pre_ref[index, to_rows, :] += times(1, from_rows)
        acc[...] = times(2)
        acc[to_rows, :] += times(3, from_rows)
        own = blocks(acc[...])
        rank = rank_of(own.shape, far)
        pre_ref[index] += flat(jnp.where(rank < SIDE - rate, turned_by(own, rate, 1 - far), 0.0))


def outer(pos, centre, w_rate_a, w_rate_b, w_rate_c):
    pixels, chans = centre.shape
    width = w_rate_a.shape[3]
    sends = (RATE_A + RATE_B + RATE_C) * SIDE
    shapes = [((3, pixels, width), F32), ((sends, width), BF), ((sends, width), BF), ((pixels, width), BF)]
    return call(
        outer_parts,
        [jax.ShapeDtypeStruct(*s) for s in shapes],
        1,
        1,
        2 * pixels * chans * width * 14,
        10 * MIB,
        28,
        [
            pltpu.VMEM(((SIDE + RATE_C) * SIDE, width), F32),
            pltpu.VMEM((RATE_C * SIDE, width), F32),
            pltpu.VMEM((len(OUTER), chans, width), BF),
            pltpu.SemaphoreType.DMA((len(OUTER),)),
        ],
        name="outer",
        n_any=3,
    )(pos, centre, w_rate_a, w_rate_b, w_rate_c)


def inner(pos, centre, part, w_point, w_rate_a, w_rate_b, w_rate_c):
    pixels, chans = centre.shape
    width = w_point.shape[1]
    return call(
        inner_parts,
        [jax.ShapeDtypeStruct((pixels, width), F32), jax.ShapeDtypeStruct((3, pixels, width), F32)],
        1,
        3,
        2 * pixels * chans * width * 10,
        10 * MIB,
        26,
        [
            pltpu.VMEM((pixels, width), F32),
            pltpu.VMEM((len(INNER), chans, width), BF),
            pltpu.SemaphoreType.DMA((len(INNER),)),
        ],
        name="inner",
        n_any=3,
    )(pos, centre, part, w_point, w_rate_a, w_rate_b, w_rate_c)


def merge_parts(
    pos_ref, pre0_ref, own_ref, row_ref, col_ref, diag_ref, cot_ref, wp_ref, joined_ref, g_ref, d0_ref, d3_ref, pre
):
    low = pos_ref[2]
    theirs = 1 - pos_ref[3]
    width = pre0_ref.shape[1]
    whole = SIDE * SIDE

    def rows_of(rate):
        return pl.multiple_of(jnp.where(low == 0, (SIDE - rate) * SIDE, 0), 16)

    pre[...] = own_ref[...]
    first = 0
    for index, rate in ((2, RATE_C), (1, RATE_B), (0, RATE_A)):
        lead = rate * SIDE
        pre[index, pl.ds(rows_of(rate), lead), :] += row_ref[first : first + lead, :].astype(F32)
        first += lead

    part = blocks(col_ref[:whole, :].astype(F32))
    rank = rank_of(part.shape, theirs)
    pre[2] += flat(jnp.where(rank < RATE_C, part, 0.0))
    pre[0] += flat(turned_by(jnp.where(rank >= RATE_C, part, 0.0), RATE_A, theirs))
    part = blocks(col_ref[whole:, :].astype(F32))
    rank = rank_of(part.shape, theirs)
    pre[1, : RATE_B * SIDE, :] += flat(jnp.where(rank < RATE_B, part, 0.0))
    pre[1, RATE_B * SIDE :, :] += flat(roll_cols(jnp.where(rank >= RATE_B, part, 0.0), RATE_B))

    part = blocks(diag_ref[: RATE_C * SIDE, :].astype(F32))
    rank = rank_of(part.shape, theirs)
    pre[2, pl.ds(rows_of(RATE_C), RATE_C * SIDE), :] += flat(jnp.where(rank < RATE_C, part, 0.0))
    few = part[:RATE_A]
    few = turned_by(jnp.where(rank[:RATE_A] >= RATE_C, few, 0.0), RATE_A, theirs)
    pre[0, pl.ds(rows_of(RATE_A), RATE_A * SIDE), :] += flat(few)
    part = blocks(diag_ref[RATE_C * SIDE :, :].astype(F32))
    rank = rank_of(part.shape, theirs)
    half = RATE_B // 2
    at = rows_of(RATE_B)
    pre[1, pl.ds(at, half * SIDE), :] += flat(jnp.where(rank < RATE_B, part, 0.0))
    last = pl.multiple_of(at + half * SIDE, 16)
    pre[1, pl.ds(last, half * SIDE), :] += flat(roll_cols(jnp.where(rank >= RATE_B, part, 0.0), RATE_B))

    slopes = {}
    for k in range(4):
        value = pre0_ref[...] if k == 0 else pre[k - 1]
        sig = jax.nn.sigmoid(value)
        joined_ref[:, k * width : (k + 1) * width] = (value * sig).astype(BF)
        if k in (0, 3):
            slopes[k] = sig * (1.0 + value * (1.0 - sig))
    proj_pre = jnp.dot(joined_ref[...], wp_ref[...], preferred_element_type=F32)
    g_proj = (cot_ref[...].astype(F32) * silu_slope(proj_pre)).astype(BF)
    g_ref[...] = g_proj
    for k, out in ((3, d3_ref), (0, d0_ref)):
        back = lax.dot_general(
            g_proj, wp_ref[k * width : (k + 1) * width, :], (((1,), (1,)), ((), ())), preferred_element_type=F32
        )
        out[...] = (back * slopes[k]).astype(BF)


def merge(pos, pre0, own, row, col, diag, cot, w_proj):
    pixels, width = pre0.shape
    block = jax.ShapeDtypeStruct((pixels, width), BF)
    return call(
        merge_parts,
        [jax.ShapeDtypeStruct((pixels, 4 * width), BF), block, block, block],
        1,
        7,
        2 * pixels * width * width * 6,
        6 * 1024 * 1024,
        18,
        [pltpu.VMEM((3, pixels, width), F32)],
        name="merge",
    )(pos, pre0, own, row, col, diag, cot, w_proj)


def pair_grads(pos_ref, joined_ref, g_ref, x_ref, d0_ref, keep_ref, *send_refs):
    core = pos_ref[4]
    over = (((0,), (0,)), ((), ()))
    grad_proj = lax.dot_general(joined_ref[...], g_ref[...], over, preferred_element_type=F32)
    grad_point = lax.dot_general(x_ref[...], d0_ref[...], over, preferred_element_type=F32)
    keep_ref[...] = jnp.where(core == 0, grad_proj, grad_point)
    half = send_refs[0].shape[0]
    for k, send_ref in enumerate(send_refs):
        part = slice(k * half, (k + 1) * half)
        send_ref[...] = jnp.where(core == 0, grad_point[part], grad_proj[part]).astype(BF)


def shards(features, cotangent, w_point, w_rate_a, w_rate_b, w_rate_c, w_proj, bucket_slot):
    image = features[0]
    rows_dev, cols_dev, chans = image.shape
    pixels = rows_dev * cols_dev
    width = w_point.shape[1]
    row, col, core = (lax.axis_index(n) for n in ("row", "col", "dp_2"))
    at_y, at_z = lax.axis_index("dp_0"), lax.axis_index("dp_1")
    pos = jnp.stack([2 * row + col, at_y, row, col, core, at_z]).astype(jnp.int32)
    replicas = lax.axis_size(DP)
    slot_count = replicas * (bucket_slot.shape[0] // replicas + 1)
    place = place_slots(bucket_slot, core, slot_count)
    centre = image.reshape(pixels, chans)
    weights = [pltpu.with_memory_space_constraint(w, pltpu.HBM) for w in (w_rate_a, w_rate_b, w_rate_c)]
    picked = pick(pos, centre)
    centre, *picked = lax.optimization_barrier((centre, *picked))
    got = [picked[0]] + [flip(picked[k], k) for k in (1, 2, 3)]
    part, *parts = outer(pos, centre, *weights)
    parts, got = lax.optimization_barrier((parts, got))
    to_row, to_col, to_diag = parts
    parts = [flip(to_row, 2), flip(to_col, 1), flip(to_diag, 3)]
    turned = turn(pos, got)
    pre0, own = inner(pos, centre, part, w_point, *weights)
    parts, pre0, own, turned = lax.optimization_barrier((parts, pre0, own, turned))
    joined, g_proj, delta0, delta3 = merge(
        pos, pre0, own, *parts, cotangent[0].reshape(pixels, width), w_proj
    )
    shared = [delta3] + [flip(delta3, k) for k in (1, 2, 3)]
    block = (4 * width, width)
    kept, *sent = call(
        pair_grads,
        [jax.ShapeDtypeStruct(block, F32)] + [jax.ShapeDtypeStruct((2 * width, width), BF)] * 2,
        1,
        4,
        4 * pixels * chans * width,
        4 * 1024 * 1024,
        16,
        name="pair",
    )(pos, joined, g_proj, centre, delta0)
    got = [swap_core(part) for part in sent]
    got, shared = lax.optimization_barrier((got, shared))
    by_owner = split_pair(pos, kept, got)
    by_owner, shared = lax.optimization_barrier((by_owner, shared))
    by_owner = [by_owner[0]] + [flip(by_owner[k], k) for k in (1, 2, 3)]
    kept, sent = tap_slots(pos, place, shared, turned, slot_count)
    sent, by_owner = lax.optimization_barrier((sent, by_owner))
    mine, other = sum_pair(by_owner)
    return reduce_slots(pos, place, kept, sent, mine, other)


def solution(mesh):
    torus = Mesh(
        mesh.devices.reshape(mesh.shape["row"], mesh.shape["col"], 4, 4, 2),
        ("row", "col", "dp_0", "dp_1", "dp_2"),
    )
    in_specs = (P(DP, "row", "col", None), P(DP, "row", "col", None), P(), P(), P(), P(), P(), P())
    out_specs = P(DP, ("row", "col"))
    return jax.shard_map(
        shards, mesh=torus, in_specs=in_specs, out_specs=out_specs, check_vma=False
    )
```

time: 127 us -> 99.3 us (0.78)
  waiting for transfers between devices: 44.9 us -> 29.4 us
  other arithmetic: 4.38 us -> 0.1 us
  starting transfers between devices: 34.8 us -> 31.1 us
  local copies, waits for them, and re-layouts: 3.78 us -> 1.38 us
  Pallas kernels: 38.6 us -> 37 us
    ppermute x9 -> x6, waiting for transfers between devices: 16.1 us -> 10.8 us  [along(): lax.ppermute(blocks[s], axis, [(i, (i + s) % count) for i in range(count)])]
    ppermute x9 -> x6, starting transfers between devices: 17.5 us -> 12.5 us  [along(): lax.ppermute(blocks[s], axis, [(i, (i + s) % count) for i in range(count)])]
    ppermute x4, waiting for transfers between devices: 5.31 us -> 0.63 us  [flip(): return lax.ppermute(x, 'row', [(0, 1), (1, 0)])]
    pallas_call x3 -> x8, Pallas kernels: 27.4 us -> 31.6 us  [the longest x1 13.6 us: outer(): call(outer_parts, [jax.ShapeDtypeStruct(*s) for s in shapes], 1, 1, 2 * p...]
    add x6 -> x0, other arithmetic: 3.82 us -> none  [the longest x1 1.68 us: reduce_slots(): total = kept + swap_core(sent).astype(F32)]
    ppermute x4, waiting for transfers between devices: 10.5 us -> 7.24 us  [flip(): return lax.ppermute(x, ('row', 'col'), [(0, 3), (3, 0), (1, 2), (2, 1)])]
    pallas_call x1, Pallas kernels: 4.84 us -> 2.24 us  [merge(): call(merge_parts, [jax.ShapeDtypeStruct((pixels, 4 * width), BF), block,...]
    ppermute x4, starting transfers between devices: 3.18 us -> 5.21 us  [flip(): return lax.ppermute(x, 'row', [(0, 1), (1, 0)])]
  transfers between devices with their start and end apart: 23 -> 22, of which waited for: 14 -> 12; matrix products, arithmetic and copies ran while one was open for 1% -> 0% of each run, Pallas kernels for 16% -> 30%
where the time goes in v1:
time: 99.3 us; the launch traced here: 99.2 us
  Pallas kernels  37 us (37%)
  starting transfers between devices  31.1 us (31%)
  waiting for transfers between devices  29.4 us (30%)
  local copies, waits for them, and re-layouts  1.38 us (1%)
    pallas_call x1, Pallas kernels, outer(): call(outer_parts, [jax.ShapeDtypeStruct(*s) for s in shapes], 1, 1, 2 * p...  13.6 us
    ppermute x6, starting transfers between devices, along(): lax.ppermute(blocks[s], axis, [(i, (i + s) % count) for i in range(count)])  12.5 us
    ppermute x6, waiting for transfers between devices, along(): lax.ppermute(blocks[s], axis, [(i, (i + s) % count) for i in range(count)])  10.8 us
    pallas_call x1, Pallas kernels, inner(): call(inner_parts, [jax.ShapeDtypeStruct((pixels, width), F32), jax.ShapeD...  9.45 us
    ppermute x4, starting transfers between devices, flip(): return lax.ppermute(x, 'col', [(0, 1), (1, 0)])  8.34 us
    ppermute x4, waiting for transfers between devices, flip(): return lax.ppermute(x, 'col', [(0, 1), (1, 0)])  7.52 us
    ppermute x4, waiting for transfers between devices, flip(): return lax.ppermute(x, ('row', 'col'), [(0, 3), (3, 0), (1, 2), (2, 1)])  7.24 us
    ppermute x4, starting transfers between devices, flip(): return lax.ppermute(x, 'row', [(0, 1), (1, 0)])  5.21 us
  transfers between devices with their start and end apart: 22, of which 12 were waited for; matrix products, arithmetic and copies ran while one was open for 0% of the time, Pallas kernels for 30%

profile of v1, /device:TPU:0, one launch (start us, length us, event | category | flops | bytes accessed | tf_op | source)
XLA Modules:
  0.0 99.2 jit_solution(8709187141130789173)
XLA Ops:
  0.1 1.3 %copy-done = bf16[1,24,24,1024]{3,2,1,0:T(8,128)(2,1)S(1)} copy-done((bf16[1,24,24,1024]{3,2,1,0:T(8,128)(2,1)S(1)}, bf16[1,24,24,1024]{3,2,1,0:T(8,128)(2,1)}, u32[]{:S(2)}) %copy-start) | copy-done | bytes 1179672
  1.4 1.9 %pick.1 = (bf16[576,256]{1,0:T(8,128)(2,1)S(1)}, bf16[576,256]{1,0:T(8,128)(2,1)S(1)}, bf16[576,256]{1,0:T(8,128)(2,1)S(1)}, bf16[576,256]{1,0:T(8,128)(2,1)S(1)}) custom-call(s32[6]{0:T(128)S(1)} %stack.27.pos_ref, bf16[576,1024]{1,0:T(8,128)(2,1)S(1)} %bitcast.8), custom_call_target="tpu_custom_call" | custom-call | flops 1207959552 | bytes 2359296 | tf_op jit(solution)/shard_map/pick/pallas_call | solution.py:196
  3.3 3.2 %collective-permute-start = (bf16[576,256]{1,0:T(8,128)(2,1)S(1)}, bf16[576,256]{1,0:T(8,128)(2,1)S(1)}, u32[]{:S(2)}, u32[]{:S(2)}) collective-permute-start(bf16[576,256]{1,0:T(8,128)(2,1)S(1)} %get-tuple-element.82), channel_id=1, source_target_pairs={{0,32},{32,0},{1,33},{33,1},{2,34},{34,2},{3,35},{35,3},{4,36},{36... | collective-permute-start | bytes 884744 | tf_op jit(solution)/shard_map/ppermute | solution.py:22
  7.7 13.6 %outer.1 = (f32[3,576,256]{2,1,0:T(8,128)S(1)}, bf16[864,256]{1,0:T(8,128)(2,1)S(1)}, bf16[864,256]{1,0:T(8,128)(2,1)S(1)}, bf16[576,256]{1,0:T(8,128)(2,1)S(1)}) custom-call(s32[6]{0:T(128)S(1)} %stack.27.pos_ref, bf16[576,1024]{1,0:T(8,128)(2,1)S(1)} %bitcast.9, bf16[3,3,1024,256]{3,2,1,0:T(8,128)(2,1)} %wa_ref.3, bf16[3,3,1024,256]{3,2,1,0:T(8,128)(2,1)} %wb_ref.3, ...), custom_call_target="tpu_custom_call" | custom-call | flops 4227858432 | bytes 10485760 | tf_op jit(solution)/shard_map/outer/pallas_call | solution.py:458
  21.3 1.7 %collective-permute-start.3 = (bf16[864,256]{1,0:T(8,128)(2,1)S(1)}, bf16[864,256]{1,0:T(8,128)(2,1)S(1)}, u32[]{:S(2)}, u32[]{:S(2)}) collective-permute-start(bf16[864,256]{1,0:T(8,128)(2,1)S(1)} %get-tuple-element.85), channel_id=1, source_target_pairs={{0,64},{64,0},{1,65},{65,1},{2,66},{66,2},{3,67},{67,3},{4,68},{68... | collective-permute-start | bytes 1327112 | tf_op jit(solution)/shard_map/ppermute | solution.py:24
  23.0 2.7 %collective-permute-start.4 = (bf16[864,256]{1,0:T(8,128)(2,1)S(1)}, bf16[864,256]{1,0:T(8,128)(2,1)S(1)}, u32[]{:S(2)}, u32[]{:S(2)}) collective-permute-start(bf16[864,256]{1,0:T(8,128)(2,1)S(1)} %get-tuple-element.86), channel_id=1, source_target_pairs={{0,32},{32,0},{1,33},{33,1},{2,34},{34,2},{3,35},{35,3},{4,36},{36... | collective-permute-start | bytes 1327112 | tf_op jit(solution)/shard_map/ppermute | solution.py:22
  26.1 9.5 %inner.1 = (f32[576,256]{1,0:T(8,128)S(1)}, f32[3,576,256]{2,1,0:T(8,128)S(1)}) custom-call(s32[6]{0:T(128)S(1)} %stack.27.pos_ref, bf16[576,1024]{1,0:T(8,128)(2,1)S(1)} %bitcast.10, f32[3,576,256]{2,1,0:T(8,128)S(1)} %get-tuple-element.88.part_ref, bf16[1024,256]{1,0:T(8,128)(2,1)S(1)} %copy-done.2, bf16[3,3,1024,256]{3,2,1,0:T(8,128)(2,1)} %wa_ref.3, ...), custom_call_target="tpu_custom_call" | custom-call | flops 3019898880 | bytes 10485760 | tf_op jit(solution)/shard_map/inner/pallas_call | solution.py:480
  35.6 1.2 %turn.1.xt_ref = bf16[2,256,1152]{2,1,0:T(8,128)(2,1)S(1)} custom-call(s32[6]{0:T(128)S(1)} %stack.27.pos_ref, bf16[576,256]{1,0:T(8,128)(2,1)S(1)} %get-tuple-element.91.x0, bf16[576,256]{1,0:T(8,128)(2,1)S(1)} %collective-permute-done.x1, bf16[576,256]{1,0:T(8,128)(2,1)S(1)} %collective-permute-done.1.x2, bf16[576,256]{1,0:T(8,128)(2,1)S(1)} %collective-permute-done.2.x3), custom_call_target="tpu_custom_call" | custom-call | flops 301989888 | bytes 2359296 | tf_op jit(solution)/shard_map/turn/pallas_call | solution.py:203
  36.8 7.5 %collective-permute-done.4.col_ref = bf16[864,256]{1,0:T(8,128)(2,1)S(1)} collective-permute-done((bf16[864,256]{1,0:T(8,128)(2,1)S(1)}, bf16[864,256]{1,0:T(8,128)(2,1)S(1)}, u32[]{:S(2)}, u32[]{:S(2)}) %collective-permute-start.4) | collective-permute-done | bytes 442400 | tf_op jit(solution)/shard_map/ppermute | solution.py:22
  44.3 2.2 %merge.1 = (bf16[576,1024]{1,0:T(8,128)(2,1)S(1)}, bf16[576,256]{1,0:T(8,128)(2,1)S(1)}, bf16[576,256]{1,0:T(8,128)(2,1)S(1)}, bf16[576,256]{1,0:T(8,128)(2,1)S(1)}) custom-call(s32[6]{0:T(128)S(1)} %stack.27.pos_ref, f32[576,256]{1,0:T(8,128)S(1)} %get-tuple-element.95.pre0_ref, f32[3,576,256]{2,1,0:T(8,128)S(1)} %get-tuple-element.96.own_ref, ...), custom_call_target="tpu_custom_call" | custom-call | flops 452984832 | bytes 6291456 | tf_op jit(solution)/shard_map/merge/pallas_call | solution.py:559
  47.2 1.5 %collective-permute-start.8 = (bf16[576,256]{1,0:T(8,128)(2,1)S(1)}, bf16[576,256]{1,0:T(8,128)(2,1)S(1)}, u32[]{:S(2)}, u32[]{:S(2)}) collective-permute-start(bf16[576,256]{1,0:T(8,128)(2,1)S(1)} %get-tuple-element.117.d0), channel_id=1, source_target_pairs={{0,32},{32,0},{1,33},{33,1},{2,34},{34,2},{3,35},{35,3},{4,36},{36... | collective-permute-start | bytes 884744 | tf_op jit(solution)/shard_map/ppermute | solution.py:22
  48.7 2.0 %collective-permute-start.9 = (bf16[576,256]{1,0:T(8,128)(2,1)S(1)}, bf16[576,256]{1,0:T(8,128)(2,1)S(1)}, u32[]{:S(2)}, u32[]{:S(2)}) collective-permute-start(bf16[576,256]{1,0:T(8,128)(2,1)S(1)} %get-tuple-element.117.d0), channel_id=1, source_target_pairs={{0,64},{64,0},{1,65},{65,1},{2,66},{66,2},{3,67},{67,3},{4,68},{68... | collective-permute-start | bytes 884744 | tf_op jit(solution)/shard_map/ppermute | solution.py:24
  50.7 1.6 %pair.1 = (f32[1024,256]{1,0:T(8,128)S(1)}, bf16[512,256]{1,0:T(8,128)(2,1)S(1)}, bf16[512,256]{1,0:T(8,128)(2,1)S(1)}) custom-call(s32[6]{0:T(128)S(1)} %stack.27.pos_ref, bf16[576,1024]{1,0:T(8,128)(2,1)S(1)} %get-tuple-element.100.joined_ref, bf16[576,256]{1,0:T(8,128)(2,1)S(1)} %get-tuple-element.101.g_ref, bf16[576,1024]{1,0:T(8,128)(2,1)S(1)} %bitcast.11, ...), custom_call_target="tpu_custom_call" | custom-call | flops 603979776 | bytes 4194304 | tf_op jit(solution)/shard_map/pair/pallas_call | solution.py:612
  53.0 1.0 %collective-permute-done.6.got0 = bf16[512,256]{1,0:T(8,128)(2,1)S(1)} collective-permute-done((bf16[512,256]{1,0:T(8,128)(2,1)S(1)}, bf16[512,256]{1,0:T(8,128)(2,1)S(1)}, u32[]{:S(2)}, u32[]{:S(2)}) %collective-permute-start.6) | collective-permute-done | bytes 262176 | tf_op jit(solution)/shard_map/ppermute | solution.py:190
  54.3 6.8 %collective-permute-done.10.d3 = bf16[576,256]{1,0:T(8,128)(2,1)S(1)} collective-permute-done((bf16[576,256]{1,0:T(8,128)(2,1)S(1)}, bf16[576,256]{1,0:T(8,128)(2,1)S(1)}, u32[]{:S(2)}, u32[]{:S(2)}) %collective-permute-start.10) | collective-permute-done | bytes 294944 | tf_op jit(solution)/shard_map/ppermute | solution.py:25
  62.5 1.0 collective-permute-start.11
  63.4 0.9 collective-permute-start.12
  64.3 2.3 %collective-permute-start.13 = (bf16[16,16,256]{2,1,0:T(8,128)(2,1)S(1)}, bf16[16,16,256]{2,1,0:T(8,128)(2,1)S(1)}, u32[]{:S(2)}, u32[]{:S(2)}) collective-permute-start(bf16[16,16,256]{2,1,0:T(8,128)(2,1)S(1)} %get-tuple-element.127), channel_id=1, source_target_pairs={{0,96},{96,0},{32,64},{64,32},{1,97},{97,1},{33,65},{65,33},{2,98}... | collective-permute-start | bytes 393224 | tf_op jit(solution)/shard_map/ppermute | solution.py:25
  66.6 3.6 %taps.1 = (f32[96,16,256]{2,1,0:T(8,128)S(1)}, bf16[96,16,256]{2,1,0:T(8,128)(2,1)S(1)}) custom-call(s32[6]{0:T(128)S(1)} %stack.27.pos_ref, s32[176]{0:T(256)S(1)} %fusion.1.place_ref, bf16[576,256]{1,0:T(8,128)(2,1)S(1)} %get-tuple-element.117.d0, bf16[576,256]{1,0:T(8,128)(2,1)S(1)} %collective-permute-done.8.d1, ...), custom_call_target="tpu_custom_call" | custom-call | flops 2113929216 | bytes 8388608 | tf_op jit(solution)/shard_map/taps/pallas_call | solution.py:249
  71.3 1.8 %collective-permute-done.15.other_ref = bf16[16,16,256]{2,1,0:T(8,128)(2,1)S(1)} collective-permute-done((bf16[16,16,256]{2,1,0:T(8,128)(2,1)S(1)}, bf16[16,16,256]{2,1,0:T(8,128)(2,1)S(1)}, u32[]{:S(2)}, u32[]{:S(2)}) %collective-permute-start.15) | collective-permute-done | bytes 131104 | tf_op jit(solution)/shard_map/ppermute | solution.py:190
  73.2 1.3 %owners.1 = (f32[24,16,256]{2,1,0:T(8,128)S(1)}, bf16[24,16,256]{2,1,0:T(8,128)(2,1)S(1)}, bf16[24,16,256]{2,1,0:T(8,128)(2,1)S(1)}, bf16[24,16,256]{2,1,0:T(8,128)(2,1)S(1)}) custom-call(s32[6]{0:T(128)S(1)} %stack.27.pos_ref, s32[176]{0:T(256)S(1)} %fusion.1.place_ref, f32[96,16,256]{2,1,0:T(8,128)S(1)} %get-tuple-element.122.keep_ref, ...), custom_call_target="tpu_custom_call" | custom-call | flops 393216 | bytes 3145728 | tf_op jit(solution)/shard_map/owners/pallas_call | solution.py:276
  74.4 1.7 %collective-permute-start.16 = (bf16[24,16,256]{2,1,0:T(8,128)(2,1)S(1)}, bf16[24,16,256]{2,1,0:T(8,128)(2,1)S(1)}, u32[]{:S(2)}, u32[]{:S(2)}) collective-permute-start(bf16[24,16,256]{2,1,0:T(8,128)(2,1)S(1)} %get-tuple-element.134), channel_id=1, source_target_pairs={{0,8},{8,16},{16,24},{24,0},{1,9},{9,17},{17,25},{25,1},{2,10},{10... | collective-permute-start | bytes 589832 | tf_op jit(solution)/shard_map/ppermute | solution.py:185
  76.1 2.9 %collective-permute-start.17 = (bf16[24,16,256]{2,1,0:T(8,128)(2,1)S(1)}, bf16[24,16,256]{2,1,0:T(8,128)(2,1)S(1)}, u32[]{:S(2)}, u32[]{:S(2)}) collective-permute-start(bf16[24,16,256]{2,1,0:T(8,128)(2,1)S(1)} %get-tuple-element.135), channel_id=1, source_target_pairs={{0,16},{8,24},{16,0},{24,8},{1,17},{9,25},{17,1},{25,9},{2,18},{10... | collective-permute-start | bytes 589832 | tf_op jit(solution)/shard_map/ppermute | solution.py:185
  79.0 1.3 %collective-permute-start.18 = (bf16[24,16,256]{2,1,0:T(8,128)(2,1)S(1)}, bf16[24,16,256]{2,1,0:T(8,128)(2,1)S(1)}, u32[]{:S(2)}, u32[]{:S(2)}) collective-permute-start(bf16[24,16,256]{2,1,0:T(8,128)(2,1)S(1)} %get-tuple-element.136), channel_id=1, source_target_pairs={{0,24},{8,0},{16,8},{24,16},{1,25},{9,1},{17,9},{25,17},{2,26},{10... | collective-permute-start | bytes 589832 | tf_op jit(solution)/shard_map/ppermute | solution.py:185
  80.3 2.4 %collective-permute-done.16.refs_1_ = bf16[24,16,256]{2,1,0:T(8,128)(2,1)S(1)} collective-permute-done((bf16[24,16,256]{2,1,0:T(8,128)(2,1)S(1)}, bf16[24,16,256]{2,1,0:T(8,128)(2,1)S(1)}, u32[]{:S(2)}, u32[]{:S(2)}) %collective-permute-start.16) | collective-permute-done | bytes 196640 | tf_op jit(solution)/shard_map/ppermute | solution.py:185
  82.7 5.4 %collective-permute-done.17.refs_2_ = bf16[24,16,256]{2,1,0:T(8,128)(2,1)S(1)} collective-permute-done((bf16[24,16,256]{2,1,0:T(8,128)(2,1)S(1)}, bf16[24,16,256]{2,1,0:T(8,128)(2,1)S(1)}, u32[]{:S(2)}, u32[]{:S(2)}) %collective-permute-start.17) | collective-permute-done | bytes 196640 | tf_op jit(solution)/shard_map/ppermute | solution.py:185
  88.8 2.0 %collective-permute-start.19 = (bf16[6,16,256]{2,1,0:T(8,128)(2,1)S(1)}, bf16[6,16,256]{2,1,0:T(8,128)(2,1)S(1)}, u32[]{:S(2)}, u32[]{:S(2)}) collective-permute-start(bf16[6,16,256]{2,1,0:T(8,128)(2,1)S(1)} %get-tuple-element.138), channel_id=1, source_target_pairs={{0,2},{2,4},{4,6},{6,0},{1,3},{3,5},{5,7},{7,1},{8,10},{10,12},{12... | collective-permute-start | bytes 147464 | tf_op jit(solution)/shard_map/ppermute | solution.py:185
  90.8 3.6 %collective-permute-start.20 = (bf16[6,16,256]{2,1,0:T(8,128)(2,1)S(1)}, bf16[6,16,256]{2,1,0:T(8,128)(2,1)S(1)}, u32[]{:S(2)}, u32[]{:S(2)}) collective-permute-start(bf16[6,16,256]{2,1,0:T(8,128)(2,1)S(1)} %get-tuple-element.139), channel_id=1, source_target_pairs={{0,4},{2,6},{4,0},{6,2},{1,5},{3,7},{5,1},{7,3},{8,12},{10,14},{12... | collective-permute-start | bytes 147464 | tf_op jit(solution)/shard_map/ppermute | solution.py:185
  94.3 1.0 %collective-permute-start.21 = (bf16[6,16,256]{2,1,0:T(8,128)(2,1)S(1)}, bf16[6,16,256]{2,1,0:T(8,128)(2,1)S(1)}, u32[]{:S(2)}, u32[]{:S(2)}) collective-permute-start(bf16[6,16,256]{2,1,0:T(8,128)(2,1)S(1)} %get-tuple-element.140), channel_id=1, source_target_pairs={{0,6},{2,0},{4,2},{6,4},{1,7},{3,1},{5,3},{7,5},{8,14},{10,8},{12,... | collective-permute-start | bytes 147464 | tf_op jit(solution)/shard_map/ppermute | solution.py:185
  95.5 1.5 %collective-permute-done.20.r2 = bf16[6,16,256]{2,1,0:T(8,128)(2,1)S(1)} collective-permute-done((bf16[6,16,256]{2,1,0:T(8,128)(2,1)S(1)}, bf16[6,16,256]{2,1,0:T(8,128)(2,1)S(1)}, u32[]{:S(2)}, u32[]{:S(2)}) %collective-permute-start.20) | collective-permute-done | bytes 49184 | tf_op jit(solution)/shard_map/ppermute | solution.py:185
  96.9 1.5 %collective-permute-done.21.r3 = bf16[6,16,256]{2,1,0:T(8,128)(2,1)S(1)} collective-permute-done((bf16[6,16,256]{2,1,0:T(8,128)(2,1)S(1)}, bf16[6,16,256]{2,1,0:T(8,128)(2,1)S(1)}, u32[]{:S(2)}, u32[]{:S(2)}) %collective-permute-start.21) | collective-permute-done | bytes 49184 | tf_op jit(solution)/shard_map/ppermute | solution.py:185
  98.4 0.7 last.1
  (38 shorter events, 6.5 us)
Async XLA Ops:
  0.1 1.3 %copy-start = (bf16[1,24,24,1024]{3,2,1,0:T(8,128)(2,1)S(1)}, bf16[1,24,24,1024]{3,2,1,0:T(8,128)(2,1)}, u32[]{:S(2)}) copy-start(bf16[1,24,24,1024]{3,2,1,0:T(8,128)(2,1)} %param.8) | copy-start | bytes 3538948
  1.4 6.3 %copy-start.1 = (bf16[1,24,24,1024]{3,2,1,0:T(8,128)(2,1)S(1)}, bf16[1,24,24,1024]{3,2,1,0:T(8,128)(2,1)}, u32[]{:S(2)}) copy-start(bf16[1,24,24,1024]{3,2,1,0:T(8,128)(2,1)} %param.8) | copy-start | bytes 3538948
  3.3 22.8 %copy-start.2 = (bf16[1024,256]{1,0:T(8,128)(2,1)S(1)}, bf16[1024,256]{1,0:T(8,128)(2,1)}, u32[]{:S(2)}) copy-start(bf16[1024,256]{1,0:T(8,128)(2,1)} %wp_ref.2) | copy-start | bytes 1572868
  3.3 17.9 %collective-permute-start = (bf16[576,256]{1,0:T(8,128)(2,1)S(1)}, bf16[576,256]{1,0:T(8,128)(2,1)S(1)}, u32[]{:S(2)}, u32[]{:S(2)}) collective-permute-start(bf16[576,256]{1,0:T(8,128)(2,1)S(1)} %get-tuple-element.82), channel_id=1, source_target_pairs={{0,32},{32,0},{1,33},{33,1},{2,34},{34,2},{3,35},{35,3},{4,36},{36... | collective-permute-start | bytes 884744 | tf_op jit(solution)/shard_map/ppermute | solution.py:22
  6.5 14.8 %collective-permute-start.1 = (bf16[576,256]{1,0:T(8,128)(2,1)S(1)}, bf16[576,256]{1,0:T(8,128)(2,1)S(1)}, u32[]{:S(2)}, u32[]{:S(2)}) collective-permute-start(bf16[576,256]{1,0:T(8,128)(2,1)S(1)} %get-tuple-element.83), channel_id=1, source_target_pairs={{0,64},{64,0},{1,65},{65,1},{2,66},{66,2},{3,67},{67,3},{4,68},{68... | collective-permute-start | bytes 884744 | tf_op jit(solution)/shard_map/ppermute | solution.py:24
  7.1 14.2 %collective-permute-start.2 = (bf16[576,256]{1,0:T(8,128)(2,1)S(1)}, bf16[576,256]{1,0:T(8,128)(2,1)S(1)}, u32[]{:S(2)}, u32[]{:S(2)}) collective-permute-start(bf16[576,256]{1,0:T(8,128)(2,1)S(1)} %get-tuple-element.84), channel_id=1, source_target_pairs={{0,96},{96,0},{32,64},{64,32},{1,97},{97,1},{33,65},{65,33},{2,98}... | collective-permute-start | bytes 884744 | tf_op jit(solution)/shard_map/ppermute | solution.py:25
  21.3 15.5 %collective-permute-start.3 = (bf16[864,256]{1,0:T(8,128)(2,1)S(1)}, bf16[864,256]{1,0:T(8,128)(2,1)S(1)}, u32[]{:S(2)}, u32[]{:S(2)}) collective-permute-start(bf16[864,256]{1,0:T(8,128)(2,1)S(1)} %get-tuple-element.85), channel_id=1, source_target_pairs={{0,64},{64,0},{1,65},{65,1},{2,66},{66,2},{3,67},{67,3},{4,68},{68... | collective-permute-start | bytes 1327112 | tf_op jit(solution)/shard_map/ppermute | solution.py:24
  23.0 21.3 %collective-permute-start.4 = (bf16[864,256]{1,0:T(8,128)(2,1)S(1)}, bf16[864,256]{1,0:T(8,128)(2,1)S(1)}, u32[]{:S(2)}, u32[]{:S(2)}) collective-permute-start(bf16[864,256]{1,0:T(8,128)(2,1)S(1)} %get-tuple-element.86), channel_id=1, source_target_pairs={{0,32},{32,0},{1,33},{33,1},{2,34},{34,2},{3,35},{35,3},{4,36},{36... | collective-permute-start | bytes 1327112 | tf_op jit(solution)/shard_map/ppermute | solution.py:22
  25.8 11.0 %collective-permute-start.5 = (bf16[576,256]{1,0:T(8,128)(2,1)S(1)}, bf16[576,256]{1,0:T(8,128)(2,1)S(1)}, u32[]{:S(2)}, u32[]{:S(2)}) collective-permute-start(bf16[576,256]{1,0:T(8,128)(2,1)S(1)} %get-tuple-element.87), channel_id=1, source_target_pairs={{0,96},{96,0},{32,64},{64,32},{1,97},{97,1},{33,65},{65,33},{2,98}... | collective-permute-start | bytes 884744 | tf_op jit(solution)/shard_map/ppermute | solution.py:25
  35.5 8.7 %copy-start.3 = (bf16[1024,256]{1,0:T(8,128)(2,1)S(1)}, bf16[1024,256]{1,0:T(8,128)(2,1)}, u32[]{:S(2)}) copy-start(bf16[1024,256]{1,0:T(8,128)(2,1)} %wp_ref.3) | copy-start | bytes 1572868
  35.6 8.7 %copy-start.4 = (bf16[1,24,24,256]{3,2,1,0:T(8,128)(2,1)S(1)}, bf16[1,24,24,256]{3,2,1,0:T(8,128)(2,1)}, u32[]{:S(2)}) copy-start(bf16[1,24,24,256]{3,2,1,0:T(8,128)(2,1)} %param.9) | copy-start | bytes 884740
  46.5 6.4 %copy-start.5 = (s32[176]{0:T(256)S(1)}, s32[176]{0:T(256)}, u32[]{:S(2)}) copy-start(s32[176]{0:T(256)} %param.15) | copy-start | bytes 2116
  46.5 14.6 %collective-permute-start.10 = (bf16[576,256]{1,0:T(8,128)(2,1)S(1)}, bf16[576,256]{1,0:T(8,128)(2,1)S(1)}, u32[]{:S(2)}, u32[]{:S(2)}) collective-permute-start(bf16[576,256]{1,0:T(8,128)(2,1)S(1)} %get-tuple-element.117.d0), channel_id=1, source_target_pairs={{0,96},{96,0},{32,64},{64,32},{1,97},{97,1},{33,65},{65,33},{2,98}... | collective-permute-start | bytes 884744 | tf_op jit(solution)/shard_map/ppermute | solution.py:25
  47.2 13.9 %collective-permute-start.8 = (bf16[576,256]{1,0:T(8,128)(2,1)S(1)}, bf16[576,256]{1,0:T(8,128)(2,1)S(1)}, u32[]{:S(2)}, u32[]{:S(2)}) collective-permute-start(bf16[576,256]{1,0:T(8,128)(2,1)S(1)} %get-tuple-element.117.d0), channel_id=1, source_target_pairs={{0,32},{32,0},{1,33},{33,1},{2,34},{34,2},{3,35},{35,3},{4,36},{36... | collective-permute-start | bytes 884744 | tf_op jit(solution)/shard_map/ppermute | solution.py:22
  48.7 13.1 %collective-permute-start.9 = (bf16[576,256]{1,0:T(8,128)(2,1)S(1)}, bf16[576,256]{1,0:T(8,128)(2,1)S(1)}, u32[]{:S(2)}, u32[]{:S(2)}) collective-permute-start(bf16[576,256]{1,0:T(8,128)(2,1)S(1)} %get-tuple-element.117.d0), channel_id=1, source_target_pairs={{0,64},{64,0},{1,65},{65,1},{2,66},{66,2},{3,67},{67,3},{4,68},{68... | collective-permute-start | bytes 884744 | tf_op jit(solution)/shard_map/ppermute | solution.py:24
  52.4 1.6 %collective-permute-start.6 = (bf16[512,256]{1,0:T(8,128)(2,1)S(1)}, bf16[512,256]{1,0:T(8,128)(2,1)S(1)}, u32[]{:S(2)}, u32[]{:S(2)}) collective-permute-start(bf16[512,256]{1,0:T(8,128)(2,1)S(1)} %get-tuple-element.104), channel_id=1, source_target_pairs={{0,1},{1,0},{2,3},{3,2},{4,5},{5,4},{6,7},{7,6},{8,9},{9,8},{10,11... | collective-permute-start | bytes 786440 | tf_op jit(solution)/shard_map/ppermute | solution.py:190
  52.4 1.9 %collective-permute-start.7 = (bf16[512,256]{1,0:T(8,128)(2,1)S(1)}, bf16[512,256]{1,0:T(8,128)(2,1)S(1)}, u32[]{:S(2)}, u32[]{:S(2)}) collective-permute-start(bf16[512,256]{1,0:T(8,128)(2,1)S(1)} %get-tuple-element.105), channel_id=1, source_target_pairs={{0,1},{1,0},{2,3},{3,2},{4,5},{5,4},{6,7},{7,6},{8,9},{9,8},{10,11... | collective-permute-start | bytes 786440 | tf_op jit(solution)/shard_map/ppermute | solution.py:190
  62.5 7.7 %collective-permute-start.11 = (bf16[16,16,256]{2,1,0:T(8,128)(2,1)S(1)}, bf16[16,16,256]{2,1,0:T(8,128)(2,1)S(1)}, u32[]{:S(2)}, u32[]{:S(2)}) collective-permute-start(bf16[16,16,256]{2,1,0:T(8,128)(2,1)S(1)} %get-tuple-element.125), channel_id=1, source_target_pairs={{0,32},{32,0},{1,33},{33,1},{2,34},{34,2},{3,35},{35,3},{4,36},{36... | collective-permute-start | bytes 393224 | tf_op jit(solution)/shard_map/ppermute | solution.py:22
  63.4 6.8 %collective-permute-start.12 = (bf16[16,16,256]{2,1,0:T(8,128)(2,1)S(1)}, bf16[16,16,256]{2,1,0:T(8,128)(2,1)S(1)}, u32[]{:S(2)}, u32[]{:S(2)}) collective-permute-start(bf16[16,16,256]{2,1,0:T(8,128)(2,1)S(1)} %get-tuple-element.126), channel_id=1, source_target_pairs={{0,64},{64,0},{1,65},{65,1},{2,66},{66,2},{3,67},{67,3},{4,68},{68... | collective-permute-start | bytes 393224 | tf_op jit(solution)/shard_map/ppermute | solution.py:24
  64.3 6.4 %collective-permute-start.13 = (bf16[16,16,256]{2,1,0:T(8,128)(2,1)S(1)}, bf16[16,16,256]{2,1,0:T(8,128)(2,1)S(1)}, u32[]{:S(2)}, u32[]{:S(2)}) collective-permute-start(bf16[16,16,256]{2,1,0:T(8,128)(2,1)S(1)} %get-tuple-element.127), channel_id=1, source_target_pairs={{0,96},{96,0},{32,64},{64,32},{1,97},{97,1},{33,65},{65,33},{2,98}... | collective-permute-start | bytes 393224 | tf_op jit(solution)/shard_map/ppermute | solution.py:25
  70.7 2.5 %collective-permute-start.14 = (bf16[96,16,256]{2,1,0:T(8,128)(2,1)S(1)}, bf16[96,16,256]{2,1,0:T(8,128)(2,1)S(1)}, u32[]{:S(2)}, u32[]{:S(2)}) collective-permute-start(bf16[96,16,256]{2,1,0:T(8,128)(2,1)S(1)} %get-tuple-element.128), channel_id=1, source_target_pairs={{0,1},{1,0},{2,3},{3,2},{4,5},{5,4},{6,7},{7,6},{8,9},{9,8},{10,11... | collective-permute-start | bytes 2359304 | tf_op jit(solution)/shard_map/ppermute | solution.py:190
  70.8 2.4 %collective-permute-start.15 = (bf16[16,16,256]{2,1,0:T(8,128)(2,1)S(1)}, bf16[16,16,256]{2,1,0:T(8,128)(2,1)S(1)}, u32[]{:S(2)}, u32[]{:S(2)}) collective-permute-start(bf16[16,16,256]{2,1,0:T(8,128)(2,1)S(1)} %get-tuple-element.141), channel_id=1, source_target_pairs={{0,1},{1,0},{2,3},{3,2},{4,5},{5,4},{6,7},{7,6},{8,9},{9,8},{10,11... | collective-permute-start | bytes 393224 | tf_op jit(solution)/shard_map/ppermute | solution.py:190
  74.4 8.3 %collective-permute-start.16 = (bf16[24,16,256]{2,1,0:T(8,128)(2,1)S(1)}, bf16[24,16,256]{2,1,0:T(8,128)(2,1)S(1)}, u32[]{:S(2)}, u32[]{:S(2)}) collective-permute-start(bf16[24,16,256]{2,1,0:T(8,128)(2,1)S(1)} %get-tuple-element.134), channel_id=1, source_target_pairs={{0,8},{8,16},{16,24},{24,0},{1,9},{9,17},{17,25},{25,1},{2,10},{10... | collective-permute-start | bytes 589832 | tf_op jit(solution)/shard_map/ppermute | solution.py:185
  76.1 12.0 %collective-permute-start.17 = (bf16[24,16,256]{2,1,0:T(8,128)(2,1)S(1)}, bf16[24,16,256]{2,1,0:T(8,128)(2,1)S(1)}, u32[]{:S(2)}, u32[]{:S(2)}) collective-permute-start(bf16[24,16,256]{2,1,0:T(8,128)(2,1)S(1)} %get-tuple-element.135), channel_id=1, source_target_pairs={{0,16},{8,24},{16,0},{24,8},{1,17},{9,25},{17,1},{25,9},{2,18},{10... | collective-permute-start | bytes 589832 | tf_op jit(solution)/shard_map/ppermute | solution.py:185
  79.0 9.1 %collective-permute-start.18 = (bf16[24,16,256]{2,1,0:T(8,128)(2,1)S(1)}, bf16[24,16,256]{2,1,0:T(8,128)(2,1)S(1)}, u32[]{:S(2)}, u32[]{:S(2)}) collective-permute-start(bf16[24,16,256]{2,1,0:T(8,128)(2,1)S(1)} %get-tuple-element.136), channel_id=1, source_target_pairs={{0,24},{8,0},{16,8},{24,16},{1,25},{9,1},{17,9},{25,17},{2,26},{10... | collective-permute-start | bytes 589832 | tf_op jit(solution)/shard_map/ppermute | solution.py:185
  88.8 6.7 %collective-permute-start.19 = (bf16[6,16,256]{2,1,0:T(8,128)(2,1)S(1)}, bf16[6,16,256]{2,1,0:T(8,128)(2,1)S(1)}, u32[]{:S(2)}, u32[]{:S(2)}) collective-permute-start(bf16[6,16,256]{2,1,0:T(8,128)(2,1)S(1)} %get-tuple-element.138), channel_id=1, source_target_pairs={{0,2},{2,4},{4,6},{6,0},{1,3},{3,5},{5,7},{7,1},{8,10},{10,12},{12... | collective-permute-start | bytes 147464 | tf_op jit(solution)/shard_map/ppermute | solution.py:185
  90.8 6.2 %collective-permute-start.20 = (bf16[6,16,256]{2,1,0:T(8,128)(2,1)S(1)}, bf16[6,16,256]{2,1,0:T(8,128)(2,1)S(1)}, u32[]{:S(2)}, u32[]{:S(2)}) collective-permute-start(bf16[6,16,256]{2,1,0:T(8,128)(2,1)S(1)} %get-tuple-element.139), channel_id=1, source_target_pairs={{0,4},{2,6},{4,0},{6,2},{1,5},{3,7},{5,1},{7,3},{8,12},{10,14},{12... | collective-permute-start | bytes 147464 | tf_op jit(solution)/shard_map/ppermute | solution.py:185
  94.3 4.1 %collective-permute-start.21 = (bf16[6,16,256]{2,1,0:T(8,128)(2,1)S(1)}, bf16[6,16,256]{2,1,0:T(8,128)(2,1)S(1)}, u32[]{:S(2)}, u32[]{:S(2)}) collective-permute-start(bf16[6,16,256]{2,1,0:T(8,128)(2,1)S(1)} %get-tuple-element.140), channel_id=1, source_target_pairs={{0,6},{2,0},{4,2},{6,4},{1,7},{3,1},{5,3},{7,5},{8,14},{10,8},{12,... | collective-permute-start | bytes 147464 | tf_op jit(solution)/shard_map/ppermute | solution.py:185

commit v2 on v1

--- a/solution.py
+++ b/solution.py
@@ -353,43 +353,48 @@
 
 def tap_copies(pos_ref, refs, jobs, held, sems):
     copies = []
-    for n, (branch, above, across) in enumerate(jobs):
-        a = 1 if above == 1 else jnp.where(pos_ref[2] == 0, above, 2 - above)
-        b = 1 if across == 1 else jnp.where(pos_ref[3] == 0, across, 2 - across)
-        copies.append(pltpu.make_async_copy(refs[branch].at[a, b], held.at[n], sems.at[n]))
+    for branch, ref in enumerate(refs):
+        for n, (above, across) in enumerate(jobs):
+            a = 1 if above == 1 else jnp.where(pos_ref[2] == 0, above, 2 - above)
+            b = 1 if across == 1 else jnp.where(pos_ref[3] == 0, across, 2 - across)
+            width = ref.shape[3]
+            to = held.at[branch, :, n * width : (n + 1) * width]
+            copies.append(pltpu.make_async_copy(ref.at[a, b], to, sems.at[branch, n]))
     return copies
 
 
-OUTER = [(k, a, b) for k in (2, 1, 0) for a, b in ((0, 0), (1, 0), (2, 0), (0, 1), (0, 2))]
-INNER = [(k, a, b) for k in (2, 1, 0) for a, b in ((1, 1), (2, 1), (1, 2), (2, 2))]
-
-
-def outer_parts(pos_ref, x_ref, wa_ref, wb_ref, wc_ref, pre_ref, row_ref, col_ref, diag_ref, ext, acc, held, sems):
+BRANCHES = ((2, RATE_C), (1, RATE_B), (0, RATE_A))
+OUTER = ((0, 0), (1, 0), (0, 1), (0, 2), (2, 0))
+INNER = ((1, 1), (1, 2), (2, 1), (2, 2))
+
+
+def outer_parts(pos_ref, x_ref, wc_ref, wb_ref, wa_ref, pre_ref, row_ref, col_ref, diag_ref, ext, acc, y, held, sems):
     low, far = pos_ref[2], pos_ref[3]
     whole = SIDE * SIDE
     width = pre_ref.shape[2]
-    copies = tap_copies(pos_ref, (wa_ref, wb_ref, wc_ref), OUTER, held, sems)
+    copies = tap_copies(pos_ref, (wc_ref, wb_ref, wa_ref), OUTER, held, sems)
     for copy in copies:
         copy.start()
     first = 0
-    for turn, (index, rate) in enumerate(((2, RATE_C), (1, RATE_B), (0, RATE_A))):
+    for turn, (index, rate) in enumerate(BRANCHES):
         lead = rate * SIDE
         inside = whole - lead
         at = row_marks(low, rate)
-
-        def times(n, rows=slice(None)):
-            copies[5 * turn + n].wait()
-            return jnp.dot(x_ref[rows, :], held[5 * turn + n], preferred_element_type=F32)
-
         own_rows = pl.ds(at["own"], whole)
         their_rows = pl.ds(at["theirs"], lead)
         kept_rows = pl.ds(at["kept"], inside)
         to_row = slice(first, first + lead)
         first += lead
+        count = len(OUTER)
+        for copy in copies[turn * count : (turn + 1) * count]:
+            copy.wait()
+        y[...] = jnp.dot(x_ref[...], held[turn, :, : 4 * width], preferred_element_type=F32)
         ext[pl.ds(pl.multiple_of(whole - at["theirs"], 16), lead), :] = jnp.zeros((lead, width), F32)
-        ext[pl.ds(at["out"], whole), :] = times(0)
-        ext[own_rows, :] += times(1)
-        ext[pl.ds(at["inward"], inside), :] += times(2, pl.ds(at["inward_from"], inside))
+        ext[pl.ds(at["out"], whole), :] = y[:, :width]
+        ext[own_rows, :] += y[:, width : 2 * width]
+        ext[pl.ds(at["inward"], inside), :] += jnp.dot(
+            x_ref[pl.ds(at["inward_from"], inside), :], held[turn, :, 4 * width :], preferred_element_type=F32
+        )
         own = blocks(ext[own_rows, :])
         ours = turned_by(own, rate, far)
         rank = rank_of(own.shape, far)
@@ -411,43 +416,41 @@
             col_ref[:whole, :] = flat(jnp.where(rank >= RATE_C, own, have)).astype(BF)
             have = blocks(diag_ref[:lead, :].astype(F32))
             diag_ref[:lead, :] = flat(jnp.where(place >= RATE_C, below, have)).astype(BF)
-        ext[pl.ds(at["out"], whole), :] = times(3)
-        pre_ref[index, kept_rows, :] += ext[lead:whole, :]
-        acc[:lead, :] += ext[their_rows, :]
-        ext[pl.ds(at["out"], whole), :] = times(4)
-        own = blocks(ext[lead:whole, :])
+        next_from = pl.multiple_of(jnp.where(low == 0, inside, 0), 16)
+        keep_from = pl.multiple_of(jnp.where(low == 0, 0, lead), 16)
+        pre_ref[index, kept_rows, :] += y[pl.ds(keep_from, inside), 2 * width : 3 * width]
+        own = blocks(y[pl.ds(keep_from, inside), 3 * width :])
         rank = rank_of(own.shape, far)
         pre_ref[index, kept_rows, :] += flat(jnp.where(rank < SIDE - rate, turned_by(own, rate, 1 - far), 0.0))
-        below = blocks(ext[their_rows, :])
-        theirs = jnp.where(place < SIDE - rate, turned_by(below, rate, 1 - far), 0.0)
-        row_ref[to_row, :] = (acc[:lead, :] + flat(theirs)).astype(BF)
-
-
-def inner_parts(pos_ref, x_ref, part_ref, wp_ref, wa_ref, wb_ref, wc_ref, pre0_ref, pre_ref, acc, held, sems):
+        below = blocks(y[pl.ds(next_from, lead), 3 * width :])
+        theirs = flat(jnp.where(place < SIDE - rate, turned_by(below, rate, 1 - far), 0.0))
+        row_ref[to_row, :] = (acc[:lead, :] + y[pl.ds(next_from, lead), 2 * width : 3 * width] + theirs).astype(BF)
+
+
+def inner_parts(pos_ref, x_ref, part_ref, wp_ref, wc_ref, wb_ref, wa_ref, pre0_ref, pre_ref, y, z, held, sems):
     low, far = pos_ref[2], pos_ref[3]
     whole = SIDE * SIDE
-    copies = tap_copies(pos_ref, (wa_ref, wb_ref, wc_ref), INNER, held, sems)
+    width = pre0_ref.shape[1]
+    copies = tap_copies(pos_ref, (wc_ref, wb_ref, wa_ref), INNER, held, sems)
     for copy in copies:
         copy.start()
     pre0_ref[...] = jnp.dot(x_ref[...], wp_ref[...], preferred_element_type=F32)
-    for turn, (index, rate) in enumerate(((2, RATE_C), (1, RATE_B), (0, RATE_A))):
+    for turn, (index, rate) in enumerate(BRANCHES):
         lead = rate * SIDE
         inside = whole - lead
         at = row_marks(low, rate)
         from_rows = pl.ds(at["inward_from"], inside)
         to_rows = pl.ds(at["inner"], inside)
-
-        def times(n, rows=slice(None)):
-            copies[4 * turn + n].wait()
-            return jnp.dot(x_ref[rows, :], held[4 * turn + n], preferred_element_type=F32)
-
-        pre_ref[index] = part_ref[index] + times(0)
-        pre_ref[index, to_rows, :] += times(1, from_rows)
-        acc[...] = times(2)
-        acc[to_rows, :] += times(3, from_rows)
-        own = blocks(acc[...])
+        count = len(INNER)
+        for copy in copies[turn * count : (turn + 1) * count]:
+            copy.wait()
+        y[...] = jnp.dot(x_ref[...], held[turn, :, : 2 * width], preferred_element_type=F32)
+        z[:inside, :] = jnp.dot(x_ref[from_rows, :], held[turn, :, 2 * width :], preferred_element_type=F32)
+        y[to_rows, :] += z[:inside, :]
+        own = blocks(y[:, width:])
         rank = rank_of(own.shape, far)
-        pre_ref[index] += flat(jnp.where(rank < SIDE - rate, turned_by(own, rate, 1 - far), 0.0))
+        moved = flat(jnp.where(rank < SIDE - rate, turned_by(own, rate, 1 - far), 0.0))
+        pre_ref[index] = part_ref[index] + y[:, :width] + moved
 
 
 def outer(pos, centre, w_rate_a, w_rate_b, w_rate_c):
@@ -466,12 +469,13 @@
         [
             pltpu.VMEM(((SIDE + RATE_C) * SIDE, width), F32),
             pltpu.VMEM((RATE_C * SIDE, width), F32),
-            pltpu.VMEM((len(OUTER), chans, width), BF),
-            pltpu.SemaphoreType.DMA((len(OUTER),)),
+            pltpu.VMEM((pixels, 4 * width), F32),
+            pltpu.VMEM((3, chans, len(OUTER) * width), BF),
+            pltpu.SemaphoreType.DMA((3, len(OUTER))),
         ],
         name="outer",
         n_any=3,
-    )(pos, centre, w_rate_a, w_rate_b, w_rate_c)
+    )(pos, centre, w_rate_c, w_rate_b, w_rate_a)
 
 
 def inner(pos, centre, part, w_point, w_rate_a, w_rate_b, w_rate_c):
@@ -486,13 +490,14 @@
         10 * MIB,
         26,
         [
-            pltpu.VMEM((pixels, width), F32),
-            pltpu.VMEM((len(INNER), chans, width), BF),
-            pltpu.SemaphoreType.DMA((len(INNER),)),
+            pltpu.VMEM((pixels, 2 * width), F32),
+            pltpu.VMEM((pixels, 2 * width), F32),
+            pltpu.VMEM((3, chans, len(INNER) * width), BF),
+            pltpu.SemaphoreType.DMA((3, len(INNER))),
         ],
         name="inner",
         n_any=3,
-    )(pos, centre, part, w_point, w_rate_a, w_rate_b, w_rate_c)
+    )(pos, centre, part, w_point, w_rate_c, w_rate_b, w_rate_a)
 
 
 def merge_parts(
@@ -598,7 +603,7 @@
     centre, *picked = lax.optimization_barrier((centre, *picked))
     got = [picked[0]] + [flip(picked[k], k) for k in (1, 2, 3)]
     part, *parts = outer(pos, centre, *weights)
-    parts, got = lax.optimization_barrier((parts, got))
+    part, got = lax.optimization_barrier((part, got))
     to_row, to_col, to_diag = parts
     parts = [flip(to_row, 2), flip(to_col, 1), flip(to_diag, 3)]
     turned = turn(pos, got)

time: 99.3 us -> 96.8 us (0.975)
  Pallas kernels: 37 us -> 29.2 us
  waiting for transfers between devices: 29.4 us -> 34.6 us
    pallas_call x1, Pallas kernels: 13.6 us -> 8.7 us  [outer(): call(outer_parts, [jax.ShapeDtypeStruct(*s) for s in shapes], 1, 1, 2 * p...]
    pallas_call x1, Pallas kernels: 9.45 us -> 6.32 us  [inner(): call(inner_parts, [jax.ShapeDtypeStruct((pixels, width), F32), jax.ShapeD...]
    ppermute x4, waiting for transfers between devices: 7.24 us -> 10.3 us  [flip(): return lax.ppermute(x, ('row', 'col'), [(0, 3), (3, 0), (1, 2), (2, 1)])]
    ppermute x4, starting transfers between devices: 5.21 us -> 3.22 us  [flip(): return lax.ppermute(x, 'row', [(0, 1), (1, 0)])]
    ppermute x4, starting transfers between devices: 8.34 us -> 9.91 us  [flip(): return lax.ppermute(x, 'col', [(0, 1), (1, 0)])]
    ppermute x4, waiting for transfers between devices: 0.63 us -> 2 us  [flip(): return lax.ppermute(x, 'row', [(0, 1), (1, 0)])]
  transfers between devices with their start and end apart: 22 -> 22, of which waited for: 12 -> 16; matrix products, arithmetic and copies ran while one was open for 0% -> 0% of each run, Pallas kernels for 30% -> 22%
where the time goes in v2:
time: 96.8 us; the launch traced here: 96.7 us
  waiting for transfers between devices  34.6 us (36%)
  starting transfers between devices  31.3 us (32%)
  Pallas kernels  29.2 us (30%)
  local copies, waits for them, and re-layouts  1.38 us (1%)
    ppermute x6, starting transfers between devices, along(): lax.ppermute(blocks[s], axis, [(i, (i + s) % count) for i in range(count)])  12.5 us
    ppermute x6, waiting for transfers between devices, along(): lax.ppermute(blocks[s], axis, [(i, (i + s) % count) for i in range(count)])  10.8 us
    ppermute x4, waiting for transfers between devices, flip(): return lax.ppermute(x, ('row', 'col'), [(0, 3), (3, 0), (1, 2), (2, 1)])  10.3 us
    ppermute x4, starting transfers between devices, flip(): return lax.ppermute(x, 'col', [(0, 1), (1, 0)])  9.91 us
    pallas_call x1, Pallas kernels, outer(): call(outer_parts, [jax.ShapeDtypeStruct(*s) for s in shapes], 1, 1, 2 * p...  8.7 us
    ppermute x4, waiting for transfers between devices, flip(): return lax.ppermute(x, 'col', [(0, 1), (1, 0)])  8.28 us
    pallas_call x1, Pallas kernels, inner(): call(inner_parts, [jax.ShapeDtypeStruct((pixels, width), F32), jax.ShapeD...  6.32 us
    ppermute x4, starting transfers between devices, flip(): return lax.ppermute(x, ('row', 'col'), [(0, 3), (3, 0), (1, 2), (2, 1)])  4.5 us
  transfers between devices with their start and end apart: 22, of which 16 were waited for; matrix products, arithmetic and copies ran while one was open for 0% of the time, Pallas kernels for 22%

profile of v2, /device:TPU:0, one launch (start us, length us, event | category | flops | bytes accessed | tf_op | source)
XLA Modules:
  0.0 96.7 jit_solution(9882098497096861565)
XLA Ops:
  0.1 1.3 %copy-done = bf16[1,24,24,1024]{3,2,1,0:T(8,128)(2,1)S(1)} copy-done((bf16[1,24,24,1024]{3,2,1,0:T(8,128)(2,1)S(1)}, bf16[1,24,24,1024]{3,2,1,0:T(8,128)(2,1)}, u32[]{:S(2)}) %copy-start) | copy-done | bytes 1179672
  1.4 1.9 %pick.1 = (bf16[576,256]{1,0:T(8,128)(2,1)S(1)}, bf16[576,256]{1,0:T(8,128)(2,1)S(1)}, bf16[576,256]{1,0:T(8,128)(2,1)S(1)}, bf16[576,256]{1,0:T(8,128)(2,1)S(1)}) custom-call(s32[6]{0:T(128)S(1)} %stack.27.pos_ref, bf16[576,1024]{1,0:T(8,128)(2,1)S(1)} %bitcast.8), custom_call_target="tpu_custom_call" | custom-call | flops 1207959552 | bytes 2359296 | tf_op jit(solution)/shard_map/pick/pallas_call | solution.py:196
  3.3 3.2 %collective-permute-start.3 = (bf16[576,256]{1,0:T(8,128)(2,1)S(1)}, bf16[576,256]{1,0:T(8,128)(2,1)S(1)}, u32[]{:S(2)}, u32[]{:S(2)}) collective-permute-start(bf16[576,256]{1,0:T(8,128)(2,1)S(1)} %get-tuple-element.81), channel_id=1, source_target_pairs={{0,32},{32,0},{1,33},{33,1},{2,34},{34,2},{3,35},{35,3},{4,36},{36... | collective-permute-start | bytes 884744 | tf_op jit(solution)/shard_map/ppermute | solution.py:22
  7.6 8.7 %outer.1 = (f32[3,576,256]{2,1,0:T(8,128)S(1)}, bf16[864,256]{1,0:T(8,128)(2,1)S(1)}, bf16[864,256]{1,0:T(8,128)(2,1)S(1)}, bf16[576,256]{1,0:T(8,128)(2,1)S(1)}) custom-call(s32[6]{0:T(128)S(1)} %stack.27.pos_ref, bf16[576,1024]{1,0:T(8,128)(2,1)S(1)} %bitcast.9, bf16[3,3,1024,256]{3,2,1,0:T(8,128)(2,1)} %wc_ref.3, bf16[3,3,1024,256]{3,2,1,0:T(8,128)(2,1)} %wb_ref.3, ...), custom_call_target="tpu_custom_call" | custom-call | flops 4227858432 | bytes 10485760 | tf_op jit(solution)/shard_map/outer/pallas_call | solution.py:461
  16.4 1.5 %collective-permute-start = (bf16[864,256]{1,0:T(8,128)(2,1)S(1)}, bf16[864,256]{1,0:T(8,128)(2,1)S(1)}, u32[]{:S(2)}, u32[]{:S(2)}) collective-permute-start(bf16[864,256]{1,0:T(8,128)(2,1)S(1)} %get-tuple-element.76), channel_id=1, source_target_pairs={{0,64},{64,0},{1,65},{65,1},{2,66},{66,2},{3,67},{67,3},{4,68},{68... | collective-permute-start | bytes 1327112 | tf_op jit(solution)/shard_map/ppermute | solution.py:24
  17.8 2.7 %collective-permute-start.1 = (bf16[864,256]{1,0:T(8,128)(2,1)S(1)}, bf16[864,256]{1,0:T(8,128)(2,1)S(1)}, u32[]{:S(2)}, u32[]{:S(2)}) collective-permute-start(bf16[864,256]{1,0:T(8,128)(2,1)S(1)} %get-tuple-element.77), channel_id=1, source_target_pairs={{0,32},{32,0},{1,33},{33,1},{2,34},{34,2},{3,35},{35,3},{4,36},{36... | collective-permute-start | bytes 1327112 | tf_op jit(solution)/shard_map/ppermute | solution.py:22
  21.3 1.2 %turn.1.xt_ref = bf16[2,256,1152]{2,1,0:T(8,128)(2,1)S(1)} custom-call(s32[6]{0:T(128)S(1)} %stack.27.pos_ref, bf16[576,256]{1,0:T(8,128)(2,1)S(1)} %get-tuple-element.87.x0, bf16[576,256]{1,0:T(8,128)(2,1)S(1)} %collective-permute-done.3.x1, bf16[576,256]{1,0:T(8,128)(2,1)S(1)} %collective-permute-done.4.x2, bf16[576,256]{1,0:T(8,128)(2,1)S(1)} %collective-permute-done.5.x3), custom_call_target="tpu_custom_call" | custom-call | flops 301989888 | bytes 2359296 | tf_op jit(solution)/shard_map/turn/pallas_call | solution.py:203
  22.5 6.3 %inner.1 = (f32[576,256]{1,0:T(8,128)S(1)}, f32[3,576,256]{2,1,0:T(8,128)S(1)}) custom-call(s32[6]{0:T(128)S(1)} %stack.27.pos_ref, bf16[576,1024]{1,0:T(8,128)(2,1)S(1)} %bitcast.10, f32[3,576,256]{2,1,0:T(8,128)S(1)} %get-tuple-element.84.part_ref, bf16[1024,256]{1,0:T(8,128)(2,1)S(1)} %copy-done.2, bf16[3,3,1024,256]{3,2,1,0:T(8,128)(2,1)} %wc_ref.3, ...), custom_call_target="tpu_custom_call" | custom-call | flops 3019898880 | bytes 10485760 | tf_op jit(solution)/shard_map/inner/pallas_call | solution.py:484
  28.9 1.8 %collective-permute-done.2.diag_ref = bf16[576,256]{1,0:T(8,128)(2,1)S(1)} collective-permute-done((bf16[576,256]{1,0:T(8,128)(2,1)S(1)}, bf16[576,256]{1,0:T(8,128)(2,1)S(1)}, u32[]{:S(2)}, u32[]{:S(2)}) %collective-permute-start.2) | collective-permute-done | bytes 294944 | tf_op jit(solution)/shard_map/ppermute | solution.py:25
  30.8 8.3 %collective-permute-done.1.col_ref = bf16[864,256]{1,0:T(8,128)(2,1)S(1)} collective-permute-done((bf16[864,256]{1,0:T(8,128)(2,1)S(1)}, bf16[864,256]{1,0:T(8,128)(2,1)S(1)}, u32[]{:S(2)}, u32[]{:S(2)}) %collective-permute-start.1) | collective-permute-done | bytes 442400 | tf_op jit(solution)/shard_map/ppermute | solution.py:22
  39.1 2.2 %merge.1 = (bf16[576,1024]{1,0:T(8,128)(2,1)S(1)}, bf16[576,256]{1,0:T(8,128)(2,1)S(1)}, bf16[576,256]{1,0:T(8,128)(2,1)S(1)}, bf16[576,256]{1,0:T(8,128)(2,1)S(1)}) custom-call(s32[6]{0:T(128)S(1)} %stack.27.pos_ref, f32[576,256]{1,0:T(8,128)S(1)} %get-tuple-element.91.pre0_ref, f32[3,576,256]{2,1,0:T(8,128)S(1)} %get-tuple-element.92.own_ref, ...), custom_call_target="tpu_custom_call" | custom-call | flops 452984832 | bytes 6291456 | tf_op jit(solution)/shard_map/merge/pallas_call | solution.py:564
  41.3 2.8 %collective-permute-start.10 = (bf16[576,256]{1,0:T(8,128)(2,1)S(1)}, bf16[576,256]{1,0:T(8,128)(2,1)S(1)}, u32[]{:S(2)}, u32[]{:S(2)}) collective-permute-start(bf16[576,256]{1,0:T(8,128)(2,1)S(1)} %get-tuple-element.113.d0), channel_id=1, source_target_pairs={{0,96},{96,0},{32,64},{64,32},{1,97},{97,1},{33,65},{65,33},{2,98}... | collective-permute-start | bytes 884744 | tf_op jit(solution)/shard_map/ppermute | solution.py:25
  44.2 0.8 collective-permute-start.8
  45.5 1.6 %pair.1 = (f32[1024,256]{1,0:T(8,128)S(1)}, bf16[512,256]{1,0:T(8,128)(2,1)S(1)}, bf16[512,256]{1,0:T(8,128)(2,1)S(1)}) custom-call(s32[6]{0:T(128)S(1)} %stack.27.pos_ref, bf16[576,1024]{1,0:T(8,128)(2,1)S(1)} %get-tuple-element.96.joined_ref, bf16[576,256]{1,0:T(8,128)(2,1)S(1)} %get-tuple-element.97.g_ref, bf16[576,1024]{1,0:T(8,128)(2,1)S(1)} %bitcast.11, ...), custom_call_target="tpu_custom_call" | custom-call | flops 603979776 | bytes 4194304 | tf_op jit(solution)/shard_map/pair/pallas_call | solution.py:617
  47.8 1.0 %collective-permute-done.6.got0 = bf16[512,256]{1,0:T(8,128)(2,1)S(1)} collective-permute-done((bf16[512,256]{1,0:T(8,128)(2,1)S(1)}, bf16[512,256]{1,0:T(8,128)(2,1)S(1)}, u32[]{:S(2)}, u32[]{:S(2)}) %collective-permute-start.6) | collective-permute-done | bytes 262176 | tf_op jit(solution)/shard_map/ppermute | solution.py:190
  49.1 7.5 %collective-permute-done.10.d3 = bf16[576,256]{1,0:T(8,128)(2,1)S(1)} collective-permute-done((bf16[576,256]{1,0:T(8,128)(2,1)S(1)}, bf16[576,256]{1,0:T(8,128)(2,1)S(1)}, u32[]{:S(2)}, u32[]{:S(2)}) %collective-permute-start.10) | collective-permute-done | bytes 294944 | tf_op jit(solution)/shard_map/ppermute | solution.py:25
  58.0 3.2 %collective-permute-start.11 = (bf16[16,16,256]{2,1,0:T(8,128)(2,1)S(1)}, bf16[16,16,256]{2,1,0:T(8,128)(2,1)S(1)}, u32[]{:S(2)}, u32[]{:S(2)}) collective-permute-start(bf16[16,16,256]{2,1,0:T(8,128)(2,1)S(1)} %get-tuple-element.121), channel_id=1, source_target_pairs={{0,32},{32,0},{1,33},{33,1},{2,34},{34,2},{3,35},{35,3},{4,36},{36... | collective-permute-start | bytes 393224 | tf_op jit(solution)/shard_map/ppermute | solution.py:22
  62.4 3.6 %taps.1 = (f32[96,16,256]{2,1,0:T(8,128)S(1)}, bf16[96,16,256]{2,1,0:T(8,128)(2,1)S(1)}) custom-call(s32[6]{0:T(128)S(1)} %stack.27.pos_ref, s32[176]{0:T(256)S(1)} %fusion.1.place_ref, bf16[576,256]{1,0:T(8,128)(2,1)S(1)} %get-tuple-element.113.d0, bf16[576,256]{1,0:T(8,128)(2,1)S(1)} %collective-permute-done.8.d1, ...), custom_call_target="tpu_custom_call" | custom-call | flops 2113929216 | bytes 8388608 | tf_op jit(solution)/shard_map/taps/pallas_call | solution.py:249
  66.0 1.0 %collective-permute-done.12 = bf16[16,16,256]{2,1,0:T(8,128)(2,1)S(1)} collective-permute-done((bf16[16,16,256]{2,1,0:T(8,128)(2,1)S(1)}, bf16[16,16,256]{2,1,0:T(8,128)(2,1)S(1)}, u32[]{:S(2)}, u32[]{:S(2)}) %collective-permute-start.12) | collective-permute-done | bytes 131104 | tf_op jit(solution)/shard_map/ppermute | solution.py:24
  67.0 1.0 %collective-permute-done.13 = bf16[16,16,256]{2,1,0:T(8,128)(2,1)S(1)} collective-permute-done((bf16[16,16,256]{2,1,0:T(8,128)(2,1)S(1)}, bf16[16,16,256]{2,1,0:T(8,128)(2,1)S(1)}, u32[]{:S(2)}, u32[]{:S(2)}) %collective-permute-start.13) | collective-permute-done | bytes 131104 | tf_op jit(solution)/shard_map/ppermute | solution.py:25
  68.7 1.8 %collective-permute-done.15.other_ref = bf16[16,16,256]{2,1,0:T(8,128)(2,1)S(1)} collective-permute-done((bf16[16,16,256]{2,1,0:T(8,128)(2,1)S(1)}, bf16[16,16,256]{2,1,0:T(8,128)(2,1)S(1)}, u32[]{:S(2)}, u32[]{:S(2)}) %collective-permute-start.15) | collective-permute-done | bytes 131104 | tf_op jit(solution)/shard_map/ppermute | solution.py:190
  70.5 1.5 %owners.1 = (f32[24,16,256]{2,1,0:T(8,128)S(1)}, bf16[24,16,256]{2,1,0:T(8,128)(2,1)S(1)}, bf16[24,16,256]{2,1,0:T(8,128)(2,1)S(1)}, bf16[24,16,256]{2,1,0:T(8,128)(2,1)S(1)}) custom-call(s32[6]{0:T(128)S(1)} %stack.27.pos_ref, s32[176]{0:T(256)S(1)} %fusion.1.place_ref, f32[96,16,256]{2,1,0:T(8,128)S(1)} %get-tuple-element.118.keep_ref, ...), custom_call_target="tpu_custom_call" | custom-call | flops 393216 | bytes 3145728 | tf_op jit(solution)/shard_map/owners/pallas_call | solution.py:276
  72.0 1.7 %collective-permute-start.16 = (bf16[24,16,256]{2,1,0:T(8,128)(2,1)S(1)}, bf16[24,16,256]{2,1,0:T(8,128)(2,1)S(1)}, u32[]{:S(2)}, u32[]{:S(2)}) collective-permute-start(bf16[24,16,256]{2,1,0:T(8,128)(2,1)S(1)} %get-tuple-element.130), channel_id=1, source_target_pairs={{0,8},{8,16},{16,24},{24,0},{1,9},{9,17},{17,25},{25,1},{2,10},{10... | collective-permute-start | bytes 589832 | tf_op jit(solution)/shard_map/ppermute | solution.py:185
  73.6 2.9 %collective-permute-start.17 = (bf16[24,16,256]{2,1,0:T(8,128)(2,1)S(1)}, bf16[24,16,256]{2,1,0:T(8,128)(2,1)S(1)}, u32[]{:S(2)}, u32[]{:S(2)}) collective-permute-start(bf16[24,16,256]{2,1,0:T(8,128)(2,1)S(1)} %get-tuple-element.131), channel_id=1, source_target_pairs={{0,16},{8,24},{16,0},{24,8},{1,17},{9,25},{17,1},{25,9},{2,18},{10... | collective-permute-start | bytes 589832 | tf_op jit(solution)/shard_map/ppermute | solution.py:185
  76.5 1.3 %collective-permute-start.18 = (bf16[24,16,256]{2,1,0:T(8,128)(2,1)S(1)}, bf16[24,16,256]{2,1,0:T(8,128)(2,1)S(1)}, u32[]{:S(2)}, u32[]{:S(2)}) collective-permute-start(bf16[24,16,256]{2,1,0:T(8,128)(2,1)S(1)} %get-tuple-element.132), channel_id=1, source_target_pairs={{0,24},{8,0},{16,8},{24,16},{1,25},{9,1},{17,9},{25,17},{2,26},{10... | collective-permute-start | bytes 589832 | tf_op jit(solution)/shard_map/ppermute | solution.py:185
  77.9 2.4 %collective-permute-done.16.refs_1_ = bf16[24,16,256]{2,1,0:T(8,128)(2,1)S(1)} collective-permute-done((bf16[24,16,256]{2,1,0:T(8,128)(2,1)S(1)}, bf16[24,16,256]{2,1,0:T(8,128)(2,1)S(1)}, u32[]{:S(2)}, u32[]{:S(2)}) %collective-permute-start.16) | collective-permute-done | bytes 196640 | tf_op jit(solution)/shard_map/ppermute | solution.py:185
  80.2 5.4 %collective-permute-done.17.refs_2_ = bf16[24,16,256]{2,1,0:T(8,128)(2,1)S(1)} collective-permute-done((bf16[24,16,256]{2,1,0:T(8,128)(2,1)S(1)}, bf16[24,16,256]{2,1,0:T(8,128)(2,1)S(1)}, u32[]{:S(2)}, u32[]{:S(2)}) %collective-permute-start.17) | collective-permute-done | bytes 196640 | tf_op jit(solution)/shard_map/ppermute | solution.py:185
  86.3 2.0 %collective-permute-start.19 = (bf16[6,16,256]{2,1,0:T(8,128)(2,1)S(1)}, bf16[6,16,256]{2,1,0:T(8,128)(2,1)S(1)}, u32[]{:S(2)}, u32[]{:S(2)}) collective-permute-start(bf16[6,16,256]{2,1,0:T(8,128)(2,1)S(1)} %get-tuple-element.134), channel_id=1, source_target_pairs={{0,2},{2,4},{4,6},{6,0},{1,3},{3,5},{5,7},{7,1},{8,10},{10,12},{12... | collective-permute-start | bytes 147464 | tf_op jit(solution)/shard_map/ppermute | solution.py:185
  88.3 3.6 %collective-permute-start.20 = (bf16[6,16,256]{2,1,0:T(8,128)(2,1)S(1)}, bf16[6,16,256]{2,1,0:T(8,128)(2,1)S(1)}, u32[]{:S(2)}, u32[]{:S(2)}) collective-permute-start(bf16[6,16,256]{2,1,0:T(8,128)(2,1)S(1)} %get-tuple-element.135), channel_id=1, source_target_pairs={{0,4},{2,6},{4,0},{6,2},{1,5},{3,7},{5,1},{7,3},{8,12},{10,14},{12... | collective-permute-start | bytes 147464 | tf_op jit(solution)/shard_map/ppermute | solution.py:185
  91.9 1.0 %collective-permute-start.21 = (bf16[6,16,256]{2,1,0:T(8,128)(2,1)S(1)}, bf16[6,16,256]{2,1,0:T(8,128)(2,1)S(1)}, u32[]{:S(2)}, u32[]{:S(2)}) collective-permute-start(bf16[6,16,256]{2,1,0:T(8,128)(2,1)S(1)} %get-tuple-element.136), channel_id=1, source_target_pairs={{0,6},{2,0},{4,2},{6,4},{1,7},{3,1},{5,3},{7,5},{8,14},{10,8},{12,... | collective-permute-start | bytes 147464 | tf_op jit(solution)/shard_map/ppermute | solution.py:185
  93.0 1.5 %collective-permute-done.20.r2 = bf16[6,16,256]{2,1,0:T(8,128)(2,1)S(1)} collective-permute-done((bf16[6,16,256]{2,1,0:T(8,128)(2,1)S(1)}, bf16[6,16,256]{2,1,0:T(8,128)(2,1)S(1)}, u32[]{:S(2)}, u32[]{:S(2)}) %collective-permute-start.20) | collective-permute-done | bytes 49184 | tf_op jit(solution)/shard_map/ppermute | solution.py:185
  94.5 1.5 %collective-permute-done.21.r3 = bf16[6,16,256]{2,1,0:T(8,128)(2,1)S(1)} collective-permute-done((bf16[6,16,256]{2,1,0:T(8,128)(2,1)S(1)}, bf16[6,16,256]{2,1,0:T(8,128)(2,1)S(1)}, u32[]{:S(2)}, u32[]{:S(2)}) %collective-permute-start.21) | collective-permute-done | bytes 49184 | tf_op jit(solution)/shard_map/ppermute | solution.py:185
  (38 shorter events, 8.5 us)
Async XLA Ops:
  0.1 1.3 %copy-start = (bf16[1,24,24,1024]{3,2,1,0:T(8,128)(2,1)S(1)}, bf16[1,24,24,1024]{3,2,1,0:T(8,128)(2,1)}, u32[]{:S(2)}) copy-start(bf16[1,24,24,1024]{3,2,1,0:T(8,128)(2,1)} %param.8) | copy-start | bytes 3538948
  1.4 6.3 %copy-start.1 = (bf16[1,24,24,1024]{3,2,1,0:T(8,128)(2,1)S(1)}, bf16[1,24,24,1024]{3,2,1,0:T(8,128)(2,1)}, u32[]{:S(2)}) copy-start(bf16[1,24,24,1024]{3,2,1,0:T(8,128)(2,1)} %param.8) | copy-start | bytes 3538948
  3.3 17.3 %collective-permute-start.3 = (bf16[576,256]{1,0:T(8,128)(2,1)S(1)}, bf16[576,256]{1,0:T(8,128)(2,1)S(1)}, u32[]{:S(2)}, u32[]{:S(2)}) collective-permute-start(bf16[576,256]{1,0:T(8,128)(2,1)S(1)} %get-tuple-element.81), channel_id=1, source_target_pairs={{0,32},{32,0},{1,33},{33,1},{2,34},{34,2},{3,35},{35,3},{4,36},{36... | collective-permute-start | bytes 884744 | tf_op jit(solution)/shard_map/ppermute | solution.py:22
  6.5 14.8 %collective-permute-start.4 = (bf16[576,256]{1,0:T(8,128)(2,1)S(1)}, bf16[576,256]{1,0:T(8,128)(2,1)S(1)}, u32[]{:S(2)}, u32[]{:S(2)}) collective-permute-start(bf16[576,256]{1,0:T(8,128)(2,1)S(1)} %get-tuple-element.82), channel_id=1, source_target_pairs={{0,64},{64,0},{1,65},{65,1},{2,66},{66,2},{3,67},{67,3},{4,68},{68... | collective-permute-start | bytes 884744 | tf_op jit(solution)/shard_map/ppermute | solution.py:24
  7.1 14.2 %collective-permute-start.5 = (bf16[576,256]{1,0:T(8,128)(2,1)S(1)}, bf16[576,256]{1,0:T(8,128)(2,1)S(1)}, u32[]{:S(2)}, u32[]{:S(2)}) collective-permute-start(bf16[576,256]{1,0:T(8,128)(2,1)S(1)} %get-tuple-element.83), channel_id=1, source_target_pairs={{0,96},{96,0},{32,64},{64,32},{1,97},{97,1},{33,65},{65,33},{2,98}... | collective-permute-start | bytes 884744 | tf_op jit(solution)/shard_map/ppermute | solution.py:25
  16.3 6.2 %copy-start.2 = (bf16[1024,256]{1,0:T(8,128)(2,1)S(1)}, bf16[1024,256]{1,0:T(8,128)(2,1)}, u32[]{:S(2)}) copy-start(bf16[1024,256]{1,0:T(8,128)(2,1)} %wp_ref.2) | copy-start | bytes 1572868
  16.4 14.4 %collective-permute-start = (bf16[864,256]{1,0:T(8,128)(2,1)S(1)}, bf16[864,256]{1,0:T(8,128)(2,1)S(1)}, u32[]{:S(2)}, u32[]{:S(2)}) collective-permute-start(bf16[864,256]{1,0:T(8,128)(2,1)S(1)} %get-tuple-element.76), channel_id=1, source_target_pairs={{0,64},{64,0},{1,65},{65,1},{2,66},{66,2},{3,67},{67,3},{4,68},{68... | collective-permute-start | bytes 1327112 | tf_op jit(solution)/shard_map/ppermute | solution.py:24
  17.8 21.2 %collective-permute-start.1 = (bf16[864,256]{1,0:T(8,128)(2,1)S(1)}, bf16[864,256]{1,0:T(8,128)(2,1)S(1)}, u32[]{:S(2)}, u32[]{:S(2)}) collective-permute-start(bf16[864,256]{1,0:T(8,128)(2,1)S(1)} %get-tuple-element.77), channel_id=1, source_target_pairs={{0,32},{32,0},{1,33},{33,1},{2,34},{34,2},{3,35},{35,3},{4,36},{36... | collective-permute-start | bytes 1327112 | tf_op jit(solution)/shard_map/ppermute | solution.py:22
  20.6 10.1 %collective-permute-start.2 = (bf16[576,256]{1,0:T(8,128)(2,1)S(1)}, bf16[576,256]{1,0:T(8,128)(2,1)S(1)}, u32[]{:S(2)}, u32[]{:S(2)}) collective-permute-start(bf16[576,256]{1,0:T(8,128)(2,1)S(1)} %get-tuple-element.78), channel_id=1, source_target_pairs={{0,96},{96,0},{32,64},{64,32},{1,97},{97,1},{33,65},{65,33},{2,98}... | collective-permute-start | bytes 884744 | tf_op jit(solution)/shard_map/ppermute | solution.py:25
  22.5 16.6 %copy-start.3 = (bf16[1024,256]{1,0:T(8,128)(2,1)S(1)}, bf16[1024,256]{1,0:T(8,128)(2,1)}, u32[]{:S(2)}) copy-start(bf16[1024,256]{1,0:T(8,128)(2,1)} %wp_ref.3) | copy-start | bytes 1572868
  22.5 16.6 %copy-start.4 = (bf16[1,24,24,256]{3,2,1,0:T(8,128)(2,1)S(1)}, bf16[1,24,24,256]{3,2,1,0:T(8,128)(2,1)}, u32[]{:S(2)}) copy-start(bf16[1,24,24,256]{3,2,1,0:T(8,128)(2,1)} %param.9) | copy-start | bytes 884740
  41.3 6.4 %copy-start.5 = (s32[176]{0:T(256)S(1)}, s32[176]{0:T(256)}, u32[]{:S(2)}) copy-start(s32[176]{0:T(256)} %param.15) | copy-start | bytes 2116
  41.3 15.3 %collective-permute-start.10 = (bf16[576,256]{1,0:T(8,128)(2,1)S(1)}, bf16[576,256]{1,0:T(8,128)(2,1)S(1)}, u32[]{:S(2)}, u32[]{:S(2)}) collective-permute-start(bf16[576,256]{1,0:T(8,128)(2,1)S(1)} %get-tuple-element.113.d0), channel_id=1, source_target_pairs={{0,96},{96,0},{32,64},{64,32},{1,97},{97,1},{33,65},{65,33},{2,98}... | collective-permute-start | bytes 884744 | tf_op jit(solution)/shard_map/ppermute | solution.py:25
  44.2 12.5 %collective-permute-start.8 = (bf16[576,256]{1,0:T(8,128)(2,1)S(1)}, bf16[576,256]{1,0:T(8,128)(2,1)S(1)}, u32[]{:S(2)}, u32[]{:S(2)}) collective-permute-start(bf16[576,256]{1,0:T(8,128)(2,1)S(1)} %get-tuple-element.113.d0), channel_id=1, source_target_pairs={{0,32},{32,0},{1,33},{33,1},{2,34},{34,2},{3,35},{35,3},{4,36},{36... | collective-permute-start | bytes 884744 | tf_op jit(solution)/shard_map/ppermute | solution.py:22
  45.0 12.4 %collective-permute-start.9 = (bf16[576,256]{1,0:T(8,128)(2,1)S(1)}, bf16[576,256]{1,0:T(8,128)(2,1)S(1)}, u32[]{:S(2)}, u32[]{:S(2)}) collective-permute-start(bf16[576,256]{1,0:T(8,128)(2,1)S(1)} %get-tuple-element.113.d0), channel_id=1, source_target_pairs={{0,64},{64,0},{1,65},{65,1},{2,66},{66,2},{3,67},{67,3},{4,68},{68... | collective-permute-start | bytes 884744 | tf_op jit(solution)/shard_map/ppermute | solution.py:24
  47.2 1.6 %collective-permute-start.6 = (bf16[512,256]{1,0:T(8,128)(2,1)S(1)}, bf16[512,256]{1,0:T(8,128)(2,1)S(1)}, u32[]{:S(2)}, u32[]{:S(2)}) collective-permute-start(bf16[512,256]{1,0:T(8,128)(2,1)S(1)} %get-tuple-element.100), channel_id=1, source_target_pairs={{0,1},{1,0},{2,3},{3,2},{4,5},{5,4},{6,7},{7,6},{8,9},{9,8},{10,11... | collective-permute-start | bytes 786440 | tf_op jit(solution)/shard_map/ppermute | solution.py:190
  47.2 1.9 %collective-permute-start.7 = (bf16[512,256]{1,0:T(8,128)(2,1)S(1)}, bf16[512,256]{1,0:T(8,128)(2,1)S(1)}, u32[]{:S(2)}, u32[]{:S(2)}) collective-permute-start(bf16[512,256]{1,0:T(8,128)(2,1)S(1)} %get-tuple-element.101), channel_id=1, source_target_pairs={{0,1},{1,0},{2,3},{3,2},{4,5},{5,4},{6,7},{7,6},{8,9},{9,8},{10,11... | collective-permute-start | bytes 786440 | tf_op jit(solution)/shard_map/ppermute | solution.py:190
  58.0 7.9 %collective-permute-start.11 = (bf16[16,16,256]{2,1,0:T(8,128)(2,1)S(1)}, bf16[16,16,256]{2,1,0:T(8,128)(2,1)S(1)}, u32[]{:S(2)}, u32[]{:S(2)}) collective-permute-start(bf16[16,16,256]{2,1,0:T(8,128)(2,1)S(1)} %get-tuple-element.121), channel_id=1, source_target_pairs={{0,32},{32,0},{1,33},{33,1},{2,34},{34,2},{3,35},{35,3},{4,36},{36... | collective-permute-start | bytes 393224 | tf_op jit(solution)/shard_map/ppermute | solution.py:22
  61.2 5.7 %collective-permute-start.12 = (bf16[16,16,256]{2,1,0:T(8,128)(2,1)S(1)}, bf16[16,16,256]{2,1,0:T(8,128)(2,1)S(1)}, u32[]{:S(2)}, u32[]{:S(2)}) collective-permute-start(bf16[16,16,256]{2,1,0:T(8,128)(2,1)S(1)} %get-tuple-element.122), channel_id=1, source_target_pairs={{0,64},{64,0},{1,65},{65,1},{2,66},{66,2},{3,67},{67,3},{4,68},{68... | collective-permute-start | bytes 393224 | tf_op jit(solution)/shard_map/ppermute | solution.py:24
  61.8 6.2 %collective-permute-start.13 = (bf16[16,16,256]{2,1,0:T(8,128)(2,1)S(1)}, bf16[16,16,256]{2,1,0:T(8,128)(2,1)S(1)}, u32[]{:S(2)}, u32[]{:S(2)}) collective-permute-start(bf16[16,16,256]{2,1,0:T(8,128)(2,1)S(1)} %get-tuple-element.123), channel_id=1, source_target_pairs={{0,96},{96,0},{32,64},{64,32},{1,97},{97,1},{33,65},{65,33},{2,98}... | collective-permute-start | bytes 393224 | tf_op jit(solution)/shard_map/ppermute | solution.py:25
  68.0 2.5 %collective-permute-start.14 = (bf16[96,16,256]{2,1,0:T(8,128)(2,1)S(1)}, bf16[96,16,256]{2,1,0:T(8,128)(2,1)S(1)}, u32[]{:S(2)}, u32[]{:S(2)}) collective-permute-start(bf16[96,16,256]{2,1,0:T(8,128)(2,1)S(1)} %get-tuple-element.124), channel_id=1, source_target_pairs={{0,1},{1,0},{2,3},{3,2},{4,5},{5,4},{6,7},{7,6},{8,9},{9,8},{10,11... | collective-permute-start | bytes 2359304 | tf_op jit(solution)/shard_map/ppermute | solution.py:190
  68.1 2.4 %collective-permute-start.15 = (bf16[16,16,256]{2,1,0:T(8,128)(2,1)S(1)}, bf16[16,16,256]{2,1,0:T(8,128)(2,1)S(1)}, u32[]{:S(2)}, u32[]{:S(2)}) collective-permute-start(bf16[16,16,256]{2,1,0:T(8,128)(2,1)S(1)} %get-tuple-element.137), channel_id=1, source_target_pairs={{0,1},{1,0},{2,3},{3,2},{4,5},{5,4},{6,7},{7,6},{8,9},{9,8},{10,11... | collective-permute-start | bytes 393224 | tf_op jit(solution)/shard_map/ppermute | solution.py:190
  72.0 8.3 %collective-permute-start.16 = (bf16[24,16,256]{2,1,0:T(8,128)(2,1)S(1)}, bf16[24,16,256]{2,1,0:T(8,128)(2,1)S(1)}, u32[]{:S(2)}, u32[]{:S(2)}) collective-permute-start(bf16[24,16,256]{2,1,0:T(8,128)(2,1)S(1)} %get-tuple-element.130), channel_id=1, source_target_pairs={{0,8},{8,16},{16,24},{24,0},{1,9},{9,17},{17,25},{25,1},{2,10},{10... | collective-permute-start | bytes 589832 | tf_op jit(solution)/shard_map/ppermute | solution.py:185
  73.6 12.0 %collective-permute-start.17 = (bf16[24,16,256]{2,1,0:T(8,128)(2,1)S(1)}, bf16[24,16,256]{2,1,0:T(8,128)(2,1)S(1)}, u32[]{:S(2)}, u32[]{:S(2)}) collective-permute-start(bf16[24,16,256]{2,1,0:T(8,128)(2,1)S(1)} %get-tuple-element.131), channel_id=1, source_target_pairs={{0,16},{8,24},{16,0},{24,8},{1,17},{9,25},{17,1},{25,9},{2,18},{10... | collective-permute-start | bytes 589832 | tf_op jit(solution)/shard_map/ppermute | solution.py:185
  76.5 9.1 %collective-permute-start.18 = (bf16[24,16,256]{2,1,0:T(8,128)(2,1)S(1)}, bf16[24,16,256]{2,1,0:T(8,128)(2,1)S(1)}, u32[]{:S(2)}, u32[]{:S(2)}) collective-permute-start(bf16[24,16,256]{2,1,0:T(8,128)(2,1)S(1)} %get-tuple-element.132), channel_id=1, source_target_pairs={{0,24},{8,0},{16,8},{24,16},{1,25},{9,1},{17,9},{25,17},{2,26},{10... | collective-permute-start | bytes 589832 | tf_op jit(solution)/shard_map/ppermute | solution.py:185
  86.3 6.7 %collective-permute-start.19 = (bf16[6,16,256]{2,1,0:T(8,128)(2,1)S(1)}, bf16[6,16,256]{2,1,0:T(8,128)(2,1)S(1)}, u32[]{:S(2)}, u32[]{:S(2)}) collective-permute-start(bf16[6,16,256]{2,1,0:T(8,128)(2,1)S(1)} %get-tuple-element.134), channel_id=1, source_target_pairs={{0,2},{2,4},{4,6},{6,0},{1,3},{3,5},{5,7},{7,1},{8,10},{10,12},{12... | collective-permute-start | bytes 147464 | tf_op jit(solution)/shard_map/ppermute | solution.py:185
  88.3 6.2 %collective-permute-start.20 = (bf16[6,16,256]{2,1,0:T(8,128)(2,1)S(1)}, bf16[6,16,256]{2,1,0:T(8,128)(2,1)S(1)}, u32[]{:S(2)}, u32[]{:S(2)}) collective-permute-start(bf16[6,16,256]{2,1,0:T(8,128)(2,1)S(1)} %get-tuple-element.135), channel_id=1, source_target_pairs={{0,4},{2,6},{4,0},{6,2},{1,5},{3,7},{5,1},{7,3},{8,12},{10,14},{12... | collective-permute-start | bytes 147464 | tf_op jit(solution)/shard_map/ppermute | solution.py:185
  91.9 4.1 %collective-permute-start.21 = (bf16[6,16,256]{2,1,0:T(8,128)(2,1)S(1)}, bf16[6,16,256]{2,1,0:T(8,128)(2,1)S(1)}, u32[]{:S(2)}, u32[]{:S(2)}) collective-permute-start(bf16[6,16,256]{2,1,0:T(8,128)(2,1)S(1)} %get-tuple-element.136), channel_id=1, source_target_pairs={{0,6},{2,0},{4,2},{6,4},{1,7},{3,1},{5,3},{7,5},{8,14},{10,8},{12,... | collective-permute-start | bytes 147464 | tf_op jit(solution)/shard_map/ppermute | solution.py:185

commit v3 on v2

--- a/solution.py
+++ b/solution.py
@@ -131,39 +131,25 @@
     send_ref[...] = buf[half:].astype(BF)
 
 
-def hand_out(total, me, outs):
-    outs[0][...] = total[me]
-    for s in range(1, len(outs)):
-        outs[s][...] = total[lax.rem(me + s, len(outs))].astype(BF)
-
-
-def join_owners(pos_ref, place_ref, keep_ref, got_ref, mine_ref, other_ref, *rest):
-    *outs, total = rest
-    count, each = total.shape[0], total.shape[1]
-    total[...] = (keep_ref[...] + got_ref[...].astype(F32)).reshape(total.shape)
+def join_owners(pos_ref, place_ref, keep_ref, got_ref, mine_ref, other_ref, o_ref, total):
+    total[...] = keep_ref[...] + got_ref[...].astype(F32)
     core = pos_ref[4]
     for n in range(mine_ref.shape[0]):
         for ref, first in ((mine_ref, 16 * core), (other_ref, 16 * (1 - core))):
             at = place_ref[first + n]
 
-            @pl.when(at < count * each)
+            @pl.when(at < total.shape[0])
             def _(ref=ref, at=at, n=n):
-                total[at // each, at % each] = ref[n].astype(F32)
-
-    hand_out(total, pos_ref[1], outs)
-
-
-def fold_next(pos_ref, *refs):
-    total = refs[-1]
-    value = refs[0][...]
-    for got in refs[1:4]:
-        value = value + got[...].astype(F32)
+                total[at] = ref[n].astype(F32)
+
+    o_ref[...] = total[...].astype(BF).reshape(o_ref.shape)
+
+
+def fold_last(r_ref, o_ref, total):
+    value = r_ref[0].astype(F32)
+    for n in range(1, r_ref.shape[0]):
+        value = value + r_ref[n].astype(F32)
     total[...] = value.reshape(total.shape)
-    hand_out(total, pos_ref[5], refs[4:-1])
-
-
-def fold_last(r0, r1, r2, r3, o_ref):
-    total = r0[...] + r1[...].astype(F32) + r2[...].astype(F32) + r3[...].astype(F32)
     width = total.shape[2]
     for i in range(total.shape[1]):
         o_ref[:, i * width : (i + 1) * width] = total[:, i, :]
@@ -177,13 +163,6 @@
         total[n * each : (n + 1) * each] = value.reshape(each, *total.shape[1:])
     for k, out in enumerate(outs):
         out[...] = total[:, jnp.bitwise_xor(pos_ref[0], k)].astype(out.dtype)
-
-
-def along(blocks, axis):
-    count = lax.axis_size(axis)
-    return [blocks[0]] + [
-        lax.ppermute(blocks[s], axis, [(i, (i + s) % count) for i in range(count)]) for s in range(1, count)
-    ]
 
 
 def swap_core(x):
@@ -265,46 +244,31 @@
 
 def reduce_slots(pos, place, kept, sent, mine, other):
     half, rows, width = kept.shape
-    ys, zs = lax.axis_size("dp_0"), lax.axis_size("dp_1")
-    each = half // ys
-    last = each // zs
-
-    def blocks(count, n):
-        shape = (n, rows, width)
-        return [jax.ShapeDtypeStruct(shape, F32)] + [jax.ShapeDtypeStruct(shape, BF)] * (count - 1)
-
+    chips = lax.axis_size("dp_0") * lax.axis_size("dp_1")
+    each = half // chips
     total = call(
         join_owners,
-        blocks(ys, each),
+        jax.ShapeDtypeStruct((chips, each * rows, width), BF),
         2,
         4,
         kept.size,
         8 * kept.size,
         12,
-        [pltpu.VMEM((ys, each, rows, width), F32)],
+        [pltpu.VMEM((half, rows, width), F32)],
         name="owners",
     )(pos, place, kept, swap_core(sent), mine, other)
-    total = call(
-        fold_next,
-        blocks(zs, last),
-        1,
-        4,
-        kept.size // 4,
-        2 * kept.size,
-        6,
-        [pltpu.VMEM((zs, last, rows, width), F32)],
-        name="fold",
-    )(pos, *along(total, "dp_0"))
+    total = lax.all_to_all(total, ("dp_0", "dp_1"), 0, 0, tiled=True)
     return call(
         fold_last,
-        jax.ShapeDtypeStruct((last, rows * width), F32),
+        jax.ShapeDtypeStruct((each, rows * width), F32),
         0,
-        4,
-        kept.size // 16,
-        kept.size // 2,
-        4,
+        1,
+        kept.size,
+        2 * kept.size,
+        8,
+        [pltpu.VMEM((each, rows, width), F32)],
         name="last",
-    )(*along(total, "dp_1"))
+    )(total)
 
 
 def silu_slope(value):

time: 96.8 us -> 94.8 us (0.979)
  blocking collectives: 0 us -> 22.3 us
  starting transfers between devices: 31.3 us -> 18.8 us
  waiting for transfers between devices: 34.6 us -> 23.8 us
  Pallas kernels: 29.2 us -> 28.1 us
    all_to_all x0 -> x1, blocking collectives: none -> 22.3 us  [reduce_slots(): total = lax.all_to_all(total, ('dp_0', 'dp_1'), 0, 0, tiled=True)]
    ppermute x6 -> x0, starting transfers between devices: 12.5 us -> none  [along(): lax.ppermute(blocks[s], axis, [(i, (i + s) % count) for i in range(count)])]
    ppermute x6 -> x0, waiting for transfers between devices: 10.8 us -> none  [along(): lax.ppermute(blocks[s], axis, [(i, (i + s) % count) for i in range(count)])]
    pallas_call x3 -> x2, Pallas kernels: 2.89 us -> 1.85 us  [the longest x1 1.05 us: reduce_slots(): call(join_owners, jax.ShapeDtypeStruct((chips, each * rows, width), BF),...]
  transfers between devices with their start and end apart: 22 -> 16, of which waited for: 16 -> 11; matrix products, arithmetic and copies ran while one was open for 0% -> 0% of each run, Pallas kernels for 22% -> 23%
where the time goes in v3:
time: 94.8 us; the launch traced here: 94.6 us
  Pallas kernels  28.1 us (30%)
  waiting for transfers between devices  23.8 us (25%)
  blocking collectives  22.3 us (24%)
  starting transfers between devices  18.8 us (20%)
  local copies, waits for them, and re-layouts  1.38 us (1%)
    all_to_all x1, blocking collectives, reduce_slots(): total = lax.all_to_all(total, ('dp_0', 'dp_1'), 0, 0, tiled=True)  22.3 us
    ppermute x4, waiting for transfers between devices, flip(): return lax.ppermute(x, ('row', 'col'), [(0, 3), (3, 0), (1, 2), (2, 1)])  10.3 us
    ppermute x4, starting transfers between devices, flip(): return lax.ppermute(x, 'col', [(0, 1), (1, 0)])  9.91 us
    pallas_call x1, Pallas kernels, outer(): call(outer_parts, [jax.ShapeDtypeStruct(*s) for s in shapes], 1, 1, 2 * p...  8.7 us
    ppermute x4, waiting for transfers between devices, flip(): return lax.ppermute(x, 'col', [(0, 1), (1, 0)])  8.28 us
    pallas_call x1, Pallas kernels, inner(): call(inner_parts, [jax.ShapeDtypeStruct((pixels, width), F32), jax.ShapeD...  6.32 us
    ppermute x4, starting transfers between devices, flip(): return lax.ppermute(x, ('row', 'col'), [(0, 3), (3, 0), (1, 2), (2, 1)])  4.5 us
    pallas_call x1, Pallas kernels, tap_slots(): call(tap_grads, [jax.ShapeDtypeStruct((half, 16, width), F32), jax.ShapeD...  3.56 us
  transfers between devices with their start and end apart: 16, of which 11 were waited for; matrix products, arithmetic and copies ran while one was open for 0% of the time, Pallas kernels for 23%

profile of v3, /device:TPU:0, one launch (start us, length us, event | category | flops | bytes accessed | tf_op | source)
XLA Modules:
  0.0 94.6 jit_solution(3444183332748720742)
XLA Ops:
  0.1 1.3 %copy-done = bf16[1,24,24,1024]{3,2,1,0:T(8,128)(2,1)S(1)} copy-done((bf16[1,24,24,1024]{3,2,1,0:T(8,128)(2,1)S(1)}, bf16[1,24,24,1024]{3,2,1,0:T(8,128)(2,1)}, u32[]{:S(2)}) %copy-start) | copy-done | bytes 1179672
  1.4 1.9 %pick.1 = (bf16[576,256]{1,0:T(8,128)(2,1)S(1)}, bf16[576,256]{1,0:T(8,128)(2,1)S(1)}, bf16[576,256]{1,0:T(8,128)(2,1)S(1)}, bf16[576,256]{1,0:T(8,128)(2,1)S(1)}) custom-call(s32[6]{0:T(128)S(1)} %stack.27.pos_ref, bf16[576,1024]{1,0:T(8,128)(2,1)S(1)} %bitcast.8), custom_call_target="tpu_custom_call" | custom-call | flops 1207959552 | bytes 2359296 | tf_op jit(solution)/shard_map/pick/pallas_call | solution.py:175
  3.3 3.2 %collective-permute-start.3 = (bf16[576,256]{1,0:T(8,128)(2,1)S(1)}, bf16[576,256]{1,0:T(8,128)(2,1)S(1)}, u32[]{:S(2)}, u32[]{:S(2)}) collective-permute-start(bf16[576,256]{1,0:T(8,128)(2,1)S(1)} %get-tuple-element.73), channel_id=1, source_target_pairs={{0,32},{32,0},{1,33},{33,1},{2,34},{34,2},{3,35},{35,3},{4,36},{36... | collective-permute-start | bytes 884744 | tf_op jit(solution)/shard_map/ppermute | solution.py:22
  6.5 0.6 collective-permute-start.4
  7.6 8.7 %outer.1 = (f32[3,576,256]{2,1,0:T(8,128)S(1)}, bf16[864,256]{1,0:T(8,128)(2,1)S(1)}, bf16[864,256]{1,0:T(8,128)(2,1)S(1)}, bf16[576,256]{1,0:T(8,128)(2,1)S(1)}) custom-call(s32[6]{0:T(128)S(1)} %stack.27.pos_ref, bf16[576,1024]{1,0:T(8,128)(2,1)S(1)} %bitcast.9, bf16[3,3,1024,256]{3,2,1,0:T(8,128)(2,1)} %wc_ref.3, bf16[3,3,1024,256]{3,2,1,0:T(8,128)(2,1)} %wb_ref.3, ...), custom_call_target="tpu_custom_call" | custom-call | flops 4227858432 | bytes 10485760 | tf_op jit(solution)/shard_map/outer/pallas_call | solution.py:425
  16.4 1.5 %collective-permute-start = (bf16[864,256]{1,0:T(8,128)(2,1)S(1)}, bf16[864,256]{1,0:T(8,128)(2,1)S(1)}, u32[]{:S(2)}, u32[]{:S(2)}) collective-permute-start(bf16[864,256]{1,0:T(8,128)(2,1)S(1)} %get-tuple-element.68), channel_id=1, source_target_pairs={{0,64},{64,0},{1,65},{65,1},{2,66},{66,2},{3,67},{67,3},{4,68},{68... | collective-permute-start | bytes 1327112 | tf_op jit(solution)/shard_map/ppermute | solution.py:24
  17.8 2.7 %collective-permute-start.1 = (bf16[864,256]{1,0:T(8,128)(2,1)S(1)}, bf16[864,256]{1,0:T(8,128)(2,1)S(1)}, u32[]{:S(2)}, u32[]{:S(2)}) collective-permute-start(bf16[864,256]{1,0:T(8,128)(2,1)S(1)} %get-tuple-element.69), channel_id=1, source_target_pairs={{0,32},{32,0},{1,33},{33,1},{2,34},{34,2},{3,35},{35,3},{4,36},{36... | collective-permute-start | bytes 1327112 | tf_op jit(solution)/shard_map/ppermute | solution.py:22
  20.6 0.6 collective-permute-start.2
  21.3 1.2 %turn.1.xt_ref = bf16[2,256,1152]{2,1,0:T(8,128)(2,1)S(1)} custom-call(s32[6]{0:T(128)S(1)} %stack.27.pos_ref, bf16[576,256]{1,0:T(8,128)(2,1)S(1)} %get-tuple-element.79.x0, bf16[576,256]{1,0:T(8,128)(2,1)S(1)} %collective-permute-done.3.x1, bf16[576,256]{1,0:T(8,128)(2,1)S(1)} %collective-permute-done.4.x2, bf16[576,256]{1,0:T(8,128)(2,1)S(1)} %collective-permute-done.5.x3), custom_call_target="tpu_custom_call" | custom-call | flops 301989888 | bytes 2359296 | tf_op jit(solution)/shard_map/turn/pallas_call | solution.py:182
  22.5 6.3 %inner.1 = (f32[576,256]{1,0:T(8,128)S(1)}, f32[3,576,256]{2,1,0:T(8,128)S(1)}) custom-call(s32[6]{0:T(128)S(1)} %stack.27.pos_ref, bf16[576,1024]{1,0:T(8,128)(2,1)S(1)} %bitcast.10, f32[3,576,256]{2,1,0:T(8,128)S(1)} %get-tuple-element.76.part_ref, bf16[1024,256]{1,0:T(8,128)(2,1)S(1)} %copy-done.2, bf16[3,3,1024,256]{3,2,1,0:T(8,128)(2,1)} %wc_ref.3, ...), custom_call_target="tpu_custom_call" | custom-call | flops 3019898880 | bytes 10485760 | tf_op jit(solution)/shard_map/inner/pallas_call | solution.py:448
  28.9 1.8 %collective-permute-done.2.diag_ref = bf16[576,256]{1,0:T(8,128)(2,1)S(1)} collective-permute-done((bf16[576,256]{1,0:T(8,128)(2,1)S(1)}, bf16[576,256]{1,0:T(8,128)(2,1)S(1)}, u32[]{:S(2)}, u32[]{:S(2)}) %collective-permute-start.2) | collective-permute-done | bytes 294944 | tf_op jit(solution)/shard_map/ppermute | solution.py:25
  30.8 8.3 %collective-permute-done.1.col_ref = bf16[864,256]{1,0:T(8,128)(2,1)S(1)} collective-permute-done((bf16[864,256]{1,0:T(8,128)(2,1)S(1)}, bf16[864,256]{1,0:T(8,128)(2,1)S(1)}, u32[]{:S(2)}, u32[]{:S(2)}) %collective-permute-start.1) | collective-permute-done | bytes 442400 | tf_op jit(solution)/shard_map/ppermute | solution.py:22
  39.1 2.2 %merge.1 = (bf16[576,1024]{1,0:T(8,128)(2,1)S(1)}, bf16[576,256]{1,0:T(8,128)(2,1)S(1)}, bf16[576,256]{1,0:T(8,128)(2,1)S(1)}, bf16[576,256]{1,0:T(8,128)(2,1)S(1)}) custom-call(s32[6]{0:T(128)S(1)} %stack.27.pos_ref, f32[576,256]{1,0:T(8,128)S(1)} %get-tuple-element.83.pre0_ref, f32[3,576,256]{2,1,0:T(8,128)S(1)} %get-tuple-element.84.own_ref, ...), custom_call_target="tpu_custom_call" | custom-call | flops 452984832 | bytes 6291456 | tf_op jit(solution)/shard_map/merge/pallas_call | solution.py:528
  41.3 2.8 %collective-permute-start.10 = (bf16[576,256]{1,0:T(8,128)(2,1)S(1)}, bf16[576,256]{1,0:T(8,128)(2,1)S(1)}, u32[]{:S(2)}, u32[]{:S(2)}) collective-permute-start(bf16[576,256]{1,0:T(8,128)(2,1)S(1)} %get-tuple-element.105.d0), channel_id=1, source_target_pairs={{0,96},{96,0},{32,64},{64,32},{1,97},{97,1},{33,65},{65,33},{2,98}... | collective-permute-start | bytes 884744 | tf_op jit(solution)/shard_map/ppermute | solution.py:25
  44.2 0.8 collective-permute-start.8
  45.0 0.6 collective-permute-start.9
  45.5 1.6 %pair.1 = (f32[1024,256]{1,0:T(8,128)S(1)}, bf16[512,256]{1,0:T(8,128)(2,1)S(1)}, bf16[512,256]{1,0:T(8,128)(2,1)S(1)}) custom-call(s32[6]{0:T(128)S(1)} %stack.27.pos_ref, bf16[576,1024]{1,0:T(8,128)(2,1)S(1)} %get-tuple-element.88.joined_ref, bf16[576,256]{1,0:T(8,128)(2,1)S(1)} %get-tuple-element.89.g_ref, bf16[576,1024]{1,0:T(8,128)(2,1)S(1)} %bitcast.11, ...), custom_call_target="tpu_custom_call" | custom-call | flops 603979776 | bytes 4194304 | tf_op jit(solution)/shard_map/pair/pallas_call | solution.py:581
  47.8 1.0 %collective-permute-done.6.got0 = bf16[512,256]{1,0:T(8,128)(2,1)S(1)} collective-permute-done((bf16[512,256]{1,0:T(8,128)(2,1)S(1)}, bf16[512,256]{1,0:T(8,128)(2,1)S(1)}, u32[]{:S(2)}, u32[]{:S(2)}) %collective-permute-start.6) | collective-permute-done | bytes 262176 | tf_op jit(solution)/shard_map/ppermute | solution.py:169
  49.1 7.5 %collective-permute-done.10.d3 = bf16[576,256]{1,0:T(8,128)(2,1)S(1)} collective-permute-done((bf16[576,256]{1,0:T(8,128)(2,1)S(1)}, bf16[576,256]{1,0:T(8,128)(2,1)S(1)}, u32[]{:S(2)}, u32[]{:S(2)}) %collective-permute-start.10) | collective-permute-done | bytes 294944 | tf_op jit(solution)/shard_map/ppermute | solution.py:25
  56.6 0.7 collective-permute-done.9.d2
  57.3 0.7 rows.1
  58.0 3.2 %collective-permute-start.11 = (bf16[16,16,256]{2,1,0:T(8,128)(2,1)S(1)}, bf16[16,16,256]{2,1,0:T(8,128)(2,1)S(1)}, u32[]{:S(2)}, u32[]{:S(2)}) collective-permute-start(bf16[16,16,256]{2,1,0:T(8,128)(2,1)S(1)} %get-tuple-element.113), channel_id=1, source_target_pairs={{0,32},{32,0},{1,33},{33,1},{2,34},{34,2},{3,35},{35,3},{4,36},{36... | collective-permute-start | bytes 393224 | tf_op jit(solution)/shard_map/ppermute | solution.py:22
  61.2 0.6 collective-permute-start.12
  61.8 0.6 collective-permute-start.13
  62.4 3.6 %taps.1 = (f32[96,16,256]{2,1,0:T(8,128)S(1)}, bf16[96,16,256]{2,1,0:T(8,128)(2,1)S(1)}) custom-call(s32[6]{0:T(128)S(1)} %stack.27.pos_ref, s32[176]{0:T(256)S(1)} %fusion.1.place_ref, bf16[576,256]{1,0:T(8,128)(2,1)S(1)} %get-tuple-element.105.d0, bf16[576,256]{1,0:T(8,128)(2,1)S(1)} %collective-permute-done.8.d1, ...), custom_call_target="tpu_custom_call" | custom-call | flops 2113929216 | bytes 8388608 | tf_op jit(solution)/shard_map/taps/pallas_call | solution.py:228
  66.0 1.0 %collective-permute-done.12 = bf16[16,16,256]{2,1,0:T(8,128)(2,1)S(1)} collective-permute-done((bf16[16,16,256]{2,1,0:T(8,128)(2,1)S(1)}, bf16[16,16,256]{2,1,0:T(8,128)(2,1)S(1)}, u32[]{:S(2)}, u32[]{:S(2)}) %collective-permute-start.12) | collective-permute-done | bytes 131104 | tf_op jit(solution)/shard_map/ppermute | solution.py:24
  67.0 1.0 %collective-permute-done.13 = bf16[16,16,256]{2,1,0:T(8,128)(2,1)S(1)} collective-permute-done((bf16[16,16,256]{2,1,0:T(8,128)(2,1)S(1)}, bf16[16,16,256]{2,1,0:T(8,128)(2,1)S(1)}, u32[]{:S(2)}, u32[]{:S(2)}) %collective-permute-start.13) | collective-permute-done | bytes 131104 | tf_op jit(solution)/shard_map/ppermute | solution.py:25
  68.1 0.6 collective-permute-start.15
  68.7 1.8 %collective-permute-done.15.other_ref = bf16[16,16,256]{2,1,0:T(8,128)(2,1)S(1)} collective-permute-done((bf16[16,16,256]{2,1,0:T(8,128)(2,1)S(1)}, bf16[16,16,256]{2,1,0:T(8,128)(2,1)S(1)}, u32[]{:S(2)}, u32[]{:S(2)}) %collective-permute-start.15) | collective-permute-done | bytes 131104 | tf_op jit(solution)/shard_map/ppermute | solution.py:169
  70.5 1.1 %owners.1 = bf16[16,96,256]{2,1,0:T(8,128)(2,1)S(1)} custom-call(s32[6]{0:T(128)S(1)} %stack.27.pos_ref, s32[176]{0:T(256)S(1)} %fusion.1.place_ref, f32[96,16,256]{2,1,0:T(8,128)S(1)} %get-tuple-element.110.keep_ref, bf16[96,16,256]{2,1,0:T(8,128)(2,1)S(1)} %collective-permute-done.14.got_ref, f32[16,16,256]{2,1,0:T(8,128)S(1)} %get-tuple-element.122.mine_ref, ...), custom_call_target="tpu_custom_call" | custom-call | flops 393216 | bytes 3145728 | tf_op jit(solution)/shard_map/owners/pallas_call | solution.py:249
  71.6 22.3 %all_to_all.5.r_ref = bf16[16,96,256]{2,1,0:T(8,128)(2,1)S(1)} all-to-all(bf16[16,96,256]{2,1,0:T(8,128)(2,1)S(1)} %owners.1), channel_id=1, replica_groups=mesh['row'=2,'col'=2,'dp_0'=4,'dp_1'=4,'dp_2'=2] {'dp_0','dp_1'}, dimensions={0} | all-to-all | bytes 1572864 | tf_op jit(solution)/shard_map/all_to_all | solution.py:260
  93.8 0.8 last.1
  (26 shorter events, 2.0 us)
Async XLA Ops:
  0.1 1.3 %copy-start = (bf16[1,24,24,1024]{3,2,1,0:T(8,128)(2,1)S(1)}, bf16[1,24,24,1024]{3,2,1,0:T(8,128)(2,1)}, u32[]{:S(2)}) copy-start(bf16[1,24,24,1024]{3,2,1,0:T(8,128)(2,1)} %param.8) | copy-start | bytes 3538948
  1.4 6.3 %copy-start.1 = (bf16[1,24,24,1024]{3,2,1,0:T(8,128)(2,1)S(1)}, bf16[1,24,24,1024]{3,2,1,0:T(8,128)(2,1)}, u32[]{:S(2)}) copy-start(bf16[1,24,24,1024]{3,2,1,0:T(8,128)(2,1)} %param.8) | copy-start | bytes 3538948
  3.3 17.3 %collective-permute-start.3 = (bf16[576,256]{1,0:T(8,128)(2,1)S(1)}, bf16[576,256]{1,0:T(8,128)(2,1)S(1)}, u32[]{:S(2)}, u32[]{:S(2)}) collective-permute-start(bf16[576,256]{1,0:T(8,128)(2,1)S(1)} %get-tuple-element.73), channel_id=1, source_target_pairs={{0,32},{32,0},{1,33},{33,1},{2,34},{34,2},{3,35},{35,3},{4,36},{36... | collective-permute-start | bytes 884744 | tf_op jit(solution)/shard_map/ppermute | solution.py:22
  6.5 14.8 %collective-permute-start.4 = (bf16[576,256]{1,0:T(8,128)(2,1)S(1)}, bf16[576,256]{1,0:T(8,128)(2,1)S(1)}, u32[]{:S(2)}, u32[]{:S(2)}) collective-permute-start(bf16[576,256]{1,0:T(8,128)(2,1)S(1)} %get-tuple-element.74), channel_id=1, source_target_pairs={{0,64},{64,0},{1,65},{65,1},{2,66},{66,2},{3,67},{67,3},{4,68},{68... | collective-permute-start | bytes 884744 | tf_op jit(solution)/shard_map/ppermute | solution.py:24
  7.1 14.2 %collective-permute-start.5 = (bf16[576,256]{1,0:T(8,128)(2,1)S(1)}, bf16[576,256]{1,0:T(8,128)(2,1)S(1)}, u32[]{:S(2)}, u32[]{:S(2)}) collective-permute-start(bf16[576,256]{1,0:T(8,128)(2,1)S(1)} %get-tuple-element.75), channel_id=1, source_target_pairs={{0,96},{96,0},{32,64},{64,32},{1,97},{97,1},{33,65},{65,33},{2,98}... | collective-permute-start | bytes 884744 | tf_op jit(solution)/shard_map/ppermute | solution.py:25
  16.3 6.2 %copy-start.2 = (bf16[1024,256]{1,0:T(8,128)(2,1)S(1)}, bf16[1024,256]{1,0:T(8,128)(2,1)}, u32[]{:S(2)}) copy-start(bf16[1024,256]{1,0:T(8,128)(2,1)} %wp_ref.2) | copy-start | bytes 1572868
  16.4 14.4 %collective-permute-start = (bf16[864,256]{1,0:T(8,128)(2,1)S(1)}, bf16[864,256]{1,0:T(8,128)(2,1)S(1)}, u32[]{:S(2)}, u32[]{:S(2)}) collective-permute-start(bf16[864,256]{1,0:T(8,128)(2,1)S(1)} %get-tuple-element.68), channel_id=1, source_target_pairs={{0,64},{64,0},{1,65},{65,1},{2,66},{66,2},{3,67},{67,3},{4,68},{68... | collective-permute-start | bytes 1327112 | tf_op jit(solution)/shard_map/ppermute | solution.py:24
  17.8 21.2 %collective-permute-start.1 = (bf16[864,256]{1,0:T(8,128)(2,1)S(1)}, bf16[864,256]{1,0:T(8,128)(2,1)S(1)}, u32[]{:S(2)}, u32[]{:S(2)}) collective-permute-start(bf16[864,256]{1,0:T(8,128)(2,1)S(1)} %get-tuple-element.69), channel_id=1, source_target_pairs={{0,32},{32,0},{1,33},{33,1},{2,34},{34,2},{3,35},{35,3},{4,36},{36... | collective-permute-start | bytes 1327112 | tf_op jit(solution)/shard_map/ppermute | solution.py:22
  20.6 10.1 %collective-permute-start.2 = (bf16[576,256]{1,0:T(8,128)(2,1)S(1)}, bf16[576,256]{1,0:T(8,128)(2,1)S(1)}, u32[]{:S(2)}, u32[]{:S(2)}) collective-permute-start(bf16[576,256]{1,0:T(8,128)(2,1)S(1)} %get-tuple-element.70), channel_id=1, source_target_pairs={{0,96},{96,0},{32,64},{64,32},{1,97},{97,1},{33,65},{65,33},{2,98}... | collective-permute-start | bytes 884744 | tf_op jit(solution)/shard_map/ppermute | solution.py:25
  22.5 16.6 %copy-start.3 = (bf16[1024,256]{1,0:T(8,128)(2,1)S(1)}, bf16[1024,256]{1,0:T(8,128)(2,1)}, u32[]{:S(2)}) copy-start(bf16[1024,256]{1,0:T(8,128)(2,1)} %wp_ref.3) | copy-start | bytes 1572868
  22.5 16.6 %copy-start.4 = (bf16[1,24,24,256]{3,2,1,0:T(8,128)(2,1)S(1)}, bf16[1,24,24,256]{3,2,1,0:T(8,128)(2,1)}, u32[]{:S(2)}) copy-start(bf16[1,24,24,256]{3,2,1,0:T(8,128)(2,1)} %param.9) | copy-start | bytes 884740
  41.3 6.4 %copy-start.5 = (s32[176]{0:T(256)S(1)}, s32[176]{0:T(256)}, u32[]{:S(2)}) copy-start(s32[176]{0:T(256)} %param.15) | copy-start | bytes 2116
  41.3 15.3 %collective-permute-start.10 = (bf16[576,256]{1,0:T(8,128)(2,1)S(1)}, bf16[576,256]{1,0:T(8,128)(2,1)S(1)}, u32[]{:S(2)}, u32[]{:S(2)}) collective-permute-start(bf16[576,256]{1,0:T(8,128)(2,1)S(1)} %get-tuple-element.105.d0), channel_id=1, source_target_pairs={{0,96},{96,0},{32,64},{64,32},{1,97},{97,1},{33,65},{65,33},{2,98}... | collective-permute-start | bytes 884744 | tf_op jit(solution)/shard_map/ppermute | solution.py:25
  44.2 12.5 %collective-permute-start.8 = (bf16[576,256]{1,0:T(8,128)(2,1)S(1)}, bf16[576,256]{1,0:T(8,128)(2,1)S(1)}, u32[]{:S(2)}, u32[]{:S(2)}) collective-permute-start(bf16[576,256]{1,0:T(8,128)(2,1)S(1)} %get-tuple-element.105.d0), channel_id=1, source_target_pairs={{0,32},{32,0},{1,33},{33,1},{2,34},{34,2},{3,35},{35,3},{4,36},{36... | collective-permute-start | bytes 884744 | tf_op jit(solution)/shard_map/ppermute | solution.py:22
  45.0 12.4 %collective-permute-start.9 = (bf16[576,256]{1,0:T(8,128)(2,1)S(1)}, bf16[576,256]{1,0:T(8,128)(2,1)S(1)}, u32[]{:S(2)}, u32[]{:S(2)}) collective-permute-start(bf16[576,256]{1,0:T(8,128)(2,1)S(1)} %get-tuple-element.105.d0), channel_id=1, source_target_pairs={{0,64},{64,0},{1,65},{65,1},{2,66},{66,2},{3,67},{67,3},{4,68},{68... | collective-permute-start | bytes 884744 | tf_op jit(solution)/shard_map/ppermute | solution.py:24
  47.2 1.6 %collective-permute-start.6 = (bf16[512,256]{1,0:T(8,128)(2,1)S(1)}, bf16[512,256]{1,0:T(8,128)(2,1)S(1)}, u32[]{:S(2)}, u32[]{:S(2)}) collective-permute-start(bf16[512,256]{1,0:T(8,128)(2,1)S(1)} %get-tuple-element.92), channel_id=1, source_target_pairs={{0,1},{1,0},{2,3},{3,2},{4,5},{5,4},{6,7},{7,6},{8,9},{9,8},{10,11... | collective-permute-start | bytes 786440 | tf_op jit(solution)/shard_map/ppermute | solution.py:169
  47.2 1.9 %collective-permute-start.7 = (bf16[512,256]{1,0:T(8,128)(2,1)S(1)}, bf16[512,256]{1,0:T(8,128)(2,1)S(1)}, u32[]{:S(2)}, u32[]{:S(2)}) collective-permute-start(bf16[512,256]{1,0:T(8,128)(2,1)S(1)} %get-tuple-element.93), channel_id=1, source_target_pairs={{0,1},{1,0},{2,3},{3,2},{4,5},{5,4},{6,7},{7,6},{8,9},{9,8},{10,11... | collective-permute-start | bytes 786440 | tf_op jit(solution)/shard_map/ppermute | solution.py:169
  58.0 7.9 %collective-permute-start.11 = (bf16[16,16,256]{2,1,0:T(8,128)(2,1)S(1)}, bf16[16,16,256]{2,1,0:T(8,128)(2,1)S(1)}, u32[]{:S(2)}, u32[]{:S(2)}) collective-permute-start(bf16[16,16,256]{2,1,0:T(8,128)(2,1)S(1)} %get-tuple-element.113), channel_id=1, source_target_pairs={{0,32},{32,0},{1,33},{33,1},{2,34},{34,2},{3,35},{35,3},{4,36},{36... | collective-permute-start | bytes 393224 | tf_op jit(solution)/shard_map/ppermute | solution.py:22
  61.2 5.7 %collective-permute-start.12 = (bf16[16,16,256]{2,1,0:T(8,128)(2,1)S(1)}, bf16[16,16,256]{2,1,0:T(8,128)(2,1)S(1)}, u32[]{:S(2)}, u32[]{:S(2)}) collective-permute-start(bf16[16,16,256]{2,1,0:T(8,128)(2,1)S(1)} %get-tuple-element.114), channel_id=1, source_target_pairs={{0,64},{64,0},{1,65},{65,1},{2,66},{66,2},{3,67},{67,3},{4,68},{68... | collective-permute-start | bytes 393224 | tf_op jit(solution)/shard_map/ppermute | solution.py:24
  61.8 6.2 %collective-permute-start.13 = (bf16[16,16,256]{2,1,0:T(8,128)(2,1)S(1)}, bf16[16,16,256]{2,1,0:T(8,128)(2,1)S(1)}, u32[]{:S(2)}, u32[]{:S(2)}) collective-permute-start(bf16[16,16,256]{2,1,0:T(8,128)(2,1)S(1)} %get-tuple-element.115), channel_id=1, source_target_pairs={{0,96},{96,0},{32,64},{64,32},{1,97},{97,1},{33,65},{65,33},{2,98}... | collective-permute-start | bytes 393224 | tf_op jit(solution)/shard_map/ppermute | solution.py:25
  68.0 2.5 %collective-permute-start.14 = (bf16[96,16,256]{2,1,0:T(8,128)(2,1)S(1)}, bf16[96,16,256]{2,1,0:T(8,128)(2,1)S(1)}, u32[]{:S(2)}, u32[]{:S(2)}) collective-permute-start(bf16[96,16,256]{2,1,0:T(8,128)(2,1)S(1)} %get-tuple-element.116), channel_id=1, source_target_pairs={{0,1},{1,0},{2,3},{3,2},{4,5},{5,4},{6,7},{7,6},{8,9},{9,8},{10,11... | collective-permute-start | bytes 2359304 | tf_op jit(solution)/shard_map/ppermute | solution.py:169
  68.1 2.4 %collective-permute-start.15 = (bf16[16,16,256]{2,1,0:T(8,128)(2,1)S(1)}, bf16[16,16,256]{2,1,0:T(8,128)(2,1)S(1)}, u32[]{:S(2)}, u32[]{:S(2)}) collective-permute-start(bf16[16,16,256]{2,1,0:T(8,128)(2,1)S(1)} %get-tuple-element.121), channel_id=1, source_target_pairs={{0,1},{1,0},{2,3},{3,2},{4,5},{5,4},{6,7},{7,6},{8,9},{9,8},{10,11... | collective-permute-start | bytes 393224 | tf_op jit(solution)/shard_map/ppermute | solution.py:169

commit v4 on v3

--- a/solution.py
+++ b/solution.py
@@ -46,16 +46,29 @@
     )
 
 
-def select_channels(pos_ref, x_ref, *o_refs):
+def select_channels(pos_ref, x_ref, *rest):
+    *o_refs, held, picks, sems = rest
     chans = x_ref.shape[1]
     width = o_refs[0].shape[1]
+    pieces = sems.shape[0]
+    each = x_ref.shape[0] // pieces
+    copies = []
+    for n in range(pieces):
+        part = pl.ds(n * each, each)
+        copies.append(pltpu.make_async_copy(x_ref.at[part, :], held.at[part, :], sems.at[n]))
+        copies[n].start()
     source = lax.broadcasted_iota(jnp.int32, (chans, width), 0)
     col = lax.broadcasted_iota(jnp.int32, (1, width), 1)
     wanted = 64 * (col // 16) + col % 16
-    for k, o_ref in enumerate(o_refs):
+    for k in range(len(o_refs)):
         c = jnp.bitwise_xor(pos_ref[0], k)
-        pick = jnp.where(source == wanted + 16 * c, 1.0, 0.0).astype(BF)
-        o_ref[...] = jnp.dot(x_ref[...], pick, preferred_element_type=F32).astype(BF)
+        picks[:, k * width : (k + 1) * width] = jnp.where(source == wanted + 16 * c, 1.0, 0.0).astype(BF)
+    for n in range(pieces):
+        copies[n].wait()
+        part = slice(n * each, (n + 1) * each)
+        for k, o_ref in enumerate(o_refs):
+            pick = picks[:, k * width : (k + 1) * width]
+            o_ref[part, :] = jnp.dot(held[part, :], pick, preferred_element_type=F32).astype(BF)
 
 
 def turn_pixels(pos_ref, x0, x1, x2, x3, o_ref, held):
@@ -172,9 +185,22 @@
 def pick(pos, centre):
     pixels, chans = centre.shape
     block = jax.ShapeDtypeStruct((pixels, chans // 4), BF)
-    return call(select_channels, [block] * 4, 1, 1, 2 * pixels * chans * chans, 4 * pixels * chans, 14, name="pick")(
-        pos, centre
-    )
+    return call(
+        select_channels,
+        [block] * 4,
+        1,
+        0,
+        2 * pixels * chans * chans,
+        4 * pixels * chans,
+        14,
+        [
+            pltpu.VMEM((pixels, chans), BF),
+            pltpu.VMEM((chans, chans), BF),
+            pltpu.SemaphoreType.DMA((2,)),
+        ],
+        name="pick",
+        n_any=1,
+    )(pos, pltpu.with_memory_space_constraint(centre, pltpu.HBM))
 
 
 def turn(pos, got):
@@ -281,12 +307,20 @@
 
 
 def turned_by(x, shift, far):
-    return jnp.where(far == 0, roll_cols(x, shift), roll_cols(x, SIDE - shift))
+    return roll_cols(x, shift if far == 0 else SIDE - shift)
 
 
 def rank_of(shape, far):
     at = lax.broadcasted_iota(jnp.int32, shape, 1)
-    return jnp.where(far == 0, at, SIDE - 1 - at)
+    return at if far == 0 else SIDE - 1 - at
+
+
+def by_side(side, body):
+    for far in range(2):
+
+        @pl.when(side == far)
+        def _(far=far):
+            body(far)
 
 
 def row_marks(low, rate):
@@ -333,32 +367,38 @@
 
 
 def outer_parts(pos_ref, x_ref, wc_ref, wb_ref, wa_ref, pre_ref, row_ref, col_ref, diag_ref, ext, acc, y, held, sems):
-    low, far = pos_ref[2], pos_ref[3]
+    low = pos_ref[2]
     whole = SIDE * SIDE
     width = pre_ref.shape[2]
+    count = len(OUTER)
     copies = tap_copies(pos_ref, (wc_ref, wb_ref, wa_ref), OUTER, held, sems)
     for copy in copies:
         copy.start()
-    first = 0
-    for turn, (index, rate) in enumerate(BRANCHES):
+
+    def products(turn):
+        rate = BRANCHES[turn][1]
+        at = row_marks(low, rate)
+        inside = whole - rate * SIDE
+        for copy in copies[turn * count : (turn + 1) * count]:
+            copy.wait()
+        y[turn] = jnp.dot(x_ref[...], held[turn, :, : 4 * width], preferred_element_type=F32)
+        acc[turn, :inside, :] = jnp.dot(
+            x_ref[pl.ds(at["inward_from"], inside), :], held[turn, :, 4 * width :], preferred_element_type=F32
+        )
+
+    def sums(turn, far):
+        index, rate = BRANCHES[turn]
         lead = rate * SIDE
         inside = whole - lead
         at = row_marks(low, rate)
         own_rows = pl.ds(at["own"], whole)
         their_rows = pl.ds(at["theirs"], lead)
         kept_rows = pl.ds(at["kept"], inside)
-        to_row = slice(first, first + lead)
-        first += lead
-        count = len(OUTER)
-        for copy in copies[turn * count : (turn + 1) * count]:
-            copy.wait()
-        y[...] = jnp.dot(x_ref[...], held[turn, :, : 4 * width], preferred_element_type=F32)
+        first = sum(r for _, r in BRANCHES[:turn]) * SIDE
         ext[pl.ds(pl.multiple_of(whole - at["theirs"], 16), lead), :] = jnp.zeros((lead, width), F32)
-        ext[pl.ds(at["out"], whole), :] = y[:, :width]
-        ext[own_rows, :] += y[:, width : 2 * width]
-        ext[pl.ds(at["inward"], inside), :] += jnp.dot(
-            x_ref[pl.ds(at["inward_from"], inside), :], held[turn, :, 4 * width :], preferred_element_type=F32
-        )
+        ext[pl.ds(at["out"], whole), :] = y[turn, :, :width]
+        ext[own_rows, :] += y[turn, :, width : 2 * width]
+        ext[pl.ds(at["inward"], inside), :] += acc[turn, :inside, :]
         own = blocks(ext[own_rows, :])
         ours = turned_by(own, rate, far)
         rank = rank_of(own.shape, far)
@@ -366,7 +406,6 @@
         below = blocks(ext[their_rows, :])
         theirs = turned_by(below, rate, far)
         place = rank_of(below.shape, far)
-        acc[:lead, :] = flat(jnp.where(place >= rate, theirs, 0.0))
         if rate == RATE_C:
             col_ref[:whole, :] = flat(jnp.where(rank < rate, ours, 0.0)).astype(BF)
             diag_ref[:lead, :] = flat(jnp.where(place < rate, theirs, 0.0)).astype(BF)
@@ -380,41 +419,54 @@
             col_ref[:whole, :] = flat(jnp.where(rank >= RATE_C, own, have)).astype(BF)
             have = blocks(diag_ref[:lead, :].astype(F32))
             diag_ref[:lead, :] = flat(jnp.where(place >= RATE_C, below, have)).astype(BF)
-        next_from = pl.multiple_of(jnp.where(low == 0, inside, 0), 16)
-        keep_from = pl.multiple_of(jnp.where(low == 0, 0, lead), 16)
-        pre_ref[index, kept_rows, :] += y[pl.ds(keep_from, inside), 2 * width : 3 * width]
-        own = blocks(y[pl.ds(keep_from, inside), 3 * width :])
-        rank = rank_of(own.shape, far)
-        pre_ref[index, kept_rows, :] += flat(jnp.where(rank < SIDE - rate, turned_by(own, rate, 1 - far), 0.0))
-        below = blocks(y[pl.ds(next_from, lead), 3 * width :])
-        theirs = flat(jnp.where(place < SIDE - rate, turned_by(below, rate, 1 - far), 0.0))
-        row_ref[to_row, :] = (acc[:lead, :] + y[pl.ds(next_from, lead), 2 * width : 3 * width] + theirs).astype(BF)
+        next_rows = pl.ds(pl.multiple_of(jnp.where(low == 0, inside, 0), 16), lead)
+        keep_rows = pl.ds(pl.multiple_of(jnp.where(low == 0, 0, lead), 16), inside)
+        own = blocks(y[turn, keep_rows, 3 * width :])
+        moved = flat(jnp.where(rank_of(own.shape, far) < SIDE - rate, turned_by(own, rate, 1 - far), 0.0))
+        pre_ref[index, kept_rows, :] += y[turn, keep_rows, 2 * width : 3 * width] + moved
+        below = blocks(y[turn, next_rows, 3 * width :])
+        total = jnp.where(place < SIDE - rate, turned_by(below, rate, 1 - far), 0.0)
+        total = flat(total + jnp.where(place >= rate, theirs, 0.0))
+        row_ref[first : first + lead, :] = (total + y[turn, next_rows, 2 * width : 3 * width]).astype(BF)
+
+    def body(far):
+        products(0)
+        products(1)
+        sums(0, far)
+        products(2)
+        sums(1, far)
+        sums(2, far)
+
+    by_side(pos_ref[3], body)
 
 
 def inner_parts(pos_ref, x_ref, part_ref, wp_ref, wc_ref, wb_ref, wa_ref, pre0_ref, pre_ref, y, z, held, sems):
-    low, far = pos_ref[2], pos_ref[3]
+    low = pos_ref[2]
     whole = SIDE * SIDE
     width = pre0_ref.shape[1]
+    count = len(INNER)
     copies = tap_copies(pos_ref, (wc_ref, wb_ref, wa_ref), INNER, held, sems)
     for copy in copies:
         copy.start()
     pre0_ref[...] = jnp.dot(x_ref[...], wp_ref[...], preferred_element_type=F32)
-    for turn, (index, rate) in enumerate(BRANCHES):
-        lead = rate * SIDE
-        inside = whole - lead
-        at = row_marks(low, rate)
-        from_rows = pl.ds(at["inward_from"], inside)
-        to_rows = pl.ds(at["inner"], inside)
-        count = len(INNER)
-        for copy in copies[turn * count : (turn + 1) * count]:
-            copy.wait()
-        y[...] = jnp.dot(x_ref[...], held[turn, :, : 2 * width], preferred_element_type=F32)
-        z[:inside, :] = jnp.dot(x_ref[from_rows, :], held[turn, :, 2 * width :], preferred_element_type=F32)
-        y[to_rows, :] += z[:inside, :]
-        own = blocks(y[:, width:])
-        rank = rank_of(own.shape, far)
-        moved = flat(jnp.where(rank < SIDE - rate, turned_by(own, rate, 1 - far), 0.0))
-        pre_ref[index] = part_ref[index] + y[:, :width] + moved
+
+    def body(far):
+        for turn, (index, rate) in enumerate(BRANCHES):
+            inside = whole - rate * SIDE
+            at = row_marks(low, rate)
+            from_rows = pl.ds(at["inward_from"], inside)
+            to_rows = pl.ds(at["inner"], inside)
+            for copy in copies[turn * count : (turn + 1) * count]:
+                copy.wait()
+            y[...] = jnp.dot(x_ref[...], held[turn, :, : 2 * width], preferred_element_type=F32)
+            z[:inside, :] = jnp.dot(x_ref[from_rows, :], held[turn, :, 2 * width :], preferred_element_type=F32)
+            y[to_rows, :] += z[:inside, :]
+            own = blocks(y[:, width:])
+            rank = rank_of(own.shape, far)
+            moved = flat(jnp.where(rank < SIDE - rate, turned_by(own, rate, 1 - far), 0.0))
+            pre_ref[index] = part_ref[index] + y[:, :width] + moved
+
+    by_side(pos_ref[3], body)
 
 
 def outer(pos, centre, w_rate_a, w_rate_b, w_rate_c):
@@ -429,11 +481,11 @@
         1,
         2 * pixels * chans * width * 14,
         10 * MIB,
-        28,
+        36,
         [
             pltpu.VMEM(((SIDE + RATE_C) * SIDE, width), F32),
-            pltpu.VMEM((RATE_C * SIDE, width), F32),
-            pltpu.VMEM((pixels, 4 * width), F32),
+            pltpu.VMEM((3, pixels, width), F32),
+            pltpu.VMEM((3, pixels, 4 * width), F32),
             pltpu.VMEM((3, chans, len(OUTER) * width), BF),
             pltpu.SemaphoreType.DMA((3, len(OUTER))),
         ],
@@ -468,7 +520,6 @@
     pos_ref, pre0_ref, own_ref, row_ref, col_ref, diag_ref, cot_ref, wp_ref, joined_ref, g_ref, d0_ref, d3_ref, pre
 ):
     low = pos_ref[2]
-    theirs = 1 - pos_ref[3]
     width = pre0_ref.shape[1]
     whole = SIDE * SIDE
 
@@ -482,29 +533,32 @@
         pre[index, pl.ds(rows_of(rate), lead), :] += row_ref[first : first + lead, :].astype(F32)
         first += lead
 
-    part = blocks(col_ref[:whole, :].astype(F32))
-    rank = rank_of(part.shape, theirs)
-    pre[2] += flat(jnp.where(rank < RATE_C, part, 0.0))
-    pre[0] += flat(turned_by(jnp.where(rank >= RATE_C, part, 0.0), RATE_A, theirs))
-    part = blocks(col_ref[whole:, :].astype(F32))
-    rank = rank_of(part.shape, theirs)
-    pre[1, : RATE_B * SIDE, :] += flat(jnp.where(rank < RATE_B, part, 0.0))
-    pre[1, RATE_B * SIDE :, :] += flat(roll_cols(jnp.where(rank >= RATE_B, part, 0.0), RATE_B))
-
-    part = blocks(diag_ref[: RATE_C * SIDE, :].astype(F32))
-    rank = rank_of(part.shape, theirs)
-    pre[2, pl.ds(rows_of(RATE_C), RATE_C * SIDE), :] += flat(jnp.where(rank < RATE_C, part, 0.0))
-    few = part[:RATE_A]
-    few = turned_by(jnp.where(rank[:RATE_A] >= RATE_C, few, 0.0), RATE_A, theirs)
-    pre[0, pl.ds(rows_of(RATE_A), RATE_A * SIDE), :] += flat(few)
-    part = blocks(diag_ref[RATE_C * SIDE :, :].astype(F32))
-    rank = rank_of(part.shape, theirs)
-    half = RATE_B // 2
-    at = rows_of(RATE_B)
-    pre[1, pl.ds(at, half * SIDE), :] += flat(jnp.where(rank < RATE_B, part, 0.0))
-    last = pl.multiple_of(at + half * SIDE, 16)
-    pre[1, pl.ds(last, half * SIDE), :] += flat(roll_cols(jnp.where(rank >= RATE_B, part, 0.0), RATE_B))
-
+    def body(far):
+        theirs = 1 - far
+        part = blocks(col_ref[:whole, :].astype(F32))
+        rank = rank_of(part.shape, theirs)
+        pre[2] += flat(jnp.where(rank < RATE_C, part, 0.0))
+        pre[0] += flat(turned_by(jnp.where(rank >= RATE_C, part, 0.0), RATE_A, theirs))
+        part = blocks(col_ref[whole:, :].astype(F32))
+        rank = rank_of(part.shape, theirs)
+        pre[1, : RATE_B * SIDE, :] += flat(jnp.where(rank < RATE_B, part, 0.0))
+        pre[1, RATE_B * SIDE :, :] += flat(roll_cols(jnp.where(rank >= RATE_B, part, 0.0), RATE_B))
+
+        part = blocks(diag_ref[: RATE_C * SIDE, :].astype(F32))
+        rank = rank_of(part.shape, theirs)
+        pre[2, pl.ds(rows_of(RATE_C), RATE_C * SIDE), :] += flat(jnp.where(rank < RATE_C, part, 0.0))
+        few = part[:RATE_A]
+        few = turned_by(jnp.where(rank[:RATE_A] >= RATE_C, few, 0.0), RATE_A, theirs)
+        pre[0, pl.ds(rows_of(RATE_A), RATE_A * SIDE), :] += flat(few)
+        part = blocks(diag_ref[RATE_C * SIDE :, :].astype(F32))
+        rank = rank_of(part.shape, theirs)
+        half = RATE_B // 2
+        at = rows_of(RATE_B)
+        pre[1, pl.ds(at, half * SIDE), :] += flat(jnp.where(rank < RATE_B, part, 0.0))
+        last = pl.multiple_of(at + half * SIDE, 16)
+        pre[1, pl.ds(last, half * SIDE), :] += flat(roll_cols(jnp.where(rank >= RATE_B, part, 0.0), RATE_B))
+
+    by_side(pos_ref[3], body)
     slopes = {}
     for k in range(4):
         value = pre0_ref[...] if k == 0 else pre[k - 1]

time: 94.8 us -> 94.8 us (level)
  local copies, waits for them, and re-layouts: 1.38 us -> 0.11 us
  Pallas kernels: 28.1 us -> 29.3 us
    unnamed x12 -> x10, local copies, waits for them, and re-layouts: 1.3 us -> 0.03 us
    pallas_call x1, Pallas kernels: 1.94 us -> 3.15 us  [pick(): call(select_channels, [block] * 4, 1, 0, 2 * pixels * chans * chans, 4 *...]
  transfers between devices with their start and end apart: 16 -> 16, of which waited for: 11 -> 10; matrix products, arithmetic and copies ran while one was open for 0% -> 0% of each run, Pallas kernels for 23% -> 22%
where the time goes in v4:
time: 94.8 us; the launch traced here: 94.7 us
  Pallas kernels  29.3 us (31%)
  waiting for transfers between devices  23.9 us (25%)
  blocking collectives  22.3 us (24%)
  starting transfers between devices  18.9 us (20%)
    all_to_all x1, blocking collectives, reduce_slots(): total = lax.all_to_all(total, ('dp_0', 'dp_1'), 0, 0, tiled=True)  22.3 us
    ppermute x4, waiting for transfers between devices, flip(): return lax.ppermute(x, ('row', 'col'), [(0, 3), (3, 0), (1, 2), (2, 1)])  10.7 us
    ppermute x4, starting transfers between devices, flip(): return lax.ppermute(x, 'col', [(0, 1), (1, 0)])  9.68 us
    pallas_call x1, Pallas kernels, outer(): call(outer_parts, [jax.ShapeDtypeStruct(*s) for s in shapes], 1, 1, 2 * p...  8.96 us
    ppermute x4, waiting for transfers between devices, flip(): return lax.ppermute(x, 'col', [(0, 1), (1, 0)])  8.37 us
    pallas_call x1, Pallas kernels, inner(): call(inner_parts, [jax.ShapeDtypeStruct((pixels, width), F32), jax.ShapeD...  5.89 us
    ppermute x4, starting transfers between devices, flip(): return lax.ppermute(x, ('row', 'col'), [(0, 3), (3, 0), (1, 2), (2, 1)])  4.68 us
    pallas_call x1, Pallas kernels, tap_slots(): call(tap_grads, [jax.ShapeDtypeStruct((half, 16, width), F32), jax.ShapeD...  3.6 us
  transfers between devices with their start and end apart: 16, of which 10 were waited for; matrix products, arithmetic and copies ran while one was open for 0% of the time, Pallas kernels for 22%

profile of v4, /device:TPU:0, one launch (start us, length us, event | category | flops | bytes accessed | tf_op | source)
XLA Modules:
  0.0 94.7 jit_solution(5987299154597250258)
XLA Ops:
  0.1 3.2 %pick.1 = (bf16[576,256]{1,0:T(8,128)(2,1)S(1)}, bf16[576,256]{1,0:T(8,128)(2,1)S(1)}, bf16[576,256]{1,0:T(8,128)(2,1)S(1)}, bf16[576,256]{1,0:T(8,128)(2,1)S(1)}) custom-call(s32[6]{0:T(128)S(1)} %stack.27.pos_ref, bf16[576,1024]{1,0:T(8,128)(2,1)} %bitcast.8), custom_call_target="tpu_custom_call" | custom-call | flops 1207959552 | bytes 2359296 | tf_op jit(solution)/shard_map/pick/pallas_call | solution.py:188
  3.2 3.2 %collective-permute-start.3 = (bf16[576,256]{1,0:T(8,128)(2,1)S(1)}, bf16[576,256]{1,0:T(8,128)(2,1)S(1)}, u32[]{:S(2)}, u32[]{:S(2)}) collective-permute-start(bf16[576,256]{1,0:T(8,128)(2,1)S(1)} %get-tuple-element.73), channel_id=1, source_target_pairs={{0,32},{32,0},{1,33},{33,1},{2,34},{34,2},{3,35},{35,3},{4,36},{36... | collective-permute-start | bytes 884744 | tf_op jit(solution)/shard_map/ppermute | solution.py:22
  6.4 0.6 collective-permute-start.4
  7.0 0.6 collective-permute-start.5
  7.6 9.0 %outer.1 = (f32[3,576,256]{2,1,0:T(8,128)S(1)}, bf16[864,256]{1,0:T(8,128)(2,1)S(1)}, bf16[864,256]{1,0:T(8,128)(2,1)S(1)}, bf16[576,256]{1,0:T(8,128)(2,1)S(1)}) custom-call(s32[6]{0:T(128)S(1)} %stack.27.pos_ref, bf16[576,1024]{1,0:T(8,128)(2,1)S(1)} %bitcast.9, bf16[3,3,1024,256]{3,2,1,0:T(8,128)(2,1)} %wc_ref.3, bf16[3,3,1024,256]{3,2,1,0:T(8,128)(2,1)} %wb_ref.3, ...), custom_call_target="tpu_custom_call" | custom-call | flops 4227858432 | bytes 10485760 | tf_op jit(solution)/shard_map/outer/pallas_call | solution.py:477
  16.6 1.5 %collective-permute-start = (bf16[864,256]{1,0:T(8,128)(2,1)S(1)}, bf16[864,256]{1,0:T(8,128)(2,1)S(1)}, u32[]{:S(2)}, u32[]{:S(2)}) collective-permute-start(bf16[864,256]{1,0:T(8,128)(2,1)S(1)} %get-tuple-element.68), channel_id=1, source_target_pairs={{0,64},{64,0},{1,65},{65,1},{2,66},{66,2},{3,67},{67,3},{4,68},{68... | collective-permute-start | bytes 1327112 | tf_op jit(solution)/shard_map/ppermute | solution.py:24
  18.1 2.5 %collective-permute-start.1 = (bf16[864,256]{1,0:T(8,128)(2,1)S(1)}, bf16[864,256]{1,0:T(8,128)(2,1)S(1)}, u32[]{:S(2)}, u32[]{:S(2)}) collective-permute-start(bf16[864,256]{1,0:T(8,128)(2,1)S(1)} %get-tuple-element.69), channel_id=1, source_target_pairs={{0,32},{32,0},{1,33},{33,1},{2,34},{34,2},{3,35},{35,3},{4,36},{36... | collective-permute-start | bytes 1327112 | tf_op jit(solution)/shard_map/ppermute | solution.py:22
  20.6 0.8 collective-permute-start.2
  21.4 1.2 %turn.1.xt_ref = bf16[2,256,1152]{2,1,0:T(8,128)(2,1)S(1)} custom-call(s32[6]{0:T(128)S(1)} %stack.27.pos_ref, bf16[576,256]{1,0:T(8,128)(2,1)S(1)} %get-tuple-element.79.x0, bf16[576,256]{1,0:T(8,128)(2,1)S(1)} %collective-permute-done.3.x1, bf16[576,256]{1,0:T(8,128)(2,1)S(1)} %collective-permute-done.4.x2, bf16[576,256]{1,0:T(8,128)(2,1)S(1)} %collective-permute-done.5.x3), custom_call_target="tpu_custom_call" | custom-call | flops 301989888 | bytes 2359296 | tf_op jit(solution)/shard_map/turn/pallas_call | solution.py:208
  22.6 5.9 %inner.1 = (f32[576,256]{1,0:T(8,128)S(1)}, f32[3,576,256]{2,1,0:T(8,128)S(1)}) custom-call(s32[6]{0:T(128)S(1)} %stack.27.pos_ref, bf16[576,1024]{1,0:T(8,128)(2,1)S(1)} %bitcast.10, f32[3,576,256]{2,1,0:T(8,128)S(1)} %get-tuple-element.76.part_ref, bf16[1024,256]{1,0:T(8,128)(2,1)S(1)} %copy-done.1, bf16[3,3,1024,256]{3,2,1,0:T(8,128)(2,1)} %wc_ref.3, ...), custom_call_target="tpu_custom_call" | custom-call | flops 3019898880 | bytes 10485760 | tf_op jit(solution)/shard_map/inner/pallas_call | solution.py:500
  28.5 2.2 %collective-permute-done.2.diag_ref = bf16[576,256]{1,0:T(8,128)(2,1)S(1)} collective-permute-done((bf16[576,256]{1,0:T(8,128)(2,1)S(1)}, bf16[576,256]{1,0:T(8,128)(2,1)S(1)}, u32[]{:S(2)}, u32[]{:S(2)}) %collective-permute-start.2) | collective-permute-done | bytes 294944 | tf_op jit(solution)/shard_map/ppermute | solution.py:25
  30.7 8.4 %collective-permute-done.1.col_ref = bf16[864,256]{1,0:T(8,128)(2,1)S(1)} collective-permute-done((bf16[864,256]{1,0:T(8,128)(2,1)S(1)}, bf16[864,256]{1,0:T(8,128)(2,1)S(1)}, u32[]{:S(2)}, u32[]{:S(2)}) %collective-permute-start.1) | collective-permute-done | bytes 442400 | tf_op jit(solution)/shard_map/ppermute | solution.py:22
  39.1 2.3 %merge.1 = (bf16[576,1024]{1,0:T(8,128)(2,1)S(1)}, bf16[576,256]{1,0:T(8,128)(2,1)S(1)}, bf16[576,256]{1,0:T(8,128)(2,1)S(1)}, bf16[576,256]{1,0:T(8,128)(2,1)S(1)}) custom-call(s32[6]{0:T(128)S(1)} %stack.27.pos_ref, f32[576,256]{1,0:T(8,128)S(1)} %get-tuple-element.83.pre0_ref, f32[3,576,256]{2,1,0:T(8,128)S(1)} %get-tuple-element.84.own_ref, ...), custom_call_target="tpu_custom_call" | custom-call | flops 452984832 | bytes 6291456 | tf_op jit(solution)/shard_map/merge/pallas_call | solution.py:582
  41.4 2.7 %collective-permute-start.10 = (bf16[576,256]{1,0:T(8,128)(2,1)S(1)}, bf16[576,256]{1,0:T(8,128)(2,1)S(1)}, u32[]{:S(2)}, u32[]{:S(2)}) collective-permute-start(bf16[576,256]{1,0:T(8,128)(2,1)S(1)} %get-tuple-element.105.d0), channel_id=1, source_target_pairs={{0,96},{96,0},{32,64},{64,32},{1,97},{97,1},{33,65},{65,33},{2,98}... | collective-permute-start | bytes 884744 | tf_op jit(solution)/shard_map/ppermute | solution.py:25
  44.2 0.8 collective-permute-start.8
  45.0 0.7 collective-permute-start.9
  45.6 1.6 %pair.1 = (f32[1024,256]{1,0:T(8,128)S(1)}, bf16[512,256]{1,0:T(8,128)(2,1)S(1)}, bf16[512,256]{1,0:T(8,128)(2,1)S(1)}) custom-call(s32[6]{0:T(128)S(1)} %stack.27.pos_ref, bf16[576,1024]{1,0:T(8,128)(2,1)S(1)} %get-tuple-element.88.joined_ref, bf16[576,256]{1,0:T(8,128)(2,1)S(1)} %get-tuple-element.89.g_ref, bf16[576,1024]{1,0:T(8,128)(2,1)S(1)} %bitcast.11, ...), custom_call_target="tpu_custom_call" | custom-call | flops 603979776 | bytes 4194304 | tf_op jit(solution)/shard_map/pair/pallas_call | solution.py:635
  47.9 1.0 %collective-permute-done.6.got0 = bf16[512,256]{1,0:T(8,128)(2,1)S(1)} collective-permute-done((bf16[512,256]{1,0:T(8,128)(2,1)S(1)}, bf16[512,256]{1,0:T(8,128)(2,1)S(1)}, u32[]{:S(2)}, u32[]{:S(2)}) %collective-permute-start.6) | collective-permute-done | bytes 262176 | tf_op jit(solution)/shard_map/ppermute | solution.py:182
  49.2 7.4 %collective-permute-done.10.d3 = bf16[576,256]{1,0:T(8,128)(2,1)S(1)} collective-permute-done((bf16[576,256]{1,0:T(8,128)(2,1)S(1)}, bf16[576,256]{1,0:T(8,128)(2,1)S(1)}, u32[]{:S(2)}, u32[]{:S(2)}) %collective-permute-start.10) | collective-permute-done | bytes 294944 | tf_op jit(solution)/shard_map/ppermute | solution.py:25
  56.6 0.7 collective-permute-done.9.d2
  57.3 0.7 rows.1
  58.1 3.2 %collective-permute-start.11 = (bf16[16,16,256]{2,1,0:T(8,128)(2,1)S(1)}, bf16[16,16,256]{2,1,0:T(8,128)(2,1)S(1)}, u32[]{:S(2)}, u32[]{:S(2)}) collective-permute-start(bf16[16,16,256]{2,1,0:T(8,128)(2,1)S(1)} %get-tuple-element.113), channel_id=1, source_target_pairs={{0,32},{32,0},{1,33},{33,1},{2,34},{34,2},{3,35},{35,3},{4,36},{36... | collective-permute-start | bytes 393224 | tf_op jit(solution)/shard_map/ppermute | solution.py:22
  61.2 0.6 collective-permute-start.12
  61.9 0.6 collective-permute-start.13
  62.5 3.6 %taps.1 = (f32[96,16,256]{2,1,0:T(8,128)S(1)}, bf16[96,16,256]{2,1,0:T(8,128)(2,1)S(1)}) custom-call(s32[6]{0:T(128)S(1)} %stack.27.pos_ref, s32[176]{0:T(256)S(1)} %fusion.1.place_ref, bf16[576,256]{1,0:T(8,128)(2,1)S(1)} %get-tuple-element.105.d0, bf16[576,256]{1,0:T(8,128)(2,1)S(1)} %collective-permute-done.8.d1, ...), custom_call_target="tpu_custom_call" | custom-call | flops 2113929216 | bytes 8388608 | tf_op jit(solution)/shard_map/taps/pallas_call | solution.py:254
  66.1 0.9 collective-permute-done.12
  67.0 1.0 %collective-permute-done.13 = bf16[16,16,256]{2,1,0:T(8,128)(2,1)S(1)} collective-permute-done((bf16[16,16,256]{2,1,0:T(8,128)(2,1)S(1)}, bf16[16,16,256]{2,1,0:T(8,128)(2,1)S(1)}, u32[]{:S(2)}, u32[]{:S(2)}) %collective-permute-start.13) | collective-permute-done | bytes 131104 | tf_op jit(solution)/shard_map/ppermute | solution.py:25
  68.1 0.6 collective-permute-start.15
  68.7 1.8 %collective-permute-done.15.other_ref = bf16[16,16,256]{2,1,0:T(8,128)(2,1)S(1)} collective-permute-done((bf16[16,16,256]{2,1,0:T(8,128)(2,1)S(1)}, bf16[16,16,256]{2,1,0:T(8,128)(2,1)S(1)}, u32[]{:S(2)}, u32[]{:S(2)}) %collective-permute-start.15) | collective-permute-done | bytes 131104 | tf_op jit(solution)/shard_map/ppermute | solution.py:182
  70.5 1.1 %owners.1 = bf16[16,96,256]{2,1,0:T(8,128)(2,1)S(1)} custom-call(s32[6]{0:T(128)S(1)} %stack.27.pos_ref, s32[176]{0:T(256)S(1)} %fusion.1.place_ref, f32[96,16,256]{2,1,0:T(8,128)S(1)} %get-tuple-element.110.keep_ref, bf16[96,16,256]{2,1,0:T(8,128)(2,1)S(1)} %collective-permute-done.14.got_ref, f32[16,16,256]{2,1,0:T(8,128)S(1)} %get-tuple-element.122.mine_ref, ...), custom_call_target="tpu_custom_call" | custom-call | flops 393216 | bytes 3145728 | tf_op jit(solution)/shard_map/owners/pallas_call | solution.py:275
  71.6 22.3 %all_to_all.5.r_ref = bf16[16,96,256]{2,1,0:T(8,128)(2,1)S(1)} all-to-all(bf16[16,96,256]{2,1,0:T(8,128)(2,1)S(1)} %owners.1), channel_id=1, replica_groups=mesh['row'=2,'col'=2,'dp_0'=4,'dp_1'=4,'dp_2'=2] {'dp_0','dp_1'}, dimensions={0} | all-to-all | bytes 1572864 | tf_op jit(solution)/shard_map/all_to_all | solution.py:286
  93.9 0.8 last.1
  (24 shorter events, 1.2 us)
Async XLA Ops:
  0.1 7.5 %copy-start = (bf16[1,24,24,1024]{3,2,1,0:T(8,128)(2,1)S(1)}, bf16[1,24,24,1024]{3,2,1,0:T(8,128)(2,1)}, u32[]{:S(2)}) copy-start(bf16[1,24,24,1024]{3,2,1,0:T(8,128)(2,1)} %param.8) | copy-start | bytes 3538948
  3.2 17.3 %collective-permute-start.3 = (bf16[576,256]{1,0:T(8,128)(2,1)S(1)}, bf16[576,256]{1,0:T(8,128)(2,1)S(1)}, u32[]{:S(2)}, u32[]{:S(2)}) collective-permute-start(bf16[576,256]{1,0:T(8,128)(2,1)S(1)} %get-tuple-element.73), channel_id=1, source_target_pairs={{0,32},{32,0},{1,33},{33,1},{2,34},{34,2},{3,35},{35,3},{4,36},{36... | collective-permute-start | bytes 884744 | tf_op jit(solution)/shard_map/ppermute | solution.py:22
  6.4 14.9 %collective-permute-start.4 = (bf16[576,256]{1,0:T(8,128)(2,1)S(1)}, bf16[576,256]{1,0:T(8,128)(2,1)S(1)}, u32[]{:S(2)}, u32[]{:S(2)}) collective-permute-start(bf16[576,256]{1,0:T(8,128)(2,1)S(1)} %get-tuple-element.74), channel_id=1, source_target_pairs={{0,64},{64,0},{1,65},{65,1},{2,66},{66,2},{3,67},{67,3},{4,68},{68... | collective-permute-start | bytes 884744 | tf_op jit(solution)/shard_map/ppermute | solution.py:24
  7.0 14.3 %collective-permute-start.5 = (bf16[576,256]{1,0:T(8,128)(2,1)S(1)}, bf16[576,256]{1,0:T(8,128)(2,1)S(1)}, u32[]{:S(2)}, u32[]{:S(2)}) collective-permute-start(bf16[576,256]{1,0:T(8,128)(2,1)S(1)} %get-tuple-element.75), channel_id=1, source_target_pairs={{0,96},{96,0},{32,64},{64,32},{1,97},{97,1},{33,65},{65,33},{2,98}... | collective-permute-start | bytes 884744 | tf_op jit(solution)/shard_map/ppermute | solution.py:25
  16.6 6.0 %copy-start.1 = (bf16[1024,256]{1,0:T(8,128)(2,1)S(1)}, bf16[1024,256]{1,0:T(8,128)(2,1)}, u32[]{:S(2)}) copy-start(bf16[1024,256]{1,0:T(8,128)(2,1)} %wp_ref.2) | copy-start | bytes 1572868
  16.6 14.2 %collective-permute-start = (bf16[864,256]{1,0:T(8,128)(2,1)S(1)}, bf16[864,256]{1,0:T(8,128)(2,1)S(1)}, u32[]{:S(2)}, u32[]{:S(2)}) collective-permute-start(bf16[864,256]{1,0:T(8,128)(2,1)S(1)} %get-tuple-element.68), channel_id=1, source_target_pairs={{0,64},{64,0},{1,65},{65,1},{2,66},{66,2},{3,67},{67,3},{4,68},{68... | collective-permute-start | bytes 1327112 | tf_op jit(solution)/shard_map/ppermute | solution.py:24
  18.1 21.0 %collective-permute-start.1 = (bf16[864,256]{1,0:T(8,128)(2,1)S(1)}, bf16[864,256]{1,0:T(8,128)(2,1)S(1)}, u32[]{:S(2)}, u32[]{:S(2)}) collective-permute-start(bf16[864,256]{1,0:T(8,128)(2,1)S(1)} %get-tuple-element.69), channel_id=1, source_target_pairs={{0,32},{32,0},{1,33},{33,1},{2,34},{34,2},{3,35},{35,3},{4,36},{36... | collective-permute-start | bytes 1327112 | tf_op jit(solution)/shard_map/ppermute | solution.py:22
  20.6 10.1 %collective-permute-start.2 = (bf16[576,256]{1,0:T(8,128)(2,1)S(1)}, bf16[576,256]{1,0:T(8,128)(2,1)S(1)}, u32[]{:S(2)}, u32[]{:S(2)}) collective-permute-start(bf16[576,256]{1,0:T(8,128)(2,1)S(1)} %get-tuple-element.70), channel_id=1, source_target_pairs={{0,96},{96,0},{32,64},{64,32},{1,97},{97,1},{33,65},{65,33},{2,98}... | collective-permute-start | bytes 884744 | tf_op jit(solution)/shard_map/ppermute | solution.py:25
  22.5 16.6 %copy-start.2 = (bf16[1024,256]{1,0:T(8,128)(2,1)S(1)}, bf16[1024,256]{1,0:T(8,128)(2,1)}, u32[]{:S(2)}) copy-start(bf16[1024,256]{1,0:T(8,128)(2,1)} %wp_ref.3) | copy-start | bytes 1572868
  22.6 16.6 %copy-start.3 = (bf16[1,24,24,256]{3,2,1,0:T(8,128)(2,1)S(1)}, bf16[1,24,24,256]{3,2,1,0:T(8,128)(2,1)}, u32[]{:S(2)}) copy-start(bf16[1,24,24,256]{3,2,1,0:T(8,128)(2,1)} %param.9) | copy-start | bytes 884740
  41.4 6.4 %copy-start.4 = (s32[176]{0:T(256)S(1)}, s32[176]{0:T(256)}, u32[]{:S(2)}) copy-start(s32[176]{0:T(256)} %param.15) | copy-start | bytes 2116
  41.4 15.2 %collective-permute-start.10 = (bf16[576,256]{1,0:T(8,128)(2,1)S(1)}, bf16[576,256]{1,0:T(8,128)(2,1)S(1)}, u32[]{:S(2)}, u32[]{:S(2)}) collective-permute-start(bf16[576,256]{1,0:T(8,128)(2,1)S(1)} %get-tuple-element.105.d0), channel_id=1, source_target_pairs={{0,96},{96,0},{32,64},{64,32},{1,97},{97,1},{33,65},{65,33},{2,98}... | collective-permute-start | bytes 884744 | tf_op jit(solution)/shard_map/ppermute | solution.py:25
  44.2 12.5 %collective-permute-start.8 = (bf16[576,256]{1,0:T(8,128)(2,1)S(1)}, bf16[576,256]{1,0:T(8,128)(2,1)S(1)}, u32[]{:S(2)}, u32[]{:S(2)}) collective-permute-start(bf16[576,256]{1,0:T(8,128)(2,1)S(1)} %get-tuple-element.105.d0), channel_id=1, source_target_pairs={{0,32},{32,0},{1,33},{33,1},{2,34},{34,2},{3,35},{35,3},{4,36},{36... | collective-permute-start | bytes 884744 | tf_op jit(solution)/shard_map/ppermute | solution.py:22
  45.0 12.4 %collective-permute-start.9 = (bf16[576,256]{1,0:T(8,128)(2,1)S(1)}, bf16[576,256]{1,0:T(8,128)(2,1)S(1)}, u32[]{:S(2)}, u32[]{:S(2)}) collective-permute-start(bf16[576,256]{1,0:T(8,128)(2,1)S(1)} %get-tuple-element.105.d0), channel_id=1, source_target_pairs={{0,64},{64,0},{1,65},{65,1},{2,66},{66,2},{3,67},{67,3},{4,68},{68... | collective-permute-start | bytes 884744 | tf_op jit(solution)/shard_map/ppermute | solution.py:24
  47.2 1.6 %collective-permute-start.6 = (bf16[512,256]{1,0:T(8,128)(2,1)S(1)}, bf16[512,256]{1,0:T(8,128)(2,1)S(1)}, u32[]{:S(2)}, u32[]{:S(2)}) collective-permute-start(bf16[512,256]{1,0:T(8,128)(2,1)S(1)} %get-tuple-element.92), channel_id=1, source_target_pairs={{0,1},{1,0},{2,3},{3,2},{4,5},{5,4},{6,7},{7,6},{8,9},{9,8},{10,11... | collective-permute-start | bytes 786440 | tf_op jit(solution)/shard_map/ppermute | solution.py:182
  47.3 1.9 %collective-permute-start.7 = (bf16[512,256]{1,0:T(8,128)(2,1)S(1)}, bf16[512,256]{1,0:T(8,128)(2,1)S(1)}, u32[]{:S(2)}, u32[]{:S(2)}) collective-permute-start(bf16[512,256]{1,0:T(8,128)(2,1)S(1)} %get-tuple-element.93), channel_id=1, source_target_pairs={{0,1},{1,0},{2,3},{3,2},{4,5},{5,4},{6,7},{7,6},{8,9},{9,8},{10,11... | collective-permute-start | bytes 786440 | tf_op jit(solution)/shard_map/ppermute | solution.py:182
  58.1 8.0 %collective-permute-start.11 = (bf16[16,16,256]{2,1,0:T(8,128)(2,1)S(1)}, bf16[16,16,256]{2,1,0:T(8,128)(2,1)S(1)}, u32[]{:S(2)}, u32[]{:S(2)}) collective-permute-start(bf16[16,16,256]{2,1,0:T(8,128)(2,1)S(1)} %get-tuple-element.113), channel_id=1, source_target_pairs={{0,32},{32,0},{1,33},{33,1},{2,34},{34,2},{3,35},{35,3},{4,36},{36... | collective-permute-start | bytes 393224 | tf_op jit(solution)/shard_map/ppermute | solution.py:22
  61.2 5.7 %collective-permute-start.12 = (bf16[16,16,256]{2,1,0:T(8,128)(2,1)S(1)}, bf16[16,16,256]{2,1,0:T(8,128)(2,1)S(1)}, u32[]{:S(2)}, u32[]{:S(2)}) collective-permute-start(bf16[16,16,256]{2,1,0:T(8,128)(2,1)S(1)} %get-tuple-element.114), channel_id=1, source_target_pairs={{0,64},{64,0},{1,65},{65,1},{2,66},{66,2},{3,67},{67,3},{4,68},{68... | collective-permute-start | bytes 393224 | tf_op jit(solution)/shard_map/ppermute | solution.py:24
  61.9 6.2 %collective-permute-start.13 = (bf16[16,16,256]{2,1,0:T(8,128)(2,1)S(1)}, bf16[16,16,256]{2,1,0:T(8,128)(2,1)S(1)}, u32[]{:S(2)}, u32[]{:S(2)}) collective-permute-start(bf16[16,16,256]{2,1,0:T(8,128)(2,1)S(1)} %get-tuple-element.115), channel_id=1, source_target_pairs={{0,96},{96,0},{32,64},{64,32},{1,97},{97,1},{33,65},{65,33},{2,98}... | collective-permute-start | bytes 393224 | tf_op jit(solution)/shard_map/ppermute | solution.py:25
  68.0 2.5 %collective-permute-start.14 = (bf16[96,16,256]{2,1,0:T(8,128)(2,1)S(1)}, bf16[96,16,256]{2,1,0:T(8,128)(2,1)S(1)}, u32[]{:S(2)}, u32[]{:S(2)}) collective-permute-start(bf16[96,16,256]{2,1,0:T(8,128)(2,1)S(1)} %get-tuple-element.116), channel_id=1, source_target_pairs={{0,1},{1,0},{2,3},{3,2},{4,5},{5,4},{6,7},{7,6},{8,9},{9,8},{10,11... | collective-permute-start | bytes 2359304 | tf_op jit(solution)/shard_map/ppermute | solution.py:182
  68.1 2.4 %collective-permute-start.15 = (bf16[16,16,256]{2,1,0:T(8,128)(2,1)S(1)}, bf16[16,16,256]{2,1,0:T(8,128)(2,1)S(1)}, u32[]{:S(2)}, u32[]{:S(2)}) collective-permute-start(bf16[16,16,256]{2,1,0:T(8,128)(2,1)S(1)} %get-tuple-element.121), channel_id=1, source_target_pairs={{0,1},{1,0},{2,3},{3,2},{4,5},{5,4},{6,7},{7,6},{8,9},{9,8},{10,11... | collective-permute-start | bytes 393224 | tf_op jit(solution)/shard_map/ppermute | solution.py:182

commit v5 on v4

--- a/solution.py
+++ b/solution.py
@@ -1,3 +1,5 @@
+import functools
+
 import jax
 import jax.numpy as jnp
 from jax import lax
@@ -90,14 +92,18 @@
     return jnp.concatenate([x[:, x.shape[1] - shift :], x[:, : x.shape[1] - shift]], axis=1)
 
 
-def tap_grads(pos_ref, place_ref, d0, d1, d2, d3, xt_ref, keep_ref, send_ref, held, padded, buf):
+def tap_grads(pos_ref, place_ref, *refs):
+    deltas, (xt_ref, keep_ref, send_ref, held, padded, buf) = refs[:8], refs[8:]
     side = RATE_C
-    pixels, width = d0.shape
-    cols = 24
+    half, width = deltas[0].shape
+    pixels = 2 * half
+    cols = SIDE
     rows = pixels // cols
-    for k, d in enumerate((d0, d1, d2, d3)):
+    for k in range(4):
         s = jnp.bitwise_xor(pos_ref[0], k)
-        held[s % 2, pl.ds((s // 2) * pixels, pixels), :] = d[...]
+        upper = s // 2
+        for first, d in ((3 * upper, deltas[k]), (1 + upper, deltas[4 + k])):
+            held[s % 2, pl.ds(pl.multiple_of(first * half, 16), half), :] = d[...]
     buf[...] = jnp.zeros_like(buf)
     tall = 2 * pixels
     lead = side * cols
@@ -249,13 +255,14 @@
 
 
 def tap_slots(pos, place, deltas, turned, slot_count):
-    pixels, width = deltas[0].shape
+    width = deltas[0].shape[1]
+    pixels = 2 * deltas[0].shape[0]
     half = slot_count // 2
     return call(
         tap_grads,
         [jax.ShapeDtypeStruct((half, 16, width), F32), jax.ShapeDtypeStruct((half, 16, width), BF)],
         2,
-        5,
+        9,
         2 * 7 * 4 * pixels * width * width,
         8 * 1024 * 1024,
         26,
@@ -366,7 +373,9 @@
 INNER = ((1, 1), (1, 2), (2, 1), (2, 2))
 
 
-def outer_parts(pos_ref, x_ref, wc_ref, wb_ref, wa_ref, pre_ref, row_ref, col_ref, diag_ref, ext, acc, y, held, sems):
+def outer_parts(
+    pos_ref, x_ref, wc_ref, wb_ref, wa_ref, pre_ref, rf_ref, cf_ref, df_ref, rn_ref, cn_ref, dn_ref, ext, acc, y, part, held, sems
+):
     low = pos_ref[2]
     whole = SIDE * SIDE
     width = pre_ref.shape[2]
@@ -394,7 +403,6 @@
         own_rows = pl.ds(at["own"], whole)
         their_rows = pl.ds(at["theirs"], lead)
         kept_rows = pl.ds(at["kept"], inside)
-        first = sum(r for _, r in BRANCHES[:turn]) * SIDE
         ext[pl.ds(pl.multiple_of(whole - at["theirs"], 16), lead), :] = jnp.zeros((lead, width), F32)
         ext[pl.ds(at["out"], whole), :] = y[turn, :, :width]
         ext[own_rows, :] += y[turn, :, width : 2 * width]
@@ -407,18 +415,35 @@
         theirs = turned_by(below, rate, far)
         place = rank_of(below.shape, far)
         if rate == RATE_C:
-            col_ref[:whole, :] = flat(jnp.where(rank < rate, ours, 0.0)).astype(BF)
-            diag_ref[:lead, :] = flat(jnp.where(place < rate, theirs, 0.0)).astype(BF)
+            part[0, :whole, :] = flat(jnp.where(rank < rate, ours, 0.0))
+            part[1, :lead, :] = flat(jnp.where(place < rate, theirs, 0.0))
         elif rate == RATE_B:
             half = rate // 2
-            col_ref[whole:, :] = flat(jnp.where(rank[:rate] < rate, ours[:rate], own[rate:])).astype(BF)
-            part = place[:half] < rate
-            diag_ref[RATE_C * SIDE :, :] = flat(jnp.where(part, theirs[:half], below[half:])).astype(BF)
+            for n in range(2):
+                top = 2 * half * n
+                pair = jnp.where(rank[:half] < rate, ours[top : top + half], own[top + half : top + 2 * half])
+                part[0, whole + half * n * SIDE : whole + half * (n + 1) * SIDE, :] = flat(pair)
+            few = place[:half] < rate
+            dn_ref[RATE_B * SIDE :, :] = flat(jnp.where(few, theirs[:half], below[half:])).astype(BF)
         else:
-            have = blocks(col_ref[:whole, :].astype(F32))
-            col_ref[:whole, :] = flat(jnp.where(rank >= RATE_C, own, have)).astype(BF)
-            have = blocks(diag_ref[:lead, :].astype(F32))
-            diag_ref[:lead, :] = flat(jnp.where(place >= RATE_C, below, have)).astype(BF)
+            have = blocks(part[0, :whole, :])
+            part[0, :whole, :] = flat(jnp.where(rank >= RATE_C, own, have))
+            mid = whole // 2
+            quarter = RATE_A * SIDE
+            for away, to in ((True, cf_ref), (False, cn_ref)):
+                lower = jnp.where(low == 0, 0, 1) if away else jnp.where(low == 0, 1, 0)
+                at_a = pl.multiple_of(lower * mid, 16)
+                at_b = pl.multiple_of(whole + lower * quarter, 16)
+                to[:mid, :] = part[0, pl.ds(at_a, mid), :].astype(BF)
+                to[mid:, :] = part[0, pl.ds(at_b, quarter), :].astype(BF)
+            away_at = pl.multiple_of(jnp.where(low == 0, 2 * quarter, 0), 16)
+            near_at = pl.multiple_of(jnp.where(low == 0, 0, quarter), 16)
+            df_ref[...] = part[1, pl.ds(away_at, quarter), :].astype(BF)
+            near = blocks(part[1, pl.ds(near_at, 2 * quarter), :])
+            dn_ref[:quarter, :] = flat(jnp.where(place >= RATE_C, below, near[:RATE_A])).astype(BF)
+            dn_ref[quarter : 2 * quarter, :] = flat(near[RATE_A:]).astype(BF)
+            rf_ref[...] = part[2, pl.ds(away_at, quarter), :].astype(BF)
+            rn_ref[: 2 * quarter, :] = part[2, pl.ds(near_at, 2 * quarter), :].astype(BF)
         next_rows = pl.ds(pl.multiple_of(jnp.where(low == 0, inside, 0), 16), lead)
         keep_rows = pl.ds(pl.multiple_of(jnp.where(low == 0, 0, lead), 16), inside)
         own = blocks(y[turn, keep_rows, 3 * width :])
@@ -427,7 +452,13 @@
         below = blocks(y[turn, next_rows, 3 * width :])
         total = jnp.where(place < SIDE - rate, turned_by(below, rate, 1 - far), 0.0)
         total = flat(total + jnp.where(place >= rate, theirs, 0.0))
-        row_ref[first : first + lead, :] = (total + y[turn, next_rows, 2 * width : 3 * width]).astype(BF)
+        total = total + y[turn, next_rows, 2 * width : 3 * width]
+        if rate == RATE_C:
+            part[2, :lead, :] = total
+        elif rate == RATE_B:
+            rn_ref[RATE_B * SIDE : 2 * RATE_B * SIDE, :] = total.astype(BF)
+        else:
+            rn_ref[2 * RATE_B * SIDE :, :] = total.astype(BF)
 
     def body(far):
         products(0)
@@ -472,8 +503,8 @@
 def outer(pos, centre, w_rate_a, w_rate_b, w_rate_c):
     pixels, chans = centre.shape
     width = w_rate_a.shape[3]
-    sends = (RATE_A + RATE_B + RATE_C) * SIDE
-    shapes = [((3, pixels, width), F32), ((sends, width), BF), ((sends, width), BF), ((pixels, width), BF)]
+    away, near = (RATE_A, 18, RATE_A), (30, 18, 18)
+    shapes = [((3, pixels, width), F32)] + [((n * SIDE, width), BF) for n in away + near]
     return call(
         outer_parts,
         [jax.ShapeDtypeStruct(*s) for s in shapes],
@@ -481,11 +512,12 @@
         1,
         2 * pixels * chans * width * 14,
         10 * MIB,
-        36,
+        40,
         [
             pltpu.VMEM(((SIDE + RATE_C) * SIDE, width), F32),
             pltpu.VMEM((3, pixels, width), F32),
             pltpu.VMEM((3, pixels, 4 * width), F32),
+            pltpu.VMEM((3, (SIDE + RATE_B) * SIDE, width), F32),
             pltpu.VMEM((3, chans, len(OUTER) * width), BF),
             pltpu.SemaphoreType.DMA((3, len(OUTER))),
         ],
@@ -517,57 +549,54 @@
 
 
 def merge_parts(
-    pos_ref, pre0_ref, own_ref, row_ref, col_ref, diag_ref, cot_ref, wp_ref, joined_ref, g_ref, d0_ref, d3_ref, pre
+    away, pos_ref, pre0_ref, own_ref, row_ref, col_ref, diag_ref, cot_ref, wp_ref, joined_ref, g_ref, d0_ref, d3_ref, pre
 ):
     low = pos_ref[2]
     width = pre0_ref.shape[1]
-    whole = SIDE * SIDE
-
-    def rows_of(rate):
-        return pl.multiple_of(jnp.where(low == 0, (SIDE - rate) * SIDE, 0), 16)
-
-    pre[...] = own_ref[...]
-    first = 0
-    for index, rate in ((2, RATE_C), (1, RATE_B), (0, RATE_A)):
-        lead = rate * SIDE
-        pre[index, pl.ds(rows_of(rate), lead), :] += row_ref[first : first + lead, :].astype(F32)
-        first += lead
+    half = SIDE * SIDE // 2
+    quarter = half // 2
+    lower = low if away else 1 - low
+    mine = pl.ds(pl.multiple_of(lower * half, 16), half)
+    touched = pl.multiple_of(jnp.where(low == 0, quarter, 0), 16)
+    pre[...] = own_ref[:, mine, :]
 
     def body(far):
         theirs = 1 - far
-        part = blocks(col_ref[:whole, :].astype(F32))
+        part = blocks(col_ref[:half, :].astype(F32))
         rank = rank_of(part.shape, theirs)
         pre[2] += flat(jnp.where(rank < RATE_C, part, 0.0))
         pre[0] += flat(turned_by(jnp.where(rank >= RATE_C, part, 0.0), RATE_A, theirs))
-        part = blocks(col_ref[whole:, :].astype(F32))
-        rank = rank_of(part.shape, theirs)
-        pre[1, : RATE_B * SIDE, :] += flat(jnp.where(rank < RATE_B, part, 0.0))
-        pre[1, RATE_B * SIDE :, :] += flat(roll_cols(jnp.where(rank >= RATE_B, part, 0.0), RATE_B))
-
-        part = blocks(diag_ref[: RATE_C * SIDE, :].astype(F32))
-        rank = rank_of(part.shape, theirs)
-        pre[2, pl.ds(rows_of(RATE_C), RATE_C * SIDE), :] += flat(jnp.where(rank < RATE_C, part, 0.0))
-        few = part[:RATE_A]
-        few = turned_by(jnp.where(rank[:RATE_A] >= RATE_C, few, 0.0), RATE_A, theirs)
-        pre[0, pl.ds(rows_of(RATE_A), RATE_A * SIDE), :] += flat(few)
-        part = blocks(diag_ref[RATE_C * SIDE :, :].astype(F32))
-        rank = rank_of(part.shape, theirs)
-        half = RATE_B // 2
-        at = rows_of(RATE_B)
-        pre[1, pl.ds(at, half * SIDE), :] += flat(jnp.where(rank < RATE_B, part, 0.0))
-        last = pl.multiple_of(at + half * SIDE, 16)
-        pre[1, pl.ds(last, half * SIDE), :] += flat(roll_cols(jnp.where(rank >= RATE_B, part, 0.0), RATE_B))
+        part = blocks(col_ref[half:, :].astype(F32))
+        rank = rank[: part.shape[0]]
+        pre[1, :quarter, :] += flat(jnp.where(rank < RATE_B, part, 0.0))
+        pre[1, quarter:, :] += flat(roll_cols(jnp.where(rank >= RATE_B, part, 0.0), RATE_B))
+        if away:
+            some = pl.ds(touched, quarter)
+            part = blocks(diag_ref[...].astype(F32))
+            part = flat(jnp.where(rank < RATE_C, part, 0.0))
+            pre[2, some, :] += row_ref[...].astype(F32) + part
+        else:
+            some = pl.ds(touched, quarter)
+            part = blocks(diag_ref[:half, :].astype(F32))
+            wide = rank_of(part.shape, theirs)
+            pre[2] += row_ref[:half, :].astype(F32) + flat(jnp.where(wide < RATE_C, part, 0.0))
+            pre[1] += row_ref[half : 2 * half, :].astype(F32)
+            few = turned_by(jnp.where(rank >= RATE_C, part[:RATE_A], 0.0), RATE_A, theirs)
+            pre[0, some, :] += row_ref[2 * half :, :].astype(F32) + flat(few)
+            part = blocks(diag_ref[half:, :].astype(F32))
+            pre[1, :quarter, :] += flat(jnp.where(rank < RATE_B, part, 0.0))
+            pre[1, quarter:, :] += flat(roll_cols(jnp.where(rank >= RATE_B, part, 0.0), RATE_B))
 
     by_side(pos_ref[3], body)
     slopes = {}
     for k in range(4):
-        value = pre0_ref[...] if k == 0 else pre[k - 1]
+        value = pre0_ref[mine, :] if k == 0 else pre[k - 1]
         sig = jax.nn.sigmoid(value)
         joined_ref[:, k * width : (k + 1) * width] = (value * sig).astype(BF)
         if k in (0, 3):
             slopes[k] = sig * (1.0 + value * (1.0 - sig))
     proj_pre = jnp.dot(joined_ref[...], wp_ref[...], preferred_element_type=F32)
-    g_proj = (cot_ref[...].astype(F32) * silu_slope(proj_pre)).astype(BF)
+    g_proj = (cot_ref[mine, :].astype(F32) * silu_slope(proj_pre)).astype(BF)
     g_ref[...] = g_proj
     for k, out in ((3, d3_ref), (0, d0_ref)):
         back = lax.dot_general(
@@ -576,27 +605,34 @@
         out[...] = (back * slopes[k]).astype(BF)
 
 
-def merge(pos, pre0, own, row, col, diag, cot, w_proj):
+def merge(away, pos, pre0, own, row, col, diag, cot, w_proj):
     pixels, width = pre0.shape
-    block = jax.ShapeDtypeStruct((pixels, width), BF)
+    half = pixels // 2
+    block = jax.ShapeDtypeStruct((half, width), BF)
     return call(
-        merge_parts,
-        [jax.ShapeDtypeStruct((pixels, 4 * width), BF), block, block, block],
+        functools.partial(merge_parts, away),
+        [jax.ShapeDtypeStruct((half, 4 * width), BF), block, block, block],
         1,
         7,
-        2 * pixels * width * width * 6,
-        6 * 1024 * 1024,
-        18,
-        [pltpu.VMEM((3, pixels, width), F32)],
+        2 * half * width * width * 6,
+        3 * MIB,
+        14,
+        [pltpu.VMEM((3, half, width), F32)],
         name="merge",
     )(pos, pre0, own, row, col, diag, cot, w_proj)
 
 
-def pair_grads(pos_ref, joined_ref, g_ref, x_ref, d0_ref, keep_ref, *send_refs):
+def pair_grads(pos_ref, ja_ref, ga_ref, da_ref, jn_ref, gn_ref, dn_ref, x_ref, keep_ref, *send_refs):
     core = pos_ref[4]
     over = (((0,), (0,)), ((), ()))
-    grad_proj = lax.dot_general(joined_ref[...], g_ref[...], over, preferred_element_type=F32)
-    grad_point = lax.dot_general(x_ref[...], d0_ref[...], over, preferred_element_type=F32)
+    rows = ja_ref.shape[0]
+    grad_proj = grad_point = None
+    for lower, (j, g, d) in ((pos_ref[2], (ja_ref, ga_ref, da_ref)), (1 - pos_ref[2], (jn_ref, gn_ref, dn_ref))):
+        x = x_ref[pl.ds(pl.multiple_of(lower * rows, 16), rows), :]
+        one = lax.dot_general(j[...], g[...], over, preferred_element_type=F32)
+        two = lax.dot_general(x, d[...], over, preferred_element_type=F32)
+        grad_proj = one if grad_proj is None else grad_proj + one
+        grad_point = two if grad_point is None else grad_point + two
     keep_ref[...] = jnp.where(core == 0, grad_proj, grad_point)
     half = send_refs[0].shape[0]
     for k, send_ref in enumerate(send_refs):
@@ -622,26 +658,26 @@
     got = [picked[0]] + [flip(picked[k], k) for k in (1, 2, 3)]
     part, *parts = outer(pos, centre, *weights)
     part, got = lax.optimization_barrier((part, got))
-    to_row, to_col, to_diag = parts
-    parts = [flip(to_row, 2), flip(to_col, 1), flip(to_diag, 3)]
+    parts = [flip(p, k) for p, k in zip(parts, (2, 1, 3, 2, 1, 3))]
     turned = turn(pos, got)
     pre0, own = inner(pos, centre, part, w_point, *weights)
-    parts, pre0, own, turned = lax.optimization_barrier((parts, pre0, own, turned))
-    joined, g_proj, delta0, delta3 = merge(
-        pos, pre0, own, *parts, cotangent[0].reshape(pixels, width), w_proj
-    )
-    shared = [delta3] + [flip(delta3, k) for k in (1, 2, 3)]
+    parts[:3], pre0, own, turned = lax.optimization_barrier((parts[:3], pre0, own, turned))
+    cot = cotangent[0].reshape(pixels, width)
+    *first, delta_a = merge(True, pos, pre0, own, *parts[:3], cot, w_proj)
+    shared = [delta_a] + [flip(delta_a, k) for k in (1, 2, 3)]
+    *last, delta_n = merge(False, pos, pre0, own, *parts[3:], cot, w_proj)
+    shared = shared + [delta_n] + [flip(delta_n, k) for k in (1, 2, 3)]
     block = (4 * width, width)
     kept, *sent = call(
         pair_grads,
         [jax.ShapeDtypeStruct(block, F32)] + [jax.ShapeDtypeStruct((2 * width, width), BF)] * 2,
         1,
-        4,
+        7,
         4 * pixels * chans * width,
         4 * 1024 * 1024,
         16,
         name="pair",
-    )(pos, joined, g_proj, centre, delta0)
+    )(pos, *first, *last, centre)
     got = [swap_core(part) for part in sent]
     got, shared = lax.optimization_barrier((got, shared))
     by_owner = split_pair(pos, kept, got)

time: 94.8 us -> 97.5 us (1.028)
  starting transfers between devices: 18.9 us -> 27.1 us
  waiting for transfers between devices: 23.9 us -> 17.3 us
  Pallas kernels: 29.3 us -> 30.3 us
    ppermute x4 -> x6, starting transfers between devices: 4.68 us -> 10.8 us  [flip(): return lax.ppermute(x, ('row', 'col'), [(0, 3), (3, 0), (1, 2), (2, 1)])]
    ppermute x4 -> x6, waiting for transfers between devices: 10.7 us -> 7.64 us  [flip(): return lax.ppermute(x, ('row', 'col'), [(0, 3), (3, 0), (1, 2), (2, 1)])]
    ppermute x4 -> x6, waiting for transfers between devices: 1.67 us -> 0.02 us  [flip(): return lax.ppermute(x, 'row', [(0, 1), (1, 0)])]
    ppermute x4 -> x6, starting transfers between devices: 3.33 us -> 4.81 us  [flip(): return lax.ppermute(x, 'row', [(0, 1), (1, 0)])]
    ppermute x4, waiting for transfers between devices: 3.18 us -> 1.81 us  [swap_core(): return lax.ppermute(x, 'dp_2', [(0, 1), (1, 0)])]
    ppermute x4 -> x6, starting transfers between devices: 9.68 us -> 10.3 us  [flip(): return lax.ppermute(x, 'col', [(0, 1), (1, 0)])]
    ppermute x4 -> x6, waiting for transfers between devices: 8.37 us -> 7.8 us  [flip(): return lax.ppermute(x, 'col', [(0, 1), (1, 0)])]
    pallas_call x1 -> x2, Pallas kernels: 2.31 us -> 2.84 us  [merge(): call(functools.partial(merge_parts, away), [jax.ShapeDtypeStruct((half, 4...]
  transfers between devices with their start and end apart: 16 -> 22, of which waited for: 10 -> 7; matrix products, arithmetic and copies ran while one was open for 0% -> 0% of each run, Pallas kernels for 22% -> 25%
where the time goes in v5:
time: 97.5 us; the launch traced here: 97.3 us
  Pallas kernels  30.3 us (31%)
  starting transfers between devices  27.1 us (28%)
  blocking collectives  22.3 us (23%)
  waiting for transfers between devices  17.3 us (18%)
    all_to_all x1, blocking collectives, reduce_slots(): total = lax.all_to_all(total, ('dp_0', 'dp_1'), 0, 0, tiled=True)  22.3 us
    ppermute x6, starting transfers between devices, flip(): return lax.ppermute(x, ('row', 'col'), [(0, 3), (3, 0), (1, 2), (2, 1)])  10.8 us
    ppermute x6, starting transfers between devices, flip(): return lax.ppermute(x, 'col', [(0, 1), (1, 0)])  10.3 us
    pallas_call x1, Pallas kernels, outer(): call(outer_parts, [jax.ShapeDtypeStruct(*s) for s in shapes], 1, 1, 2 * p...  8.98 us
    ppermute x6, waiting for transfers between devices, flip(): return lax.ppermute(x, 'col', [(0, 1), (1, 0)])  7.8 us
    ppermute x6, waiting for transfers between devices, flip(): return lax.ppermute(x, ('row', 'col'), [(0, 3), (3, 0), (1, 2), (2, 1)])  7.64 us
    pallas_call x1, Pallas kernels, inner(): call(inner_parts, [jax.ShapeDtypeStruct((pixels, width), F32), jax.ShapeD...  6.11 us
    ppermute x6, starting transfers between devices, flip(): return lax.ppermute(x, 'row', [(0, 1), (1, 0)])  4.81 us
  transfers between devices with their start and end apart: 22, of which 7 were waited for; matrix products, arithmetic and copies ran while one was open for 0% of the time, Pallas kernels for 25%

profile of v5, /device:TPU:0, one launch (start us, length us, event | category | flops | bytes accessed | tf_op | source)
XLA Modules:
  0.0 97.3 jit_solution(8087648207655004008)
XLA Ops:
  0.1 3.2 %pick.1 = (bf16[576,256]{1,0:T(8,128)(2,1)S(1)}, bf16[576,256]{1,0:T(8,128)(2,1)S(1)}, bf16[576,256]{1,0:T(8,128)(2,1)S(1)}, bf16[576,256]{1,0:T(8,128)(2,1)S(1)}) custom-call(s32[6]{0:T(128)S(1)} %stack.27.pos_ref, bf16[576,1024]{1,0:T(8,128)(2,1)} %bitcast.8), custom_call_target="tpu_custom_call" | custom-call | flops 1207959552 | bytes 2359296 | tf_op jit(solution)/shard_map/pick/pallas_call | solution.py:194
  3.3 3.2 %collective-permute-start.3 = (bf16[576,256]{1,0:T(8,128)(2,1)S(1)}, bf16[576,256]{1,0:T(8,128)(2,1)S(1)}, u32[]{:S(2)}, u32[]{:S(2)}) collective-permute-start(bf16[576,256]{1,0:T(8,128)(2,1)S(1)} %get-tuple-element.88), channel_id=1, source_target_pairs={{0,32},{32,0},{1,33},{33,1},{2,34},{34,2},{3,35},{35,3},{4,36},{36... | collective-permute-start | bytes 884744 | tf_op jit(solution)/shard_map/ppermute | solution.py:24
  7.6 9.0 %outer.1 = (f32[3,576,256]{2,1,0:T(8,128)S(1)}, bf16[144,256]{1,0:T(8,128)(2,1)S(1)}, bf16[432,256]{1,0:T(8,128)(2,1)S(1)}, bf16[144,256]{1,0:T(8,128)(2,1)S(1)}...) custom-call(s32[6]{0:T(128)S(1)} %stack.27.pos_ref, ...), custom_call_target="tpu_custom_call" | custom-call | flops 4227858432 | bytes 10485760 | tf_op jit(solution)/shard_map/outer/pallas_call | solution.py:508
  16.6 1.5 %collective-permute-start = (bf16[144,256]{1,0:T(8,128)(2,1)S(1)}, bf16[144,256]{1,0:T(8,128)(2,1)S(1)}, u32[]{:S(2)}, u32[]{:S(2)}) collective-permute-start(bf16[144,256]{1,0:T(8,128)(2,1)S(1)} %get-tuple-element.83), channel_id=1, source_target_pairs={{0,64},{64,0},{1,65},{65,1},{2,66},{66,2},{3,67},{67,3},{4,68},{68... | collective-permute-start | bytes 221192 | tf_op jit(solution)/shard_map/ppermute | solution.py:26
  18.1 0.6 collective-permute-start.6
  18.7 2.8 %collective-permute-start.1 = (bf16[432,256]{1,0:T(8,128)(2,1)S(1)}, bf16[432,256]{1,0:T(8,128)(2,1)S(1)}, u32[]{:S(2)}, u32[]{:S(2)}) collective-permute-start(bf16[432,256]{1,0:T(8,128)(2,1)S(1)} %get-tuple-element.84), channel_id=1, source_target_pairs={{0,32},{32,0},{1,33},{33,1},{2,34},{34,2},{3,35},{35,3},{4,36},{36... | collective-permute-start | bytes 663560 | tf_op jit(solution)/shard_map/ppermute | solution.py:24
  21.5 1.3 %collective-permute-start.2 = (bf16[144,256]{1,0:T(8,128)(2,1)S(1)}, bf16[144,256]{1,0:T(8,128)(2,1)S(1)}, u32[]{:S(2)}, u32[]{:S(2)}) collective-permute-start(bf16[144,256]{1,0:T(8,128)(2,1)S(1)} %get-tuple-element.85), channel_id=1, source_target_pairs={{0,96},{96,0},{32,64},{64,32},{1,97},{97,1},{33,65},{65,33},{2,98}... | collective-permute-start | bytes 221192 | tf_op jit(solution)/shard_map/ppermute | solution.py:27
  22.8 2.0 %collective-permute-start.7 = (bf16[432,256]{1,0:T(8,128)(2,1)S(1)}, bf16[432,256]{1,0:T(8,128)(2,1)S(1)}, u32[]{:S(2)}, u32[]{:S(2)}) collective-permute-start(bf16[432,256]{1,0:T(8,128)(2,1)S(1)} %get-tuple-element.107), channel_id=1, source_target_pairs={{0,32},{32,0},{1,33},{33,1},{2,34},{34,2},{3,35},{35,3},{4,36},{36... | collective-permute-start | bytes 663560 | tf_op jit(solution)/shard_map/ppermute | solution.py:24
  24.8 1.0 %collective-permute-start.8 = (bf16[432,256]{1,0:T(8,128)(2,1)S(1)}, bf16[432,256]{1,0:T(8,128)(2,1)S(1)}, u32[]{:S(2)}, u32[]{:S(2)}) collective-permute-start(bf16[432,256]{1,0:T(8,128)(2,1)S(1)} %get-tuple-element.108), channel_id=1, source_target_pairs={{0,96},{96,0},{32,64},{64,32},{1,97},{97,1},{33,65},{65,33},{2,98}... | collective-permute-start | bytes 663560 | tf_op jit(solution)/shard_map/ppermute | solution.py:27
  25.8 6.1 %inner.1 = (f32[576,256]{1,0:T(8,128)S(1)}, f32[3,576,256]{2,1,0:T(8,128)S(1)}) custom-call(s32[6]{0:T(128)S(1)} %stack.27.pos_ref, bf16[576,1024]{1,0:T(8,128)(2,1)S(1)} %bitcast.10, f32[3,576,256]{2,1,0:T(8,128)S(1)} %get-tuple-element.91.part_ref, bf16[1024,256]{1,0:T(8,128)(2,1)S(1)} %copy-done.3, bf16[3,3,1024,256]{3,2,1,0:T(8,128)(2,1)} %wc_ref.3, ...), custom_call_target="tpu_custom_call" | custom-call | flops 3019898880 | bytes 10485760 | tf_op jit(solution)/shard_map/inner/pallas_call | solution.py:532
  31.9 1.2 %turn.1.refs_8_ = bf16[2,256,1152]{2,1,0:T(8,128)(2,1)S(1)} custom-call(s32[6]{0:T(128)S(1)} %stack.27.pos_ref, bf16[576,256]{1,0:T(8,128)(2,1)S(1)} %get-tuple-element.94.x0, bf16[576,256]{1,0:T(8,128)(2,1)S(1)} %collective-permute-done.3.x1, bf16[576,256]{1,0:T(8,128)(2,1)S(1)} %collective-permute-done.4.x2, bf16[576,256]{1,0:T(8,128)(2,1)S(1)} %collective-permute-done.5.x3), custom_call_target="tpu_custom_call" | custom-call | flops 301989888 | bytes 2359296 | tf_op jit(solution)/shard_map/turn/pallas_call | solution.py:214
  33.1 3.5 %collective-permute-done.1.col_ref = bf16[432,256]{1,0:T(8,128)(2,1)S(1)} collective-permute-done((bf16[432,256]{1,0:T(8,128)(2,1)S(1)}, bf16[432,256]{1,0:T(8,128)(2,1)S(1)}, u32[]{:S(2)}, u32[]{:S(2)}) %collective-permute-start.1) | collective-permute-done | bytes 221216 | tf_op jit(solution)/shard_map/ppermute | solution.py:24
  36.6 1.4 %merge.2 = (bf16[288,1024]{1,0:T(8,128)(2,1)S(1)}, bf16[288,256]{1,0:T(8,128)(2,1)S(1)}, bf16[288,256]{1,0:T(8,128)(2,1)S(1)}, bf16[288,256]{1,0:T(8,128)(2,1)S(1)}) custom-call(s32[6]{0:T(128)S(1)} %stack.27.pos_ref, f32[576,256]{1,0:T(8,128)S(1)} %get-tuple-element.98.pre0_ref, f32[3,576,256]{2,1,0:T(8,128)S(1)} %get-tuple-element.99.own_ref, ...), custom_call_target="tpu_custom_call" | custom-call | flops 226492416 | bytes 3145728 | tf_op jit(solution)/shard_map/merge/pallas_call | solution.py:612
  37.9 1.9 %collective-permute-start.11 = (bf16[288,256]{1,0:T(8,128)(2,1)S(1)}, bf16[288,256]{1,0:T(8,128)(2,1)S(1)}, u32[]{:S(2)}, u32[]{:S(2)}) collective-permute-start(bf16[288,256]{1,0:T(8,128)(2,1)S(1)} %get-tuple-element.131.refs_0_), channel_id=1, source_target_pairs={{0,32},{32,0},{1,33},{33,1},{2,34},{34,2},{3,35},{35,3},{4,36},{36... | collective-permute-start | bytes 442376 | tf_op jit(solution)/shard_map/ppermute | solution.py:24
  39.9 0.7 collective-permute-start.12
  40.6 1.5 %collective-permute-start.13 = (bf16[288,256]{1,0:T(8,128)(2,1)S(1)}, bf16[288,256]{1,0:T(8,128)(2,1)S(1)}, u32[]{:S(2)}, u32[]{:S(2)}) collective-permute-start(bf16[288,256]{1,0:T(8,128)(2,1)S(1)} %get-tuple-element.131.refs_0_), channel_id=1, source_target_pairs={{0,96},{96,0},{32,64},{64,32},{1,97},{97,1},{33,65},{65,33},{2,98}... | collective-permute-start | bytes 442376 | tf_op jit(solution)/shard_map/ppermute | solution.py:27
  42.1 3.5 %collective-permute-done.8.diag_ref = bf16[432,256]{1,0:T(8,128)(2,1)S(1)} collective-permute-done((bf16[432,256]{1,0:T(8,128)(2,1)S(1)}, bf16[432,256]{1,0:T(8,128)(2,1)S(1)}, u32[]{:S(2)}, u32[]{:S(2)}) %collective-permute-start.8) | collective-permute-done | bytes 221216 | tf_op jit(solution)/shard_map/ppermute | solution.py:27
  45.6 1.5 %merge.3 = (bf16[288,1024]{1,0:T(8,128)(2,1)S(1)}, bf16[288,256]{1,0:T(8,128)(2,1)S(1)}, bf16[288,256]{1,0:T(8,128)(2,1)S(1)}, bf16[288,256]{1,0:T(8,128)(2,1)S(1)}) custom-call(s32[6]{0:T(128)S(1)} %stack.27.pos_ref, f32[576,256]{1,0:T(8,128)S(1)} %get-tuple-element.98.pre0_ref, f32[3,576,256]{2,1,0:T(8,128)S(1)} %get-tuple-element.99.own_ref, ...), custom_call_target="tpu_custom_call" | custom-call | flops 226492416 | bytes 3145728 | tf_op jit(solution)/shard_map/merge/pallas_call | solution.py:612
  47.1 1.9 %pair.1 = (f32[1024,256]{1,0:T(8,128)S(1)}, bf16[512,256]{1,0:T(8,128)(2,1)S(1)}, bf16[512,256]{1,0:T(8,128)(2,1)S(1)}) custom-call(s32[6]{0:T(128)S(1)} %stack.27.pos_ref, bf16[288,1024]{1,0:T(8,128)(2,1)S(1)} %get-tuple-element.103.ja_ref, bf16[288,256]{1,0:T(8,128)(2,1)S(1)} %get-tuple-element.104.ga_ref, bf16[288,256]{1,0:T(8,128)(2,1)S(1)} %get-tuple-element.105.da_ref, ...), custom_call_target="tpu_custom_call" | custom-call | flops 603979776 | bytes 4194304 | tf_op jit(solution)/shard_map/pair/pallas_call | solution.py:671
  49.9 3.8 %collective-permute-start.16 = (bf16[288,256]{1,0:T(8,128)(2,1)S(1)}, bf16[288,256]{1,0:T(8,128)(2,1)S(1)}, u32[]{:S(2)}, u32[]{:S(2)}) collective-permute-start(bf16[288,256]{1,0:T(8,128)(2,1)S(1)} %get-tuple-element.135.refs_4_), channel_id=1, source_target_pairs={{0,96},{96,0},{32,64},{64,32},{1,97},{97,1},{33,65},{65,33},{2,98}... | collective-permute-start | bytes 442376 | tf_op jit(solution)/shard_map/ppermute | solution.py:27
  53.8 4.1 %collective-permute-done.14.refs_5_ = bf16[288,256]{1,0:T(8,128)(2,1)S(1)} collective-permute-done((bf16[288,256]{1,0:T(8,128)(2,1)S(1)}, bf16[288,256]{1,0:T(8,128)(2,1)S(1)}, u32[]{:S(2)}, u32[]{:S(2)}) %collective-permute-start.14) | collective-permute-done | bytes 147488 | tf_op jit(solution)/shard_map/ppermute | solution.py:24
  57.9 2.3 %collective-permute-done.16.refs_7_ = bf16[288,256]{1,0:T(8,128)(2,1)S(1)} collective-permute-done((bf16[288,256]{1,0:T(8,128)(2,1)S(1)}, bf16[288,256]{1,0:T(8,128)(2,1)S(1)}, u32[]{:S(2)}, u32[]{:S(2)}) %collective-permute-start.16) | collective-permute-done | bytes 147488 | tf_op jit(solution)/shard_map/ppermute | solution.py:27
  60.2 0.7 rows.1
  61.2 1.2 %collective-permute-start.18 = (bf16[16,16,256]{2,1,0:T(8,128)(2,1)S(1)}, bf16[16,16,256]{2,1,0:T(8,128)(2,1)S(1)}, u32[]{:S(2)}, u32[]{:S(2)}) collective-permute-start(bf16[16,16,256]{2,1,0:T(8,128)(2,1)S(1)} %get-tuple-element.144), channel_id=1, source_target_pairs={{0,64},{64,0},{1,65},{65,1},{2,66},{66,2},{3,67},{67,3},{4,68},{68... | collective-permute-start | bytes 393224 | tf_op jit(solution)/shard_map/ppermute | solution.py:26
  62.4 2.6 %collective-permute-start.19 = (bf16[16,16,256]{2,1,0:T(8,128)(2,1)S(1)}, bf16[16,16,256]{2,1,0:T(8,128)(2,1)S(1)}, u32[]{:S(2)}, u32[]{:S(2)}) collective-permute-start(bf16[16,16,256]{2,1,0:T(8,128)(2,1)S(1)} %get-tuple-element.145), channel_id=1, source_target_pairs={{0,96},{96,0},{32,64},{64,32},{1,97},{97,1},{33,65},{65,33},{2,98}... | collective-permute-start | bytes 393224 | tf_op jit(solution)/shard_map/ppermute | solution.py:27
  65.1 3.6 %taps.1 = (f32[96,16,256]{2,1,0:T(8,128)S(1)}, bf16[96,16,256]{2,1,0:T(8,128)(2,1)S(1)}) custom-call(s32[6]{0:T(128)S(1)} %stack.27.pos_ref, s32[176]{0:T(256)S(1)} %fusion.1.place_ref, bf16[288,256]{1,0:T(8,128)(2,1)S(1)} %get-tuple-element.131.refs_0_, bf16[288,256]{1,0:T(8,128)(2,1)S(1)} %collective-permute-done.11.refs_1_, ...), custom_call_target="tpu_custom_call" | custom-call | flops 2113929216 | bytes 8388608 | tf_op jit(solution)/shard_map/taps/pallas_call | solution.py:261
  68.8 1.9 %collective-permute-done.19 = bf16[16,16,256]{2,1,0:T(8,128)(2,1)S(1)} collective-permute-done((bf16[16,16,256]{2,1,0:T(8,128)(2,1)S(1)}, bf16[16,16,256]{2,1,0:T(8,128)(2,1)S(1)}, u32[]{:S(2)}, u32[]{:S(2)}) %collective-permute-start.19) | collective-permute-done | bytes 131104 | tf_op jit(solution)/shard_map/ppermute | solution.py:27
  70.8 0.6 collective-permute-start.21
  71.4 1.8 %collective-permute-done.21.other_ref = bf16[16,16,256]{2,1,0:T(8,128)(2,1)S(1)} collective-permute-done((bf16[16,16,256]{2,1,0:T(8,128)(2,1)S(1)}, bf16[16,16,256]{2,1,0:T(8,128)(2,1)S(1)}, u32[]{:S(2)}, u32[]{:S(2)}) %collective-permute-start.21) | collective-permute-done | bytes 131104 | tf_op jit(solution)/shard_map/ppermute | solution.py:188
  73.2 1.1 %owners.1 = bf16[16,96,256]{2,1,0:T(8,128)(2,1)S(1)} custom-call(s32[6]{0:T(128)S(1)} %stack.27.pos_ref, s32[176]{0:T(256)S(1)} %fusion.1.place_ref, f32[96,16,256]{2,1,0:T(8,128)S(1)} %get-tuple-element.140.keep_ref, bf16[96,16,256]{2,1,0:T(8,128)(2,1)S(1)} %collective-permute-done.20.got_ref, f32[16,16,256]{2,1,0:T(8,128)S(1)} %get-tuple-element.152.mine_ref, ...), custom_call_target="tpu_custom_call" | custom-call | flops 393216 | bytes 3145728 | tf_op jit(solution)/shard_map/owners/pallas_call | solution.py:282
  74.2 22.3 %all_to_all.5.r_ref = bf16[16,96,256]{2,1,0:T(8,128)(2,1)S(1)} all-to-all(bf16[16,96,256]{2,1,0:T(8,128)(2,1)S(1)} %owners.1), channel_id=1, replica_groups=mesh['row'=2,'col'=2,'dp_0'=4,'dp_1'=4,'dp_2'=2] {'dp_0','dp_1'}, dimensions={0} | all-to-all | bytes 1572864 | tf_op jit(solution)/shard_map/all_to_all | solution.py:293
  96.5 0.8 last.1
  (37 shorter events, 2.8 us)
Async XLA Ops:
  0.1 7.5 %copy-start = (bf16[1,24,24,1024]{3,2,1,0:T(8,128)(2,1)S(1)}, bf16[1,24,24,1024]{3,2,1,0:T(8,128)(2,1)}, u32[]{:S(2)}) copy-start(bf16[1,24,24,1024]{3,2,1,0:T(8,128)(2,1)} %param.8) | copy-start | bytes 3538948
  3.2 22.5 %copy-start.3 = (bf16[1024,256]{1,0:T(8,128)(2,1)S(1)}, bf16[1024,256]{1,0:T(8,128)(2,1)}, u32[]{:S(2)}) copy-start(bf16[1024,256]{1,0:T(8,128)(2,1)} %wp_ref.3) | copy-start | bytes 1572868
  3.3 15.4 %collective-permute-start.3 = (bf16[576,256]{1,0:T(8,128)(2,1)S(1)}, bf16[576,256]{1,0:T(8,128)(2,1)S(1)}, u32[]{:S(2)}, u32[]{:S(2)}) collective-permute-start(bf16[576,256]{1,0:T(8,128)(2,1)S(1)} %get-tuple-element.88), channel_id=1, source_target_pairs={{0,32},{32,0},{1,33},{33,1},{2,34},{34,2},{3,35},{35,3},{4,36},{36... | collective-permute-start | bytes 884744 | tf_op jit(solution)/shard_map/ppermute | solution.py:24
  6.5 15.1 %collective-permute-start.4 = (bf16[576,256]{1,0:T(8,128)(2,1)S(1)}, bf16[576,256]{1,0:T(8,128)(2,1)S(1)}, u32[]{:S(2)}, u32[]{:S(2)}) collective-permute-start(bf16[576,256]{1,0:T(8,128)(2,1)S(1)} %get-tuple-element.89), channel_id=1, source_target_pairs={{0,64},{64,0},{1,65},{65,1},{2,66},{66,2},{3,67},{67,3},{4,68},{68... | collective-permute-start | bytes 884744 | tf_op jit(solution)/shard_map/ppermute | solution.py:26
  7.0 15.8 %collective-permute-start.5 = (bf16[576,256]{1,0:T(8,128)(2,1)S(1)}, bf16[576,256]{1,0:T(8,128)(2,1)S(1)}, u32[]{:S(2)}, u32[]{:S(2)}) collective-permute-start(bf16[576,256]{1,0:T(8,128)(2,1)S(1)} %get-tuple-element.90), channel_id=1, source_target_pairs={{0,96},{96,0},{32,64},{64,32},{1,97},{97,1},{33,65},{65,33},{2,98}... | collective-permute-start | bytes 884744 | tf_op jit(solution)/shard_map/ppermute | solution.py:27
  16.6 8.2 %collective-permute-start = (bf16[144,256]{1,0:T(8,128)(2,1)S(1)}, bf16[144,256]{1,0:T(8,128)(2,1)S(1)}, u32[]{:S(2)}, u32[]{:S(2)}) collective-permute-start(bf16[144,256]{1,0:T(8,128)(2,1)S(1)} %get-tuple-element.83), channel_id=1, source_target_pairs={{0,64},{64,0},{1,65},{65,1},{2,66},{66,2},{3,67},{67,3},{4,68},{68... | collective-permute-start | bytes 221192 | tf_op jit(solution)/shard_map/ppermute | solution.py:26
  18.1 27.6 %collective-permute-start.6 = (bf16[720,256]{1,0:T(8,128)(2,1)S(1)}, bf16[720,256]{1,0:T(8,128)(2,1)S(1)}, u32[]{:S(2)}, u32[]{:S(2)}) collective-permute-start(bf16[720,256]{1,0:T(8,128)(2,1)S(1)} %get-tuple-element.106), channel_id=1, source_target_pairs={{0,64},{64,0},{1,65},{65,1},{2,66},{66,2},{3,67},{67,3},{4,68},{68... | collective-permute-start | bytes 1105928 | tf_op jit(solution)/shard_map/ppermute | solution.py:26
  18.7 17.9 %collective-permute-start.1 = (bf16[432,256]{1,0:T(8,128)(2,1)S(1)}, bf16[432,256]{1,0:T(8,128)(2,1)S(1)}, u32[]{:S(2)}, u32[]{:S(2)}) collective-permute-start(bf16[432,256]{1,0:T(8,128)(2,1)S(1)} %get-tuple-element.84), channel_id=1, source_target_pairs={{0,32},{32,0},{1,33},{33,1},{2,34},{34,2},{3,35},{35,3},{4,36},{36... | collective-permute-start | bytes 663560 | tf_op jit(solution)/shard_map/ppermute | solution.py:24
  21.5 11.6 %collective-permute-start.2 = (bf16[144,256]{1,0:T(8,128)(2,1)S(1)}, bf16[144,256]{1,0:T(8,128)(2,1)S(1)}, u32[]{:S(2)}, u32[]{:S(2)}) collective-permute-start(bf16[144,256]{1,0:T(8,128)(2,1)S(1)} %get-tuple-element.85), channel_id=1, source_target_pairs={{0,96},{96,0},{32,64},{64,32},{1,97},{97,1},{33,65},{65,33},{2,98}... | collective-permute-start | bytes 221192 | tf_op jit(solution)/shard_map/ppermute | solution.py:27
  22.8 17.8 %collective-permute-start.7 = (bf16[432,256]{1,0:T(8,128)(2,1)S(1)}, bf16[432,256]{1,0:T(8,128)(2,1)S(1)}, u32[]{:S(2)}, u32[]{:S(2)}) collective-permute-start(bf16[432,256]{1,0:T(8,128)(2,1)S(1)} %get-tuple-element.107), channel_id=1, source_target_pairs={{0,32},{32,0},{1,33},{33,1},{2,34},{34,2},{3,35},{35,3},{4,36},{36... | collective-permute-start | bytes 663560 | tf_op jit(solution)/shard_map/ppermute | solution.py:24
  24.8 20.8 %collective-permute-start.8 = (bf16[432,256]{1,0:T(8,128)(2,1)S(1)}, bf16[432,256]{1,0:T(8,128)(2,1)S(1)}, u32[]{:S(2)}, u32[]{:S(2)}) collective-permute-start(bf16[432,256]{1,0:T(8,128)(2,1)S(1)} %get-tuple-element.108), channel_id=1, source_target_pairs={{0,96},{96,0},{32,64},{64,32},{1,97},{97,1},{33,65},{65,33},{2,98}... | collective-permute-start | bytes 663560 | tf_op jit(solution)/shard_map/ppermute | solution.py:27
  31.9 4.7 %copy-start.1 = (bf16[1024,256]{1,0:T(8,128)(2,1)S(1)}, bf16[1024,256]{1,0:T(8,128)(2,1)}, u32[]{:S(2)}) copy-start(bf16[1024,256]{1,0:T(8,128)(2,1)} %wp_ref.5) | copy-start | bytes 1572868
  31.9 4.7 %copy-start.2 = (bf16[1,24,24,256]{3,2,1,0:T(8,128)(2,1)S(1)}, bf16[1,24,24,256]{3,2,1,0:T(8,128)(2,1)}, u32[]{:S(2)}) copy-start(bf16[1,24,24,256]{3,2,1,0:T(8,128)(2,1)} %param.9) | copy-start | bytes 884740
  37.9 11.7 %collective-permute-start.11 = (bf16[288,256]{1,0:T(8,128)(2,1)S(1)}, bf16[288,256]{1,0:T(8,128)(2,1)S(1)}, u32[]{:S(2)}, u32[]{:S(2)}) collective-permute-start(bf16[288,256]{1,0:T(8,128)(2,1)S(1)} %get-tuple-element.131.refs_0_), channel_id=1, source_target_pairs={{0,32},{32,0},{1,33},{33,1},{2,34},{34,2},{3,35},{35,3},{4,36},{36... | collective-permute-start | bytes 442376 | tf_op jit(solution)/shard_map/ppermute | solution.py:24
  39.9 9.8 %collective-permute-start.12 = (bf16[288,256]{1,0:T(8,128)(2,1)S(1)}, bf16[288,256]{1,0:T(8,128)(2,1)S(1)}, u32[]{:S(2)}, u32[]{:S(2)}) collective-permute-start(bf16[288,256]{1,0:T(8,128)(2,1)S(1)} %get-tuple-element.131.refs_0_), channel_id=1, source_target_pairs={{0,64},{64,0},{1,65},{65,1},{2,66},{66,2},{3,67},{67,3},{4,68},{68... | collective-permute-start | bytes 442376 | tf_op jit(solution)/shard_map/ppermute | solution.py:26
  40.6 9.3 %collective-permute-start.13 = (bf16[288,256]{1,0:T(8,128)(2,1)S(1)}, bf16[288,256]{1,0:T(8,128)(2,1)S(1)}, u32[]{:S(2)}, u32[]{:S(2)}) collective-permute-start(bf16[288,256]{1,0:T(8,128)(2,1)S(1)} %get-tuple-element.131.refs_0_), channel_id=1, source_target_pairs={{0,96},{96,0},{32,64},{64,32},{1,97},{97,1},{33,65},{65,33},{2,98}... | collective-permute-start | bytes 442376 | tf_op jit(solution)/shard_map/ppermute | solution.py:27
  47.1 6.6 %copy-start.4 = (s32[176]{0:T(256)S(1)}, s32[176]{0:T(256)}, u32[]{:S(2)}) copy-start(s32[176]{0:T(256)} %param.15) | copy-start | bytes 2116
  49.1 11.1 %collective-permute-start.10 = (bf16[512,256]{1,0:T(8,128)(2,1)S(1)}, bf16[512,256]{1,0:T(8,128)(2,1)S(1)}, u32[]{:S(2)}, u32[]{:S(2)}) collective-permute-start(bf16[512,256]{1,0:T(8,128)(2,1)S(1)} %get-tuple-element.114), channel_id=1, source_target_pairs={{0,1},{1,0},{2,3},{3,2},{4,5},{5,4},{6,7},{7,6},{8,9},{9,8},{10,11... | collective-permute-start | bytes 786440 | tf_op jit(solution)/shard_map/ppermute | solution.py:188
  49.2 11.0 %collective-permute-start.9 = (bf16[512,256]{1,0:T(8,128)(2,1)S(1)}, bf16[512,256]{1,0:T(8,128)(2,1)S(1)}, u32[]{:S(2)}, u32[]{:S(2)}) collective-permute-start(bf16[512,256]{1,0:T(8,128)(2,1)S(1)} %get-tuple-element.113), channel_id=1, source_target_pairs={{0,1},{1,0},{2,3},{3,2},{4,5},{5,4},{6,7},{7,6},{8,9},{9,8},{10,11... | collective-permute-start | bytes 786440 | tf_op jit(solution)/shard_map/ppermute | solution.py:188
  49.7 8.2 %collective-permute-start.14 = (bf16[288,256]{1,0:T(8,128)(2,1)S(1)}, bf16[288,256]{1,0:T(8,128)(2,1)S(1)}, u32[]{:S(2)}, u32[]{:S(2)}) collective-permute-start(bf16[288,256]{1,0:T(8,128)(2,1)S(1)} %get-tuple-element.135.refs_4_), channel_id=1, source_target_pairs={{0,32},{32,0},{1,33},{33,1},{2,34},{34,2},{3,35},{35,3},{4,36},{36... | collective-permute-start | bytes 442376 | tf_op jit(solution)/shard_map/ppermute | solution.py:24
  49.7 8.2 %collective-permute-start.15 = (bf16[288,256]{1,0:T(8,128)(2,1)S(1)}, bf16[288,256]{1,0:T(8,128)(2,1)S(1)}, u32[]{:S(2)}, u32[]{:S(2)}) collective-permute-start(bf16[288,256]{1,0:T(8,128)(2,1)S(1)} %get-tuple-element.135.refs_4_), channel_id=1, source_target_pairs={{0,64},{64,0},{1,65},{65,1},{2,66},{66,2},{3,67},{67,3},{4,68},{68... | collective-permute-start | bytes 442376 | tf_op jit(solution)/shard_map/ppermute | solution.py:26
  49.9 10.2 %collective-permute-start.16 = (bf16[288,256]{1,0:T(8,128)(2,1)S(1)}, bf16[288,256]{1,0:T(8,128)(2,1)S(1)}, u32[]{:S(2)}, u32[]{:S(2)}) collective-permute-start(bf16[288,256]{1,0:T(8,128)(2,1)S(1)} %get-tuple-element.135.refs_4_), channel_id=1, source_target_pairs={{0,96},{96,0},{32,64},{64,32},{1,97},{97,1},{33,65},{65,33},{2,98}... | collective-permute-start | bytes 442376 | tf_op jit(solution)/shard_map/ppermute | solution.py:27
  60.9 8.0 %collective-permute-start.17 = (bf16[16,16,256]{2,1,0:T(8,128)(2,1)S(1)}, bf16[16,16,256]{2,1,0:T(8,128)(2,1)S(1)}, u32[]{:S(2)}, u32[]{:S(2)}) collective-permute-start(bf16[16,16,256]{2,1,0:T(8,128)(2,1)S(1)} %get-tuple-element.143), channel_id=1, source_target_pairs={{0,32},{32,0},{1,33},{33,1},{2,34},{34,2},{3,35},{35,3},{4,36},{36... | collective-permute-start | bytes 393224 | tf_op jit(solution)/shard_map/ppermute | solution.py:24
  61.2 7.6 %collective-permute-start.18 = (bf16[16,16,256]{2,1,0:T(8,128)(2,1)S(1)}, bf16[16,16,256]{2,1,0:T(8,128)(2,1)S(1)}, u32[]{:S(2)}, u32[]{:S(2)}) collective-permute-start(bf16[16,16,256]{2,1,0:T(8,128)(2,1)S(1)} %get-tuple-element.144), channel_id=1, source_target_pairs={{0,64},{64,0},{1,65},{65,1},{2,66},{66,2},{3,67},{67,3},{4,68},{68... | collective-permute-start | bytes 393224 | tf_op jit(solution)/shard_map/ppermute | solution.py:26
  62.4 8.3 %collective-permute-start.19 = (bf16[16,16,256]{2,1,0:T(8,128)(2,1)S(1)}, bf16[16,16,256]{2,1,0:T(8,128)(2,1)S(1)}, u32[]{:S(2)}, u32[]{:S(2)}) collective-permute-start(bf16[16,16,256]{2,1,0:T(8,128)(2,1)S(1)} %get-tuple-element.145), channel_id=1, source_target_pairs={{0,96},{96,0},{32,64},{64,32},{1,97},{97,1},{33,65},{65,33},{2,98}... | collective-permute-start | bytes 393224 | tf_op jit(solution)/shard_map/ppermute | solution.py:27
  70.7 2.5 %collective-permute-start.20 = (bf16[96,16,256]{2,1,0:T(8,128)(2,1)S(1)}, bf16[96,16,256]{2,1,0:T(8,128)(2,1)S(1)}, u32[]{:S(2)}, u32[]{:S(2)}) collective-permute-start(bf16[96,16,256]{2,1,0:T(8,128)(2,1)S(1)} %get-tuple-element.146), channel_id=1, source_target_pairs={{0,1},{1,0},{2,3},{3,2},{4,5},{5,4},{6,7},{7,6},{8,9},{9,8},{10,11... | collective-permute-start | bytes 2359304 | tf_op jit(solution)/shard_map/ppermute | solution.py:188
  70.8 2.4 %collective-permute-start.21 = (bf16[16,16,256]{2,1,0:T(8,128)(2,1)S(1)}, bf16[16,16,256]{2,1,0:T(8,128)(2,1)S(1)}, u32[]{:S(2)}, u32[]{:S(2)}) collective-permute-start(bf16[16,16,256]{2,1,0:T(8,128)(2,1)S(1)} %get-tuple-element.151), channel_id=1, source_target_pairs={{0,1},{1,0},{2,3},{3,2},{4,5},{5,4},{6,7},{7,6},{8,9},{9,8},{10,11... | collective-permute-start | bytes 393224 | tf_op jit(solution)/shard_map/ppermute | solution.py:188

commit v6 on v3

--- a/solution.py
+++ b/solution.py
@@ -46,16 +46,29 @@
     )
 
 
-def select_channels(pos_ref, x_ref, *o_refs):
-    chans = x_ref.shape[1]
-    width = o_refs[0].shape[1]
-    source = lax.broadcasted_iota(jnp.int32, (chans, width), 0)
-    col = lax.broadcasted_iota(jnp.int32, (1, width), 1)
-    wanted = 64 * (col // 16) + col % 16
-    for k, o_ref in enumerate(o_refs):
-        c = jnp.bitwise_xor(pos_ref[0], k)
-        pick = jnp.where(source == wanted + 16 * c, 1.0, 0.0).astype(BF)
-        o_ref[...] = jnp.dot(x_ref[...], pick, preferred_element_type=F32).astype(BF)
+def select_channels(pos_ref, x_ref, *rest):
+    *o_refs, held, sems = rest
+    lanes = 128
+    group = lanes * len(o_refs)
+    pieces = sems.shape[0]
+    each = x_ref.shape[0] // pieces
+    copies = []
+    for n in range(pieces):
+        part = pl.ds(n * each, each)
+        copies.append(pltpu.make_async_copy(x_ref.at[part, :], held.at[part, :], sems.at[n]))
+        copies[n].start()
+    source = lax.broadcasted_iota(jnp.int32, (group, group), 0)
+    col = lax.broadcasted_iota(jnp.int32, (1, group), 1)
+    owner = jnp.bitwise_xor(pos_ref[0], col // lanes)
+    wanted = 64 * ((col % lanes) // 16) + 16 * owner + col % 16
+    picks = jnp.where(source == wanted, 1.0, 0.0).astype(BF)
+    for n in range(pieces):
+        copies[n].wait()
+        rows = slice(n * each, (n + 1) * each)
+        for p in range(x_ref.shape[1] // group):
+            taken = jnp.dot(held[rows, p * group : (p + 1) * group], picks, preferred_element_type=F32).astype(BF)
+            for k, o_ref in enumerate(o_refs):
+                o_ref[rows, p * lanes : (p + 1) * lanes] = taken[:, k * lanes : (k + 1) * lanes]
 
 
 def turn_pixels(pos_ref, x0, x1, x2, x3, o_ref, held):
@@ -172,9 +185,18 @@
 def pick(pos, centre):
     pixels, chans = centre.shape
     block = jax.ShapeDtypeStruct((pixels, chans // 4), BF)
-    return call(select_channels, [block] * 4, 1, 1, 2 * pixels * chans * chans, 4 * pixels * chans, 14, name="pick")(
-        pos, centre
-    )
+    return call(
+        select_channels,
+        [block] * 4,
+        1,
+        0,
+        pixels * chans * chans,
+        4 * pixels * chans,
+        12,
+        [pltpu.VMEM((pixels, chans), BF), pltpu.SemaphoreType.DMA((2,))],
+        name="pick",
+        n_any=1,
+    )(pos, pltpu.with_memory_space_constraint(centre, pltpu.HBM))
 
 
 def turn(pos, got):
@@ -271,8 +293,12 @@
     )(total)
 
 
+def sigmoid(value):
+    return 0.5 + 0.5 * jnp.tanh(0.5 * value)
+
+
 def silu_slope(value):
-    sig = jax.nn.sigmoid(value)
+    sig = sigmoid(value)
     return sig * (1.0 + value * (1.0 - sig))
 
 
@@ -508,7 +534,7 @@
     slopes = {}
     for k in range(4):
         value = pre0_ref[...] if k == 0 else pre[k - 1]
-        sig = jax.nn.sigmoid(value)
+        sig = sigmoid(value)
         joined_ref[:, k * width : (k + 1) * width] = (value * sig).astype(BF)
         if k in (0, 3):
             slopes[k] = sig * (1.0 + value * (1.0 - sig))

time: 94.8 us -> 94.3 us (level)
  local copies, waits for them, and re-layouts: 1.38 us -> 0.11 us
    unnamed x12 -> x10, local copies, waits for them, and re-layouts: 1.3 us -> 0.03 us
where the time goes in v6:
time: 94.3 us; the launch traced here: 94.1 us
  Pallas kernels  28.8 us (31%)
  waiting for transfers between devices  23.9 us (25%)
  blocking collectives  22.3 us (24%)
  starting transfers between devices  18.8 us (20%)
    all_to_all x1, blocking collectives, reduce_slots(): total = lax.all_to_all(total, ('dp_0', 'dp_1'), 0, 0, tiled=True)  22.3 us
    ppermute x4, waiting for transfers between devices, flip(): return lax.ppermute(x, ('row', 'col'), [(0, 3), (3, 0), (1, 2), (2, 1)])  10.4 us
    ppermute x4, starting transfers between devices, flip(): return lax.ppermute(x, 'col', [(0, 1), (1, 0)])  9.91 us
    pallas_call x1, Pallas kernels, outer(): call(outer_parts, [jax.ShapeDtypeStruct(*s) for s in shapes], 1, 1, 2 * p...  8.68 us
    ppermute x4, waiting for transfers between devices, flip(): return lax.ppermute(x, 'col', [(0, 1), (1, 0)])  8.26 us
    pallas_call x1, Pallas kernels, inner(): call(inner_parts, [jax.ShapeDtypeStruct((pixels, width), F32), jax.ShapeD...  6.26 us
    ppermute x4, starting transfers between devices, flip(): return lax.ppermute(x, ('row', 'col'), [(0, 3), (3, 0), (1, 2), (2, 1)])  4.53 us
    pallas_call x1, Pallas kernels, tap_slots(): call(tap_grads, [jax.ShapeDtypeStruct((half, 16, width), F32), jax.ShapeD...  3.56 us
  transfers between devices with their start and end apart: 16, of which 11 were waited for; matrix products, arithmetic and copies ran while one was open for 0% of the time, Pallas kernels for 23%

profile of v6, /device:TPU:0, one launch (start us, length us, event | category | flops | bytes accessed | tf_op | source)
XLA Modules:
  0.0 94.1 jit_solution(229164260457243702)
XLA Ops:
  0.1 2.6 %pick.1 = (bf16[576,256]{1,0:T(8,128)(2,1)S(1)}, bf16[576,256]{1,0:T(8,128)(2,1)S(1)}, bf16[576,256]{1,0:T(8,128)(2,1)S(1)}, bf16[576,256]{1,0:T(8,128)(2,1)S(1)}) custom-call(s32[6]{0:T(128)S(1)} %stack.27.pos_ref, bf16[576,1024]{1,0:T(8,128)(2,1)} %bitcast.8), custom_call_target="tpu_custom_call" | custom-call | flops 603979776 | bytes 2359296 | tf_op jit(solution)/shard_map/pick/pallas_call | solution.py:188
  2.6 3.2 %collective-permute-start.3 = (bf16[576,256]{1,0:T(8,128)(2,1)S(1)}, bf16[576,256]{1,0:T(8,128)(2,1)S(1)}, u32[]{:S(2)}, u32[]{:S(2)}) collective-permute-start(bf16[576,256]{1,0:T(8,128)(2,1)S(1)} %get-tuple-element.73), channel_id=1, source_target_pairs={{0,32},{32,0},{1,33},{33,1},{2,34},{34,2},{3,35},{35,3},{4,36},{36... | collective-permute-start | bytes 884744 | tf_op jit(solution)/shard_map/ppermute | solution.py:22
  5.8 0.6 collective-permute-start.4
  6.4 0.6 collective-permute-start.5
  7.0 8.7 %outer.1 = (f32[3,576,256]{2,1,0:T(8,128)S(1)}, bf16[864,256]{1,0:T(8,128)(2,1)S(1)}, bf16[864,256]{1,0:T(8,128)(2,1)S(1)}, bf16[576,256]{1,0:T(8,128)(2,1)S(1)}) custom-call(s32[6]{0:T(128)S(1)} %stack.27.pos_ref, bf16[576,1024]{1,0:T(8,128)(2,1)S(1)} %bitcast.9, bf16[3,3,1024,256]{3,2,1,0:T(8,128)(2,1)} %wc_ref.3, bf16[3,3,1024,256]{3,2,1,0:T(8,128)(2,1)} %wb_ref.3, ...), custom_call_target="tpu_custom_call" | custom-call | flops 4227858432 | bytes 10485760 | tf_op jit(solution)/shard_map/outer/pallas_call | solution.py:451
  15.7 1.5 %collective-permute-start = (bf16[864,256]{1,0:T(8,128)(2,1)S(1)}, bf16[864,256]{1,0:T(8,128)(2,1)S(1)}, u32[]{:S(2)}, u32[]{:S(2)}) collective-permute-start(bf16[864,256]{1,0:T(8,128)(2,1)S(1)} %get-tuple-element.68), channel_id=1, source_target_pairs={{0,64},{64,0},{1,65},{65,1},{2,66},{66,2},{3,67},{67,3},{4,68},{68... | collective-permute-start | bytes 1327112 | tf_op jit(solution)/shard_map/ppermute | solution.py:24
  17.2 2.7 %collective-permute-start.1 = (bf16[864,256]{1,0:T(8,128)(2,1)S(1)}, bf16[864,256]{1,0:T(8,128)(2,1)S(1)}, u32[]{:S(2)}, u32[]{:S(2)}) collective-permute-start(bf16[864,256]{1,0:T(8,128)(2,1)S(1)} %get-tuple-element.69), channel_id=1, source_target_pairs={{0,32},{32,0},{1,33},{33,1},{2,34},{34,2},{3,35},{35,3},{4,36},{36... | collective-permute-start | bytes 1327112 | tf_op jit(solution)/shard_map/ppermute | solution.py:22
  19.9 0.6 collective-permute-start.2
  20.7 1.2 %turn.1.xt_ref = bf16[2,256,1152]{2,1,0:T(8,128)(2,1)S(1)} custom-call(s32[6]{0:T(128)S(1)} %stack.27.pos_ref, bf16[576,256]{1,0:T(8,128)(2,1)S(1)} %get-tuple-element.79.x0, bf16[576,256]{1,0:T(8,128)(2,1)S(1)} %collective-permute-done.3.x1, bf16[576,256]{1,0:T(8,128)(2,1)S(1)} %collective-permute-done.4.x2, bf16[576,256]{1,0:T(8,128)(2,1)S(1)} %collective-permute-done.5.x3), custom_call_target="tpu_custom_call" | custom-call | flops 301989888 | bytes 2359296 | tf_op jit(solution)/shard_map/turn/pallas_call | solution.py:204
  21.9 6.3 %inner.1 = (f32[576,256]{1,0:T(8,128)S(1)}, f32[3,576,256]{2,1,0:T(8,128)S(1)}) custom-call(s32[6]{0:T(128)S(1)} %stack.27.pos_ref, bf16[576,1024]{1,0:T(8,128)(2,1)S(1)} %bitcast.10, f32[3,576,256]{2,1,0:T(8,128)S(1)} %get-tuple-element.76.part_ref, bf16[1024,256]{1,0:T(8,128)(2,1)S(1)} %copy-done.1, bf16[3,3,1024,256]{3,2,1,0:T(8,128)(2,1)} %wc_ref.3, ...), custom_call_target="tpu_custom_call" | custom-call | flops 3019898880 | bytes 10485760 | tf_op jit(solution)/shard_map/inner/pallas_call | solution.py:474
  28.1 1.9 %collective-permute-done.2.diag_ref = bf16[576,256]{1,0:T(8,128)(2,1)S(1)} collective-permute-done((bf16[576,256]{1,0:T(8,128)(2,1)S(1)}, bf16[576,256]{1,0:T(8,128)(2,1)S(1)}, u32[]{:S(2)}, u32[]{:S(2)}) %collective-permute-start.2) | collective-permute-done | bytes 294944 | tf_op jit(solution)/shard_map/ppermute | solution.py:25
  30.1 8.3 %collective-permute-done.1.col_ref = bf16[864,256]{1,0:T(8,128)(2,1)S(1)} collective-permute-done((bf16[864,256]{1,0:T(8,128)(2,1)S(1)}, bf16[864,256]{1,0:T(8,128)(2,1)S(1)}, u32[]{:S(2)}, u32[]{:S(2)}) %collective-permute-start.1) | collective-permute-done | bytes 442400 | tf_op jit(solution)/shard_map/ppermute | solution.py:22
  38.4 2.4 %merge.1 = (bf16[576,1024]{1,0:T(8,128)(2,1)S(1)}, bf16[576,256]{1,0:T(8,128)(2,1)S(1)}, bf16[576,256]{1,0:T(8,128)(2,1)S(1)}, bf16[576,256]{1,0:T(8,128)(2,1)S(1)}) custom-call(s32[6]{0:T(128)S(1)} %stack.27.pos_ref, f32[576,256]{1,0:T(8,128)S(1)} %get-tuple-element.83.pre0_ref, f32[3,576,256]{2,1,0:T(8,128)S(1)} %get-tuple-element.84.own_ref, ...), custom_call_target="tpu_custom_call" | custom-call | flops 452984832 | bytes 6291456 | tf_op jit(solution)/shard_map/merge/pallas_call | solution.py:554
  40.8 2.8 %collective-permute-start.10 = (bf16[576,256]{1,0:T(8,128)(2,1)S(1)}, bf16[576,256]{1,0:T(8,128)(2,1)S(1)}, u32[]{:S(2)}, u32[]{:S(2)}) collective-permute-start(bf16[576,256]{1,0:T(8,128)(2,1)S(1)} %get-tuple-element.105.d0), channel_id=1, source_target_pairs={{0,96},{96,0},{32,64},{64,32},{1,97},{97,1},{33,65},{65,33},{2,98}... | collective-permute-start | bytes 884744 | tf_op jit(solution)/shard_map/ppermute | solution.py:25
  43.6 0.8 collective-permute-start.8
  44.4 0.5 collective-permute-start.9
  45.0 1.6 %pair.1 = (f32[1024,256]{1,0:T(8,128)S(1)}, bf16[512,256]{1,0:T(8,128)(2,1)S(1)}, bf16[512,256]{1,0:T(8,128)(2,1)S(1)}) custom-call(s32[6]{0:T(128)S(1)} %stack.27.pos_ref, bf16[576,1024]{1,0:T(8,128)(2,1)S(1)} %get-tuple-element.88.joined_ref, bf16[576,256]{1,0:T(8,128)(2,1)S(1)} %get-tuple-element.89.g_ref, bf16[576,1024]{1,0:T(8,128)(2,1)S(1)} %bitcast.11, ...), custom_call_target="tpu_custom_call" | custom-call | flops 603979776 | bytes 4194304 | tf_op jit(solution)/shard_map/pair/pallas_call | solution.py:607
  47.2 1.0 %collective-permute-done.6.got0 = bf16[512,256]{1,0:T(8,128)(2,1)S(1)} collective-permute-done((bf16[512,256]{1,0:T(8,128)(2,1)S(1)}, bf16[512,256]{1,0:T(8,128)(2,1)S(1)}, u32[]{:S(2)}, u32[]{:S(2)}) %collective-permute-start.6) | collective-permute-done | bytes 262176 | tf_op jit(solution)/shard_map/ppermute | solution.py:182
  48.6 7.5 %collective-permute-done.10.d3 = bf16[576,256]{1,0:T(8,128)(2,1)S(1)} collective-permute-done((bf16[576,256]{1,0:T(8,128)(2,1)S(1)}, bf16[576,256]{1,0:T(8,128)(2,1)S(1)}, u32[]{:S(2)}, u32[]{:S(2)}) %collective-permute-start.10) | collective-permute-done | bytes 294944 | tf_op jit(solution)/shard_map/ppermute | solution.py:25
  56.1 0.7 collective-permute-done.9.d2
  56.8 0.7 rows.1
  57.5 3.2 %collective-permute-start.11 = (bf16[16,16,256]{2,1,0:T(8,128)(2,1)S(1)}, bf16[16,16,256]{2,1,0:T(8,128)(2,1)S(1)}, u32[]{:S(2)}, u32[]{:S(2)}) collective-permute-start(bf16[16,16,256]{2,1,0:T(8,128)(2,1)S(1)} %get-tuple-element.113), channel_id=1, source_target_pairs={{0,32},{32,0},{1,33},{33,1},{2,34},{34,2},{3,35},{35,3},{4,36},{36... | collective-permute-start | bytes 393224 | tf_op jit(solution)/shard_map/ppermute | solution.py:22
  60.7 0.6 collective-permute-start.12
  61.3 0.5 collective-permute-start.13
  61.9 3.6 %taps.1 = (f32[96,16,256]{2,1,0:T(8,128)S(1)}, bf16[96,16,256]{2,1,0:T(8,128)(2,1)S(1)}) custom-call(s32[6]{0:T(128)S(1)} %stack.27.pos_ref, s32[176]{0:T(256)S(1)} %fusion.1.place_ref, bf16[576,256]{1,0:T(8,128)(2,1)S(1)} %get-tuple-element.105.d0, bf16[576,256]{1,0:T(8,128)(2,1)S(1)} %collective-permute-done.8.d1, ...), custom_call_target="tpu_custom_call" | custom-call | flops 2113929216 | bytes 8388608 | tf_op jit(solution)/shard_map/taps/pallas_call | solution.py:250
  65.4 1.0 %collective-permute-done.12 = bf16[16,16,256]{2,1,0:T(8,128)(2,1)S(1)} collective-permute-done((bf16[16,16,256]{2,1,0:T(8,128)(2,1)S(1)}, bf16[16,16,256]{2,1,0:T(8,128)(2,1)S(1)}, u32[]{:S(2)}, u32[]{:S(2)}) %collective-permute-start.12) | collective-permute-done | bytes 131104 | tf_op jit(solution)/shard_map/ppermute | solution.py:24
  66.5 1.0 %collective-permute-done.13 = bf16[16,16,256]{2,1,0:T(8,128)(2,1)S(1)} collective-permute-done((bf16[16,16,256]{2,1,0:T(8,128)(2,1)S(1)}, bf16[16,16,256]{2,1,0:T(8,128)(2,1)S(1)}, u32[]{:S(2)}, u32[]{:S(2)}) %collective-permute-start.13) | collective-permute-done | bytes 131104 | tf_op jit(solution)/shard_map/ppermute | solution.py:25
  67.6 0.6 collective-permute-start.15
  68.2 1.8 %collective-permute-done.15.other_ref = bf16[16,16,256]{2,1,0:T(8,128)(2,1)S(1)} collective-permute-done((bf16[16,16,256]{2,1,0:T(8,128)(2,1)S(1)}, bf16[16,16,256]{2,1,0:T(8,128)(2,1)S(1)}, u32[]{:S(2)}, u32[]{:S(2)}) %collective-permute-start.15) | collective-permute-done | bytes 131104 | tf_op jit(solution)/shard_map/ppermute | solution.py:182
  70.0 1.1 %owners.1 = bf16[16,96,256]{2,1,0:T(8,128)(2,1)S(1)} custom-call(s32[6]{0:T(128)S(1)} %stack.27.pos_ref, s32[176]{0:T(256)S(1)} %fusion.1.place_ref, f32[96,16,256]{2,1,0:T(8,128)S(1)} %get-tuple-element.110.keep_ref, bf16[96,16,256]{2,1,0:T(8,128)(2,1)S(1)} %collective-permute-done.14.got_ref, f32[16,16,256]{2,1,0:T(8,128)S(1)} %get-tuple-element.122.mine_ref, ...), custom_call_target="tpu_custom_call" | custom-call | flops 393216 | bytes 3145728 | tf_op jit(solution)/shard_map/owners/pallas_call | solution.py:271
  71.0 22.3 %all_to_all.5.r_ref = bf16[16,96,256]{2,1,0:T(8,128)(2,1)S(1)} all-to-all(bf16[16,96,256]{2,1,0:T(8,128)(2,1)S(1)} %owners.1), channel_id=1, replica_groups=mesh['row'=2,'col'=2,'dp_0'=4,'dp_1'=4,'dp_2'=2] {'dp_0','dp_1'}, dimensions={0} | all-to-all | bytes 1572864 | tf_op jit(solution)/shard_map/all_to_all | solution.py:282
  93.3 0.8 last.1
  (24 shorter events, 1.5 us)
Async XLA Ops:
  0.0 7.0 %copy-start = (bf16[1,24,24,1024]{3,2,1,0:T(8,128)(2,1)S(1)}, bf16[1,24,24,1024]{3,2,1,0:T(8,128)(2,1)}, u32[]{:S(2)}) copy-start(bf16[1,24,24,1024]{3,2,1,0:T(8,128)(2,1)} %param.8) | copy-start | bytes 3538948
  2.6 17.2 %collective-permute-start.3 = (bf16[576,256]{1,0:T(8,128)(2,1)S(1)}, bf16[576,256]{1,0:T(8,128)(2,1)S(1)}, u32[]{:S(2)}, u32[]{:S(2)}) collective-permute-start(bf16[576,256]{1,0:T(8,128)(2,1)S(1)} %get-tuple-element.73), channel_id=1, source_target_pairs={{0,32},{32,0},{1,33},{33,1},{2,34},{34,2},{3,35},{35,3},{4,36},{36... | collective-permute-start | bytes 884744 | tf_op jit(solution)/shard_map/ppermute | solution.py:22
  5.8 14.8 %collective-permute-start.4 = (bf16[576,256]{1,0:T(8,128)(2,1)S(1)}, bf16[576,256]{1,0:T(8,128)(2,1)S(1)}, u32[]{:S(2)}, u32[]{:S(2)}) collective-permute-start(bf16[576,256]{1,0:T(8,128)(2,1)S(1)} %get-tuple-element.74), channel_id=1, source_target_pairs={{0,64},{64,0},{1,65},{65,1},{2,66},{66,2},{3,67},{67,3},{4,68},{68... | collective-permute-start | bytes 884744 | tf_op jit(solution)/shard_map/ppermute | solution.py:24
  6.4 14.2 %collective-permute-start.5 = (bf16[576,256]{1,0:T(8,128)(2,1)S(1)}, bf16[576,256]{1,0:T(8,128)(2,1)S(1)}, u32[]{:S(2)}, u32[]{:S(2)}) collective-permute-start(bf16[576,256]{1,0:T(8,128)(2,1)S(1)} %get-tuple-element.75), channel_id=1, source_target_pairs={{0,96},{96,0},{32,64},{64,32},{1,97},{97,1},{33,65},{65,33},{2,98}... | collective-permute-start | bytes 884744 | tf_op jit(solution)/shard_map/ppermute | solution.py:25
  15.7 6.2 %copy-start.1 = (bf16[1024,256]{1,0:T(8,128)(2,1)S(1)}, bf16[1024,256]{1,0:T(8,128)(2,1)}, u32[]{:S(2)}) copy-start(bf16[1024,256]{1,0:T(8,128)(2,1)} %wp_ref.2) | copy-start | bytes 1572868
  15.7 14.5 %collective-permute-start = (bf16[864,256]{1,0:T(8,128)(2,1)S(1)}, bf16[864,256]{1,0:T(8,128)(2,1)S(1)}, u32[]{:S(2)}, u32[]{:S(2)}) collective-permute-start(bf16[864,256]{1,0:T(8,128)(2,1)S(1)} %get-tuple-element.68), channel_id=1, source_target_pairs={{0,64},{64,0},{1,65},{65,1},{2,66},{66,2},{3,67},{67,3},{4,68},{68... | collective-permute-start | bytes 1327112 | tf_op jit(solution)/shard_map/ppermute | solution.py:24
  17.2 21.2 %collective-permute-start.1 = (bf16[864,256]{1,0:T(8,128)(2,1)S(1)}, bf16[864,256]{1,0:T(8,128)(2,1)S(1)}, u32[]{:S(2)}, u32[]{:S(2)}) collective-permute-start(bf16[864,256]{1,0:T(8,128)(2,1)S(1)} %get-tuple-element.69), channel_id=1, source_target_pairs={{0,32},{32,0},{1,33},{33,1},{2,34},{34,2},{3,35},{35,3},{4,36},{36... | collective-permute-start | bytes 1327112 | tf_op jit(solution)/shard_map/ppermute | solution.py:22
  19.9 10.1 %collective-permute-start.2 = (bf16[576,256]{1,0:T(8,128)(2,1)S(1)}, bf16[576,256]{1,0:T(8,128)(2,1)S(1)}, u32[]{:S(2)}, u32[]{:S(2)}) collective-permute-start(bf16[576,256]{1,0:T(8,128)(2,1)S(1)} %get-tuple-element.70), channel_id=1, source_target_pairs={{0,96},{96,0},{32,64},{64,32},{1,97},{97,1},{33,65},{65,33},{2,98}... | collective-permute-start | bytes 884744 | tf_op jit(solution)/shard_map/ppermute | solution.py:25
  21.8 16.6 %copy-start.2 = (bf16[1024,256]{1,0:T(8,128)(2,1)S(1)}, bf16[1024,256]{1,0:T(8,128)(2,1)}, u32[]{:S(2)}) copy-start(bf16[1024,256]{1,0:T(8,128)(2,1)} %wp_ref.3) | copy-start | bytes 1572868
  21.9 16.5 %copy-start.3 = (bf16[1,24,24,256]{3,2,1,0:T(8,128)(2,1)S(1)}, bf16[1,24,24,256]{3,2,1,0:T(8,128)(2,1)}, u32[]{:S(2)}) copy-start(bf16[1,24,24,256]{3,2,1,0:T(8,128)(2,1)} %param.9) | copy-start | bytes 884740
  40.8 6.4 %copy-start.4 = (s32[176]{0:T(256)S(1)}, s32[176]{0:T(256)}, u32[]{:S(2)}) copy-start(s32[176]{0:T(256)} %param.15) | copy-start | bytes 2116
  40.8 15.3 %collective-permute-start.10 = (bf16[576,256]{1,0:T(8,128)(2,1)S(1)}, bf16[576,256]{1,0:T(8,128)(2,1)S(1)}, u32[]{:S(2)}, u32[]{:S(2)}) collective-permute-start(bf16[576,256]{1,0:T(8,128)(2,1)S(1)} %get-tuple-element.105.d0), channel_id=1, source_target_pairs={{0,96},{96,0},{32,64},{64,32},{1,97},{97,1},{33,65},{65,33},{2,98}... | collective-permute-start | bytes 884744 | tf_op jit(solution)/shard_map/ppermute | solution.py:25
  43.6 12.5 %collective-permute-start.8 = (bf16[576,256]{1,0:T(8,128)(2,1)S(1)}, bf16[576,256]{1,0:T(8,128)(2,1)S(1)}, u32[]{:S(2)}, u32[]{:S(2)}) collective-permute-start(bf16[576,256]{1,0:T(8,128)(2,1)S(1)} %get-tuple-element.105.d0), channel_id=1, source_target_pairs={{0,32},{32,0},{1,33},{33,1},{2,34},{34,2},{3,35},{35,3},{4,36},{36... | collective-permute-start | bytes 884744 | tf_op jit(solution)/shard_map/ppermute | solution.py:22
  44.4 12.4 %collective-permute-start.9 = (bf16[576,256]{1,0:T(8,128)(2,1)S(1)}, bf16[576,256]{1,0:T(8,128)(2,1)S(1)}, u32[]{:S(2)}, u32[]{:S(2)}) collective-permute-start(bf16[576,256]{1,0:T(8,128)(2,1)S(1)} %get-tuple-element.105.d0), channel_id=1, source_target_pairs={{0,64},{64,0},{1,65},{65,1},{2,66},{66,2},{3,67},{67,3},{4,68},{68... | collective-permute-start | bytes 884744 | tf_op jit(solution)/shard_map/ppermute | solution.py:24
  46.6 1.6 %collective-permute-start.6 = (bf16[512,256]{1,0:T(8,128)(2,1)S(1)}, bf16[512,256]{1,0:T(8,128)(2,1)S(1)}, u32[]{:S(2)}, u32[]{:S(2)}) collective-permute-start(bf16[512,256]{1,0:T(8,128)(2,1)S(1)} %get-tuple-element.92), channel_id=1, source_target_pairs={{0,1},{1,0},{2,3},{3,2},{4,5},{5,4},{6,7},{7,6},{8,9},{9,8},{10,11... | collective-permute-start | bytes 786440 | tf_op jit(solution)/shard_map/ppermute | solution.py:182
  46.7 1.9 %collective-permute-start.7 = (bf16[512,256]{1,0:T(8,128)(2,1)S(1)}, bf16[512,256]{1,0:T(8,128)(2,1)S(1)}, u32[]{:S(2)}, u32[]{:S(2)}) collective-permute-start(bf16[512,256]{1,0:T(8,128)(2,1)S(1)} %get-tuple-element.93), channel_id=1, source_target_pairs={{0,1},{1,0},{2,3},{3,2},{4,5},{5,4},{6,7},{7,6},{8,9},{9,8},{10,11... | collective-permute-start | bytes 786440 | tf_op jit(solution)/shard_map/ppermute | solution.py:182
  57.5 7.9 %collective-permute-start.11 = (bf16[16,16,256]{2,1,0:T(8,128)(2,1)S(1)}, bf16[16,16,256]{2,1,0:T(8,128)(2,1)S(1)}, u32[]{:S(2)}, u32[]{:S(2)}) collective-permute-start(bf16[16,16,256]{2,1,0:T(8,128)(2,1)S(1)} %get-tuple-element.113), channel_id=1, source_target_pairs={{0,32},{32,0},{1,33},{33,1},{2,34},{34,2},{3,35},{35,3},{4,36},{36... | collective-permute-start | bytes 393224 | tf_op jit(solution)/shard_map/ppermute | solution.py:22
  60.7 5.7 %collective-permute-start.12 = (bf16[16,16,256]{2,1,0:T(8,128)(2,1)S(1)}, bf16[16,16,256]{2,1,0:T(8,128)(2,1)S(1)}, u32[]{:S(2)}, u32[]{:S(2)}) collective-permute-start(bf16[16,16,256]{2,1,0:T(8,128)(2,1)S(1)} %get-tuple-element.114), channel_id=1, source_target_pairs={{0,64},{64,0},{1,65},{65,1},{2,66},{66,2},{3,67},{67,3},{4,68},{68... | collective-permute-start | bytes 393224 | tf_op jit(solution)/shard_map/ppermute | solution.py:24
  61.3 6.2 %collective-permute-start.13 = (bf16[16,16,256]{2,1,0:T(8,128)(2,1)S(1)}, bf16[16,16,256]{2,1,0:T(8,128)(2,1)S(1)}, u32[]{:S(2)}, u32[]{:S(2)}) collective-permute-start(bf16[16,16,256]{2,1,0:T(8,128)(2,1)S(1)} %get-tuple-element.115), channel_id=1, source_target_pairs={{0,96},{96,0},{32,64},{64,32},{1,97},{97,1},{33,65},{65,33},{2,98}... | collective-permute-start | bytes 393224 | tf_op jit(solution)/shard_map/ppermute | solution.py:25
  67.5 2.5 %collective-permute-start.14 = (bf16[96,16,256]{2,1,0:T(8,128)(2,1)S(1)}, bf16[96,16,256]{2,1,0:T(8,128)(2,1)S(1)}, u32[]{:S(2)}, u32[]{:S(2)}) collective-permute-start(bf16[96,16,256]{2,1,0:T(8,128)(2,1)S(1)} %get-tuple-element.116), channel_id=1, source_target_pairs={{0,1},{1,0},{2,3},{3,2},{4,5},{5,4},{6,7},{7,6},{8,9},{9,8},{10,11... | collective-permute-start | bytes 2359304 | tf_op jit(solution)/shard_map/ppermute | solution.py:182
  67.6 2.4 %collective-permute-start.15 = (bf16[16,16,256]{2,1,0:T(8,128)(2,1)S(1)}, bf16[16,16,256]{2,1,0:T(8,128)(2,1)S(1)}, u32[]{:S(2)}, u32[]{:S(2)}) collective-permute-start(bf16[16,16,256]{2,1,0:T(8,128)(2,1)S(1)} %get-tuple-element.121), channel_id=1, source_target_pairs={{0,1},{1,0},{2,3},{3,2},{4,5},{5,4},{6,7},{7,6},{8,9},{9,8},{10,11... | collective-permute-start | bytes 393224 | tf_op jit(solution)/shard_map/ppermute | solution.py:182

commit v7 on v6

--- a/solution.py
+++ b/solution.py
@@ -615,10 +615,10 @@
         name="pair",
     )(pos, joined, g_proj, centre, delta0)
     got = [swap_core(part) for part in sent]
-    got, shared = lax.optimization_barrier((got, shared))
     by_owner = split_pair(pos, kept, got)
-    by_owner, shared = lax.optimization_barrier((by_owner, shared))
-    by_owner = [by_owner[0]] + [flip(by_owner[k], k) for k in (1, 2, 3)]
+    early = [flip(by_owner[k], k) for k in (1, 2)]
+    late, early, shared = lax.optimization_barrier((by_owner[3], early, shared))
+    by_owner = [by_owner[0], *early, flip(late, 3)]
     kept, sent = tap_slots(pos, place, shared, turned, slot_count)
     sent, by_owner = lax.optimization_barrier((sent, by_owner))
     mine, other = sum_pair(by_owner)

time: 94.3 us -> 98.5 us (1.045)
  waiting for transfers between devices: 23.9 us -> 28.2 us
    ppermute x4, waiting for transfers between devices: 2.05 us -> 8.79 us  [flip(): return lax.ppermute(x, 'row', [(0, 1), (1, 0)])]
    ppermute x4, waiting for transfers between devices: 10.4 us -> 3.76 us  [flip(): return lax.ppermute(x, ('row', 'col'), [(0, 3), (3, 0), (1, 2), (2, 1)])]
    ppermute x4, waiting for transfers between devices: 8.26 us -> 13.8 us  [flip(): return lax.ppermute(x, 'col', [(0, 1), (1, 0)])]
    ppermute x4, starting transfers between devices: 4.53 us -> 2.41 us  [flip(): return lax.ppermute(x, ('row', 'col'), [(0, 3), (3, 0), (1, 2), (2, 1)])]
    ppermute x4, starting transfers between devices: 9.91 us -> 11.9 us  [flip(): return lax.ppermute(x, 'col', [(0, 1), (1, 0)])]
    ppermute x4, waiting for transfers between devices: 3.18 us -> 1.81 us  [swap_core(): return lax.ppermute(x, 'dp_2', [(0, 1), (1, 0)])]
  transfers between devices with their start and end apart: 16 -> 16, of which waited for: 11 -> 10; matrix products, arithmetic and copies ran while one was open for 0% -> 0% of each run, Pallas kernels for 23% -> 21%
where the time goes in v7:
time: 98.5 us; the launch traced here: 98.4 us
  Pallas kernels  28.8 us (29%)
  waiting for transfers between devices  28.2 us (29%)
  blocking collectives  22.3 us (23%)
  starting transfers between devices  18.8 us (19%)
    all_to_all x1, blocking collectives, reduce_slots(): total = lax.all_to_all(total, ('dp_0', 'dp_1'), 0, 0, tiled=True)  22.3 us
    ppermute x4, waiting for transfers between devices, flip(): return lax.ppermute(x, 'col', [(0, 1), (1, 0)])  13.8 us
    ppermute x4, starting transfers between devices, flip(): return lax.ppermute(x, 'col', [(0, 1), (1, 0)])  11.9 us
    ppermute x4, waiting for transfers between devices, flip(): return lax.ppermute(x, 'row', [(0, 1), (1, 0)])  8.79 us
    pallas_call x1, Pallas kernels, outer(): call(outer_parts, [jax.ShapeDtypeStruct(*s) for s in shapes], 1, 1, 2 * p...  8.68 us
    pallas_call x1, Pallas kernels, inner(): call(inner_parts, [jax.ShapeDtypeStruct((pixels, width), F32), jax.ShapeD...  6.26 us
    ppermute x4, waiting for transfers between devices, flip(): return lax.ppermute(x, ('row', 'col'), [(0, 3), (3, 0), (1, 2), (2, 1)])  3.76 us
    pallas_call x1, Pallas kernels, tap_slots(): call(tap_grads, [jax.ShapeDtypeStruct((half, 16, width), F32), jax.ShapeD...  3.56 us
  transfers between devices with their start and end apart: 16, of which 10 were waited for; matrix products, arithmetic and copies ran while one was open for 0% of the time, Pallas kernels for 21%

profile of v7, /device:TPU:0, one launch (start us, length us, event | category | flops | bytes accessed | tf_op | source)
XLA Modules:
  0.0 98.4 jit_solution(1849104054877231446)
XLA Ops:
  0.1 2.6 %pick.1 = (bf16[576,256]{1,0:T(8,128)(2,1)S(1)}, bf16[576,256]{1,0:T(8,128)(2,1)S(1)}, bf16[576,256]{1,0:T(8,128)(2,1)S(1)}, bf16[576,256]{1,0:T(8,128)(2,1)S(1)}) custom-call(s32[6]{0:T(128)S(1)} %stack.27.pos_ref, bf16[576,1024]{1,0:T(8,128)(2,1)} %bitcast.8), custom_call_target="tpu_custom_call" | custom-call | flops 603979776 | bytes 2359296 | tf_op jit(solution)/shard_map/pick/pallas_call | solution.py:188
  2.6 3.2 %collective-permute-start.3 = (bf16[576,256]{1,0:T(8,128)(2,1)S(1)}, bf16[576,256]{1,0:T(8,128)(2,1)S(1)}, u32[]{:S(2)}, u32[]{:S(2)}) collective-permute-start(bf16[576,256]{1,0:T(8,128)(2,1)S(1)} %get-tuple-element.66), channel_id=1, source_target_pairs={{0,32},{32,0},{1,33},{33,1},{2,34},{34,2},{3,35},{35,3},{4,36},{36... | collective-permute-start | bytes 884744 | tf_op jit(solution)/shard_map/ppermute | solution.py:22
  5.8 0.6 collective-permute-start.4
  6.4 0.6 collective-permute-start.5
  7.0 8.7 %outer.1 = (f32[3,576,256]{2,1,0:T(8,128)S(1)}, bf16[864,256]{1,0:T(8,128)(2,1)S(1)}, bf16[864,256]{1,0:T(8,128)(2,1)S(1)}, bf16[576,256]{1,0:T(8,128)(2,1)S(1)}) custom-call(s32[6]{0:T(128)S(1)} %stack.27.pos_ref, bf16[576,1024]{1,0:T(8,128)(2,1)S(1)} %bitcast.9, bf16[3,3,1024,256]{3,2,1,0:T(8,128)(2,1)} %wc_ref.3, bf16[3,3,1024,256]{3,2,1,0:T(8,128)(2,1)} %wb_ref.3, ...), custom_call_target="tpu_custom_call" | custom-call | flops 4227858432 | bytes 10485760 | tf_op jit(solution)/shard_map/outer/pallas_call | solution.py:451
  15.7 1.5 %collective-permute-start = (bf16[864,256]{1,0:T(8,128)(2,1)S(1)}, bf16[864,256]{1,0:T(8,128)(2,1)S(1)}, u32[]{:S(2)}, u32[]{:S(2)}) collective-permute-start(bf16[864,256]{1,0:T(8,128)(2,1)S(1)} %get-tuple-element.61), channel_id=1, source_target_pairs={{0,64},{64,0},{1,65},{65,1},{2,66},{66,2},{3,67},{67,3},{4,68},{68... | collective-permute-start | bytes 1327112 | tf_op jit(solution)/shard_map/ppermute | solution.py:24
  17.2 2.7 %collective-permute-start.1 = (bf16[864,256]{1,0:T(8,128)(2,1)S(1)}, bf16[864,256]{1,0:T(8,128)(2,1)S(1)}, u32[]{:S(2)}, u32[]{:S(2)}) collective-permute-start(bf16[864,256]{1,0:T(8,128)(2,1)S(1)} %get-tuple-element.62), channel_id=1, source_target_pairs={{0,32},{32,0},{1,33},{33,1},{2,34},{34,2},{3,35},{35,3},{4,36},{36... | collective-permute-start | bytes 1327112 | tf_op jit(solution)/shard_map/ppermute | solution.py:22
  19.9 0.6 collective-permute-start.2
  20.7 1.2 %turn.1.xt_ref = bf16[2,256,1152]{2,1,0:T(8,128)(2,1)S(1)} custom-call(s32[6]{0:T(128)S(1)} %stack.27.pos_ref, bf16[576,256]{1,0:T(8,128)(2,1)S(1)} %get-tuple-element.72.x0, bf16[576,256]{1,0:T(8,128)(2,1)S(1)} %collective-permute-done.3.x1, bf16[576,256]{1,0:T(8,128)(2,1)S(1)} %collective-permute-done.4.x2, bf16[576,256]{1,0:T(8,128)(2,1)S(1)} %collective-permute-done.5.x3), custom_call_target="tpu_custom_call" | custom-call | flops 301989888 | bytes 2359296 | tf_op jit(solution)/shard_map/turn/pallas_call | solution.py:204
  21.9 6.3 %inner.1 = (f32[576,256]{1,0:T(8,128)S(1)}, f32[3,576,256]{2,1,0:T(8,128)S(1)}) custom-call(s32[6]{0:T(128)S(1)} %stack.27.pos_ref, bf16[576,1024]{1,0:T(8,128)(2,1)S(1)} %bitcast.10, f32[3,576,256]{2,1,0:T(8,128)S(1)} %get-tuple-element.69.part_ref, bf16[1024,256]{1,0:T(8,128)(2,1)S(1)} %copy-done.1, bf16[3,3,1024,256]{3,2,1,0:T(8,128)(2,1)} %wc_ref.3, ...), custom_call_target="tpu_custom_call" | custom-call | flops 3019898880 | bytes 10485760 | tf_op jit(solution)/shard_map/inner/pallas_call | solution.py:474
  28.1 1.9 %collective-permute-done.2.diag_ref = bf16[576,256]{1,0:T(8,128)(2,1)S(1)} collective-permute-done((bf16[576,256]{1,0:T(8,128)(2,1)S(1)}, bf16[576,256]{1,0:T(8,128)(2,1)S(1)}, u32[]{:S(2)}, u32[]{:S(2)}) %collective-permute-start.2) | collective-permute-done | bytes 294944 | tf_op jit(solution)/shard_map/ppermute | solution.py:25
  30.1 8.3 %collective-permute-done.1.col_ref = bf16[864,256]{1,0:T(8,128)(2,1)S(1)} collective-permute-done((bf16[864,256]{1,0:T(8,128)(2,1)S(1)}, bf16[864,256]{1,0:T(8,128)(2,1)S(1)}, u32[]{:S(2)}, u32[]{:S(2)}) %collective-permute-start.1) | collective-permute-done | bytes 442400 | tf_op jit(solution)/shard_map/ppermute | solution.py:22
  38.4 2.4 %merge.1 = (bf16[576,1024]{1,0:T(8,128)(2,1)S(1)}, bf16[576,256]{1,0:T(8,128)(2,1)S(1)}, bf16[576,256]{1,0:T(8,128)(2,1)S(1)}, bf16[576,256]{1,0:T(8,128)(2,1)S(1)}) custom-call(s32[6]{0:T(128)S(1)} %stack.27.pos_ref, f32[576,256]{1,0:T(8,128)S(1)} %get-tuple-element.76.pre0_ref, f32[3,576,256]{2,1,0:T(8,128)S(1)} %get-tuple-element.77.own_ref, ...), custom_call_target="tpu_custom_call" | custom-call | flops 452984832 | bytes 6291456 | tf_op jit(solution)/shard_map/merge/pallas_call | solution.py:554
  40.8 1.6 %pair.1 = (f32[1024,256]{1,0:T(8,128)S(1)}, bf16[512,256]{1,0:T(8,128)(2,1)S(1)}, bf16[512,256]{1,0:T(8,128)(2,1)S(1)}) custom-call(s32[6]{0:T(128)S(1)} %stack.27.pos_ref, bf16[576,1024]{1,0:T(8,128)(2,1)S(1)} %get-tuple-element.81.joined_ref, bf16[576,256]{1,0:T(8,128)(2,1)S(1)} %get-tuple-element.82.g_ref, bf16[576,1024]{1,0:T(8,128)(2,1)S(1)} %bitcast.11, ...), custom_call_target="tpu_custom_call" | custom-call | flops 603979776 | bytes 4194304 | tf_op jit(solution)/shard_map/pair/pallas_call | solution.py:607
  43.0 3.0 %collective-permute-start.10 = (bf16[576,256]{1,0:T(8,128)(2,1)S(1)}, bf16[576,256]{1,0:T(8,128)(2,1)S(1)}, u32[]{:S(2)}, u32[]{:S(2)}) collective-permute-start(bf16[576,256]{1,0:T(8,128)(2,1)S(1)} %get-tuple-element.91.d0), channel_id=1, source_target_pairs={{0,32},{32,0},{1,33},{33,1},{2,34},{34,2},{3,35},{35,3},{4,36},{36... | collective-permute-start | bytes 884744 | tf_op jit(solution)/shard_map/ppermute | solution.py:22
  46.0 0.6 collective-permute-start.11
  46.6 0.5 collective-permute-start.12
  47.2 0.7 rows.1
  47.9 3.0 %collective-permute-start.8 = (bf16[16,16,256]{2,1,0:T(8,128)(2,1)S(1)}, bf16[16,16,256]{2,1,0:T(8,128)(2,1)S(1)}, u32[]{:S(2)}, u32[]{:S(2)}) collective-permute-start(bf16[16,16,256]{2,1,0:T(8,128)(2,1)S(1)} %get-tuple-element.88), channel_id=1, source_target_pairs={{0,32},{32,0},{1,33},{33,1},{2,34},{34,2},{3,35},{35,3},{4,36},{36... | collective-permute-start | bytes 393224 | tf_op jit(solution)/shard_map/ppermute | solution.py:22
  50.9 0.6 collective-permute-start.9
  51.6 2.9 %collective-permute-done.10.d1 = bf16[576,256]{1,0:T(8,128)(2,1)S(1)} collective-permute-done((bf16[576,256]{1,0:T(8,128)(2,1)S(1)}, bf16[576,256]{1,0:T(8,128)(2,1)S(1)}, u32[]{:S(2)}, u32[]{:S(2)}) %collective-permute-start.10) | collective-permute-done | bytes 294944 | tf_op jit(solution)/shard_map/ppermute | solution.py:22
  54.4 6.4 %collective-permute-done.11.d2 = bf16[576,256]{1,0:T(8,128)(2,1)S(1)} collective-permute-done((bf16[576,256]{1,0:T(8,128)(2,1)S(1)}, bf16[576,256]{1,0:T(8,128)(2,1)S(1)}, u32[]{:S(2)}, u32[]{:S(2)}) %collective-permute-start.11) | collective-permute-done | bytes 294944 | tf_op jit(solution)/shard_map/ppermute | solution.py:24
  60.8 2.7 %collective-permute-done.8 = bf16[16,16,256]{2,1,0:T(8,128)(2,1)S(1)} collective-permute-done((bf16[16,16,256]{2,1,0:T(8,128)(2,1)S(1)}, bf16[16,16,256]{2,1,0:T(8,128)(2,1)S(1)}, u32[]{:S(2)}, u32[]{:S(2)}) %collective-permute-start.8) | collective-permute-done | bytes 131104 | tf_op jit(solution)/shard_map/ppermute | solution.py:22
  63.5 2.1 %collective-permute-done.9 = bf16[16,16,256]{2,1,0:T(8,128)(2,1)S(1)} collective-permute-done((bf16[16,16,256]{2,1,0:T(8,128)(2,1)S(1)}, bf16[16,16,256]{2,1,0:T(8,128)(2,1)S(1)}, u32[]{:S(2)}, u32[]{:S(2)}) %collective-permute-start.9) | collective-permute-done | bytes 131104 | tf_op jit(solution)/shard_map/ppermute | solution.py:24
  65.6 0.7 collective-permute-start.13
  66.3 3.6 %taps.1 = (f32[96,16,256]{2,1,0:T(8,128)S(1)}, bf16[96,16,256]{2,1,0:T(8,128)(2,1)S(1)}) custom-call(s32[6]{0:T(128)S(1)} %stack.27.pos_ref, s32[176]{0:T(256)S(1)} %fusion.1.place_ref, bf16[576,256]{1,0:T(8,128)(2,1)S(1)} %get-tuple-element.91.d0, bf16[576,256]{1,0:T(8,128)(2,1)S(1)} %collective-permute-done.10.d1, ...), custom_call_target="tpu_custom_call" | custom-call | flops 2113929216 | bytes 8388608 | tf_op jit(solution)/shard_map/taps/pallas_call | solution.py:250
  69.9 1.9 %collective-permute-done.13 = bf16[16,16,256]{2,1,0:T(8,128)(2,1)S(1)} collective-permute-done((bf16[16,16,256]{2,1,0:T(8,128)(2,1)S(1)}, bf16[16,16,256]{2,1,0:T(8,128)(2,1)S(1)}, u32[]{:S(2)}, u32[]{:S(2)}) %collective-permute-start.13) | collective-permute-done | bytes 131104 | tf_op jit(solution)/shard_map/ppermute | solution.py:25
  71.9 0.6 collective-permute-start.15
  72.5 1.8 %collective-permute-done.15.other_ref = bf16[16,16,256]{2,1,0:T(8,128)(2,1)S(1)} collective-permute-done((bf16[16,16,256]{2,1,0:T(8,128)(2,1)S(1)}, bf16[16,16,256]{2,1,0:T(8,128)(2,1)S(1)}, u32[]{:S(2)}, u32[]{:S(2)}) %collective-permute-start.15) | collective-permute-done | bytes 131104 | tf_op jit(solution)/shard_map/ppermute | solution.py:182
  74.3 1.1 %owners.1 = bf16[16,96,256]{2,1,0:T(8,128)(2,1)S(1)} custom-call(s32[6]{0:T(128)S(1)} %stack.27.pos_ref, s32[176]{0:T(256)S(1)} %fusion.1.place_ref, f32[96,16,256]{2,1,0:T(8,128)S(1)} %get-tuple-element.96.keep_ref, bf16[96,16,256]{2,1,0:T(8,128)(2,1)S(1)} %collective-permute-done.14.got_ref, f32[16,16,256]{2,1,0:T(8,128)S(1)} %get-tuple-element.108.mine_ref, ...), custom_call_target="tpu_custom_call" | custom-call | flops 393216 | bytes 3145728 | tf_op jit(solution)/shard_map/owners/pallas_call | solution.py:271
  75.3 22.3 %all_to_all.5.r_ref = bf16[16,96,256]{2,1,0:T(8,128)(2,1)S(1)} all-to-all(bf16[16,96,256]{2,1,0:T(8,128)(2,1)S(1)} %owners.1), channel_id=1, replica_groups=mesh['row'=2,'col'=2,'dp_0'=4,'dp_1'=4,'dp_2'=2] {'dp_0','dp_1'}, dimensions={0} | all-to-all | bytes 1572864 | tf_op jit(solution)/shard_map/all_to_all | solution.py:282
  97.6 0.8 last.1
  (24 shorter events, 1.1 us)
Async XLA Ops:
  0.0 7.0 %copy-start = (bf16[1,24,24,1024]{3,2,1,0:T(8,128)(2,1)S(1)}, bf16[1,24,24,1024]{3,2,1,0:T(8,128)(2,1)}, u32[]{:S(2)}) copy-start(bf16[1,24,24,1024]{3,2,1,0:T(8,128)(2,1)} %param.8) | copy-start | bytes 3538948
  2.6 17.2 %collective-permute-start.3 = (bf16[576,256]{1,0:T(8,128)(2,1)S(1)}, bf16[576,256]{1,0:T(8,128)(2,1)S(1)}, u32[]{:S(2)}, u32[]{:S(2)}) collective-permute-start(bf16[576,256]{1,0:T(8,128)(2,1)S(1)} %get-tuple-element.66), channel_id=1, source_target_pairs={{0,32},{32,0},{1,33},{33,1},{2,34},{34,2},{3,35},{35,3},{4,36},{36... | collective-permute-start | bytes 884744 | tf_op jit(solution)/shard_map/ppermute | solution.py:22
  5.8 14.8 %collective-permute-start.4 = (bf16[576,256]{1,0:T(8,128)(2,1)S(1)}, bf16[576,256]{1,0:T(8,128)(2,1)S(1)}, u32[]{:S(2)}, u32[]{:S(2)}) collective-permute-start(bf16[576,256]{1,0:T(8,128)(2,1)S(1)} %get-tuple-element.67), channel_id=1, source_target_pairs={{0,64},{64,0},{1,65},{65,1},{2,66},{66,2},{3,67},{67,3},{4,68},{68... | collective-permute-start | bytes 884744 | tf_op jit(solution)/shard_map/ppermute | solution.py:24
  6.4 14.2 %collective-permute-start.5 = (bf16[576,256]{1,0:T(8,128)(2,1)S(1)}, bf16[576,256]{1,0:T(8,128)(2,1)S(1)}, u32[]{:S(2)}, u32[]{:S(2)}) collective-permute-start(bf16[576,256]{1,0:T(8,128)(2,1)S(1)} %get-tuple-element.68), channel_id=1, source_target_pairs={{0,96},{96,0},{32,64},{64,32},{1,97},{97,1},{33,65},{65,33},{2,98}... | collective-permute-start | bytes 884744 | tf_op jit(solution)/shard_map/ppermute | solution.py:25
  15.7 6.2 %copy-start.1 = (bf16[1024,256]{1,0:T(8,128)(2,1)S(1)}, bf16[1024,256]{1,0:T(8,128)(2,1)}, u32[]{:S(2)}) copy-start(bf16[1024,256]{1,0:T(8,128)(2,1)} %wp_ref.2) | copy-start | bytes 1572868
  15.7 14.5 %collective-permute-start = (bf16[864,256]{1,0:T(8,128)(2,1)S(1)}, bf16[864,256]{1,0:T(8,128)(2,1)S(1)}, u32[]{:S(2)}, u32[]{:S(2)}) collective-permute-start(bf16[864,256]{1,0:T(8,128)(2,1)S(1)} %get-tuple-element.61), channel_id=1, source_target_pairs={{0,64},{64,0},{1,65},{65,1},{2,66},{66,2},{3,67},{67,3},{4,68},{68... | collective-permute-start | bytes 1327112 | tf_op jit(solution)/shard_map/ppermute | solution.py:24
  17.2 21.2 %collective-permute-start.1 = (bf16[864,256]{1,0:T(8,128)(2,1)S(1)}, bf16[864,256]{1,0:T(8,128)(2,1)S(1)}, u32[]{:S(2)}, u32[]{:S(2)}) collective-permute-start(bf16[864,256]{1,0:T(8,128)(2,1)S(1)} %get-tuple-element.62), channel_id=1, source_target_pairs={{0,32},{32,0},{1,33},{33,1},{2,34},{34,2},{3,35},{35,3},{4,36},{36... | collective-permute-start | bytes 1327112 | tf_op jit(solution)/shard_map/ppermute | solution.py:22
  19.9 10.1 %collective-permute-start.2 = (bf16[576,256]{1,0:T(8,128)(2,1)S(1)}, bf16[576,256]{1,0:T(8,128)(2,1)S(1)}, u32[]{:S(2)}, u32[]{:S(2)}) collective-permute-start(bf16[576,256]{1,0:T(8,128)(2,1)S(1)} %get-tuple-element.63), channel_id=1, source_target_pairs={{0,96},{96,0},{32,64},{64,32},{1,97},{97,1},{33,65},{65,33},{2,98}... | collective-permute-start | bytes 884744 | tf_op jit(solution)/shard_map/ppermute | solution.py:25
  21.8 16.6 %copy-start.2 = (bf16[1024,256]{1,0:T(8,128)(2,1)S(1)}, bf16[1024,256]{1,0:T(8,128)(2,1)}, u32[]{:S(2)}) copy-start(bf16[1024,256]{1,0:T(8,128)(2,1)} %wp_ref.3) | copy-start | bytes 1572868
  21.9 16.5 %copy-start.3 = (bf16[1,24,24,256]{3,2,1,0:T(8,128)(2,1)S(1)}, bf16[1,24,24,256]{3,2,1,0:T(8,128)(2,1)}, u32[]{:S(2)}) copy-start(bf16[1,24,24,256]{3,2,1,0:T(8,128)(2,1)} %param.9) | copy-start | bytes 884740
  40.8 10.8 %copy-start.4 = (s32[176]{0:T(256)S(1)}, s32[176]{0:T(256)}, u32[]{:S(2)}) copy-start(s32[176]{0:T(256)} %param.15) | copy-start | bytes 2116
  42.4 4.8 %collective-permute-start.6 = (bf16[512,256]{1,0:T(8,128)(2,1)S(1)}, bf16[512,256]{1,0:T(8,128)(2,1)S(1)}, u32[]{:S(2)}, u32[]{:S(2)}) collective-permute-start(bf16[512,256]{1,0:T(8,128)(2,1)S(1)} %get-tuple-element.85), channel_id=1, source_target_pairs={{0,1},{1,0},{2,3},{3,2},{4,5},{5,4},{6,7},{7,6},{8,9},{9,8},{10,11... | collective-permute-start | bytes 786440 | tf_op jit(solution)/shard_map/ppermute | solution.py:182
  42.5 4.7 %collective-permute-start.7 = (bf16[512,256]{1,0:T(8,128)(2,1)S(1)}, bf16[512,256]{1,0:T(8,128)(2,1)S(1)}, u32[]{:S(2)}, u32[]{:S(2)}) collective-permute-start(bf16[512,256]{1,0:T(8,128)(2,1)S(1)} %get-tuple-element.86), channel_id=1, source_target_pairs={{0,1},{1,0},{2,3},{3,2},{4,5},{5,4},{6,7},{7,6},{8,9},{9,8},{10,11... | collective-permute-start | bytes 786440 | tf_op jit(solution)/shard_map/ppermute | solution.py:182
  43.0 11.4 %collective-permute-start.10 = (bf16[576,256]{1,0:T(8,128)(2,1)S(1)}, bf16[576,256]{1,0:T(8,128)(2,1)S(1)}, u32[]{:S(2)}, u32[]{:S(2)}) collective-permute-start(bf16[576,256]{1,0:T(8,128)(2,1)S(1)} %get-tuple-element.91.d0), channel_id=1, source_target_pairs={{0,32},{32,0},{1,33},{33,1},{2,34},{34,2},{3,35},{35,3},{4,36},{36... | collective-permute-start | bytes 884744 | tf_op jit(solution)/shard_map/ppermute | solution.py:22
  46.0 14.8 %collective-permute-start.11 = (bf16[576,256]{1,0:T(8,128)(2,1)S(1)}, bf16[576,256]{1,0:T(8,128)(2,1)S(1)}, u32[]{:S(2)}, u32[]{:S(2)}) collective-permute-start(bf16[576,256]{1,0:T(8,128)(2,1)S(1)} %get-tuple-element.91.d0), channel_id=1, source_target_pairs={{0,64},{64,0},{1,65},{65,1},{2,66},{66,2},{3,67},{67,3},{4,68},{68... | collective-permute-start | bytes 884744 | tf_op jit(solution)/shard_map/ppermute | solution.py:24
  46.6 14.2 %collective-permute-start.12 = (bf16[576,256]{1,0:T(8,128)(2,1)S(1)}, bf16[576,256]{1,0:T(8,128)(2,1)S(1)}, u32[]{:S(2)}, u32[]{:S(2)}) collective-permute-start(bf16[576,256]{1,0:T(8,128)(2,1)S(1)} %get-tuple-element.91.d0), channel_id=1, source_target_pairs={{0,96},{96,0},{32,64},{64,32},{1,97},{97,1},{33,65},{65,33},{2,98}... | collective-permute-start | bytes 884744 | tf_op jit(solution)/shard_map/ppermute | solution.py:25
  47.9 15.6 %collective-permute-start.8 = (bf16[16,16,256]{2,1,0:T(8,128)(2,1)S(1)}, bf16[16,16,256]{2,1,0:T(8,128)(2,1)S(1)}, u32[]{:S(2)}, u32[]{:S(2)}) collective-permute-start(bf16[16,16,256]{2,1,0:T(8,128)(2,1)S(1)} %get-tuple-element.88), channel_id=1, source_target_pairs={{0,32},{32,0},{1,33},{33,1},{2,34},{34,2},{3,35},{35,3},{4,36},{36... | collective-permute-start | bytes 393224 | tf_op jit(solution)/shard_map/ppermute | solution.py:22
  50.9 14.7 %collective-permute-start.9 = (bf16[16,16,256]{2,1,0:T(8,128)(2,1)S(1)}, bf16[16,16,256]{2,1,0:T(8,128)(2,1)S(1)}, u32[]{:S(2)}, u32[]{:S(2)}) collective-permute-start(bf16[16,16,256]{2,1,0:T(8,128)(2,1)S(1)} %get-tuple-element.89), channel_id=1, source_target_pairs={{0,64},{64,0},{1,65},{65,1},{2,66},{66,2},{3,67},{67,3},{4,68},{68... | collective-permute-start | bytes 393224 | tf_op jit(solution)/shard_map/ppermute | solution.py:24
  65.6 6.2 %collective-permute-start.13 = (bf16[16,16,256]{2,1,0:T(8,128)(2,1)S(1)}, bf16[16,16,256]{2,1,0:T(8,128)(2,1)S(1)}, u32[]{:S(2)}, u32[]{:S(2)}) collective-permute-start(bf16[16,16,256]{2,1,0:T(8,128)(2,1)S(1)} %get-tuple-element.101), channel_id=1, source_target_pairs={{0,96},{96,0},{32,64},{64,32},{1,97},{97,1},{33,65},{65,33},{2,98}... | collective-permute-start | bytes 393224 | tf_op jit(solution)/shard_map/ppermute | solution.py:25
  71.8 2.5 %collective-permute-start.14 = (bf16[96,16,256]{2,1,0:T(8,128)(2,1)S(1)}, bf16[96,16,256]{2,1,0:T(8,128)(2,1)S(1)}, u32[]{:S(2)}, u32[]{:S(2)}) collective-permute-start(bf16[96,16,256]{2,1,0:T(8,128)(2,1)S(1)} %get-tuple-element.102), channel_id=1, source_target_pairs={{0,1},{1,0},{2,3},{3,2},{4,5},{5,4},{6,7},{7,6},{8,9},{9,8},{10,11... | collective-permute-start | bytes 2359304 | tf_op jit(solution)/shard_map/ppermute | solution.py:182
  71.9 2.4 %collective-permute-start.15 = (bf16[16,16,256]{2,1,0:T(8,128)(2,1)S(1)}, bf16[16,16,256]{2,1,0:T(8,128)(2,1)S(1)}, u32[]{:S(2)}, u32[]{:S(2)}) collective-permute-start(bf16[16,16,256]{2,1,0:T(8,128)(2,1)S(1)} %get-tuple-element.107), channel_id=1, source_target_pairs={{0,1},{1,0},{2,3},{3,2},{4,5},{5,4},{6,7},{7,6},{8,9},{9,8},{10,11... | collective-permute-start | bytes 393224 | tf_op jit(solution)/shard_map/ppermute | solution.py:182

commit v8 on v6

--- a/solution.py
+++ b/solution.py
@@ -105,9 +105,10 @@
     halves = [held[g].astype(F32).reshape(2 * rows, cols, width) for g in range(2)]
     at = lax.broadcasted_iota(jnp.int32, (2 * rows, cols, width), 1)
     rest = cols - side
-    for across in (-1, 0, 1):
-        padded[:, pl.ds(0, lead), :] = zeros
-        padded[:, pl.ds(lead + tall, lead), :] = zeros
+    for across in (0, 1, -1):
+        turn = across + 1
+        padded[turn, :, pl.ds(0, lead), :] = zeros
+        padded[turn, :, pl.ds(lead + tall, lead), :] = zeros
         if across == 0:
             shifted = halves
         elif across == 1:
@@ -123,7 +124,7 @@
                 jnp.where(at < rest, rolled[1], 0.0),
             ]
         for g in range(2):
-            padded[g, pl.ds(lead, tall), :] = shifted[g].reshape(tall, width).astype(BF)
+            padded[turn, g, pl.ds(lead, tall), :] = shifted[g].reshape(tall, width).astype(BF)
         for above in (-1, 0, 1):
             first, last = {-1: (0, 32), 0: (0, 48), 1: (16, 48)}[above]
             base = first - side * above + side
@@ -131,7 +132,7 @@
             for g in range(2):
                 part = jnp.dot(
                     xt_ref[g, :, first * cols : last * cols],
-                    padded[g, base * cols : (base + last - first) * cols, :],
+                    padded[turn, g, base * cols : (base + last - first) * cols, :],
                     preferred_element_type=F32,
                 )
                 total = part if total is None else total + part
@@ -223,8 +224,8 @@
         [jax.ShapeDtypeStruct(shape, F32)] + [jax.ShapeDtypeStruct(shape, BF)] * 3,
         1,
         3,
-        kept.size,
-        8 * kept.size,
+        0,
+        0,
         10,
         [pltpu.VMEM((slices, 4, 16, width), F32)],
         name="rows",
@@ -257,7 +258,7 @@
         26,
         [
             pltpu.VMEM((2, 2 * pixels, width), BF),
-            pltpu.VMEM((2, 2 * pixels + 2 * RATE_C * SIDE, width), BF),
+            pltpu.VMEM((3, 2, 2 * pixels + 2 * RATE_C * SIDE, width), BF),
             pltpu.VMEM((slot_count, 16, width), F32),
         ],
         name="taps",
@@ -615,7 +616,6 @@
         name="pair",
     )(pos, joined, g_proj, centre, delta0)
     got = [swap_core(part) for part in sent]
-    got, shared = lax.optimization_barrier((got, shared))
     by_owner = split_pair(pos, kept, got)
     by_owner, shared = lax.optimization_barrier((by_owner, shared))
     by_owner = [by_owner[0]] + [flip(by_owner[k], k) for k in (1, 2, 3)]

time: 94.3 us -> 93.5 us (level)
  transfers between devices with their start and end apart: 16 -> 16, of which waited for: 11 -> 11; matrix products, arithmetic and copies ran while one was open for 0% -> 0% of each run, Pallas kernels for 23% -> 24%
where the time goes in v8:
time: 93.5 us; the launch traced here: 93.3 us
  Pallas kernels  28.8 us (31%)
  waiting for transfers between devices  23.2 us (25%)
  blocking collectives  22.3 us (24%)
  starting transfers between devices  18.7 us (20%)
    all_to_all x1, blocking collectives, reduce_slots(): total = lax.all_to_all(total, ('dp_0', 'dp_1'), 0, 0, tiled=True)  22.3 us
    ppermute x4, starting transfers between devices, flip(): return lax.ppermute(x, 'col', [(0, 1), (1, 0)])  9.83 us
    ppermute x4, waiting for transfers between devices, flip(): return lax.ppermute(x, ('row', 'col'), [(0, 3), (3, 0), (1, 2), (2, 1)])  9.72 us
    pallas_call x1, Pallas kernels, outer(): call(outer_parts, [jax.ShapeDtypeStruct(*s) for s in shapes], 1, 1, 2 * p...  8.68 us
    ppermute x4, waiting for transfers between devices, flip(): return lax.ppermute(x, 'col', [(0, 1), (1, 0)])  8.26 us
    pallas_call x1, Pallas kernels, inner(): call(inner_parts, [jax.ShapeDtypeStruct((pixels, width), F32), jax.ShapeD...  6.26 us
    ppermute x4, starting transfers between devices, flip(): return lax.ppermute(x, ('row', 'col'), [(0, 3), (3, 0), (1, 2), (2, 1)])  4.51 us
    pallas_call x1, Pallas kernels, tap_slots(): call(tap_grads, [jax.ShapeDtypeStruct((half, 16, width), F32), jax.ShapeD...  3.57 us
  transfers between devices with their start and end apart: 16, of which 11 were waited for; matrix products, arithmetic and copies ran while one was open for 0% of the time, Pallas kernels for 24%

profile of v8, /device:TPU:0, one launch (start us, length us, event | category | flops | bytes accessed | tf_op | source)
XLA Modules:
  0.0 93.3 jit_solution(3226864607379767650)
XLA Ops:
  0.1 2.6 %pick.1 = (bf16[576,256]{1,0:T(8,128)(2,1)S(1)}, bf16[576,256]{1,0:T(8,128)(2,1)S(1)}, bf16[576,256]{1,0:T(8,128)(2,1)S(1)}, bf16[576,256]{1,0:T(8,128)(2,1)S(1)}) custom-call(s32[6]{0:T(128)S(1)} %stack.27.pos_ref, bf16[576,1024]{1,0:T(8,128)(2,1)} %bitcast.8), custom_call_target="tpu_custom_call" | custom-call | flops 603979776 | bytes 2359296 | tf_op jit(solution)/shard_map/pick/pallas_call | solution.py:189
  2.6 3.2 %collective-permute-start.3 = (bf16[576,256]{1,0:T(8,128)(2,1)S(1)}, bf16[576,256]{1,0:T(8,128)(2,1)S(1)}, u32[]{:S(2)}, u32[]{:S(2)}) collective-permute-start(bf16[576,256]{1,0:T(8,128)(2,1)S(1)} %get-tuple-element.67), channel_id=1, source_target_pairs={{0,32},{32,0},{1,33},{33,1},{2,34},{34,2},{3,35},{35,3},{4,36},{36... | collective-permute-start | bytes 884744 | tf_op jit(solution)/shard_map/ppermute | solution.py:22
  5.8 0.6 collective-permute-start.4
  6.4 0.6 collective-permute-start.5
  7.0 8.7 %outer.1 = (f32[3,576,256]{2,1,0:T(8,128)S(1)}, bf16[864,256]{1,0:T(8,128)(2,1)S(1)}, bf16[864,256]{1,0:T(8,128)(2,1)S(1)}, bf16[576,256]{1,0:T(8,128)(2,1)S(1)}) custom-call(s32[6]{0:T(128)S(1)} %stack.27.pos_ref, bf16[576,1024]{1,0:T(8,128)(2,1)S(1)} %bitcast.9, bf16[3,3,1024,256]{3,2,1,0:T(8,128)(2,1)} %wc_ref.3, bf16[3,3,1024,256]{3,2,1,0:T(8,128)(2,1)} %wb_ref.3, ...), custom_call_target="tpu_custom_call" | custom-call | flops 4227858432 | bytes 10485760 | tf_op jit(solution)/shard_map/outer/pallas_call | solution.py:452
  15.7 1.5 %collective-permute-start = (bf16[864,256]{1,0:T(8,128)(2,1)S(1)}, bf16[864,256]{1,0:T(8,128)(2,1)S(1)}, u32[]{:S(2)}, u32[]{:S(2)}) collective-permute-start(bf16[864,256]{1,0:T(8,128)(2,1)S(1)} %get-tuple-element.62), channel_id=1, source_target_pairs={{0,64},{64,0},{1,65},{65,1},{2,66},{66,2},{3,67},{67,3},{4,68},{68... | collective-permute-start | bytes 1327112 | tf_op jit(solution)/shard_map/ppermute | solution.py:24
  17.2 2.7 %collective-permute-start.1 = (bf16[864,256]{1,0:T(8,128)(2,1)S(1)}, bf16[864,256]{1,0:T(8,128)(2,1)S(1)}, u32[]{:S(2)}, u32[]{:S(2)}) collective-permute-start(bf16[864,256]{1,0:T(8,128)(2,1)S(1)} %get-tuple-element.63), channel_id=1, source_target_pairs={{0,32},{32,0},{1,33},{33,1},{2,34},{34,2},{3,35},{35,3},{4,36},{36... | collective-permute-start | bytes 1327112 | tf_op jit(solution)/shard_map/ppermute | solution.py:22
  19.9 0.6 collective-permute-start.2
  20.7 1.2 %turn.1.xt_ref = bf16[2,256,1152]{2,1,0:T(8,128)(2,1)S(1)} custom-call(s32[6]{0:T(128)S(1)} %stack.27.pos_ref, bf16[576,256]{1,0:T(8,128)(2,1)S(1)} %get-tuple-element.73.x0, bf16[576,256]{1,0:T(8,128)(2,1)S(1)} %collective-permute-done.3.x1, bf16[576,256]{1,0:T(8,128)(2,1)S(1)} %collective-permute-done.4.x2, bf16[576,256]{1,0:T(8,128)(2,1)S(1)} %collective-permute-done.5.x3), custom_call_target="tpu_custom_call" | custom-call | flops 301989888 | bytes 2359296 | tf_op jit(solution)/shard_map/turn/pallas_call | solution.py:205
  21.9 6.3 %inner.1 = (f32[576,256]{1,0:T(8,128)S(1)}, f32[3,576,256]{2,1,0:T(8,128)S(1)}) custom-call(s32[6]{0:T(128)S(1)} %stack.27.pos_ref, bf16[576,1024]{1,0:T(8,128)(2,1)S(1)} %bitcast.10, f32[3,576,256]{2,1,0:T(8,128)S(1)} %get-tuple-element.70.part_ref, bf16[1024,256]{1,0:T(8,128)(2,1)S(1)} %copy-done.1, bf16[3,3,1024,256]{3,2,1,0:T(8,128)(2,1)} %wc_ref.3, ...), custom_call_target="tpu_custom_call" | custom-call | flops 3019898880 | bytes 10485760 | tf_op jit(solution)/shard_map/inner/pallas_call | solution.py:475
  28.1 1.9 %collective-permute-done.2.diag_ref = bf16[576,256]{1,0:T(8,128)(2,1)S(1)} collective-permute-done((bf16[576,256]{1,0:T(8,128)(2,1)S(1)}, bf16[576,256]{1,0:T(8,128)(2,1)S(1)}, u32[]{:S(2)}, u32[]{:S(2)}) %collective-permute-start.2) | collective-permute-done | bytes 294944 | tf_op jit(solution)/shard_map/ppermute | solution.py:25
  30.1 8.3 %collective-permute-done.1.col_ref = bf16[864,256]{1,0:T(8,128)(2,1)S(1)} collective-permute-done((bf16[864,256]{1,0:T(8,128)(2,1)S(1)}, bf16[864,256]{1,0:T(8,128)(2,1)S(1)}, u32[]{:S(2)}, u32[]{:S(2)}) %collective-permute-start.1) | collective-permute-done | bytes 442400 | tf_op jit(solution)/shard_map/ppermute | solution.py:22
  38.4 2.4 %merge.1 = (bf16[576,1024]{1,0:T(8,128)(2,1)S(1)}, bf16[576,256]{1,0:T(8,128)(2,1)S(1)}, bf16[576,256]{1,0:T(8,128)(2,1)S(1)}, bf16[576,256]{1,0:T(8,128)(2,1)S(1)}) custom-call(s32[6]{0:T(128)S(1)} %stack.27.pos_ref, f32[576,256]{1,0:T(8,128)S(1)} %get-tuple-element.77.pre0_ref, f32[3,576,256]{2,1,0:T(8,128)S(1)} %get-tuple-element.78.own_ref, ...), custom_call_target="tpu_custom_call" | custom-call | flops 452984832 | bytes 6291456 | tf_op jit(solution)/shard_map/merge/pallas_call | solution.py:555
  40.8 2.8 %collective-permute-start.10 = (bf16[576,256]{1,0:T(8,128)(2,1)S(1)}, bf16[576,256]{1,0:T(8,128)(2,1)S(1)}, u32[]{:S(2)}, u32[]{:S(2)}) collective-permute-start(bf16[576,256]{1,0:T(8,128)(2,1)S(1)} %get-tuple-element.93.d0), channel_id=1, source_target_pairs={{0,96},{96,0},{32,64},{64,32},{1,97},{97,1},{33,65},{65,33},{2,98}... | collective-permute-start | bytes 884744 | tf_op jit(solution)/shard_map/ppermute | solution.py:25
  43.6 0.8 collective-permute-start.8
  44.4 0.5 collective-permute-start.9
  45.0 1.6 %pair.1 = (f32[1024,256]{1,0:T(8,128)S(1)}, bf16[512,256]{1,0:T(8,128)(2,1)S(1)}, bf16[512,256]{1,0:T(8,128)(2,1)S(1)}) custom-call(s32[6]{0:T(128)S(1)} %stack.27.pos_ref, bf16[576,1024]{1,0:T(8,128)(2,1)S(1)} %get-tuple-element.82.joined_ref, bf16[576,256]{1,0:T(8,128)(2,1)S(1)} %get-tuple-element.83.g_ref, bf16[576,1024]{1,0:T(8,128)(2,1)S(1)} %bitcast.11, ...), custom_call_target="tpu_custom_call" | custom-call | flops 603979776 | bytes 4194304 | tf_op jit(solution)/shard_map/pair/pallas_call | solution.py:608
  47.2 1.0 %collective-permute-done.6.got0 = bf16[512,256]{1,0:T(8,128)(2,1)S(1)} collective-permute-done((bf16[512,256]{1,0:T(8,128)(2,1)S(1)}, bf16[512,256]{1,0:T(8,128)(2,1)S(1)}, u32[]{:S(2)}, u32[]{:S(2)}) %collective-permute-start.6) | collective-permute-done | bytes 262176 | tf_op jit(solution)/shard_map/ppermute | solution.py:183
  48.6 0.7 rows.1
  49.3 6.8 %collective-permute-done.10.d3 = bf16[576,256]{1,0:T(8,128)(2,1)S(1)} collective-permute-done((bf16[576,256]{1,0:T(8,128)(2,1)S(1)}, bf16[576,256]{1,0:T(8,128)(2,1)S(1)}, u32[]{:S(2)}, u32[]{:S(2)}) %collective-permute-start.10) | collective-permute-done | bytes 294944 | tf_op jit(solution)/shard_map/ppermute | solution.py:25
  56.1 0.7 collective-permute-done.9.d2
  56.8 3.1 %collective-permute-start.11 = (bf16[16,16,256]{2,1,0:T(8,128)(2,1)S(1)}, bf16[16,16,256]{2,1,0:T(8,128)(2,1)S(1)}, u32[]{:S(2)}, u32[]{:S(2)}) collective-permute-start(bf16[16,16,256]{2,1,0:T(8,128)(2,1)S(1)} %get-tuple-element.101), channel_id=1, source_target_pairs={{0,32},{32,0},{1,33},{33,1},{2,34},{34,2},{3,35},{35,3},{4,36},{36... | collective-permute-start | bytes 393224 | tf_op jit(solution)/shard_map/ppermute | solution.py:22
  59.9 0.6 collective-permute-start.12
  60.5 0.5 collective-permute-start.13
  61.1 3.6 %taps.1 = (f32[96,16,256]{2,1,0:T(8,128)S(1)}, bf16[96,16,256]{2,1,0:T(8,128)(2,1)S(1)}) custom-call(s32[6]{0:T(128)S(1)} %stack.27.pos_ref, s32[176]{0:T(256)S(1)} %fusion.1.place_ref, bf16[576,256]{1,0:T(8,128)(2,1)S(1)} %get-tuple-element.93.d0, bf16[576,256]{1,0:T(8,128)(2,1)S(1)} %collective-permute-done.8.d1, ...), custom_call_target="tpu_custom_call" | custom-call | flops 2113929216 | bytes 8388608 | tf_op jit(solution)/shard_map/taps/pallas_call | solution.py:251
  64.7 1.0 %collective-permute-done.12 = bf16[16,16,256]{2,1,0:T(8,128)(2,1)S(1)} collective-permute-done((bf16[16,16,256]{2,1,0:T(8,128)(2,1)S(1)}, bf16[16,16,256]{2,1,0:T(8,128)(2,1)S(1)}, u32[]{:S(2)}, u32[]{:S(2)}) %collective-permute-start.12) | collective-permute-done | bytes 131104 | tf_op jit(solution)/shard_map/ppermute | solution.py:24
  65.7 1.1 %collective-permute-done.13 = bf16[16,16,256]{2,1,0:T(8,128)(2,1)S(1)} collective-permute-done((bf16[16,16,256]{2,1,0:T(8,128)(2,1)S(1)}, bf16[16,16,256]{2,1,0:T(8,128)(2,1)S(1)}, u32[]{:S(2)}, u32[]{:S(2)}) %collective-permute-start.13) | collective-permute-done | bytes 131104 | tf_op jit(solution)/shard_map/ppermute | solution.py:25
  66.8 0.6 collective-permute-start.15
  67.4 1.8 %collective-permute-done.15.other_ref = bf16[16,16,256]{2,1,0:T(8,128)(2,1)S(1)} collective-permute-done((bf16[16,16,256]{2,1,0:T(8,128)(2,1)S(1)}, bf16[16,16,256]{2,1,0:T(8,128)(2,1)S(1)}, u32[]{:S(2)}, u32[]{:S(2)}) %collective-permute-start.15) | collective-permute-done | bytes 131104 | tf_op jit(solution)/shard_map/ppermute | solution.py:183
  69.2 1.1 %owners.1 = bf16[16,96,256]{2,1,0:T(8,128)(2,1)S(1)} custom-call(s32[6]{0:T(128)S(1)} %stack.27.pos_ref, s32[176]{0:T(256)S(1)} %fusion.1.place_ref, f32[96,16,256]{2,1,0:T(8,128)S(1)} %get-tuple-element.98.keep_ref, bf16[96,16,256]{2,1,0:T(8,128)(2,1)S(1)} %collective-permute-done.14.got_ref, f32[16,16,256]{2,1,0:T(8,128)S(1)} %get-tuple-element.110.mine_ref, ...), custom_call_target="tpu_custom_call" | custom-call | flops 393216 | bytes 3145728 | tf_op jit(solution)/shard_map/owners/pallas_call | solution.py:272
  70.3 22.3 %all_to_all.5.r_ref = bf16[16,96,256]{2,1,0:T(8,128)(2,1)S(1)} all-to-all(bf16[16,96,256]{2,1,0:T(8,128)(2,1)S(1)} %owners.1), channel_id=1, replica_groups=mesh['row'=2,'col'=2,'dp_0'=4,'dp_1'=4,'dp_2'=2] {'dp_0','dp_1'}, dimensions={0} | all-to-all | bytes 1572864 | tf_op jit(solution)/shard_map/all_to_all | solution.py:283
  92.5 0.8 last.1
  (24 shorter events, 1.5 us)
Async XLA Ops:
  0.0 7.0 %copy-start = (bf16[1,24,24,1024]{3,2,1,0:T(8,128)(2,1)S(1)}, bf16[1,24,24,1024]{3,2,1,0:T(8,128)(2,1)}, u32[]{:S(2)}) copy-start(bf16[1,24,24,1024]{3,2,1,0:T(8,128)(2,1)} %param.8) | copy-start | bytes 3538948
  2.6 17.2 %collective-permute-start.3 = (bf16[576,256]{1,0:T(8,128)(2,1)S(1)}, bf16[576,256]{1,0:T(8,128)(2,1)S(1)}, u32[]{:S(2)}, u32[]{:S(2)}) collective-permute-start(bf16[576,256]{1,0:T(8,128)(2,1)S(1)} %get-tuple-element.67), channel_id=1, source_target_pairs={{0,32},{32,0},{1,33},{33,1},{2,34},{34,2},{3,35},{35,3},{4,36},{36... | collective-permute-start | bytes 884744 | tf_op jit(solution)/shard_map/ppermute | solution.py:22
  5.8 14.8 %collective-permute-start.4 = (bf16[576,256]{1,0:T(8,128)(2,1)S(1)}, bf16[576,256]{1,0:T(8,128)(2,1)S(1)}, u32[]{:S(2)}, u32[]{:S(2)}) collective-permute-start(bf16[576,256]{1,0:T(8,128)(2,1)S(1)} %get-tuple-element.68), channel_id=1, source_target_pairs={{0,64},{64,0},{1,65},{65,1},{2,66},{66,2},{3,67},{67,3},{4,68},{68... | collective-permute-start | bytes 884744 | tf_op jit(solution)/shard_map/ppermute | solution.py:24
  6.4 14.2 %collective-permute-start.5 = (bf16[576,256]{1,0:T(8,128)(2,1)S(1)}, bf16[576,256]{1,0:T(8,128)(2,1)S(1)}, u32[]{:S(2)}, u32[]{:S(2)}) collective-permute-start(bf16[576,256]{1,0:T(8,128)(2,1)S(1)} %get-tuple-element.69), channel_id=1, source_target_pairs={{0,96},{96,0},{32,64},{64,32},{1,97},{97,1},{33,65},{65,33},{2,98}... | collective-permute-start | bytes 884744 | tf_op jit(solution)/shard_map/ppermute | solution.py:25
  15.7 6.2 %copy-start.1 = (bf16[1024,256]{1,0:T(8,128)(2,1)S(1)}, bf16[1024,256]{1,0:T(8,128)(2,1)}, u32[]{:S(2)}) copy-start(bf16[1024,256]{1,0:T(8,128)(2,1)} %wp_ref.2) | copy-start | bytes 1572868
  15.7 14.5 %collective-permute-start = (bf16[864,256]{1,0:T(8,128)(2,1)S(1)}, bf16[864,256]{1,0:T(8,128)(2,1)S(1)}, u32[]{:S(2)}, u32[]{:S(2)}) collective-permute-start(bf16[864,256]{1,0:T(8,128)(2,1)S(1)} %get-tuple-element.62), channel_id=1, source_target_pairs={{0,64},{64,0},{1,65},{65,1},{2,66},{66,2},{3,67},{67,3},{4,68},{68... | collective-permute-start | bytes 1327112 | tf_op jit(solution)/shard_map/ppermute | solution.py:24
  17.2 21.2 %collective-permute-start.1 = (bf16[864,256]{1,0:T(8,128)(2,1)S(1)}, bf16[864,256]{1,0:T(8,128)(2,1)S(1)}, u32[]{:S(2)}, u32[]{:S(2)}) collective-permute-start(bf16[864,256]{1,0:T(8,128)(2,1)S(1)} %get-tuple-element.63), channel_id=1, source_target_pairs={{0,32},{32,0},{1,33},{33,1},{2,34},{34,2},{3,35},{35,3},{4,36},{36... | collective-permute-start | bytes 1327112 | tf_op jit(solution)/shard_map/ppermute | solution.py:22
  19.9 10.1 %collective-permute-start.2 = (bf16[576,256]{1,0:T(8,128)(2,1)S(1)}, bf16[576,256]{1,0:T(8,128)(2,1)S(1)}, u32[]{:S(2)}, u32[]{:S(2)}) collective-permute-start(bf16[576,256]{1,0:T(8,128)(2,1)S(1)} %get-tuple-element.64), channel_id=1, source_target_pairs={{0,96},{96,0},{32,64},{64,32},{1,97},{97,1},{33,65},{65,33},{2,98}... | collective-permute-start | bytes 884744 | tf_op jit(solution)/shard_map/ppermute | solution.py:25
  21.8 16.6 %copy-start.2 = (bf16[1024,256]{1,0:T(8,128)(2,1)S(1)}, bf16[1024,256]{1,0:T(8,128)(2,1)}, u32[]{:S(2)}) copy-start(bf16[1024,256]{1,0:T(8,128)(2,1)} %wp_ref.3) | copy-start | bytes 1572868
  21.9 16.5 %copy-start.3 = (bf16[1,24,24,256]{3,2,1,0:T(8,128)(2,1)S(1)}, bf16[1,24,24,256]{3,2,1,0:T(8,128)(2,1)}, u32[]{:S(2)}) copy-start(bf16[1,24,24,256]{3,2,1,0:T(8,128)(2,1)} %param.9) | copy-start | bytes 884740
  40.8 6.4 %copy-start.4 = (s32[176]{0:T(256)S(1)}, s32[176]{0:T(256)}, u32[]{:S(2)}) copy-start(s32[176]{0:T(256)} %param.15) | copy-start | bytes 2116
  40.8 15.3 %collective-permute-start.10 = (bf16[576,256]{1,0:T(8,128)(2,1)S(1)}, bf16[576,256]{1,0:T(8,128)(2,1)S(1)}, u32[]{:S(2)}, u32[]{:S(2)}) collective-permute-start(bf16[576,256]{1,0:T(8,128)(2,1)S(1)} %get-tuple-element.93.d0), channel_id=1, source_target_pairs={{0,96},{96,0},{32,64},{64,32},{1,97},{97,1},{33,65},{65,33},{2,98}... | collective-permute-start | bytes 884744 | tf_op jit(solution)/shard_map/ppermute | solution.py:25
  43.6 12.5 %collective-permute-start.8 = (bf16[576,256]{1,0:T(8,128)(2,1)S(1)}, bf16[576,256]{1,0:T(8,128)(2,1)S(1)}, u32[]{:S(2)}, u32[]{:S(2)}) collective-permute-start(bf16[576,256]{1,0:T(8,128)(2,1)S(1)} %get-tuple-element.93.d0), channel_id=1, source_target_pairs={{0,32},{32,0},{1,33},{33,1},{2,34},{34,2},{3,35},{35,3},{4,36},{36... | collective-permute-start | bytes 884744 | tf_op jit(solution)/shard_map/ppermute | solution.py:22
  44.4 12.4 %collective-permute-start.9 = (bf16[576,256]{1,0:T(8,128)(2,1)S(1)}, bf16[576,256]{1,0:T(8,128)(2,1)S(1)}, u32[]{:S(2)}, u32[]{:S(2)}) collective-permute-start(bf16[576,256]{1,0:T(8,128)(2,1)S(1)} %get-tuple-element.93.d0), channel_id=1, source_target_pairs={{0,64},{64,0},{1,65},{65,1},{2,66},{66,2},{3,67},{67,3},{4,68},{68... | collective-permute-start | bytes 884744 | tf_op jit(solution)/shard_map/ppermute | solution.py:24
  46.6 1.6 %collective-permute-start.6 = (bf16[512,256]{1,0:T(8,128)(2,1)S(1)}, bf16[512,256]{1,0:T(8,128)(2,1)S(1)}, u32[]{:S(2)}, u32[]{:S(2)}) collective-permute-start(bf16[512,256]{1,0:T(8,128)(2,1)S(1)} %get-tuple-element.86), channel_id=1, source_target_pairs={{0,1},{1,0},{2,3},{3,2},{4,5},{5,4},{6,7},{7,6},{8,9},{9,8},{10,11... | collective-permute-start | bytes 786440 | tf_op jit(solution)/shard_map/ppermute | solution.py:183
  46.7 1.9 %collective-permute-start.7 = (bf16[512,256]{1,0:T(8,128)(2,1)S(1)}, bf16[512,256]{1,0:T(8,128)(2,1)S(1)}, u32[]{:S(2)}, u32[]{:S(2)}) collective-permute-start(bf16[512,256]{1,0:T(8,128)(2,1)S(1)} %get-tuple-element.87), channel_id=1, source_target_pairs={{0,1},{1,0},{2,3},{3,2},{4,5},{5,4},{6,7},{7,6},{8,9},{9,8},{10,11... | collective-permute-start | bytes 786440 | tf_op jit(solution)/shard_map/ppermute | solution.py:183
  56.8 7.8 %collective-permute-start.11 = (bf16[16,16,256]{2,1,0:T(8,128)(2,1)S(1)}, bf16[16,16,256]{2,1,0:T(8,128)(2,1)S(1)}, u32[]{:S(2)}, u32[]{:S(2)}) collective-permute-start(bf16[16,16,256]{2,1,0:T(8,128)(2,1)S(1)} %get-tuple-element.101), channel_id=1, source_target_pairs={{0,32},{32,0},{1,33},{33,1},{2,34},{34,2},{3,35},{35,3},{4,36},{36... | collective-permute-start | bytes 393224 | tf_op jit(solution)/shard_map/ppermute | solution.py:22
  59.9 5.7 %collective-permute-start.12 = (bf16[16,16,256]{2,1,0:T(8,128)(2,1)S(1)}, bf16[16,16,256]{2,1,0:T(8,128)(2,1)S(1)}, u32[]{:S(2)}, u32[]{:S(2)}) collective-permute-start(bf16[16,16,256]{2,1,0:T(8,128)(2,1)S(1)} %get-tuple-element.102), channel_id=1, source_target_pairs={{0,64},{64,0},{1,65},{65,1},{2,66},{66,2},{3,67},{67,3},{4,68},{68... | collective-permute-start | bytes 393224 | tf_op jit(solution)/shard_map/ppermute | solution.py:24
  60.5 6.2 %collective-permute-start.13 = (bf16[16,16,256]{2,1,0:T(8,128)(2,1)S(1)}, bf16[16,16,256]{2,1,0:T(8,128)(2,1)S(1)}, u32[]{:S(2)}, u32[]{:S(2)}) collective-permute-start(bf16[16,16,256]{2,1,0:T(8,128)(2,1)S(1)} %get-tuple-element.103), channel_id=1, source_target_pairs={{0,96},{96,0},{32,64},{64,32},{1,97},{97,1},{33,65},{65,33},{2,98}... | collective-permute-start | bytes 393224 | tf_op jit(solution)/shard_map/ppermute | solution.py:25
  66.7 2.5 %collective-permute-start.14 = (bf16[96,16,256]{2,1,0:T(8,128)(2,1)S(1)}, bf16[96,16,256]{2,1,0:T(8,128)(2,1)S(1)}, u32[]{:S(2)}, u32[]{:S(2)}) collective-permute-start(bf16[96,16,256]{2,1,0:T(8,128)(2,1)S(1)} %get-tuple-element.104), channel_id=1, source_target_pairs={{0,1},{1,0},{2,3},{3,2},{4,5},{5,4},{6,7},{7,6},{8,9},{9,8},{10,11... | collective-permute-start | bytes 2359304 | tf_op jit(solution)/shard_map/ppermute | solution.py:183
  66.8 2.4 %collective-permute-start.15 = (bf16[16,16,256]{2,1,0:T(8,128)(2,1)S(1)}, bf16[16,16,256]{2,1,0:T(8,128)(2,1)S(1)}, u32[]{:S(2)}, u32[]{:S(2)}) collective-permute-start(bf16[16,16,256]{2,1,0:T(8,128)(2,1)S(1)} %get-tuple-element.109), channel_id=1, source_target_pairs={{0,1},{1,0},{2,3},{3,2},{4,5},{5,4},{6,7},{7,6},{8,9},{9,8},{10,11... | collective-permute-start | bytes 393224 | tf_op jit(solution)/shard_map/ppermute | solution.py:183

commit v9 on v8

--- a/solution.py
+++ b/solution.py
@@ -617,8 +617,9 @@
     )(pos, joined, g_proj, centre, delta0)
     got = [swap_core(part) for part in sent]
     by_owner = split_pair(pos, kept, got)
-    by_owner, shared = lax.optimization_barrier((by_owner, shared))
-    by_owner = [by_owner[0]] + [flip(by_owner[k], k) for k in (1, 2, 3)]
+    across = flip(by_owner[1], 1)
+    late, shared = lax.optimization_barrier((by_owner[2:], shared))
+    by_owner = [by_owner[0], across, flip(late[0], 2), flip(late[1], 3)]
     kept, sent = tap_slots(pos, place, shared, turned, slot_count)
     sent, by_owner = lax.optimization_barrier((sent, by_owner))
     mine, other = sum_pair(by_owner)

time: 93.5 us -> 93.7 us (level)
  starting transfers between devices: 18.7 us -> 21.2 us
  waiting for transfers between devices: 23.2 us -> 20.8 us
    ppermute x4, waiting for transfers between devices: 9.72 us -> 7.63 us  [flip(): return lax.ppermute(x, ('row', 'col'), [(0, 3), (3, 0), (1, 2), (2, 1)])]
    ppermute x4, starting transfers between devices: 3.21 us -> 5.08 us  [flip(): return lax.ppermute(x, 'row', [(0, 1), (1, 0)])]
  transfers between devices with their start and end apart: 16 -> 16, of which waited for: 11 -> 10; matrix products, arithmetic and copies ran while one was open for 0% -> 0% of each run, Pallas kernels for 24% -> 24%
where the time goes in v9:
time: 93.7 us; the launch traced here: 93.5 us
  Pallas kernels  28.8 us (31%)
  blocking collectives  22.3 us (24%)
  starting transfers between devices  21.2 us (23%)
  waiting for transfers between devices  20.8 us (22%)
    all_to_all x1, blocking collectives, reduce_slots(): total = lax.all_to_all(total, ('dp_0', 'dp_1'), 0, 0, tiled=True)  22.3 us
    ppermute x4, starting transfers between devices, flip(): return lax.ppermute(x, 'col', [(0, 1), (1, 0)])  9.81 us
    pallas_call x1, Pallas kernels, outer(): call(outer_parts, [jax.ShapeDtypeStruct(*s) for s in shapes], 1, 1, 2 * p...  8.68 us
    ppermute x4, waiting for transfers between devices, flip(): return lax.ppermute(x, 'col', [(0, 1), (1, 0)])  8.26 us
    ppermute x4, waiting for transfers between devices, flip(): return lax.ppermute(x, ('row', 'col'), [(0, 3), (3, 0), (1, 2), (2, 1)])  7.63 us
    pallas_call x1, Pallas kernels, inner(): call(inner_parts, [jax.ShapeDtypeStruct((pixels, width), F32), jax.ShapeD...  6.26 us
    ppermute x4, starting transfers between devices, flip(): return lax.ppermute(x, ('row', 'col'), [(0, 3), (3, 0), (1, 2), (2, 1)])  5.18 us
    ppermute x4, starting transfers between devices, flip(): return lax.ppermute(x, 'row', [(0, 1), (1, 0)])  5.08 us
  transfers between devices with their start and end apart: 16, of which 10 were waited for; matrix products, arithmetic and copies ran while one was open for 0% of the time, Pallas kernels for 24%

profile of v9, /device:TPU:0, one launch (start us, length us, event | category | flops | bytes accessed | tf_op | source)
XLA Modules:
  0.0 93.5 jit_solution(16647594455465748348)
XLA Ops:
  0.1 2.6 %pick.1 = (bf16[576,256]{1,0:T(8,128)(2,1)S(1)}, bf16[576,256]{1,0:T(8,128)(2,1)S(1)}, bf16[576,256]{1,0:T(8,128)(2,1)S(1)}, bf16[576,256]{1,0:T(8,128)(2,1)S(1)}) custom-call(s32[6]{0:T(128)S(1)} %stack.27.pos_ref, bf16[576,1024]{1,0:T(8,128)(2,1)} %bitcast.8), custom_call_target="tpu_custom_call" | custom-call | flops 603979776 | bytes 2359296 | tf_op jit(solution)/shard_map/pick/pallas_call | solution.py:189
  2.6 3.2 %collective-permute-start.3 = (bf16[576,256]{1,0:T(8,128)(2,1)S(1)}, bf16[576,256]{1,0:T(8,128)(2,1)S(1)}, u32[]{:S(2)}, u32[]{:S(2)}) collective-permute-start(bf16[576,256]{1,0:T(8,128)(2,1)S(1)} %get-tuple-element.65), channel_id=1, source_target_pairs={{0,32},{32,0},{1,33},{33,1},{2,34},{34,2},{3,35},{35,3},{4,36},{36... | collective-permute-start | bytes 884744 | tf_op jit(solution)/shard_map/ppermute | solution.py:22
  5.8 0.6 collective-permute-start.4
  6.4 0.6 collective-permute-start.5
  7.0 8.7 %outer.1 = (f32[3,576,256]{2,1,0:T(8,128)S(1)}, bf16[864,256]{1,0:T(8,128)(2,1)S(1)}, bf16[864,256]{1,0:T(8,128)(2,1)S(1)}, bf16[576,256]{1,0:T(8,128)(2,1)S(1)}) custom-call(s32[6]{0:T(128)S(1)} %stack.27.pos_ref, bf16[576,1024]{1,0:T(8,128)(2,1)S(1)} %bitcast.9, bf16[3,3,1024,256]{3,2,1,0:T(8,128)(2,1)} %wc_ref.3, bf16[3,3,1024,256]{3,2,1,0:T(8,128)(2,1)} %wb_ref.3, ...), custom_call_target="tpu_custom_call" | custom-call | flops 4227858432 | bytes 10485760 | tf_op jit(solution)/shard_map/outer/pallas_call | solution.py:452
  15.7 1.5 %collective-permute-start = (bf16[864,256]{1,0:T(8,128)(2,1)S(1)}, bf16[864,256]{1,0:T(8,128)(2,1)S(1)}, u32[]{:S(2)}, u32[]{:S(2)}) collective-permute-start(bf16[864,256]{1,0:T(8,128)(2,1)S(1)} %get-tuple-element.60), channel_id=1, source_target_pairs={{0,64},{64,0},{1,65},{65,1},{2,66},{66,2},{3,67},{67,3},{4,68},{68... | collective-permute-start | bytes 1327112 | tf_op jit(solution)/shard_map/ppermute | solution.py:24
  17.2 2.7 %collective-permute-start.1 = (bf16[864,256]{1,0:T(8,128)(2,1)S(1)}, bf16[864,256]{1,0:T(8,128)(2,1)S(1)}, u32[]{:S(2)}, u32[]{:S(2)}) collective-permute-start(bf16[864,256]{1,0:T(8,128)(2,1)S(1)} %get-tuple-element.61), channel_id=1, source_target_pairs={{0,32},{32,0},{1,33},{33,1},{2,34},{34,2},{3,35},{35,3},{4,36},{36... | collective-permute-start | bytes 1327112 | tf_op jit(solution)/shard_map/ppermute | solution.py:22
  19.9 0.6 collective-permute-start.2
  20.7 1.2 %turn.1.xt_ref = bf16[2,256,1152]{2,1,0:T(8,128)(2,1)S(1)} custom-call(s32[6]{0:T(128)S(1)} %stack.27.pos_ref, bf16[576,256]{1,0:T(8,128)(2,1)S(1)} %get-tuple-element.71.x0, bf16[576,256]{1,0:T(8,128)(2,1)S(1)} %collective-permute-done.3.x1, bf16[576,256]{1,0:T(8,128)(2,1)S(1)} %collective-permute-done.4.x2, bf16[576,256]{1,0:T(8,128)(2,1)S(1)} %collective-permute-done.5.x3), custom_call_target="tpu_custom_call" | custom-call | flops 301989888 | bytes 2359296 | tf_op jit(solution)/shard_map/turn/pallas_call | solution.py:205
  21.9 6.3 %inner.1 = (f32[576,256]{1,0:T(8,128)S(1)}, f32[3,576,256]{2,1,0:T(8,128)S(1)}) custom-call(s32[6]{0:T(128)S(1)} %stack.27.pos_ref, bf16[576,1024]{1,0:T(8,128)(2,1)S(1)} %bitcast.10, f32[3,576,256]{2,1,0:T(8,128)S(1)} %get-tuple-element.68.part_ref, bf16[1024,256]{1,0:T(8,128)(2,1)S(1)} %copy-done.1, bf16[3,3,1024,256]{3,2,1,0:T(8,128)(2,1)} %wc_ref.3, ...), custom_call_target="tpu_custom_call" | custom-call | flops 3019898880 | bytes 10485760 | tf_op jit(solution)/shard_map/inner/pallas_call | solution.py:475
  28.1 1.9 %collective-permute-done.2.diag_ref = bf16[576,256]{1,0:T(8,128)(2,1)S(1)} collective-permute-done((bf16[576,256]{1,0:T(8,128)(2,1)S(1)}, bf16[576,256]{1,0:T(8,128)(2,1)S(1)}, u32[]{:S(2)}, u32[]{:S(2)}) %collective-permute-start.2) | collective-permute-done | bytes 294944 | tf_op jit(solution)/shard_map/ppermute | solution.py:25
  30.1 8.3 %collective-permute-done.1.col_ref = bf16[864,256]{1,0:T(8,128)(2,1)S(1)} collective-permute-done((bf16[864,256]{1,0:T(8,128)(2,1)S(1)}, bf16[864,256]{1,0:T(8,128)(2,1)S(1)}, u32[]{:S(2)}, u32[]{:S(2)}) %collective-permute-start.1) | collective-permute-done | bytes 442400 | tf_op jit(solution)/shard_map/ppermute | solution.py:22
  38.4 2.4 %merge.1 = (bf16[576,1024]{1,0:T(8,128)(2,1)S(1)}, bf16[576,256]{1,0:T(8,128)(2,1)S(1)}, bf16[576,256]{1,0:T(8,128)(2,1)S(1)}, bf16[576,256]{1,0:T(8,128)(2,1)S(1)}) custom-call(s32[6]{0:T(128)S(1)} %stack.27.pos_ref, f32[576,256]{1,0:T(8,128)S(1)} %get-tuple-element.75.pre0_ref, f32[3,576,256]{2,1,0:T(8,128)S(1)} %get-tuple-element.76.own_ref, ...), custom_call_target="tpu_custom_call" | custom-call | flops 452984832 | bytes 6291456 | tf_op jit(solution)/shard_map/merge/pallas_call | solution.py:555
  40.8 2.8 %collective-permute-start.10 = (bf16[576,256]{1,0:T(8,128)(2,1)S(1)}, bf16[576,256]{1,0:T(8,128)(2,1)S(1)}, u32[]{:S(2)}, u32[]{:S(2)}) collective-permute-start(bf16[576,256]{1,0:T(8,128)(2,1)S(1)} %get-tuple-element.89.d0), channel_id=1, source_target_pairs={{0,96},{96,0},{32,64},{64,32},{1,97},{97,1},{33,65},{65,33},{2,98}... | collective-permute-start | bytes 884744 | tf_op jit(solution)/shard_map/ppermute | solution.py:25
  43.6 0.8 collective-permute-start.8
  44.4 0.5 collective-permute-start.9
  45.0 1.6 %pair.1 = (f32[1024,256]{1,0:T(8,128)S(1)}, bf16[512,256]{1,0:T(8,128)(2,1)S(1)}, bf16[512,256]{1,0:T(8,128)(2,1)S(1)}) custom-call(s32[6]{0:T(128)S(1)} %stack.27.pos_ref, bf16[576,1024]{1,0:T(8,128)(2,1)S(1)} %get-tuple-element.80.joined_ref, bf16[576,256]{1,0:T(8,128)(2,1)S(1)} %get-tuple-element.81.g_ref, bf16[576,1024]{1,0:T(8,128)(2,1)S(1)} %bitcast.11, ...), custom_call_target="tpu_custom_call" | custom-call | flops 603979776 | bytes 4194304 | tf_op jit(solution)/shard_map/pair/pallas_call | solution.py:608
  46.7 0.5 collective-permute-start.7
  47.2 1.0 %collective-permute-done.6.got0 = bf16[512,256]{1,0:T(8,128)(2,1)S(1)} collective-permute-done((bf16[512,256]{1,0:T(8,128)(2,1)S(1)}, bf16[512,256]{1,0:T(8,128)(2,1)S(1)}, u32[]{:S(2)}, u32[]{:S(2)}) %collective-permute-start.6) | collective-permute-done | bytes 262176 | tf_op jit(solution)/shard_map/ppermute | solution.py:183
  48.6 0.7 rows.1
  49.3 3.1 %collective-permute-start.11 = (bf16[16,16,256]{2,1,0:T(8,128)(2,1)S(1)}, bf16[16,16,256]{2,1,0:T(8,128)(2,1)S(1)}, u32[]{:S(2)}, u32[]{:S(2)}) collective-permute-start(bf16[16,16,256]{2,1,0:T(8,128)(2,1)S(1)} %get-tuple-element.97), channel_id=1, source_target_pairs={{0,32},{32,0},{1,33},{33,1},{2,34},{34,2},{3,35},{35,3},{4,36},{36... | collective-permute-start | bytes 393224 | tf_op jit(solution)/shard_map/ppermute | solution.py:22
  52.4 4.4 %collective-permute-done.10.d3 = bf16[576,256]{1,0:T(8,128)(2,1)S(1)} collective-permute-done((bf16[576,256]{1,0:T(8,128)(2,1)S(1)}, bf16[576,256]{1,0:T(8,128)(2,1)S(1)}, u32[]{:S(2)}, u32[]{:S(2)}) %collective-permute-start.10) | collective-permute-done | bytes 294944 | tf_op jit(solution)/shard_map/ppermute | solution.py:25
  56.8 1.4 %collective-permute-done.9.d2 = bf16[576,256]{1,0:T(8,128)(2,1)S(1)} collective-permute-done((bf16[576,256]{1,0:T(8,128)(2,1)S(1)}, bf16[576,256]{1,0:T(8,128)(2,1)S(1)}, u32[]{:S(2)}, u32[]{:S(2)}) %collective-permute-start.9) | collective-permute-done | bytes 294944 | tf_op jit(solution)/shard_map/ppermute | solution.py:24
  58.2 2.5 %collective-permute-start.12 = (bf16[16,16,256]{2,1,0:T(8,128)(2,1)S(1)}, bf16[16,16,256]{2,1,0:T(8,128)(2,1)S(1)}, u32[]{:S(2)}, u32[]{:S(2)}) collective-permute-start(bf16[16,16,256]{2,1,0:T(8,128)(2,1)S(1)} %get-tuple-element.98), channel_id=1, source_target_pairs={{0,64},{64,0},{1,65},{65,1},{2,66},{66,2},{3,67},{67,3},{4,68},{68... | collective-permute-start | bytes 393224 | tf_op jit(solution)/shard_map/ppermute | solution.py:24
  60.7 1.2 %collective-permute-start.13 = (bf16[16,16,256]{2,1,0:T(8,128)(2,1)S(1)}, bf16[16,16,256]{2,1,0:T(8,128)(2,1)S(1)}, u32[]{:S(2)}, u32[]{:S(2)}) collective-permute-start(bf16[16,16,256]{2,1,0:T(8,128)(2,1)S(1)} %get-tuple-element.99), channel_id=1, source_target_pairs={{0,96},{96,0},{32,64},{64,32},{1,97},{97,1},{33,65},{65,33},{2,98}... | collective-permute-start | bytes 393224 | tf_op jit(solution)/shard_map/ppermute | solution.py:25
  61.9 3.6 %taps.1 = (f32[96,16,256]{2,1,0:T(8,128)S(1)}, bf16[96,16,256]{2,1,0:T(8,128)(2,1)S(1)}) custom-call(s32[6]{0:T(128)S(1)} %stack.27.pos_ref, s32[176]{0:T(256)S(1)} %fusion.1.place_ref, bf16[576,256]{1,0:T(8,128)(2,1)S(1)} %get-tuple-element.89.d0, bf16[576,256]{1,0:T(8,128)(2,1)S(1)} %collective-permute-done.8.d1, ...), custom_call_target="tpu_custom_call" | custom-call | flops 2113929216 | bytes 8388608 | tf_op jit(solution)/shard_map/taps/pallas_call | solution.py:251
  65.5 1.4 %collective-permute-done.13 = bf16[16,16,256]{2,1,0:T(8,128)(2,1)S(1)} collective-permute-done((bf16[16,16,256]{2,1,0:T(8,128)(2,1)S(1)}, bf16[16,16,256]{2,1,0:T(8,128)(2,1)S(1)}, u32[]{:S(2)}, u32[]{:S(2)}) %collective-permute-start.13) | collective-permute-done | bytes 131104 | tf_op jit(solution)/shard_map/ppermute | solution.py:25
  67.0 0.6 collective-permute-start.15
  67.5 1.8 %collective-permute-done.15.other_ref = bf16[16,16,256]{2,1,0:T(8,128)(2,1)S(1)} collective-permute-done((bf16[16,16,256]{2,1,0:T(8,128)(2,1)S(1)}, bf16[16,16,256]{2,1,0:T(8,128)(2,1)S(1)}, u32[]{:S(2)}, u32[]{:S(2)}) %collective-permute-start.15) | collective-permute-done | bytes 131104 | tf_op jit(solution)/shard_map/ppermute | solution.py:183
  69.4 1.1 %owners.1 = bf16[16,96,256]{2,1,0:T(8,128)(2,1)S(1)} custom-call(s32[6]{0:T(128)S(1)} %stack.27.pos_ref, s32[176]{0:T(256)S(1)} %fusion.1.place_ref, f32[96,16,256]{2,1,0:T(8,128)S(1)} %get-tuple-element.94.keep_ref, bf16[96,16,256]{2,1,0:T(8,128)(2,1)S(1)} %collective-permute-done.14.got_ref, f32[16,16,256]{2,1,0:T(8,128)S(1)} %get-tuple-element.106.mine_ref, ...), custom_call_target="tpu_custom_call" | custom-call | flops 393216 | bytes 3145728 | tf_op jit(solution)/shard_map/owners/pallas_call | solution.py:272
  70.4 22.3 %all_to_all.5.r_ref = bf16[16,96,256]{2,1,0:T(8,128)(2,1)S(1)} all-to-all(bf16[16,96,256]{2,1,0:T(8,128)(2,1)S(1)} %owners.1), channel_id=1, replica_groups=mesh['row'=2,'col'=2,'dp_0'=4,'dp_1'=4,'dp_2'=2] {'dp_0','dp_1'}, dimensions={0} | all-to-all | bytes 1572864 | tf_op jit(solution)/shard_map/all_to_all | solution.py:283
  92.7 0.8 last.1
  (24 shorter events, 1.0 us)
Async XLA Ops:
  0.0 7.0 %copy-start = (bf16[1,24,24,1024]{3,2,1,0:T(8,128)(2,1)S(1)}, bf16[1,24,24,1024]{3,2,1,0:T(8,128)(2,1)}, u32[]{:S(2)}) copy-start(bf16[1,24,24,1024]{3,2,1,0:T(8,128)(2,1)} %param.8) | copy-start | bytes 3538948
  2.6 17.2 %collective-permute-start.3 = (bf16[576,256]{1,0:T(8,128)(2,1)S(1)}, bf16[576,256]{1,0:T(8,128)(2,1)S(1)}, u32[]{:S(2)}, u32[]{:S(2)}) collective-permute-start(bf16[576,256]{1,0:T(8,128)(2,1)S(1)} %get-tuple-element.65), channel_id=1, source_target_pairs={{0,32},{32,0},{1,33},{33,1},{2,34},{34,2},{3,35},{35,3},{4,36},{36... | collective-permute-start | bytes 884744 | tf_op jit(solution)/shard_map/ppermute | solution.py:22
  5.8 14.8 %collective-permute-start.4 = (bf16[576,256]{1,0:T(8,128)(2,1)S(1)}, bf16[576,256]{1,0:T(8,128)(2,1)S(1)}, u32[]{:S(2)}, u32[]{:S(2)}) collective-permute-start(bf16[576,256]{1,0:T(8,128)(2,1)S(1)} %get-tuple-element.66), channel_id=1, source_target_pairs={{0,64},{64,0},{1,65},{65,1},{2,66},{66,2},{3,67},{67,3},{4,68},{68... | collective-permute-start | bytes 884744 | tf_op jit(solution)/shard_map/ppermute | solution.py:24
  6.4 14.2 %collective-permute-start.5 = (bf16[576,256]{1,0:T(8,128)(2,1)S(1)}, bf16[576,256]{1,0:T(8,128)(2,1)S(1)}, u32[]{:S(2)}, u32[]{:S(2)}) collective-permute-start(bf16[576,256]{1,0:T(8,128)(2,1)S(1)} %get-tuple-element.67), channel_id=1, source_target_pairs={{0,96},{96,0},{32,64},{64,32},{1,97},{97,1},{33,65},{65,33},{2,98}... | collective-permute-start | bytes 884744 | tf_op jit(solution)/shard_map/ppermute | solution.py:25
  15.7 6.2 %copy-start.1 = (bf16[1024,256]{1,0:T(8,128)(2,1)S(1)}, bf16[1024,256]{1,0:T(8,128)(2,1)}, u32[]{:S(2)}) copy-start(bf16[1024,256]{1,0:T(8,128)(2,1)} %wp_ref.2) | copy-start | bytes 1572868
  15.7 14.5 %collective-permute-start = (bf16[864,256]{1,0:T(8,128)(2,1)S(1)}, bf16[864,256]{1,0:T(8,128)(2,1)S(1)}, u32[]{:S(2)}, u32[]{:S(2)}) collective-permute-start(bf16[864,256]{1,0:T(8,128)(2,1)S(1)} %get-tuple-element.60), channel_id=1, source_target_pairs={{0,64},{64,0},{1,65},{65,1},{2,66},{66,2},{3,67},{67,3},{4,68},{68... | collective-permute-start | bytes 1327112 | tf_op jit(solution)/shard_map/ppermute | solution.py:24
  17.2 21.2 %collective-permute-start.1 = (bf16[864,256]{1,0:T(8,128)(2,1)S(1)}, bf16[864,256]{1,0:T(8,128)(2,1)S(1)}, u32[]{:S(2)}, u32[]{:S(2)}) collective-permute-start(bf16[864,256]{1,0:T(8,128)(2,1)S(1)} %get-tuple-element.61), channel_id=1, source_target_pairs={{0,32},{32,0},{1,33},{33,1},{2,34},{34,2},{3,35},{35,3},{4,36},{36... | collective-permute-start | bytes 1327112 | tf_op jit(solution)/shard_map/ppermute | solution.py:22
  19.9 10.1 %collective-permute-start.2 = (bf16[576,256]{1,0:T(8,128)(2,1)S(1)}, bf16[576,256]{1,0:T(8,128)(2,1)S(1)}, u32[]{:S(2)}, u32[]{:S(2)}) collective-permute-start(bf16[576,256]{1,0:T(8,128)(2,1)S(1)} %get-tuple-element.62), channel_id=1, source_target_pairs={{0,96},{96,0},{32,64},{64,32},{1,97},{97,1},{33,65},{65,33},{2,98}... | collective-permute-start | bytes 884744 | tf_op jit(solution)/shard_map/ppermute | solution.py:25
  21.8 16.6 %copy-start.2 = (bf16[1024,256]{1,0:T(8,128)(2,1)S(1)}, bf16[1024,256]{1,0:T(8,128)(2,1)}, u32[]{:S(2)}) copy-start(bf16[1024,256]{1,0:T(8,128)(2,1)} %wp_ref.3) | copy-start | bytes 1572868
  21.9 16.5 %copy-start.3 = (bf16[1,24,24,256]{3,2,1,0:T(8,128)(2,1)S(1)}, bf16[1,24,24,256]{3,2,1,0:T(8,128)(2,1)}, u32[]{:S(2)}) copy-start(bf16[1,24,24,256]{3,2,1,0:T(8,128)(2,1)} %param.9) | copy-start | bytes 884740
  40.8 6.4 %copy-start.4 = (s32[176]{0:T(256)S(1)}, s32[176]{0:T(256)}, u32[]{:S(2)}) copy-start(s32[176]{0:T(256)} %param.15) | copy-start | bytes 2116
  40.8 16.0 %collective-permute-start.10 = (bf16[576,256]{1,0:T(8,128)(2,1)S(1)}, bf16[576,256]{1,0:T(8,128)(2,1)S(1)}, u32[]{:S(2)}, u32[]{:S(2)}) collective-permute-start(bf16[576,256]{1,0:T(8,128)(2,1)S(1)} %get-tuple-element.89.d0), channel_id=1, source_target_pairs={{0,96},{96,0},{32,64},{64,32},{1,97},{97,1},{33,65},{65,33},{2,98}... | collective-permute-start | bytes 884744 | tf_op jit(solution)/shard_map/ppermute | solution.py:25
  43.6 13.2 %collective-permute-start.8 = (bf16[576,256]{1,0:T(8,128)(2,1)S(1)}, bf16[576,256]{1,0:T(8,128)(2,1)S(1)}, u32[]{:S(2)}, u32[]{:S(2)}) collective-permute-start(bf16[576,256]{1,0:T(8,128)(2,1)S(1)} %get-tuple-element.89.d0), channel_id=1, source_target_pairs={{0,32},{32,0},{1,33},{33,1},{2,34},{34,2},{3,35},{35,3},{4,36},{36... | collective-permute-start | bytes 884744 | tf_op jit(solution)/shard_map/ppermute | solution.py:22
  44.4 13.8 %collective-permute-start.9 = (bf16[576,256]{1,0:T(8,128)(2,1)S(1)}, bf16[576,256]{1,0:T(8,128)(2,1)S(1)}, u32[]{:S(2)}, u32[]{:S(2)}) collective-permute-start(bf16[576,256]{1,0:T(8,128)(2,1)S(1)} %get-tuple-element.89.d0), channel_id=1, source_target_pairs={{0,64},{64,0},{1,65},{65,1},{2,66},{66,2},{3,67},{67,3},{4,68},{68... | collective-permute-start | bytes 884744 | tf_op jit(solution)/shard_map/ppermute | solution.py:24
  46.6 1.6 %collective-permute-start.6 = (bf16[512,256]{1,0:T(8,128)(2,1)S(1)}, bf16[512,256]{1,0:T(8,128)(2,1)S(1)}, u32[]{:S(2)}, u32[]{:S(2)}) collective-permute-start(bf16[512,256]{1,0:T(8,128)(2,1)S(1)} %get-tuple-element.84), channel_id=1, source_target_pairs={{0,1},{1,0},{2,3},{3,2},{4,5},{5,4},{6,7},{7,6},{8,9},{9,8},{10,11... | collective-permute-start | bytes 786440 | tf_op jit(solution)/shard_map/ppermute | solution.py:183
  46.7 1.9 %collective-permute-start.7 = (bf16[512,256]{1,0:T(8,128)(2,1)S(1)}, bf16[512,256]{1,0:T(8,128)(2,1)S(1)}, u32[]{:S(2)}, u32[]{:S(2)}) collective-permute-start(bf16[512,256]{1,0:T(8,128)(2,1)S(1)} %get-tuple-element.85), channel_id=1, source_target_pairs={{0,1},{1,0},{2,3},{3,2},{4,5},{5,4},{6,7},{7,6},{8,9},{9,8},{10,11... | collective-permute-start | bytes 786440 | tf_op jit(solution)/shard_map/ppermute | solution.py:183
  49.3 16.2 %collective-permute-start.11 = (bf16[16,16,256]{2,1,0:T(8,128)(2,1)S(1)}, bf16[16,16,256]{2,1,0:T(8,128)(2,1)S(1)}, u32[]{:S(2)}, u32[]{:S(2)}) collective-permute-start(bf16[16,16,256]{2,1,0:T(8,128)(2,1)S(1)} %get-tuple-element.97), channel_id=1, source_target_pairs={{0,32},{32,0},{1,33},{33,1},{2,34},{34,2},{3,35},{35,3},{4,36},{36... | collective-permute-start | bytes 393224 | tf_op jit(solution)/shard_map/ppermute | solution.py:22
  58.2 7.3 %collective-permute-start.12 = (bf16[16,16,256]{2,1,0:T(8,128)(2,1)S(1)}, bf16[16,16,256]{2,1,0:T(8,128)(2,1)S(1)}, u32[]{:S(2)}, u32[]{:S(2)}) collective-permute-start(bf16[16,16,256]{2,1,0:T(8,128)(2,1)S(1)} %get-tuple-element.98), channel_id=1, source_target_pairs={{0,64},{64,0},{1,65},{65,1},{2,66},{66,2},{3,67},{67,3},{4,68},{68... | collective-permute-start | bytes 393224 | tf_op jit(solution)/shard_map/ppermute | solution.py:24
  60.7 6.2 %collective-permute-start.13 = (bf16[16,16,256]{2,1,0:T(8,128)(2,1)S(1)}, bf16[16,16,256]{2,1,0:T(8,128)(2,1)S(1)}, u32[]{:S(2)}, u32[]{:S(2)}) collective-permute-start(bf16[16,16,256]{2,1,0:T(8,128)(2,1)S(1)} %get-tuple-element.99), channel_id=1, source_target_pairs={{0,96},{96,0},{32,64},{64,32},{1,97},{97,1},{33,65},{65,33},{2,98}... | collective-permute-start | bytes 393224 | tf_op jit(solution)/shard_map/ppermute | solution.py:25
  66.9 2.5 %collective-permute-start.14 = (bf16[96,16,256]{2,1,0:T(8,128)(2,1)S(1)}, bf16[96,16,256]{2,1,0:T(8,128)(2,1)S(1)}, u32[]{:S(2)}, u32[]{:S(2)}) collective-permute-start(bf16[96,16,256]{2,1,0:T(8,128)(2,1)S(1)} %get-tuple-element.100), channel_id=1, source_target_pairs={{0,1},{1,0},{2,3},{3,2},{4,5},{5,4},{6,7},{7,6},{8,9},{9,8},{10,11... | collective-permute-start | bytes 2359304 | tf_op jit(solution)/shard_map/ppermute | solution.py:183
  67.0 2.4 %collective-permute-start.15 = (bf16[16,16,256]{2,1,0:T(8,128)(2,1)S(1)}, bf16[16,16,256]{2,1,0:T(8,128)(2,1)S(1)}, u32[]{:S(2)}, u32[]{:S(2)}) collective-permute-start(bf16[16,16,256]{2,1,0:T(8,128)(2,1)S(1)} %get-tuple-element.105), channel_id=1, source_target_pairs={{0,1},{1,0},{2,3},{3,2},{4,5},{5,4},{6,7},{7,6},{8,9},{9,8},{10,11... | collective-permute-start | bytes 393224 | tf_op jit(solution)/shard_map/ppermute | solution.py:183

commit v10 on v8

--- a/solution.py
+++ b/solution.py
@@ -15,6 +15,7 @@
 BF = jnp.bfloat16
 F32 = jnp.float32
 MIB = 1024 * 1024
+EDGE = 8
 
 
 def flip(x, mask):
@@ -71,7 +72,7 @@
                 o_ref[rows, p * lanes : (p + 1) * lanes] = taken[:, k * lanes : (k + 1) * lanes]
 
 
-def turn_pixels(pos_ref, x0, x1, x2, x3, o_ref, held):
+def turn_pixels(pos_ref, x0, x1, x2, x3, o_ref, edge_ref, held):
     pixels, width = x0.shape
     for k, x in enumerate((x0, x1, x2, x3)):
         s = jnp.bitwise_xor(pos_ref[0], k)
@@ -84,13 +85,18 @@
         o_ref[g] = lax.dot_general(
             eye, held[g], (((1,), (1,)), ((), ())), preferred_element_type=F32
         ).astype(BF)
+        wide = held[g].astype(F32).reshape(-1, SIDE, width)
+        near = wide[:, SIDE - EDGE :] if g == 0 else wide[:, :EDGE]
+        edge_ref[g] = lax.dot_general(
+            eye, near.reshape(-1, width).astype(BF), (((1,), (1,)), ((), ())), preferred_element_type=F32
+        ).astype(BF)
 
 
 def roll_cols(x, shift):
     return jnp.concatenate([x[:, x.shape[1] - shift :], x[:, : x.shape[1] - shift]], axis=1)
 
 
-def tap_grads(pos_ref, place_ref, d0, d1, d2, d3, xt_ref, keep_ref, send_ref, held, padded, buf):
+def tap_grads(pos_ref, place_ref, d0, d1, d2, d3, xt_ref, xe_ref, keep_ref, send_ref, held, padded, edge, buf):
     side = RATE_C
     pixels, width = d0.shape
     cols = 24
@@ -123,16 +129,25 @@
                 jnp.where(at < rest, rolled[0], rolled[1]),
                 jnp.where(at < rest, rolled[1], 0.0),
             ]
+        thin = {1: 0, -1: 1}.get(across)
         for g in range(2):
-            padded[turn, g, pl.ds(lead, tall), :] = shifted[g].reshape(tall, width).astype(BF)
+            if g == thin:
+                near = shifted[g][:, SIDE - EDGE :] if g == 0 else shifted[g][:, :EDGE]
+                short = side * EDGE
+                edge[g, pl.ds(0, short), :] = jnp.zeros((short, width), BF)
+                edge[g, pl.ds(short, 2 * rows * EDGE), :] = near.reshape(2 * rows * EDGE, width).astype(BF)
+                edge[g, pl.ds(short + 2 * rows * EDGE, short), :] = jnp.zeros((short, width), BF)
+            else:
+                padded[turn, g, pl.ds(lead, tall), :] = shifted[g].reshape(tall, width).astype(BF)
         for above in (-1, 0, 1):
             first, last = {-1: (0, 32), 0: (0, 48), 1: (16, 48)}[above]
             base = first - side * above + side
             total = None
             for g in range(2):
+                left, right, each = (xe_ref, edge.at[g], EDGE) if g == thin else (xt_ref, padded.at[turn, g], cols)
                 part = jnp.dot(
-                    xt_ref[g, :, first * cols : last * cols],
-                    padded[turn, g, base * cols : (base + last - first) * cols, :],
+                    left[g, :, first * each : last * each],
+                    right[base * each : (base + last - first) * each, :],
                     preferred_element_type=F32,
                 )
                 total = part if total is None else total + part
@@ -204,7 +219,10 @@
     pixels, width = got[0].shape
     return call(
         turn_pixels,
-        jax.ShapeDtypeStruct((2, width, 2 * pixels), BF),
+        [
+            jax.ShapeDtypeStruct((2, width, 2 * pixels), BF),
+            jax.ShapeDtypeStruct((2, width, 2 * pixels // SIDE * EDGE), BF),
+        ],
         1,
         4,
         8 * pixels * width * width,
@@ -252,17 +270,18 @@
         tap_grads,
         [jax.ShapeDtypeStruct((half, 16, width), F32), jax.ShapeDtypeStruct((half, 16, width), BF)],
         2,
-        5,
+        6,
         2 * 7 * 4 * pixels * width * width,
         8 * 1024 * 1024,
         26,
         [
             pltpu.VMEM((2, 2 * pixels, width), BF),
             pltpu.VMEM((3, 2, 2 * pixels + 2 * RATE_C * SIDE, width), BF),
+            pltpu.VMEM((2, (2 * SIDE + 2 * RATE_C) * EDGE, width), BF),
             pltpu.VMEM((slot_count, 16, width), F32),
         ],
         name="taps",
-    )(pos, place, *deltas, turned)
+    )(pos, place, *deltas, *turned)
 
 
 def reduce_slots(pos, place, kept, sent, mine, other):
@@ -418,14 +437,17 @@
         row_ref[to_row, :] = (acc[:lead, :] + y[pl.ds(next_from, lead), 2 * width : 3 * width] + theirs).astype(BF)
 
 
-def inner_parts(pos_ref, x_ref, part_ref, wp_ref, wc_ref, wb_ref, wa_ref, pre0_ref, pre_ref, y, z, held, sems):
+def inner_parts(pos_ref, x_ref, part_ref, wp_ref, wc_ref, wb_ref, wa_ref, joined_ref, slope_ref, pre_ref, y, z, held, sems):
     low, far = pos_ref[2], pos_ref[3]
     whole = SIDE * SIDE
-    width = pre0_ref.shape[1]
+    width = joined_ref.shape[1]
     copies = tap_copies(pos_ref, (wc_ref, wb_ref, wa_ref), INNER, held, sems)
     for copy in copies:
         copy.start()
-    pre0_ref[...] = jnp.dot(x_ref[...], wp_ref[...], preferred_element_type=F32)
+    value = jnp.dot(x_ref[...], wp_ref[...], preferred_element_type=F32)
+    sig = sigmoid(value)
+    joined_ref[...] = (value * sig).astype(BF)
+    slope_ref[...] = sig * (1.0 + value * (1.0 - sig))
     for turn, (index, rate) in enumerate(BRANCHES):
         lead = rate * SIDE
         inside = whole - lead
@@ -474,7 +496,11 @@
     width = w_point.shape[1]
     return call(
         inner_parts,
-        [jax.ShapeDtypeStruct((pixels, width), F32), jax.ShapeDtypeStruct((3, pixels, width), F32)],
+        [
+            jax.ShapeDtypeStruct((pixels, width), BF),
+            jax.ShapeDtypeStruct((pixels, width), F32),
+            jax.ShapeDtypeStruct((3, pixels, width), F32),
+        ],
         1,
         3,
         2 * pixels * chans * width * 10,
@@ -492,11 +518,11 @@
 
 
 def merge_parts(
-    pos_ref, pre0_ref, own_ref, row_ref, col_ref, diag_ref, cot_ref, wp_ref, joined_ref, g_ref, d0_ref, d3_ref, pre
+    pos_ref, joined0_ref, own_ref, row_ref, col_ref, diag_ref, cot_ref, wp_ref, joined_ref, g_ref, d3_ref, pre
 ):
     low = pos_ref[2]
     theirs = 1 - pos_ref[3]
-    width = pre0_ref.shape[1]
+    width = joined0_ref.shape[1]
     whole = SIDE * SIDE
 
     def rows_of(rate):
@@ -532,29 +558,31 @@
     last = pl.multiple_of(at + half * SIDE, 16)
     pre[1, pl.ds(last, half * SIDE), :] += flat(roll_cols(jnp.where(rank >= RATE_B, part, 0.0), RATE_B))
 
-    slopes = {}
-    for k in range(4):
-        value = pre0_ref[...] if k == 0 else pre[k - 1]
+    joined_ref[:, :width] = joined0_ref[...]
+    for k in range(1, 4):
+        value = pre[k - 1]
         sig = sigmoid(value)
         joined_ref[:, k * width : (k + 1) * width] = (value * sig).astype(BF)
-        if k in (0, 3):
-            slopes[k] = sig * (1.0 + value * (1.0 - sig))
+    slope = sig * (1.0 + value * (1.0 - sig))
     proj_pre = jnp.dot(joined_ref[...], wp_ref[...], preferred_element_type=F32)
     g_proj = (cot_ref[...].astype(F32) * silu_slope(proj_pre)).astype(BF)
     g_ref[...] = g_proj
-    for k, out in ((3, d3_ref), (0, d0_ref)):
-        back = lax.dot_general(
-            g_proj, wp_ref[k * width : (k + 1) * width, :], (((1,), (1,)), ((), ())), preferred_element_type=F32
-        )
-        out[...] = (back * slopes[k]).astype(BF)
-
-
-def merge(pos, pre0, own, row, col, diag, cot, w_proj):
-    pixels, width = pre0.shape
+    d3_ref[...] = (back_through(g_proj, wp_ref, 3) * slope).astype(BF)
+
+
+def back_through(g_proj, wp_ref, k):
+    width = g_proj.shape[1]
+    return lax.dot_general(
+        g_proj, wp_ref[k * width : (k + 1) * width, :], (((1,), (1,)), ((), ())), preferred_element_type=F32
+    )
+
+
+def merge(pos, joined0, own, row, col, diag, cot, w_proj):
+    pixels, width = joined0.shape
     block = jax.ShapeDtypeStruct((pixels, width), BF)
     return call(
         merge_parts,
-        [jax.ShapeDtypeStruct((pixels, 4 * width), BF), block, block, block],
+        [jax.ShapeDtypeStruct((pixels, 4 * width), BF), block, block],
         1,
         7,
         2 * pixels * width * width * 6,
@@ -562,14 +590,15 @@
         18,
         [pltpu.VMEM((3, pixels, width), F32)],
         name="merge",
-    )(pos, pre0, own, row, col, diag, cot, w_proj)
-
-
-def pair_grads(pos_ref, joined_ref, g_ref, x_ref, d0_ref, keep_ref, *send_refs):
+    )(pos, joined0, own, row, col, diag, cot, w_proj)
+
+
+def pair_grads(pos_ref, joined_ref, g_ref, x_ref, slope_ref, wp_ref, keep_ref, *send_refs):
     core = pos_ref[4]
     over = (((0,), (0,)), ((), ()))
     grad_proj = lax.dot_general(joined_ref[...], g_ref[...], over, preferred_element_type=F32)
-    grad_point = lax.dot_general(x_ref[...], d0_ref[...], over, preferred_element_type=F32)
+    delta = (back_through(g_ref[...], wp_ref, 0) * slope_ref[...]).astype(BF)
+    grad_point = lax.dot_general(x_ref[...], delta, over, preferred_element_type=F32)
     keep_ref[...] = jnp.where(core == 0, grad_proj, grad_point)
     half = send_refs[0].shape[0]
     for k, send_ref in enumerate(send_refs):
@@ -598,10 +627,10 @@
     to_row, to_col, to_diag = parts
     parts = [flip(to_row, 2), flip(to_col, 1), flip(to_diag, 3)]
     turned = turn(pos, got)
-    pre0, own = inner(pos, centre, part, w_point, *weights)
-    parts, pre0, own, turned = lax.optimization_barrier((parts, pre0, own, turned))
-    joined, g_proj, delta0, delta3 = merge(
-        pos, pre0, own, *parts, cotangent[0].reshape(pixels, width), w_proj
+    joined0, slope0, own = inner(pos, centre, part, w_point, *weights)
+    parts, joined0, own, turned = lax.optimization_barrier((parts, joined0, own, turned))
+    joined, g_proj, delta3 = merge(
+        pos, joined0, own, *parts, cotangent[0].reshape(pixels, width), w_proj
     )
     shared = [delta3] + [flip(delta3, k) for k in (1, 2, 3)]
     block = (4 * width, width)
@@ -609,12 +638,12 @@
         pair_grads,
         [jax.ShapeDtypeStruct(block, F32)] + [jax.ShapeDtypeStruct((2 * width, width), BF)] * 2,
         1,
-        4,
+        5,
         4 * pixels * chans * width,
         4 * 1024 * 1024,
         16,
         name="pair",
-    )(pos, joined, g_proj, centre, delta0)
+    )(pos, joined, g_proj, centre, slope0, w_proj)
     got = [swap_core(part) for part in sent]
     by_owner = split_pair(pos, kept, got)
     by_owner, shared = lax.optimization_barrier((by_owner, shared))

time: 93.5 us -> 93.2 us (level)
  no operation moved by 1% of the time
where the time goes in v10:
time: 93.2 us; the launch traced here: 93.1 us
  Pallas kernels  29 us (31%)
  waiting for transfers between devices  22.7 us (24%)
  blocking collectives  22.3 us (24%)
  starting transfers between devices  18.7 us (20%)
    all_to_all x1, blocking collectives, reduce_slots(): total = lax.all_to_all(total, ('dp_0', 'dp_1'), 0, 0, tiled=True)  22.3 us
    ppermute x4, starting transfers between devices, flip(): return lax.ppermute(x, 'col', [(0, 1), (1, 0)])  9.84 us
    ppermute x4, waiting for transfers between devices, flip(): return lax.ppermute(x, ('row', 'col'), [(0, 3), (3, 0), (1, 2), (2, 1)])  8.79 us
    pallas_call x1, Pallas kernels, outer(): call(outer_parts, [jax.ShapeDtypeStruct(*s) for s in shapes], 1, 1, 2 * p...  8.68 us
    ppermute x4, waiting for transfers between devices, flip(): return lax.ppermute(x, 'col', [(0, 1), (1, 0)])  8.25 us
    pallas_call x1, Pallas kernels, inner(): call(inner_parts, [jax.ShapeDtypeStruct((pixels, width), BF), jax.ShapeDt...  6.14 us
    ppermute x4, starting transfers between devices, flip(): return lax.ppermute(x, ('row', 'col'), [(0, 3), (3, 0), (1, 2), (2, 1)])  4.53 us
    ppermute x4, waiting for transfers between devices, swap_core(): return lax.ppermute(x, 'dp_2', [(0, 1), (1, 0)])  3.18 us
  transfers between devices with their start and end apart: 16, of which 11 were waited for; matrix products, arithmetic and copies ran while one was open for 0% of the time, Pallas kernels for 24%

profile of v10, /device:TPU:0, one launch (start us, length us, event | category | flops | bytes accessed | tf_op | source)
XLA Modules:
  0.0 93.1 jit_solution(10817792037068965754)
XLA Ops:
  0.1 2.6 %pick.1 = (bf16[576,256]{1,0:T(8,128)(2,1)S(1)}, bf16[576,256]{1,0:T(8,128)(2,1)S(1)}, bf16[576,256]{1,0:T(8,128)(2,1)S(1)}, bf16[576,256]{1,0:T(8,128)(2,1)S(1)}) custom-call(s32[6]{0:T(128)S(1)} %stack.27.pos_ref, bf16[576,1024]{1,0:T(8,128)(2,1)} %bitcast.8), custom_call_target="tpu_custom_call" | custom-call | flops 603979776 | bytes 2359296 | tf_op jit(solution)/shard_map/pick/pallas_call | solution.py:204
  2.7 3.2 %collective-permute-start.3 = (bf16[576,256]{1,0:T(8,128)(2,1)S(1)}, bf16[576,256]{1,0:T(8,128)(2,1)S(1)}, u32[]{:S(2)}, u32[]{:S(2)}) collective-permute-start(bf16[576,256]{1,0:T(8,128)(2,1)S(1)} %get-tuple-element.70), channel_id=1, source_target_pairs={{0,32},{32,0},{1,33},{33,1},{2,34},{34,2},{3,35},{35,3},{4,36},{36... | collective-permute-start | bytes 884744 | tf_op jit(solution)/shard_map/ppermute | solution.py:23
  5.8 0.6 collective-permute-start.4
  6.4 0.6 collective-permute-start.5
  7.0 8.7 %outer.1 = (f32[3,576,256]{2,1,0:T(8,128)S(1)}, bf16[864,256]{1,0:T(8,128)(2,1)S(1)}, bf16[864,256]{1,0:T(8,128)(2,1)S(1)}, bf16[576,256]{1,0:T(8,128)(2,1)S(1)}) custom-call(s32[6]{0:T(128)S(1)} %stack.27.pos_ref, bf16[576,1024]{1,0:T(8,128)(2,1)S(1)} %bitcast.9, bf16[3,3,1024,256]{3,2,1,0:T(8,128)(2,1)} %wc_ref.3, bf16[3,3,1024,256]{3,2,1,0:T(8,128)(2,1)} %wb_ref.3, ...), custom_call_target="tpu_custom_call" | custom-call | flops 4227858432 | bytes 10485760 | tf_op jit(solution)/shard_map/outer/pallas_call | solution.py:474
  15.7 1.5 %collective-permute-start = (bf16[864,256]{1,0:T(8,128)(2,1)S(1)}, bf16[864,256]{1,0:T(8,128)(2,1)S(1)}, u32[]{:S(2)}, u32[]{:S(2)}) collective-permute-start(bf16[864,256]{1,0:T(8,128)(2,1)S(1)} %get-tuple-element.65), channel_id=1, source_target_pairs={{0,64},{64,0},{1,65},{65,1},{2,66},{66,2},{3,67},{67,3},{4,68},{68... | collective-permute-start | bytes 1327112 | tf_op jit(solution)/shard_map/ppermute | solution.py:25
  17.1 2.7 %collective-permute-start.1 = (bf16[864,256]{1,0:T(8,128)(2,1)S(1)}, bf16[864,256]{1,0:T(8,128)(2,1)S(1)}, u32[]{:S(2)}, u32[]{:S(2)}) collective-permute-start(bf16[864,256]{1,0:T(8,128)(2,1)S(1)} %get-tuple-element.66), channel_id=1, source_target_pairs={{0,32},{32,0},{1,33},{33,1},{2,34},{34,2},{3,35},{35,3},{4,36},{36... | collective-permute-start | bytes 1327112 | tf_op jit(solution)/shard_map/ppermute | solution.py:23
  19.9 0.6 collective-permute-start.2
  20.7 1.3 %turn.1 = (bf16[2,256,1152]{2,1,0:T(8,128)(2,1)S(1)}, bf16[2,256,384]{2,1,0:T(8,128)(2,1)S(1)}) custom-call(s32[6]{0:T(128)S(1)} %stack.27.pos_ref, bf16[576,256]{1,0:T(8,128)(2,1)S(1)} %get-tuple-element.76.x0, bf16[576,256]{1,0:T(8,128)(2,1)S(1)} %collective-permute-done.3.x1, bf16[576,256]{1,0:T(8,128)(2,1)S(1)} %collective-permute-done.4.x2, ...), custom_call_target="tpu_custom_call" | custom-call | flops 301989888 | bytes 2359296 | tf_op jit(solution)/shard_map/turn/pallas_call | solution.py:220
  22.0 6.1 %inner.1 = (bf16[576,256]{1,0:T(8,128)(2,1)S(1)}, f32[576,256]{1,0:T(8,128)S(1)}, f32[3,576,256]{2,1,0:T(8,128)S(1)}) custom-call(s32[6]{0:T(128)S(1)} %stack.27.pos_ref, bf16[576,1024]{1,0:T(8,128)(2,1)S(1)} %bitcast.10, f32[3,576,256]{2,1,0:T(8,128)S(1)} %get-tuple-element.73.part_ref, bf16[1024,256]{1,0:T(8,128)(2,1)S(1)} %copy-done.2, ...), custom_call_target="tpu_custom_call" | custom-call | flops 3019898880 | bytes 10485760 | tf_op jit(solution)/shard_map/inner/pallas_call | solution.py:497
  28.2 1.8 %collective-permute-done.2.diag_ref = bf16[576,256]{1,0:T(8,128)(2,1)S(1)} collective-permute-done((bf16[576,256]{1,0:T(8,128)(2,1)S(1)}, bf16[576,256]{1,0:T(8,128)(2,1)S(1)}, u32[]{:S(2)}, u32[]{:S(2)}) %collective-permute-start.2) | collective-permute-done | bytes 294944 | tf_op jit(solution)/shard_map/ppermute | solution.py:26
  30.1 8.2 %collective-permute-done.1.col_ref = bf16[864,256]{1,0:T(8,128)(2,1)S(1)} collective-permute-done((bf16[864,256]{1,0:T(8,128)(2,1)S(1)}, bf16[864,256]{1,0:T(8,128)(2,1)S(1)}, u32[]{:S(2)}, u32[]{:S(2)}) %collective-permute-start.1) | collective-permute-done | bytes 442400 | tf_op jit(solution)/shard_map/ppermute | solution.py:23
  38.4 2.1 %merge.1 = (bf16[576,1024]{1,0:T(8,128)(2,1)S(1)}, bf16[576,256]{1,0:T(8,128)(2,1)S(1)}, bf16[576,256]{1,0:T(8,128)(2,1)S(1)}) custom-call(s32[6]{0:T(128)S(1)} %stack.27.pos_ref, bf16[576,256]{1,0:T(8,128)(2,1)S(1)} %get-tuple-element.82.joined0_ref, f32[3,576,256]{2,1,0:T(8,128)S(1)} %get-tuple-element.83.own_ref, ...), custom_call_target="tpu_custom_call" | custom-call | flops 452984832 | bytes 6291456 | tf_op jit(solution)/shard_map/merge/pallas_call | solution.py:583
  40.5 2.9 %collective-permute-start.10 = (bf16[576,256]{1,0:T(8,128)(2,1)S(1)}, bf16[576,256]{1,0:T(8,128)(2,1)S(1)}, u32[]{:S(2)}, u32[]{:S(2)}) collective-permute-start(bf16[576,256]{1,0:T(8,128)(2,1)S(1)} %get-tuple-element.98.d0), channel_id=1, source_target_pairs={{0,96},{96,0},{32,64},{64,32},{1,97},{97,1},{33,65},{65,33},{2,98}... | collective-permute-start | bytes 884744 | tf_op jit(solution)/shard_map/ppermute | solution.py:26
  43.4 0.8 collective-permute-start.8
  44.2 0.5 collective-permute-start.9
  44.7 2.5 %pair.1 = (f32[1024,256]{1,0:T(8,128)S(1)}, bf16[512,256]{1,0:T(8,128)(2,1)S(1)}, bf16[512,256]{1,0:T(8,128)(2,1)S(1)}) custom-call(s32[6]{0:T(128)S(1)} %stack.27.pos_ref, bf16[576,1024]{1,0:T(8,128)(2,1)S(1)} %get-tuple-element.87.joined_ref, bf16[576,256]{1,0:T(8,128)(2,1)S(1)} %get-tuple-element.88.g_ref, bf16[576,1024]{1,0:T(8,128)(2,1)S(1)} %bitcast.11, ...), custom_call_target="tpu_custom_call" | custom-call | flops 603979776 | bytes 4194304 | tf_op jit(solution)/shard_map/pair/pallas_call | solution.py:637
  47.8 1.0 %collective-permute-done.6.got0 = bf16[512,256]{1,0:T(8,128)(2,1)S(1)} collective-permute-done((bf16[512,256]{1,0:T(8,128)(2,1)S(1)}, bf16[512,256]{1,0:T(8,128)(2,1)S(1)}, u32[]{:S(2)}, u32[]{:S(2)}) %collective-permute-start.6) | collective-permute-done | bytes 262176 | tf_op jit(solution)/shard_map/ppermute | solution.py:198
  49.2 0.7 rows.1
  49.9 5.9 %collective-permute-done.10.d3 = bf16[576,256]{1,0:T(8,128)(2,1)S(1)} collective-permute-done((bf16[576,256]{1,0:T(8,128)(2,1)S(1)}, bf16[576,256]{1,0:T(8,128)(2,1)S(1)}, u32[]{:S(2)}, u32[]{:S(2)}) %collective-permute-start.10) | collective-permute-done | bytes 294944 | tf_op jit(solution)/shard_map/ppermute | solution.py:26
  55.8 0.7 collective-permute-done.9.d2
  56.5 3.1 %collective-permute-start.11 = (bf16[16,16,256]{2,1,0:T(8,128)(2,1)S(1)}, bf16[16,16,256]{2,1,0:T(8,128)(2,1)S(1)}, u32[]{:S(2)}, u32[]{:S(2)}) collective-permute-start(bf16[16,16,256]{2,1,0:T(8,128)(2,1)S(1)} %get-tuple-element.107), channel_id=1, source_target_pairs={{0,32},{32,0},{1,33},{33,1},{2,34},{34,2},{3,35},{35,3},{4,36},{36... | collective-permute-start | bytes 393224 | tf_op jit(solution)/shard_map/ppermute | solution.py:23
  59.7 0.6 collective-permute-start.12
  60.3 0.5 collective-permute-start.13
  60.8 3.1 %taps.1 = (f32[96,16,256]{2,1,0:T(8,128)S(1)}, bf16[96,16,256]{2,1,0:T(8,128)(2,1)S(1)}) custom-call(s32[6]{0:T(128)S(1)} %stack.27.pos_ref, s32[176]{0:T(256)S(1)} %fusion.1.place_ref, bf16[576,256]{1,0:T(8,128)(2,1)S(1)} %get-tuple-element.98.d0, bf16[576,256]{1,0:T(8,128)(2,1)S(1)} %collective-permute-done.8.d1, ...), custom_call_target="tpu_custom_call" | custom-call | flops 2113929216 | bytes 8388608 | tf_op jit(solution)/shard_map/taps/pallas_call | solution.py:269
  63.9 1.5 %collective-permute-done.12 = bf16[16,16,256]{2,1,0:T(8,128)(2,1)S(1)} collective-permute-done((bf16[16,16,256]{2,1,0:T(8,128)(2,1)S(1)}, bf16[16,16,256]{2,1,0:T(8,128)(2,1)S(1)}, u32[]{:S(2)}, u32[]{:S(2)}) %collective-permute-start.12) | collective-permute-done | bytes 131104 | tf_op jit(solution)/shard_map/ppermute | solution.py:25
  65.4 1.1 %collective-permute-done.13 = bf16[16,16,256]{2,1,0:T(8,128)(2,1)S(1)} collective-permute-done((bf16[16,16,256]{2,1,0:T(8,128)(2,1)S(1)}, bf16[16,16,256]{2,1,0:T(8,128)(2,1)S(1)}, u32[]{:S(2)}, u32[]{:S(2)}) %collective-permute-start.13) | collective-permute-done | bytes 131104 | tf_op jit(solution)/shard_map/ppermute | solution.py:26
  66.5 0.6 collective-permute-start.15
  67.1 1.8 %collective-permute-done.15.other_ref = bf16[16,16,256]{2,1,0:T(8,128)(2,1)S(1)} collective-permute-done((bf16[16,16,256]{2,1,0:T(8,128)(2,1)S(1)}, bf16[16,16,256]{2,1,0:T(8,128)(2,1)S(1)}, u32[]{:S(2)}, u32[]{:S(2)}) %collective-permute-start.15) | collective-permute-done | bytes 131104 | tf_op jit(solution)/shard_map/ppermute | solution.py:198
  68.9 1.1 %owners.1 = bf16[16,96,256]{2,1,0:T(8,128)(2,1)S(1)} custom-call(s32[6]{0:T(128)S(1)} %stack.27.pos_ref, s32[176]{0:T(256)S(1)} %fusion.1.place_ref, f32[96,16,256]{2,1,0:T(8,128)S(1)} %get-tuple-element.104.keep_ref, bf16[96,16,256]{2,1,0:T(8,128)(2,1)S(1)} %collective-permute-done.14.got_ref, f32[16,16,256]{2,1,0:T(8,128)S(1)} %get-tuple-element.116.mine_ref, ...), custom_call_target="tpu_custom_call" | custom-call | flops 393216 | bytes 3145728 | tf_op jit(solution)/shard_map/owners/pallas_call | solution.py:291
  70.0 22.3 %all_to_all.5.r_ref = bf16[16,96,256]{2,1,0:T(8,128)(2,1)S(1)} all-to-all(bf16[16,96,256]{2,1,0:T(8,128)(2,1)S(1)} %owners.1), channel_id=1, replica_groups=mesh['row'=2,'col'=2,'dp_0'=4,'dp_1'=4,'dp_2'=2] {'dp_0','dp_1'}, dimensions={0} | all-to-all | bytes 1572864 | tf_op jit(solution)/shard_map/all_to_all | solution.py:302
  92.3 0.8 last.1
  (24 shorter events, 1.5 us)
Async XLA Ops:
  0.0 7.0 %copy-start = (bf16[1,24,24,1024]{3,2,1,0:T(8,128)(2,1)S(1)}, bf16[1,24,24,1024]{3,2,1,0:T(8,128)(2,1)}, u32[]{:S(2)}) copy-start(bf16[1,24,24,1024]{3,2,1,0:T(8,128)(2,1)} %param.8) | copy-start | bytes 3538948
  2.6 19.3 %copy-start.2 = (bf16[1024,256]{1,0:T(8,128)(2,1)S(1)}, bf16[1024,256]{1,0:T(8,128)(2,1)}, u32[]{:S(2)}) copy-start(bf16[1024,256]{1,0:T(8,128)(2,1)} %wp_ref.3) | copy-start | bytes 1572868
  2.7 17.2 %collective-permute-start.3 = (bf16[576,256]{1,0:T(8,128)(2,1)S(1)}, bf16[576,256]{1,0:T(8,128)(2,1)S(1)}, u32[]{:S(2)}, u32[]{:S(2)}) collective-permute-start(bf16[576,256]{1,0:T(8,128)(2,1)S(1)} %get-tuple-element.70), channel_id=1, source_target_pairs={{0,32},{32,0},{1,33},{33,1},{2,34},{34,2},{3,35},{35,3},{4,36},{36... | collective-permute-start | bytes 884744 | tf_op jit(solution)/shard_map/ppermute | solution.py:23
  5.8 14.8 %collective-permute-start.4 = (bf16[576,256]{1,0:T(8,128)(2,1)S(1)}, bf16[576,256]{1,0:T(8,128)(2,1)S(1)}, u32[]{:S(2)}, u32[]{:S(2)}) collective-permute-start(bf16[576,256]{1,0:T(8,128)(2,1)S(1)} %get-tuple-element.71), channel_id=1, source_target_pairs={{0,64},{64,0},{1,65},{65,1},{2,66},{66,2},{3,67},{67,3},{4,68},{68... | collective-permute-start | bytes 884744 | tf_op jit(solution)/shard_map/ppermute | solution.py:25
  6.4 14.2 %collective-permute-start.5 = (bf16[576,256]{1,0:T(8,128)(2,1)S(1)}, bf16[576,256]{1,0:T(8,128)(2,1)S(1)}, u32[]{:S(2)}, u32[]{:S(2)}) collective-permute-start(bf16[576,256]{1,0:T(8,128)(2,1)S(1)} %get-tuple-element.72), channel_id=1, source_target_pairs={{0,96},{96,0},{32,64},{64,32},{1,97},{97,1},{33,65},{65,33},{2,98}... | collective-permute-start | bytes 884744 | tf_op jit(solution)/shard_map/ppermute | solution.py:26
  15.7 14.5 %collective-permute-start = (bf16[864,256]{1,0:T(8,128)(2,1)S(1)}, bf16[864,256]{1,0:T(8,128)(2,1)S(1)}, u32[]{:S(2)}, u32[]{:S(2)}) collective-permute-start(bf16[864,256]{1,0:T(8,128)(2,1)S(1)} %get-tuple-element.65), channel_id=1, source_target_pairs={{0,64},{64,0},{1,65},{65,1},{2,66},{66,2},{3,67},{67,3},{4,68},{68... | collective-permute-start | bytes 1327112 | tf_op jit(solution)/shard_map/ppermute | solution.py:25
  17.1 21.2 %collective-permute-start.1 = (bf16[864,256]{1,0:T(8,128)(2,1)S(1)}, bf16[864,256]{1,0:T(8,128)(2,1)S(1)}, u32[]{:S(2)}, u32[]{:S(2)}) collective-permute-start(bf16[864,256]{1,0:T(8,128)(2,1)S(1)} %get-tuple-element.66), channel_id=1, source_target_pairs={{0,32},{32,0},{1,33},{33,1},{2,34},{34,2},{3,35},{35,3},{4,36},{36... | collective-permute-start | bytes 1327112 | tf_op jit(solution)/shard_map/ppermute | solution.py:23
  19.9 10.1 %collective-permute-start.2 = (bf16[576,256]{1,0:T(8,128)(2,1)S(1)}, bf16[576,256]{1,0:T(8,128)(2,1)S(1)}, u32[]{:S(2)}, u32[]{:S(2)}) collective-permute-start(bf16[576,256]{1,0:T(8,128)(2,1)S(1)} %get-tuple-element.67), channel_id=1, source_target_pairs={{0,96},{96,0},{32,64},{64,32},{1,97},{97,1},{33,65},{65,33},{2,98}... | collective-permute-start | bytes 884744 | tf_op jit(solution)/shard_map/ppermute | solution.py:26
  22.0 16.4 %copy-start.1 = (bf16[1024,256]{1,0:T(8,128)(2,1)S(1)}, bf16[1024,256]{1,0:T(8,128)(2,1)}, u32[]{:S(2)}) copy-start(bf16[1024,256]{1,0:T(8,128)(2,1)} %wp_ref.5) | copy-start | bytes 1572868
  22.0 16.4 %copy-start.3 = (bf16[1,24,24,256]{3,2,1,0:T(8,128)(2,1)S(1)}, bf16[1,24,24,256]{3,2,1,0:T(8,128)(2,1)}, u32[]{:S(2)}) copy-start(bf16[1,24,24,256]{3,2,1,0:T(8,128)(2,1)} %param.9) | copy-start | bytes 884740
  40.5 15.3 %collective-permute-start.10 = (bf16[576,256]{1,0:T(8,128)(2,1)S(1)}, bf16[576,256]{1,0:T(8,128)(2,1)S(1)}, u32[]{:S(2)}, u32[]{:S(2)}) collective-permute-start(bf16[576,256]{1,0:T(8,128)(2,1)S(1)} %get-tuple-element.98.d0), channel_id=1, source_target_pairs={{0,96},{96,0},{32,64},{64,32},{1,97},{97,1},{33,65},{65,33},{2,98}... | collective-permute-start | bytes 884744 | tf_op jit(solution)/shard_map/ppermute | solution.py:26
  43.4 12.5 %collective-permute-start.8 = (bf16[576,256]{1,0:T(8,128)(2,1)S(1)}, bf16[576,256]{1,0:T(8,128)(2,1)S(1)}, u32[]{:S(2)}, u32[]{:S(2)}) collective-permute-start(bf16[576,256]{1,0:T(8,128)(2,1)S(1)} %get-tuple-element.98.d0), channel_id=1, source_target_pairs={{0,32},{32,0},{1,33},{33,1},{2,34},{34,2},{3,35},{35,3},{4,36},{36... | collective-permute-start | bytes 884744 | tf_op jit(solution)/shard_map/ppermute | solution.py:23
  44.2 12.4 %collective-permute-start.9 = (bf16[576,256]{1,0:T(8,128)(2,1)S(1)}, bf16[576,256]{1,0:T(8,128)(2,1)S(1)}, u32[]{:S(2)}, u32[]{:S(2)}) collective-permute-start(bf16[576,256]{1,0:T(8,128)(2,1)S(1)} %get-tuple-element.98.d0), channel_id=1, source_target_pairs={{0,64},{64,0},{1,65},{65,1},{2,66},{66,2},{3,67},{67,3},{4,68},{68... | collective-permute-start | bytes 884744 | tf_op jit(solution)/shard_map/ppermute | solution.py:25
  44.7 3.1 %copy-start.4 = (s32[176]{0:T(256)S(1)}, s32[176]{0:T(256)}, u32[]{:S(2)}) copy-start(s32[176]{0:T(256)} %param.15) | copy-start | bytes 2116
  47.2 1.6 %collective-permute-start.6 = (bf16[512,256]{1,0:T(8,128)(2,1)S(1)}, bf16[512,256]{1,0:T(8,128)(2,1)S(1)}, u32[]{:S(2)}, u32[]{:S(2)}) collective-permute-start(bf16[512,256]{1,0:T(8,128)(2,1)S(1)} %get-tuple-element.91), channel_id=1, source_target_pairs={{0,1},{1,0},{2,3},{3,2},{4,5},{5,4},{6,7},{7,6},{8,9},{9,8},{10,11... | collective-permute-start | bytes 786440 | tf_op jit(solution)/shard_map/ppermute | solution.py:198
  47.3 1.9 %collective-permute-start.7 = (bf16[512,256]{1,0:T(8,128)(2,1)S(1)}, bf16[512,256]{1,0:T(8,128)(2,1)S(1)}, u32[]{:S(2)}, u32[]{:S(2)}) collective-permute-start(bf16[512,256]{1,0:T(8,128)(2,1)S(1)} %get-tuple-element.92), channel_id=1, source_target_pairs={{0,1},{1,0},{2,3},{3,2},{4,5},{5,4},{6,7},{7,6},{8,9},{9,8},{10,11... | collective-permute-start | bytes 786440 | tf_op jit(solution)/shard_map/ppermute | solution.py:198
  56.5 7.4 %collective-permute-start.11 = (bf16[16,16,256]{2,1,0:T(8,128)(2,1)S(1)}, bf16[16,16,256]{2,1,0:T(8,128)(2,1)S(1)}, u32[]{:S(2)}, u32[]{:S(2)}) collective-permute-start(bf16[16,16,256]{2,1,0:T(8,128)(2,1)S(1)} %get-tuple-element.107), channel_id=1, source_target_pairs={{0,32},{32,0},{1,33},{33,1},{2,34},{34,2},{3,35},{35,3},{4,36},{36... | collective-permute-start | bytes 393224 | tf_op jit(solution)/shard_map/ppermute | solution.py:23
  59.7 5.7 %collective-permute-start.12 = (bf16[16,16,256]{2,1,0:T(8,128)(2,1)S(1)}, bf16[16,16,256]{2,1,0:T(8,128)(2,1)S(1)}, u32[]{:S(2)}, u32[]{:S(2)}) collective-permute-start(bf16[16,16,256]{2,1,0:T(8,128)(2,1)S(1)} %get-tuple-element.108), channel_id=1, source_target_pairs={{0,64},{64,0},{1,65},{65,1},{2,66},{66,2},{3,67},{67,3},{4,68},{68... | collective-permute-start | bytes 393224 | tf_op jit(solution)/shard_map/ppermute | solution.py:25
  60.3 6.2 %collective-permute-start.13 = (bf16[16,16,256]{2,1,0:T(8,128)(2,1)S(1)}, bf16[16,16,256]{2,1,0:T(8,128)(2,1)S(1)}, u32[]{:S(2)}, u32[]{:S(2)}) collective-permute-start(bf16[16,16,256]{2,1,0:T(8,128)(2,1)S(1)} %get-tuple-element.109), channel_id=1, source_target_pairs={{0,96},{96,0},{32,64},{64,32},{1,97},{97,1},{33,65},{65,33},{2,98}... | collective-permute-start | bytes 393224 | tf_op jit(solution)/shard_map/ppermute | solution.py:26
  66.4 2.5 %collective-permute-start.14 = (bf16[96,16,256]{2,1,0:T(8,128)(2,1)S(1)}, bf16[96,16,256]{2,1,0:T(8,128)(2,1)S(1)}, u32[]{:S(2)}, u32[]{:S(2)}) collective-permute-start(bf16[96,16,256]{2,1,0:T(8,128)(2,1)S(1)} %get-tuple-element.110), channel_id=1, source_target_pairs={{0,1},{1,0},{2,3},{3,2},{4,5},{5,4},{6,7},{7,6},{8,9},{9,8},{10,11... | collective-permute-start | bytes 2359304 | tf_op jit(solution)/shard_map/ppermute | solution.py:198
  66.5 2.4 %collective-permute-start.15 = (bf16[16,16,256]{2,1,0:T(8,128)(2,1)S(1)}, bf16[16,16,256]{2,1,0:T(8,128)(2,1)S(1)}, u32[]{:S(2)}, u32[]{:S(2)}) collective-permute-start(bf16[16,16,256]{2,1,0:T(8,128)(2,1)S(1)} %get-tuple-element.115), channel_id=1, source_target_pairs={{0,1},{1,0},{2,3},{3,2},{4,5},{5,4},{6,7},{7,6},{8,9},{9,8},{10,11... | collective-permute-start | bytes 393224 | tf_op jit(solution)/shard_map/ppermute | solution.py:198

commit v11 on v10

--- a/solution.py
+++ b/solution.py
@@ -47,10 +47,21 @@
     )
 
 
+LANES = 128
+
+
+def pick_matrix(me, first, count):
+    shape = (4 * LANES, count * LANES)
+    source = lax.broadcasted_iota(jnp.int32, shape, 0)
+    col = lax.broadcasted_iota(jnp.int32, (1, shape[1]), 1)
+    owner = jnp.bitwise_xor(me, col // LANES + first)
+    wanted = 64 * ((col % LANES) // 16) + 16 * owner + col % 16
+    return jnp.where(source == wanted, 1.0, 0.0).astype(BF)
+
+
 def select_channels(pos_ref, x_ref, *rest):
     *o_refs, held, sems = rest
-    lanes = 128
-    group = lanes * len(o_refs)
+    group = 4 * LANES
     pieces = sems.shape[0]
     each = x_ref.shape[0] // pieces
     copies = []
@@ -58,25 +69,27 @@
         part = pl.ds(n * each, each)
         copies.append(pltpu.make_async_copy(x_ref.at[part, :], held.at[part, :], sems.at[n]))
         copies[n].start()
-    source = lax.broadcasted_iota(jnp.int32, (group, group), 0)
-    col = lax.broadcasted_iota(jnp.int32, (1, group), 1)
-    owner = jnp.bitwise_xor(pos_ref[0], col // lanes)
-    wanted = 64 * ((col % lanes) // 16) + 16 * owner + col % 16
-    picks = jnp.where(source == wanted, 1.0, 0.0).astype(BF)
+    picks = pick_matrix(pos_ref[0], 1, len(o_refs))
     for n in range(pieces):
         copies[n].wait()
         rows = slice(n * each, (n + 1) * each)
         for p in range(x_ref.shape[1] // group):
             taken = jnp.dot(held[rows, p * group : (p + 1) * group], picks, preferred_element_type=F32).astype(BF)
             for k, o_ref in enumerate(o_refs):
-                o_ref[rows, p * lanes : (p + 1) * lanes] = taken[:, k * lanes : (k + 1) * lanes]
-
-
-def turn_pixels(pos_ref, x0, x1, x2, x3, o_ref, edge_ref, held):
-    pixels, width = x0.shape
-    for k, x in enumerate((x0, x1, x2, x3)):
+                o_ref[rows, p * LANES : (p + 1) * LANES] = taken[:, k * LANES : (k + 1) * LANES]
+
+
+def turn_pixels(pos_ref, x_ref, x1, x2, x3, o_ref, edge_ref, held):
+    pixels, width = x1.shape
+    mine = pl.multiple_of((pos_ref[0] // 2) * pixels, 16)
+    group = 4 * LANES
+    picks = pick_matrix(pos_ref[0], 0, 1)
+    for p in range(width // LANES):
+        taken = jnp.dot(x_ref[:, p * group : (p + 1) * group], picks, preferred_element_type=F32).astype(BF)
+        held[pos_ref[0] % 2, pl.ds(mine, pixels), p * LANES : (p + 1) * LANES] = taken
+    for k, x in ((1, x1), (2, x2), (3, x3)):
         s = jnp.bitwise_xor(pos_ref[0], k)
-        held[s % 2, pl.ds((s // 2) * pixels, pixels), :] = x[...]
+        held[s % 2, pl.ds(pl.multiple_of((s // 2) * pixels, 16), pixels), :] = x[...]
     eye = (
         lax.broadcasted_iota(jnp.int32, (width, width), 0)
         == lax.broadcasted_iota(jnp.int32, (width, width), 1)
@@ -203,7 +216,7 @@
     block = jax.ShapeDtypeStruct((pixels, chans // 4), BF)
     return call(
         select_channels,
-        [block] * 4,
+        [block] * 3,
         1,
         0,
         pixels * chans * chans,
@@ -215,7 +228,7 @@
     )(pos, pltpu.with_memory_space_constraint(centre, pltpu.HBM))
 
 
-def turn(pos, got):
+def turn(pos, centre, got):
     pixels, width = got[0].shape
     return call(
         turn_pixels,
@@ -230,7 +243,7 @@
         12,
         [pltpu.VMEM((2, 2 * pixels, width), BF)],
         name="turn",
-    )(pos, *got)
+    )(pos, centre, *got)
 
 
 def split_pair(pos, kept, got):
@@ -528,21 +541,20 @@
     def rows_of(rate):
         return pl.multiple_of(jnp.where(low == 0, (SIDE - rate) * SIDE, 0), 16)
 
-    pre[...] = own_ref[...]
+    part = blocks(col_ref[:whole, :].astype(F32))
+    rank = rank_of(part.shape, theirs)
+    pre[2] = own_ref[2] + flat(jnp.where(rank < RATE_C, part, 0.0))
+    pre[0] = own_ref[0] + flat(turned_by(jnp.where(rank >= RATE_C, part, 0.0), RATE_A, theirs))
+    part = blocks(col_ref[whole:, :].astype(F32))
+    rank = rank_of(part.shape, theirs)
+    half = RATE_B * SIDE
+    pre[1, :half, :] = own_ref[1, :half, :] + flat(jnp.where(rank < RATE_B, part, 0.0))
+    pre[1, half:, :] = own_ref[1, half:, :] + flat(roll_cols(jnp.where(rank >= RATE_B, part, 0.0), RATE_B))
     first = 0
     for index, rate in ((2, RATE_C), (1, RATE_B), (0, RATE_A)):
         lead = rate * SIDE
         pre[index, pl.ds(rows_of(rate), lead), :] += row_ref[first : first + lead, :].astype(F32)
         first += lead
-
-    part = blocks(col_ref[:whole, :].astype(F32))
-    rank = rank_of(part.shape, theirs)
-    pre[2] += flat(jnp.where(rank < RATE_C, part, 0.0))
-    pre[0] += flat(turned_by(jnp.where(rank >= RATE_C, part, 0.0), RATE_A, theirs))
-    part = blocks(col_ref[whole:, :].astype(F32))
-    rank = rank_of(part.shape, theirs)
-    pre[1, : RATE_B * SIDE, :] += flat(jnp.where(rank < RATE_B, part, 0.0))
-    pre[1, RATE_B * SIDE :, :] += flat(roll_cols(jnp.where(rank >= RATE_B, part, 0.0), RATE_B))
 
     part = blocks(diag_ref[: RATE_C * SIDE, :].astype(F32))
     rank = rank_of(part.shape, theirs)
@@ -621,12 +633,12 @@
     weights = [pltpu.with_memory_space_constraint(w, pltpu.HBM) for w in (w_rate_a, w_rate_b, w_rate_c)]
     picked = pick(pos, centre)
     centre, *picked = lax.optimization_barrier((centre, *picked))
-    got = [picked[0]] + [flip(picked[k], k) for k in (1, 2, 3)]
+    got = [flip(picked[k - 1], k) for k in (1, 2, 3)]
     part, *parts = outer(pos, centre, *weights)
     part, got = lax.optimization_barrier((part, got))
     to_row, to_col, to_diag = parts
     parts = [flip(to_row, 2), flip(to_col, 1), flip(to_diag, 3)]
-    turned = turn(pos, got)
+    turned = turn(pos, centre, got)
     joined0, slope0, own = inner(pos, centre, part, w_point, *weights)
     parts, joined0, own, turned = lax.optimization_barrier((parts, joined0, own, turned))
     joined, g_proj, delta3 = merge(

time: 93.2 us -> 93.1 us (level)
  transfers between devices with their start and end apart: 16 -> 16, of which waited for: 11 -> 11; matrix products, arithmetic and copies ran while one was open for 0% -> 0% of each run, Pallas kernels for 24% -> 25%
where the time goes in v11:
time: 93.1 us; the launch traced here: 93 us
  Pallas kernels  29.4 us (32%)
  blocking collectives  22.3 us (24%)
  waiting for transfers between devices  22.2 us (24%)
  starting transfers between devices  18.7 us (20%)
    all_to_all x1, blocking collectives, reduce_slots(): total = lax.all_to_all(total, ('dp_0', 'dp_1'), 0, 0, tiled=True)  22.3 us
    ppermute x4, starting transfers between devices, flip(): return lax.ppermute(x, 'col', [(0, 1), (1, 0)])  9.84 us
    pallas_call x1, Pallas kernels, outer(): call(outer_parts, [jax.ShapeDtypeStruct(*s) for s in shapes], 1, 1, 2 * p...  8.67 us
    ppermute x4, waiting for transfers between devices, flip(): return lax.ppermute(x, ('row', 'col'), [(0, 3), (3, 0), (1, 2), (2, 1)])  8.26 us
    ppermute x4, waiting for transfers between devices, flip(): return lax.ppermute(x, 'col', [(0, 1), (1, 0)])  8.26 us
    pallas_call x1, Pallas kernels, inner(): call(inner_parts, [jax.ShapeDtypeStruct((pixels, width), BF), jax.ShapeDt...  6.14 us
    ppermute x4, starting transfers between devices, flip(): return lax.ppermute(x, ('row', 'col'), [(0, 3), (3, 0), (1, 2), (2, 1)])  4.5 us
    ppermute x4, starting transfers between devices, flip(): return lax.ppermute(x, 'row', [(0, 1), (1, 0)])  3.21 us
  transfers between devices with their start and end apart: 16, of which 11 were waited for; matrix products, arithmetic and copies ran while one was open for 0% of the time, Pallas kernels for 25%

profile of v11, /device:TPU:0, one launch (start us, length us, event | category | flops | bytes accessed | tf_op | source)
XLA Modules:
  0.0 93.0 jit_solution(4856095776789092925)
XLA Ops:
  0.1 2.5 %pick.1 = (bf16[576,256]{1,0:T(8,128)(2,1)S(1)}, bf16[576,256]{1,0:T(8,128)(2,1)S(1)}, bf16[576,256]{1,0:T(8,128)(2,1)S(1)}) custom-call(s32[6]{0:T(128)S(1)} %stack.27.pos_ref, bf16[576,1024]{1,0:T(8,128)(2,1)} %bitcast.8), custom_call_target="tpu_custom_call" | custom-call | flops 603979776 | bytes 2359296 | tf_op jit(solution)/shard_map/pick/pallas_call | solution.py:217
  2.6 3.2 %collective-permute-start.3 = (bf16[576,256]{1,0:T(8,128)(2,1)S(1)}, bf16[576,256]{1,0:T(8,128)(2,1)S(1)}, u32[]{:S(2)}, u32[]{:S(2)}) collective-permute-start(bf16[576,256]{1,0:T(8,128)(2,1)S(1)} %get-tuple-element.65), channel_id=1, source_target_pairs={{0,32},{32,0},{1,33},{33,1},{2,34},{34,2},{3,35},{35,3},{4,36},{36... | collective-permute-start | bytes 884744 | tf_op jit(solution)/shard_map/ppermute | solution.py:23
  5.8 0.6 collective-permute-start.4
  6.4 0.5 collective-permute-start.5
  7.0 8.7 %outer.1 = (f32[3,576,256]{2,1,0:T(8,128)S(1)}, bf16[864,256]{1,0:T(8,128)(2,1)S(1)}, bf16[864,256]{1,0:T(8,128)(2,1)S(1)}, bf16[576,256]{1,0:T(8,128)(2,1)S(1)}) custom-call(s32[6]{0:T(128)S(1)} %stack.27.pos_ref, bf16[576,1024]{1,0:T(8,128)(2,1)S(1)} %bitcast.9, bf16[3,3,1024,256]{3,2,1,0:T(8,128)(2,1)} %wc_ref.3, bf16[3,3,1024,256]{3,2,1,0:T(8,128)(2,1)} %wb_ref.3, ...), custom_call_target="tpu_custom_call" | custom-call | flops 4227858432 | bytes 10485760 | tf_op jit(solution)/shard_map/outer/pallas_call | solution.py:487
  15.7 1.5 %collective-permute-start = (bf16[864,256]{1,0:T(8,128)(2,1)S(1)}, bf16[864,256]{1,0:T(8,128)(2,1)S(1)}, u32[]{:S(2)}, u32[]{:S(2)}) collective-permute-start(bf16[864,256]{1,0:T(8,128)(2,1)S(1)} %get-tuple-element.61), channel_id=1, source_target_pairs={{0,64},{64,0},{1,65},{65,1},{2,66},{66,2},{3,67},{67,3},{4,68},{68... | collective-permute-start | bytes 1327112 | tf_op jit(solution)/shard_map/ppermute | solution.py:25
  17.1 2.7 %collective-permute-start.1 = (bf16[864,256]{1,0:T(8,128)(2,1)S(1)}, bf16[864,256]{1,0:T(8,128)(2,1)S(1)}, u32[]{:S(2)}, u32[]{:S(2)}) collective-permute-start(bf16[864,256]{1,0:T(8,128)(2,1)S(1)} %get-tuple-element.62), channel_id=1, source_target_pairs={{0,32},{32,0},{1,33},{33,1},{2,34},{34,2},{3,35},{35,3},{4,36},{36... | collective-permute-start | bytes 1327112 | tf_op jit(solution)/shard_map/ppermute | solution.py:23
  19.9 0.6 collective-permute-start.2
  20.7 1.8 %turn.1 = (bf16[2,256,1152]{2,1,0:T(8,128)(2,1)S(1)}, bf16[2,256,384]{2,1,0:T(8,128)(2,1)S(1)}) custom-call(s32[6]{0:T(128)S(1)} %stack.27.pos_ref, bf16[576,1024]{1,0:T(8,128)(2,1)S(1)} %bitcast.10, bf16[576,256]{1,0:T(8,128)(2,1)S(1)} %collective-permute-done.3.x1, bf16[576,256]{1,0:T(8,128)(2,1)S(1)} %collective-permute-done.4.x2, ...), custom_call_target="tpu_custom_call" | custom-call | flops 301989888 | bytes 2359296 | tf_op jit(solution)/shard_map/turn/pallas_call | solution.py:233
  22.5 6.1 %inner.1 = (bf16[576,256]{1,0:T(8,128)(2,1)S(1)}, f32[576,256]{1,0:T(8,128)S(1)}, f32[3,576,256]{2,1,0:T(8,128)S(1)}) custom-call(s32[6]{0:T(128)S(1)} %stack.27.pos_ref, bf16[576,1024]{1,0:T(8,128)(2,1)S(1)} %bitcast.11, f32[3,576,256]{2,1,0:T(8,128)S(1)} %get-tuple-element.68.part_ref, bf16[1024,256]{1,0:T(8,128)(2,1)S(1)} %copy-done.2, ...), custom_call_target="tpu_custom_call" | custom-call | flops 3019898880 | bytes 10485760 | tf_op jit(solution)/shard_map/inner/pallas_call | solution.py:510
  28.7 1.3 %collective-permute-done.2.diag_ref = bf16[576,256]{1,0:T(8,128)(2,1)S(1)} collective-permute-done((bf16[576,256]{1,0:T(8,128)(2,1)S(1)}, bf16[576,256]{1,0:T(8,128)(2,1)S(1)}, u32[]{:S(2)}, u32[]{:S(2)}) %collective-permute-start.2) | collective-permute-done | bytes 294944 | tf_op jit(solution)/shard_map/ppermute | solution.py:26
  30.1 8.3 %collective-permute-done.1.col_ref = bf16[864,256]{1,0:T(8,128)(2,1)S(1)} collective-permute-done((bf16[864,256]{1,0:T(8,128)(2,1)S(1)}, bf16[864,256]{1,0:T(8,128)(2,1)S(1)}, u32[]{:S(2)}, u32[]{:S(2)}) %collective-permute-start.1) | collective-permute-done | bytes 442400 | tf_op jit(solution)/shard_map/ppermute | solution.py:23
  38.4 2.0 %merge.1 = (bf16[576,1024]{1,0:T(8,128)(2,1)S(1)}, bf16[576,256]{1,0:T(8,128)(2,1)S(1)}, bf16[576,256]{1,0:T(8,128)(2,1)S(1)}) custom-call(s32[6]{0:T(128)S(1)} %stack.27.pos_ref, bf16[576,256]{1,0:T(8,128)(2,1)S(1)} %get-tuple-element.76.joined0_ref, f32[3,576,256]{2,1,0:T(8,128)S(1)} %get-tuple-element.77.own_ref, ...), custom_call_target="tpu_custom_call" | custom-call | flops 452984832 | bytes 6291456 | tf_op jit(solution)/shard_map/merge/pallas_call | solution.py:595
  40.4 2.8 %collective-permute-start.10 = (bf16[576,256]{1,0:T(8,128)(2,1)S(1)}, bf16[576,256]{1,0:T(8,128)(2,1)S(1)}, u32[]{:S(2)}, u32[]{:S(2)}) collective-permute-start(bf16[576,256]{1,0:T(8,128)(2,1)S(1)} %get-tuple-element.92.d0), channel_id=1, source_target_pairs={{0,96},{96,0},{32,64},{64,32},{1,97},{97,1},{33,65},{65,33},{2,98}... | collective-permute-start | bytes 884744 | tf_op jit(solution)/shard_map/ppermute | solution.py:26
  43.3 0.8 collective-permute-start.8
  44.1 0.5 collective-permute-start.9
  44.6 2.5 %pair.1 = (f32[1024,256]{1,0:T(8,128)S(1)}, bf16[512,256]{1,0:T(8,128)(2,1)S(1)}, bf16[512,256]{1,0:T(8,128)(2,1)S(1)}) custom-call(s32[6]{0:T(128)S(1)} %stack.27.pos_ref, bf16[576,1024]{1,0:T(8,128)(2,1)S(1)} %get-tuple-element.81.joined_ref, bf16[576,256]{1,0:T(8,128)(2,1)S(1)} %get-tuple-element.82.g_ref, bf16[576,1024]{1,0:T(8,128)(2,1)S(1)} %bitcast.12, ...), custom_call_target="tpu_custom_call" | custom-call | flops 603979776 | bytes 4194304 | tf_op jit(solution)/shard_map/pair/pallas_call | solution.py:649
  47.8 1.0 %collective-permute-done.6.got0 = bf16[512,256]{1,0:T(8,128)(2,1)S(1)} collective-permute-done((bf16[512,256]{1,0:T(8,128)(2,1)S(1)}, bf16[512,256]{1,0:T(8,128)(2,1)S(1)}, u32[]{:S(2)}, u32[]{:S(2)}) %collective-permute-start.6) | collective-permute-done | bytes 262176 | tf_op jit(solution)/shard_map/ppermute | solution.py:211
  49.1 0.7 rows.1
  49.8 5.9 %collective-permute-done.10.d3 = bf16[576,256]{1,0:T(8,128)(2,1)S(1)} collective-permute-done((bf16[576,256]{1,0:T(8,128)(2,1)S(1)}, bf16[576,256]{1,0:T(8,128)(2,1)S(1)}, u32[]{:S(2)}, u32[]{:S(2)}) %collective-permute-start.10) | collective-permute-done | bytes 294944 | tf_op jit(solution)/shard_map/ppermute | solution.py:26
  55.7 0.7 collective-permute-done.9.d2
  56.4 3.1 %collective-permute-start.11 = (bf16[16,16,256]{2,1,0:T(8,128)(2,1)S(1)}, bf16[16,16,256]{2,1,0:T(8,128)(2,1)S(1)}, u32[]{:S(2)}, u32[]{:S(2)}) collective-permute-start(bf16[16,16,256]{2,1,0:T(8,128)(2,1)S(1)} %get-tuple-element.101), channel_id=1, source_target_pairs={{0,32},{32,0},{1,33},{33,1},{2,34},{34,2},{3,35},{35,3},{4,36},{36... | collective-permute-start | bytes 393224 | tf_op jit(solution)/shard_map/ppermute | solution.py:23
  59.5 0.6 collective-permute-start.12
  60.2 0.5 collective-permute-start.13
  60.7 3.1 %taps.1 = (f32[96,16,256]{2,1,0:T(8,128)S(1)}, bf16[96,16,256]{2,1,0:T(8,128)(2,1)S(1)}) custom-call(s32[6]{0:T(128)S(1)} %stack.27.pos_ref, s32[176]{0:T(256)S(1)} %fusion.1.place_ref, bf16[576,256]{1,0:T(8,128)(2,1)S(1)} %get-tuple-element.92.d0, bf16[576,256]{1,0:T(8,128)(2,1)S(1)} %collective-permute-done.8.d1, ...), custom_call_target="tpu_custom_call" | custom-call | flops 2113929216 | bytes 8388608 | tf_op jit(solution)/shard_map/taps/pallas_call | solution.py:282
  63.8 1.4 %collective-permute-done.12 = bf16[16,16,256]{2,1,0:T(8,128)(2,1)S(1)} collective-permute-done((bf16[16,16,256]{2,1,0:T(8,128)(2,1)S(1)}, bf16[16,16,256]{2,1,0:T(8,128)(2,1)S(1)}, u32[]{:S(2)}, u32[]{:S(2)}) %collective-permute-start.12) | collective-permute-done | bytes 131104 | tf_op jit(solution)/shard_map/ppermute | solution.py:25
  65.3 1.1 %collective-permute-done.13 = bf16[16,16,256]{2,1,0:T(8,128)(2,1)S(1)} collective-permute-done((bf16[16,16,256]{2,1,0:T(8,128)(2,1)S(1)}, bf16[16,16,256]{2,1,0:T(8,128)(2,1)S(1)}, u32[]{:S(2)}, u32[]{:S(2)}) %collective-permute-start.13) | collective-permute-done | bytes 131104 | tf_op jit(solution)/shard_map/ppermute | solution.py:26
  66.4 0.6 collective-permute-start.15
  67.0 1.8 %collective-permute-done.15.other_ref = bf16[16,16,256]{2,1,0:T(8,128)(2,1)S(1)} collective-permute-done((bf16[16,16,256]{2,1,0:T(8,128)(2,1)S(1)}, bf16[16,16,256]{2,1,0:T(8,128)(2,1)S(1)}, u32[]{:S(2)}, u32[]{:S(2)}) %collective-permute-start.15) | collective-permute-done | bytes 131104 | tf_op jit(solution)/shard_map/ppermute | solution.py:211
  68.8 1.1 %owners.1 = bf16[16,96,256]{2,1,0:T(8,128)(2,1)S(1)} custom-call(s32[6]{0:T(128)S(1)} %stack.27.pos_ref, s32[176]{0:T(256)S(1)} %fusion.1.place_ref, f32[96,16,256]{2,1,0:T(8,128)S(1)} %get-tuple-element.98.keep_ref, bf16[96,16,256]{2,1,0:T(8,128)(2,1)S(1)} %collective-permute-done.14.got_ref, f32[16,16,256]{2,1,0:T(8,128)S(1)} %get-tuple-element.110.mine_ref, ...), custom_call_target="tpu_custom_call" | custom-call | flops 393216 | bytes 3145728 | tf_op jit(solution)/shard_map/owners/pallas_call | solution.py:304
  69.9 22.3 %all_to_all.5.r_ref = bf16[16,96,256]{2,1,0:T(8,128)(2,1)S(1)} all-to-all(bf16[16,96,256]{2,1,0:T(8,128)(2,1)S(1)} %owners.1), channel_id=1, replica_groups=mesh['row'=2,'col'=2,'dp_0'=4,'dp_1'=4,'dp_2'=2] {'dp_0','dp_1'}, dimensions={0} | all-to-all | bytes 1572864 | tf_op jit(solution)/shard_map/all_to_all | solution.py:315
  92.2 0.8 last.1
  (24 shorter events, 1.5 us)
Async XLA Ops:
  0.0 7.0 %copy-start = (bf16[1,24,24,1024]{3,2,1,0:T(8,128)(2,1)S(1)}, bf16[1,24,24,1024]{3,2,1,0:T(8,128)(2,1)}, u32[]{:S(2)}) copy-start(bf16[1,24,24,1024]{3,2,1,0:T(8,128)(2,1)} %param.8) | copy-start | bytes 3538948
  2.6 17.2 %collective-permute-start.3 = (bf16[576,256]{1,0:T(8,128)(2,1)S(1)}, bf16[576,256]{1,0:T(8,128)(2,1)S(1)}, u32[]{:S(2)}, u32[]{:S(2)}) collective-permute-start(bf16[576,256]{1,0:T(8,128)(2,1)S(1)} %get-tuple-element.65), channel_id=1, source_target_pairs={{0,32},{32,0},{1,33},{33,1},{2,34},{34,2},{3,35},{35,3},{4,36},{36... | collective-permute-start | bytes 884744 | tf_op jit(solution)/shard_map/ppermute | solution.py:23
  5.8 14.8 %collective-permute-start.4 = (bf16[576,256]{1,0:T(8,128)(2,1)S(1)}, bf16[576,256]{1,0:T(8,128)(2,1)S(1)}, u32[]{:S(2)}, u32[]{:S(2)}) collective-permute-start(bf16[576,256]{1,0:T(8,128)(2,1)S(1)} %get-tuple-element.66), channel_id=1, source_target_pairs={{0,64},{64,0},{1,65},{65,1},{2,66},{66,2},{3,67},{67,3},{4,68},{68... | collective-permute-start | bytes 884744 | tf_op jit(solution)/shard_map/ppermute | solution.py:25
  6.4 14.2 %collective-permute-start.5 = (bf16[576,256]{1,0:T(8,128)(2,1)S(1)}, bf16[576,256]{1,0:T(8,128)(2,1)S(1)}, u32[]{:S(2)}, u32[]{:S(2)}) collective-permute-start(bf16[576,256]{1,0:T(8,128)(2,1)S(1)} %get-tuple-element.67), channel_id=1, source_target_pairs={{0,96},{96,0},{32,64},{64,32},{1,97},{97,1},{33,65},{65,33},{2,98}... | collective-permute-start | bytes 884744 | tf_op jit(solution)/shard_map/ppermute | solution.py:26
  15.7 6.8 %copy-start.2 = (bf16[1024,256]{1,0:T(8,128)(2,1)S(1)}, bf16[1024,256]{1,0:T(8,128)(2,1)}, u32[]{:S(2)}) copy-start(bf16[1024,256]{1,0:T(8,128)(2,1)} %wp_ref.3) | copy-start | bytes 1572868
  15.7 14.5 %collective-permute-start = (bf16[864,256]{1,0:T(8,128)(2,1)S(1)}, bf16[864,256]{1,0:T(8,128)(2,1)S(1)}, u32[]{:S(2)}, u32[]{:S(2)}) collective-permute-start(bf16[864,256]{1,0:T(8,128)(2,1)S(1)} %get-tuple-element.61), channel_id=1, source_target_pairs={{0,64},{64,0},{1,65},{65,1},{2,66},{66,2},{3,67},{67,3},{4,68},{68... | collective-permute-start | bytes 1327112 | tf_op jit(solution)/shard_map/ppermute | solution.py:25
  17.1 21.3 %collective-permute-start.1 = (bf16[864,256]{1,0:T(8,128)(2,1)S(1)}, bf16[864,256]{1,0:T(8,128)(2,1)S(1)}, u32[]{:S(2)}, u32[]{:S(2)}) collective-permute-start(bf16[864,256]{1,0:T(8,128)(2,1)S(1)} %get-tuple-element.62), channel_id=1, source_target_pairs={{0,32},{32,0},{1,33},{33,1},{2,34},{34,2},{3,35},{35,3},{4,36},{36... | collective-permute-start | bytes 1327112 | tf_op jit(solution)/shard_map/ppermute | solution.py:23
  19.9 10.1 %collective-permute-start.2 = (bf16[576,256]{1,0:T(8,128)(2,1)S(1)}, bf16[576,256]{1,0:T(8,128)(2,1)S(1)}, u32[]{:S(2)}, u32[]{:S(2)}) collective-permute-start(bf16[576,256]{1,0:T(8,128)(2,1)S(1)} %get-tuple-element.63), channel_id=1, source_target_pairs={{0,96},{96,0},{32,64},{64,32},{1,97},{97,1},{33,65},{65,33},{2,98}... | collective-permute-start | bytes 884744 | tf_op jit(solution)/shard_map/ppermute | solution.py:26
  22.5 15.9 %copy-start.1 = (bf16[1024,256]{1,0:T(8,128)(2,1)S(1)}, bf16[1024,256]{1,0:T(8,128)(2,1)}, u32[]{:S(2)}) copy-start(bf16[1024,256]{1,0:T(8,128)(2,1)} %wp_ref.5) | copy-start | bytes 1572868
  22.5 15.9 %copy-start.3 = (bf16[1,24,24,256]{3,2,1,0:T(8,128)(2,1)S(1)}, bf16[1,24,24,256]{3,2,1,0:T(8,128)(2,1)}, u32[]{:S(2)}) copy-start(bf16[1,24,24,256]{3,2,1,0:T(8,128)(2,1)} %param.9) | copy-start | bytes 884740
  40.4 15.3 %collective-permute-start.10 = (bf16[576,256]{1,0:T(8,128)(2,1)S(1)}, bf16[576,256]{1,0:T(8,128)(2,1)S(1)}, u32[]{:S(2)}, u32[]{:S(2)}) collective-permute-start(bf16[576,256]{1,0:T(8,128)(2,1)S(1)} %get-tuple-element.92.d0), channel_id=1, source_target_pairs={{0,96},{96,0},{32,64},{64,32},{1,97},{97,1},{33,65},{65,33},{2,98}... | collective-permute-start | bytes 884744 | tf_op jit(solution)/shard_map/ppermute | solution.py:26
  43.3 12.5 %collective-permute-start.8 = (bf16[576,256]{1,0:T(8,128)(2,1)S(1)}, bf16[576,256]{1,0:T(8,128)(2,1)S(1)}, u32[]{:S(2)}, u32[]{:S(2)}) collective-permute-start(bf16[576,256]{1,0:T(8,128)(2,1)S(1)} %get-tuple-element.92.d0), channel_id=1, source_target_pairs={{0,32},{32,0},{1,33},{33,1},{2,34},{34,2},{3,35},{35,3},{4,36},{36... | collective-permute-start | bytes 884744 | tf_op jit(solution)/shard_map/ppermute | solution.py:23
  44.1 12.4 %collective-permute-start.9 = (bf16[576,256]{1,0:T(8,128)(2,1)S(1)}, bf16[576,256]{1,0:T(8,128)(2,1)S(1)}, u32[]{:S(2)}, u32[]{:S(2)}) collective-permute-start(bf16[576,256]{1,0:T(8,128)(2,1)S(1)} %get-tuple-element.92.d0), channel_id=1, source_target_pairs={{0,64},{64,0},{1,65},{65,1},{2,66},{66,2},{3,67},{67,3},{4,68},{68... | collective-permute-start | bytes 884744 | tf_op jit(solution)/shard_map/ppermute | solution.py:25
  44.6 3.1 %copy-start.4 = (s32[176]{0:T(256)S(1)}, s32[176]{0:T(256)}, u32[]{:S(2)}) copy-start(s32[176]{0:T(256)} %param.15) | copy-start | bytes 2116
  47.1 1.6 %collective-permute-start.6 = (bf16[512,256]{1,0:T(8,128)(2,1)S(1)}, bf16[512,256]{1,0:T(8,128)(2,1)S(1)}, u32[]{:S(2)}, u32[]{:S(2)}) collective-permute-start(bf16[512,256]{1,0:T(8,128)(2,1)S(1)} %get-tuple-element.85), channel_id=1, source_target_pairs={{0,1},{1,0},{2,3},{3,2},{4,5},{5,4},{6,7},{7,6},{8,9},{9,8},{10,11... | collective-permute-start | bytes 786440 | tf_op jit(solution)/shard_map/ppermute | solution.py:211
  47.2 1.9 %collective-permute-start.7 = (bf16[512,256]{1,0:T(8,128)(2,1)S(1)}, bf16[512,256]{1,0:T(8,128)(2,1)S(1)}, u32[]{:S(2)}, u32[]{:S(2)}) collective-permute-start(bf16[512,256]{1,0:T(8,128)(2,1)S(1)} %get-tuple-element.86), channel_id=1, source_target_pairs={{0,1},{1,0},{2,3},{3,2},{4,5},{5,4},{6,7},{7,6},{8,9},{9,8},{10,11... | collective-permute-start | bytes 786440 | tf_op jit(solution)/shard_map/ppermute | solution.py:211
  56.4 7.4 %collective-permute-start.11 = (bf16[16,16,256]{2,1,0:T(8,128)(2,1)S(1)}, bf16[16,16,256]{2,1,0:T(8,128)(2,1)S(1)}, u32[]{:S(2)}, u32[]{:S(2)}) collective-permute-start(bf16[16,16,256]{2,1,0:T(8,128)(2,1)S(1)} %get-tuple-element.101), channel_id=1, source_target_pairs={{0,32},{32,0},{1,33},{33,1},{2,34},{34,2},{3,35},{35,3},{4,36},{36... | collective-permute-start | bytes 393224 | tf_op jit(solution)/shard_map/ppermute | solution.py:23
  59.5 5.7 %collective-permute-start.12 = (bf16[16,16,256]{2,1,0:T(8,128)(2,1)S(1)}, bf16[16,16,256]{2,1,0:T(8,128)(2,1)S(1)}, u32[]{:S(2)}, u32[]{:S(2)}) collective-permute-start(bf16[16,16,256]{2,1,0:T(8,128)(2,1)S(1)} %get-tuple-element.102), channel_id=1, source_target_pairs={{0,64},{64,0},{1,65},{65,1},{2,66},{66,2},{3,67},{67,3},{4,68},{68... | collective-permute-start | bytes 393224 | tf_op jit(solution)/shard_map/ppermute | solution.py:25
  60.2 6.2 %collective-permute-start.13 = (bf16[16,16,256]{2,1,0:T(8,128)(2,1)S(1)}, bf16[16,16,256]{2,1,0:T(8,128)(2,1)S(1)}, u32[]{:S(2)}, u32[]{:S(2)}) collective-permute-start(bf16[16,16,256]{2,1,0:T(8,128)(2,1)S(1)} %get-tuple-element.103), channel_id=1, source_target_pairs={{0,96},{96,0},{32,64},{64,32},{1,97},{97,1},{33,65},{65,33},{2,98}... | collective-permute-start | bytes 393224 | tf_op jit(solution)/shard_map/ppermute | solution.py:26
  66.3 2.5 %collective-permute-start.14 = (bf16[96,16,256]{2,1,0:T(8,128)(2,1)S(1)}, bf16[96,16,256]{2,1,0:T(8,128)(2,1)S(1)}, u32[]{:S(2)}, u32[]{:S(2)}) collective-permute-start(bf16[96,16,256]{2,1,0:T(8,128)(2,1)S(1)} %get-tuple-element.104), channel_id=1, source_target_pairs={{0,1},{1,0},{2,3},{3,2},{4,5},{5,4},{6,7},{7,6},{8,9},{9,8},{10,11... | collective-permute-start | bytes 2359304 | tf_op jit(solution)/shard_map/ppermute | solution.py:211
  66.4 2.4 %collective-permute-start.15 = (bf16[16,16,256]{2,1,0:T(8,128)(2,1)S(1)}, bf16[16,16,256]{2,1,0:T(8,128)(2,1)S(1)}, u32[]{:S(2)}, u32[]{:S(2)}) collective-permute-start(bf16[16,16,256]{2,1,0:T(8,128)(2,1)S(1)} %get-tuple-element.109), channel_id=1, source_target_pairs={{0,1},{1,0},{2,3},{3,2},{4,5},{5,4},{6,7},{7,6},{8,9},{9,8},{10,11... | collective-permute-start | bytes 393224 | tf_op jit(solution)/shard_map/ppermute | solution.py:211

commit v12 on v11

--- a/solution.py
+++ b/solution.py
@@ -60,7 +60,7 @@
 
 
 def select_channels(pos_ref, x_ref, *rest):
-    *o_refs, held, sems = rest
+    held, *o_refs, sems = rest
     group = 4 * LANES
     pieces = sems.shape[0]
     each = x_ref.shape[0] // pieces
@@ -216,13 +216,13 @@
     block = jax.ShapeDtypeStruct((pixels, chans // 4), BF)
     return call(
         select_channels,
-        [block] * 3,
+        [jax.ShapeDtypeStruct((pixels, chans), BF)] + [block] * 3,
         1,
         0,
         pixels * chans * chans,
         4 * pixels * chans,
         12,
-        [pltpu.VMEM((pixels, chans), BF), pltpu.SemaphoreType.DMA((2,))],
+        [pltpu.SemaphoreType.DMA((3,))],
         name="pick",
         n_any=1,
     )(pos, pltpu.with_memory_space_constraint(centre, pltpu.HBM))
@@ -631,8 +631,7 @@
     place = place_slots(bucket_slot, core, slot_count)
     centre = image.reshape(pixels, chans)
     weights = [pltpu.with_memory_space_constraint(w, pltpu.HBM) for w in (w_rate_a, w_rate_b, w_rate_c)]
-    picked = pick(pos, centre)
-    centre, *picked = lax.optimization_barrier((centre, *picked))
+    centre, *picked = pick(pos, centre)
     got = [flip(picked[k - 1], k) for k in (1, 2, 3)]
     part, *parts = outer(pos, centre, *weights)
     part, got = lax.optimization_barrier((part, got))

time: 93.1 us -> 93.2 us (level)
  no operation moved by 1% of the time
where the time goes in v12:
time: 93.2 us; the launch traced here: 93.1 us
  Pallas kernels  29.6 us (32%)
  blocking collectives  22.3 us (24%)
  waiting for transfers between devices  22.1 us (24%)
  starting transfers between devices  18.7 us (20%)
    all_to_all x1, blocking collectives, reduce_slots(): total = lax.all_to_all(total, ('dp_0', 'dp_1'), 0, 0, tiled=True)  22.3 us
    ppermute x4, starting transfers between devices, flip(): return lax.ppermute(x, 'col', [(0, 1), (1, 0)])  9.84 us
    pallas_call x1, Pallas kernels, outer(): call(outer_parts, [jax.ShapeDtypeStruct(*s) for s in shapes], 1, 1, 2 * p...  8.69 us
    ppermute x4, waiting for transfers between devices, flip(): return lax.ppermute(x, 'col', [(0, 1), (1, 0)])  8.28 us
    ppermute x4, waiting for transfers between devices, flip(): return lax.ppermute(x, ('row', 'col'), [(0, 3), (3, 0), (1, 2), (2, 1)])  8.22 us
    pallas_call x1, Pallas kernels, inner(): call(inner_parts, [jax.ShapeDtypeStruct((pixels, width), BF), jax.ShapeDt...  6.18 us
    ppermute x4, starting transfers between devices, flip(): return lax.ppermute(x, ('row', 'col'), [(0, 3), (3, 0), (1, 2), (2, 1)])  4.48 us
    ppermute x4, starting transfers between devices, flip(): return lax.ppermute(x, 'row', [(0, 1), (1, 0)])  3.24 us
  transfers between devices with their start and end apart: 16, of which 11 were waited for; matrix products, arithmetic and copies ran while one was open for 0% of the time, Pallas kernels for 25%

profile of v12, /device:TPU:0, one launch (start us, length us, event | category | flops | bytes accessed | tf_op | source)
XLA Modules:
  0.0 93.1 jit_solution(9396162282616430336)
XLA Ops:
  0.1 2.7 %pick.1 = (bf16[576,1024]{1,0:T(8,128)(2,1)S(1)}, bf16[576,256]{1,0:T(8,128)(2,1)S(1)}, bf16[576,256]{1,0:T(8,128)(2,1)S(1)}, bf16[576,256]{1,0:T(8,128)(2,1)S(1)}) custom-call(s32[6]{0:T(128)S(1)} %stack.27.pos_ref, bf16[576,1024]{1,0:T(8,128)(2,1)} %bitcast.9), custom_call_target="tpu_custom_call" | custom-call | flops 603979776 | bytes 2359296 | tf_op jit(solution)/shard_map/pick/pallas_call | solution.py:217
  2.8 3.2 %collective-permute-start.3 = (bf16[576,256]{1,0:T(8,128)(2,1)S(1)}, bf16[576,256]{1,0:T(8,128)(2,1)S(1)}, u32[]{:S(2)}, u32[]{:S(2)}) collective-permute-start(bf16[576,256]{1,0:T(8,128)(2,1)S(1)} %get-tuple-element.59), channel_id=1, source_target_pairs={{0,32},{32,0},{1,33},{33,1},{2,34},{34,2},{3,35},{35,3},{4,36},{36... | collective-permute-start | bytes 884744 | tf_op jit(solution)/shard_map/ppermute | solution.py:23
  5.9 0.6 collective-permute-start.4
  6.5 0.6 collective-permute-start.5
  7.1 8.7 %outer.1 = (f32[3,576,256]{2,1,0:T(8,128)S(1)}, bf16[864,256]{1,0:T(8,128)(2,1)S(1)}, bf16[864,256]{1,0:T(8,128)(2,1)S(1)}, bf16[576,256]{1,0:T(8,128)(2,1)S(1)}) custom-call(s32[6]{0:T(128)S(1)} %stack.27.pos_ref, bf16[576,1024]{1,0:T(8,128)(2,1)S(1)} %get-tuple-element.54.x_ref, bf16[3,3,1024,256]{3,2,1,0:T(8,128)(2,1)} %wc_ref.3, ...), custom_call_target="tpu_custom_call" | custom-call | flops 4227858432 | bytes 10485760 | tf_op jit(solution)/shard_map/outer/pallas_call | solution.py:487
  15.8 1.5 %collective-permute-start = (bf16[864,256]{1,0:T(8,128)(2,1)S(1)}, bf16[864,256]{1,0:T(8,128)(2,1)S(1)}, u32[]{:S(2)}, u32[]{:S(2)}) collective-permute-start(bf16[864,256]{1,0:T(8,128)(2,1)S(1)} %get-tuple-element.55), channel_id=1, source_target_pairs={{0,64},{64,0},{1,65},{65,1},{2,66},{66,2},{3,67},{67,3},{4,68},{68... | collective-permute-start | bytes 1327112 | tf_op jit(solution)/shard_map/ppermute | solution.py:25
  17.3 2.7 %collective-permute-start.1 = (bf16[864,256]{1,0:T(8,128)(2,1)S(1)}, bf16[864,256]{1,0:T(8,128)(2,1)S(1)}, u32[]{:S(2)}, u32[]{:S(2)}) collective-permute-start(bf16[864,256]{1,0:T(8,128)(2,1)S(1)} %get-tuple-element.56), channel_id=1, source_target_pairs={{0,32},{32,0},{1,33},{33,1},{2,34},{34,2},{3,35},{35,3},{4,36},{36... | collective-permute-start | bytes 1327112 | tf_op jit(solution)/shard_map/ppermute | solution.py:23
  20.0 0.6 collective-permute-start.2
  20.8 1.8 %turn.1 = (bf16[2,256,1152]{2,1,0:T(8,128)(2,1)S(1)}, bf16[2,256,384]{2,1,0:T(8,128)(2,1)S(1)}) custom-call(s32[6]{0:T(128)S(1)} %stack.27.pos_ref, bf16[576,1024]{1,0:T(8,128)(2,1)S(1)} %get-tuple-element.54.x_ref, bf16[576,256]{1,0:T(8,128)(2,1)S(1)} %collective-permute-done.3.x1, bf16[576,256]{1,0:T(8,128)(2,1)S(1)} %collective-permute-done.4.x2, ...), custom_call_target="tpu_custom_call" | custom-call | flops 301989888 | bytes 2359296 | tf_op jit(solution)/shard_map/turn/pallas_call | solution.py:233
  22.6 6.2 %inner.1 = (bf16[576,256]{1,0:T(8,128)(2,1)S(1)}, f32[576,256]{1,0:T(8,128)S(1)}, f32[3,576,256]{2,1,0:T(8,128)S(1)}) custom-call(s32[6]{0:T(128)S(1)} %stack.27.pos_ref, bf16[576,1024]{1,0:T(8,128)(2,1)S(1)} %get-tuple-element.54.x_ref, f32[3,576,256]{2,1,0:T(8,128)S(1)} %get-tuple-element.62.part_ref, bf16[1024,256]{1,0:T(8,128)(2,1)S(1)} %copy-done.1, ...), custom_call_target="tpu_custom_call" | custom-call | flops 3019898880 | bytes 10485760 | tf_op jit(solution)/shard_map/inner/pallas_call | solution.py:510
  28.8 1.3 %collective-permute-done.2.diag_ref = bf16[576,256]{1,0:T(8,128)(2,1)S(1)} collective-permute-done((bf16[576,256]{1,0:T(8,128)(2,1)S(1)}, bf16[576,256]{1,0:T(8,128)(2,1)S(1)}, u32[]{:S(2)}, u32[]{:S(2)}) %collective-permute-start.2) | collective-permute-done | bytes 294944 | tf_op jit(solution)/shard_map/ppermute | solution.py:26
  30.2 8.3 %collective-permute-done.1.col_ref = bf16[864,256]{1,0:T(8,128)(2,1)S(1)} collective-permute-done((bf16[864,256]{1,0:T(8,128)(2,1)S(1)}, bf16[864,256]{1,0:T(8,128)(2,1)S(1)}, u32[]{:S(2)}, u32[]{:S(2)}) %collective-permute-start.1) | collective-permute-done | bytes 442400 | tf_op jit(solution)/shard_map/ppermute | solution.py:23
  38.5 2.0 %merge.1 = (bf16[576,1024]{1,0:T(8,128)(2,1)S(1)}, bf16[576,256]{1,0:T(8,128)(2,1)S(1)}, bf16[576,256]{1,0:T(8,128)(2,1)S(1)}) custom-call(s32[6]{0:T(128)S(1)} %stack.27.pos_ref, bf16[576,256]{1,0:T(8,128)(2,1)S(1)} %get-tuple-element.70.joined0_ref, f32[3,576,256]{2,1,0:T(8,128)S(1)} %get-tuple-element.71.own_ref, ...), custom_call_target="tpu_custom_call" | custom-call | flops 452984832 | bytes 6291456 | tf_op jit(solution)/shard_map/merge/pallas_call | solution.py:595
  40.6 2.8 %collective-permute-start.10 = (bf16[576,256]{1,0:T(8,128)(2,1)S(1)}, bf16[576,256]{1,0:T(8,128)(2,1)S(1)}, u32[]{:S(2)}, u32[]{:S(2)}) collective-permute-start(bf16[576,256]{1,0:T(8,128)(2,1)S(1)} %get-tuple-element.86.d0), channel_id=1, source_target_pairs={{0,96},{96,0},{32,64},{64,32},{1,97},{97,1},{33,65},{65,33},{2,98}... | collective-permute-start | bytes 884744 | tf_op jit(solution)/shard_map/ppermute | solution.py:26
  43.4 0.8 collective-permute-start.8
  44.2 0.6 collective-permute-start.9
  44.7 2.5 %pair.1 = (f32[1024,256]{1,0:T(8,128)S(1)}, bf16[512,256]{1,0:T(8,128)(2,1)S(1)}, bf16[512,256]{1,0:T(8,128)(2,1)S(1)}) custom-call(s32[6]{0:T(128)S(1)} %stack.27.pos_ref, bf16[576,1024]{1,0:T(8,128)(2,1)S(1)} %get-tuple-element.75.joined_ref, bf16[576,256]{1,0:T(8,128)(2,1)S(1)} %get-tuple-element.76.g_ref, bf16[576,1024]{1,0:T(8,128)(2,1)S(1)} %get-tuple-element.54.x_ref, ...), custom_call_target="tpu_custom_call" | custom-call | flops 603979776 | bytes 4194304 | tf_op jit(solution)/shard_map/pair/pallas_call | solution.py:648
  47.9 1.0 %collective-permute-done.6.got0 = bf16[512,256]{1,0:T(8,128)(2,1)S(1)} collective-permute-done((bf16[512,256]{1,0:T(8,128)(2,1)S(1)}, bf16[512,256]{1,0:T(8,128)(2,1)S(1)}, u32[]{:S(2)}, u32[]{:S(2)}) %collective-permute-start.6) | collective-permute-done | bytes 262176 | tf_op jit(solution)/shard_map/ppermute | solution.py:211
  49.3 0.7 rows.1
  50.0 5.8 %collective-permute-done.10.d3 = bf16[576,256]{1,0:T(8,128)(2,1)S(1)} collective-permute-done((bf16[576,256]{1,0:T(8,128)(2,1)S(1)}, bf16[576,256]{1,0:T(8,128)(2,1)S(1)}, u32[]{:S(2)}, u32[]{:S(2)}) %collective-permute-start.10) | collective-permute-done | bytes 294944 | tf_op jit(solution)/shard_map/ppermute | solution.py:26
  55.8 0.7 collective-permute-done.9.d2
  56.5 3.1 %collective-permute-start.11 = (bf16[16,16,256]{2,1,0:T(8,128)(2,1)S(1)}, bf16[16,16,256]{2,1,0:T(8,128)(2,1)S(1)}, u32[]{:S(2)}, u32[]{:S(2)}) collective-permute-start(bf16[16,16,256]{2,1,0:T(8,128)(2,1)S(1)} %get-tuple-element.95), channel_id=1, source_target_pairs={{0,32},{32,0},{1,33},{33,1},{2,34},{34,2},{3,35},{35,3},{4,36},{36... | collective-permute-start | bytes 393224 | tf_op jit(solution)/shard_map/ppermute | solution.py:23
  59.7 0.6 collective-permute-start.12
  60.3 0.5 collective-permute-start.13
  60.8 3.1 %taps.1 = (f32[96,16,256]{2,1,0:T(8,128)S(1)}, bf16[96,16,256]{2,1,0:T(8,128)(2,1)S(1)}) custom-call(s32[6]{0:T(128)S(1)} %stack.27.pos_ref, s32[176]{0:T(256)S(1)} %fusion.1.place_ref, bf16[576,256]{1,0:T(8,128)(2,1)S(1)} %get-tuple-element.86.d0, bf16[576,256]{1,0:T(8,128)(2,1)S(1)} %collective-permute-done.8.d1, ...), custom_call_target="tpu_custom_call" | custom-call | flops 2113929216 | bytes 8388608 | tf_op jit(solution)/shard_map/taps/pallas_call | solution.py:282
  63.9 1.4 %collective-permute-done.12 = bf16[16,16,256]{2,1,0:T(8,128)(2,1)S(1)} collective-permute-done((bf16[16,16,256]{2,1,0:T(8,128)(2,1)S(1)}, bf16[16,16,256]{2,1,0:T(8,128)(2,1)S(1)}, u32[]{:S(2)}, u32[]{:S(2)}) %collective-permute-start.12) | collective-permute-done | bytes 131104 | tf_op jit(solution)/shard_map/ppermute | solution.py:25
  65.4 1.1 %collective-permute-done.13 = bf16[16,16,256]{2,1,0:T(8,128)(2,1)S(1)} collective-permute-done((bf16[16,16,256]{2,1,0:T(8,128)(2,1)S(1)}, bf16[16,16,256]{2,1,0:T(8,128)(2,1)S(1)}, u32[]{:S(2)}, u32[]{:S(2)}) %collective-permute-start.13) | collective-permute-done | bytes 131104 | tf_op jit(solution)/shard_map/ppermute | solution.py:26
  66.5 0.6 collective-permute-start.15
  67.1 1.8 %collective-permute-done.15.other_ref = bf16[16,16,256]{2,1,0:T(8,128)(2,1)S(1)} collective-permute-done((bf16[16,16,256]{2,1,0:T(8,128)(2,1)S(1)}, bf16[16,16,256]{2,1,0:T(8,128)(2,1)S(1)}, u32[]{:S(2)}, u32[]{:S(2)}) %collective-permute-start.15) | collective-permute-done | bytes 131104 | tf_op jit(solution)/shard_map/ppermute | solution.py:211
  68.9 1.1 %owners.1 = bf16[16,96,256]{2,1,0:T(8,128)(2,1)S(1)} custom-call(s32[6]{0:T(128)S(1)} %stack.27.pos_ref, s32[176]{0:T(256)S(1)} %fusion.1.place_ref, f32[96,16,256]{2,1,0:T(8,128)S(1)} %get-tuple-element.92.keep_ref, bf16[96,16,256]{2,1,0:T(8,128)(2,1)S(1)} %collective-permute-done.14.got_ref, f32[16,16,256]{2,1,0:T(8,128)S(1)} %get-tuple-element.104.mine_ref, ...), custom_call_target="tpu_custom_call" | custom-call | flops 393216 | bytes 3145728 | tf_op jit(solution)/shard_map/owners/pallas_call | solution.py:304
  70.0 22.3 %all_to_all.5.r_ref = bf16[16,96,256]{2,1,0:T(8,128)(2,1)S(1)} all-to-all(bf16[16,96,256]{2,1,0:T(8,128)(2,1)S(1)} %owners.1), channel_id=1, replica_groups=mesh['row'=2,'col'=2,'dp_0'=4,'dp_1'=4,'dp_2'=2] {'dp_0','dp_1'}, dimensions={0} | all-to-all | bytes 1572864 | tf_op jit(solution)/shard_map/all_to_all | solution.py:315
  92.3 0.8 last.1
  (22 shorter events, 1.5 us)
Async XLA Ops:
  2.8 17.2 %collective-permute-start.3 = (bf16[576,256]{1,0:T(8,128)(2,1)S(1)}, bf16[576,256]{1,0:T(8,128)(2,1)S(1)}, u32[]{:S(2)}, u32[]{:S(2)}) collective-permute-start(bf16[576,256]{1,0:T(8,128)(2,1)S(1)} %get-tuple-element.59), channel_id=1, source_target_pairs={{0,32},{32,0},{1,33},{33,1},{2,34},{34,2},{3,35},{35,3},{4,36},{36... | collective-permute-start | bytes 884744 | tf_op jit(solution)/shard_map/ppermute | solution.py:23
  5.9 14.8 %collective-permute-start.4 = (bf16[576,256]{1,0:T(8,128)(2,1)S(1)}, bf16[576,256]{1,0:T(8,128)(2,1)S(1)}, u32[]{:S(2)}, u32[]{:S(2)}) collective-permute-start(bf16[576,256]{1,0:T(8,128)(2,1)S(1)} %get-tuple-element.60), channel_id=1, source_target_pairs={{0,64},{64,0},{1,65},{65,1},{2,66},{66,2},{3,67},{67,3},{4,68},{68... | collective-permute-start | bytes 884744 | tf_op jit(solution)/shard_map/ppermute | solution.py:25
  6.5 14.2 %collective-permute-start.5 = (bf16[576,256]{1,0:T(8,128)(2,1)S(1)}, bf16[576,256]{1,0:T(8,128)(2,1)S(1)}, u32[]{:S(2)}, u32[]{:S(2)}) collective-permute-start(bf16[576,256]{1,0:T(8,128)(2,1)S(1)} %get-tuple-element.61), channel_id=1, source_target_pairs={{0,96},{96,0},{32,64},{64,32},{1,97},{97,1},{33,65},{65,33},{2,98}... | collective-permute-start | bytes 884744 | tf_op jit(solution)/shard_map/ppermute | solution.py:26
  15.8 6.8 %copy-start.1 = (bf16[1024,256]{1,0:T(8,128)(2,1)S(1)}, bf16[1024,256]{1,0:T(8,128)(2,1)}, u32[]{:S(2)}) copy-start(bf16[1024,256]{1,0:T(8,128)(2,1)} %wp_ref.3) | copy-start | bytes 1572868
  15.8 14.4 %collective-permute-start = (bf16[864,256]{1,0:T(8,128)(2,1)S(1)}, bf16[864,256]{1,0:T(8,128)(2,1)S(1)}, u32[]{:S(2)}, u32[]{:S(2)}) collective-permute-start(bf16[864,256]{1,0:T(8,128)(2,1)S(1)} %get-tuple-element.55), channel_id=1, source_target_pairs={{0,64},{64,0},{1,65},{65,1},{2,66},{66,2},{3,67},{67,3},{4,68},{68... | collective-permute-start | bytes 1327112 | tf_op jit(solution)/shard_map/ppermute | solution.py:25
  17.3 21.2 %collective-permute-start.1 = (bf16[864,256]{1,0:T(8,128)(2,1)S(1)}, bf16[864,256]{1,0:T(8,128)(2,1)S(1)}, u32[]{:S(2)}, u32[]{:S(2)}) collective-permute-start(bf16[864,256]{1,0:T(8,128)(2,1)S(1)} %get-tuple-element.56), channel_id=1, source_target_pairs={{0,32},{32,0},{1,33},{33,1},{2,34},{34,2},{3,35},{35,3},{4,36},{36... | collective-permute-start | bytes 1327112 | tf_op jit(solution)/shard_map/ppermute | solution.py:23
  20.0 10.1 %collective-permute-start.2 = (bf16[576,256]{1,0:T(8,128)(2,1)S(1)}, bf16[576,256]{1,0:T(8,128)(2,1)S(1)}, u32[]{:S(2)}, u32[]{:S(2)}) collective-permute-start(bf16[576,256]{1,0:T(8,128)(2,1)S(1)} %get-tuple-element.57), channel_id=1, source_target_pairs={{0,96},{96,0},{32,64},{64,32},{1,97},{97,1},{33,65},{65,33},{2,98}... | collective-permute-start | bytes 884744 | tf_op jit(solution)/shard_map/ppermute | solution.py:26
  22.6 15.9 %copy-start = (bf16[1024,256]{1,0:T(8,128)(2,1)S(1)}, bf16[1024,256]{1,0:T(8,128)(2,1)}, u32[]{:S(2)}) copy-start(bf16[1024,256]{1,0:T(8,128)(2,1)} %wp_ref.5) | copy-start | bytes 1572868
  22.6 15.9 %copy-start.2 = (bf16[1,24,24,256]{3,2,1,0:T(8,128)(2,1)S(1)}, bf16[1,24,24,256]{3,2,1,0:T(8,128)(2,1)}, u32[]{:S(2)}) copy-start(bf16[1,24,24,256]{3,2,1,0:T(8,128)(2,1)} %param.9) | copy-start | bytes 884740
  40.6 15.3 %collective-permute-start.10 = (bf16[576,256]{1,0:T(8,128)(2,1)S(1)}, bf16[576,256]{1,0:T(8,128)(2,1)S(1)}, u32[]{:S(2)}, u32[]{:S(2)}) collective-permute-start(bf16[576,256]{1,0:T(8,128)(2,1)S(1)} %get-tuple-element.86.d0), channel_id=1, source_target_pairs={{0,96},{96,0},{32,64},{64,32},{1,97},{97,1},{33,65},{65,33},{2,98}... | collective-permute-start | bytes 884744 | tf_op jit(solution)/shard_map/ppermute | solution.py:26
  43.4 12.5 %collective-permute-start.8 = (bf16[576,256]{1,0:T(8,128)(2,1)S(1)}, bf16[576,256]{1,0:T(8,128)(2,1)S(1)}, u32[]{:S(2)}, u32[]{:S(2)}) collective-permute-start(bf16[576,256]{1,0:T(8,128)(2,1)S(1)} %get-tuple-element.86.d0), channel_id=1, source_target_pairs={{0,32},{32,0},{1,33},{33,1},{2,34},{34,2},{3,35},{35,3},{4,36},{36... | collective-permute-start | bytes 884744 | tf_op jit(solution)/shard_map/ppermute | solution.py:23
  44.2 12.4 %collective-permute-start.9 = (bf16[576,256]{1,0:T(8,128)(2,1)S(1)}, bf16[576,256]{1,0:T(8,128)(2,1)S(1)}, u32[]{:S(2)}, u32[]{:S(2)}) collective-permute-start(bf16[576,256]{1,0:T(8,128)(2,1)S(1)} %get-tuple-element.86.d0), channel_id=1, source_target_pairs={{0,64},{64,0},{1,65},{65,1},{2,66},{66,2},{3,67},{67,3},{4,68},{68... | collective-permute-start | bytes 884744 | tf_op jit(solution)/shard_map/ppermute | solution.py:25
  44.7 3.1 %copy-start.3 = (s32[176]{0:T(256)S(1)}, s32[176]{0:T(256)}, u32[]{:S(2)}) copy-start(s32[176]{0:T(256)} %param.15) | copy-start | bytes 2116
  47.3 1.6 %collective-permute-start.6 = (bf16[512,256]{1,0:T(8,128)(2,1)S(1)}, bf16[512,256]{1,0:T(8,128)(2,1)S(1)}, u32[]{:S(2)}, u32[]{:S(2)}) collective-permute-start(bf16[512,256]{1,0:T(8,128)(2,1)S(1)} %get-tuple-element.79), channel_id=1, source_target_pairs={{0,1},{1,0},{2,3},{3,2},{4,5},{5,4},{6,7},{7,6},{8,9},{9,8},{10,11... | collective-permute-start | bytes 786440 | tf_op jit(solution)/shard_map/ppermute | solution.py:211
  47.4 1.9 %collective-permute-start.7 = (bf16[512,256]{1,0:T(8,128)(2,1)S(1)}, bf16[512,256]{1,0:T(8,128)(2,1)S(1)}, u32[]{:S(2)}, u32[]{:S(2)}) collective-permute-start(bf16[512,256]{1,0:T(8,128)(2,1)S(1)} %get-tuple-element.80), channel_id=1, source_target_pairs={{0,1},{1,0},{2,3},{3,2},{4,5},{5,4},{6,7},{7,6},{8,9},{9,8},{10,11... | collective-permute-start | bytes 786440 | tf_op jit(solution)/shard_map/ppermute | solution.py:211
  56.5 7.4 %collective-permute-start.11 = (bf16[16,16,256]{2,1,0:T(8,128)(2,1)S(1)}, bf16[16,16,256]{2,1,0:T(8,128)(2,1)S(1)}, u32[]{:S(2)}, u32[]{:S(2)}) collective-permute-start(bf16[16,16,256]{2,1,0:T(8,128)(2,1)S(1)} %get-tuple-element.95), channel_id=1, source_target_pairs={{0,32},{32,0},{1,33},{33,1},{2,34},{34,2},{3,35},{35,3},{4,36},{36... | collective-permute-start | bytes 393224 | tf_op jit(solution)/shard_map/ppermute | solution.py:23
  59.7 5.7 %collective-permute-start.12 = (bf16[16,16,256]{2,1,0:T(8,128)(2,1)S(1)}, bf16[16,16,256]{2,1,0:T(8,128)(2,1)S(1)}, u32[]{:S(2)}, u32[]{:S(2)}) collective-permute-start(bf16[16,16,256]{2,1,0:T(8,128)(2,1)S(1)} %get-tuple-element.96), channel_id=1, source_target_pairs={{0,64},{64,0},{1,65},{65,1},{2,66},{66,2},{3,67},{67,3},{4,68},{68... | collective-permute-start | bytes 393224 | tf_op jit(solution)/shard_map/ppermute | solution.py:25
  60.3 6.2 %collective-permute-start.13 = (bf16[16,16,256]{2,1,0:T(8,128)(2,1)S(1)}, bf16[16,16,256]{2,1,0:T(8,128)(2,1)S(1)}, u32[]{:S(2)}, u32[]{:S(2)}) collective-permute-start(bf16[16,16,256]{2,1,0:T(8,128)(2,1)S(1)} %get-tuple-element.97), channel_id=1, source_target_pairs={{0,96},{96,0},{32,64},{64,32},{1,97},{97,1},{33,65},{65,33},{2,98}... | collective-permute-start | bytes 393224 | tf_op jit(solution)/shard_map/ppermute | solution.py:26
  66.4 2.5 %collective-permute-start.14 = (bf16[96,16,256]{2,1,0:T(8,128)(2,1)S(1)}, bf16[96,16,256]{2,1,0:T(8,128)(2,1)S(1)}, u32[]{:S(2)}, u32[]{:S(2)}) collective-permute-start(bf16[96,16,256]{2,1,0:T(8,128)(2,1)S(1)} %get-tuple-element.98), channel_id=1, source_target_pairs={{0,1},{1,0},{2,3},{3,2},{4,5},{5,4},{6,7},{7,6},{8,9},{9,8},{10,11... | collective-permute-start | bytes 2359304 | tf_op jit(solution)/shard_map/ppermute | solution.py:211
  66.5 2.4 %collective-permute-start.15 = (bf16[16,16,256]{2,1,0:T(8,128)(2,1)S(1)}, bf16[16,16,256]{2,1,0:T(8,128)(2,1)S(1)}, u32[]{:S(2)}, u32[]{:S(2)}) collective-permute-start(bf16[16,16,256]{2,1,0:T(8,128)(2,1)S(1)} %get-tuple-element.103), channel_id=1, source_target_pairs={{0,1},{1,0},{2,3},{3,2},{4,5},{5,4},{6,7},{7,6},{8,9},{9,8},{10,11... | collective-permute-start | bytes 393224 | tf_op jit(solution)/shard_map/ppermute | solution.py:211

commit v13 on v10

--- a/solution.py
+++ b/solution.py
@@ -160,18 +160,18 @@
     send_ref[...] = buf[half:].astype(BF)
 
 
-def join_owners(pos_ref, place_ref, keep_ref, got_ref, mine_ref, other_ref, o_ref, total):
-    total[...] = keep_ref[...] + got_ref[...].astype(F32)
+def join_owners(pos_ref, place_ref, keep_ref, got_ref, mine_ref, other_ref, o_ref):
+    o_ref[...] = (keep_ref[...] + got_ref[...].astype(F32)).astype(BF).reshape(o_ref.shape)
+    each = o_ref.shape[1] // 16
     core = pos_ref[4]
     for n in range(mine_ref.shape[0]):
         for ref, first in ((mine_ref, 16 * core), (other_ref, 16 * (1 - core))):
             at = place_ref[first + n]
 
-            @pl.when(at < total.shape[0])
+            @pl.when(at < o_ref.shape[0] * each)
             def _(ref=ref, at=at, n=n):
-                total[at] = ref[n].astype(F32)
-
-    o_ref[...] = total[...].astype(BF).reshape(o_ref.shape)
+                rows = pl.ds(pl.multiple_of((at % each) * 16, 16), 16)
+                o_ref[at // each, rows, :] = ref[n].astype(BF)
 
 
 def fold_last(r_ref, o_ref, total):
@@ -295,8 +295,7 @@
         4,
         kept.size,
         8 * kept.size,
-        12,
-        [pltpu.VMEM((half, rows, width), F32)],
+        8,
         name="owners",
     )(pos, place, kept, swap_core(sent), mine, other)
     total = lax.all_to_all(total, ("dp_0", "dp_1"), 0, 0, tiled=True)

time: 93.2 us -> 93.3 us (level)
  no operation moved by 1% of the time
where the time goes in v13:
time: 93.3 us; the launch traced here: 93.1 us
  Pallas kernels  29.1 us (31%)
  waiting for transfers between devices  22.7 us (24%)
  blocking collectives  22.2 us (24%)
  starting transfers between devices  18.7 us (20%)
    all_to_all x1, blocking collectives, reduce_slots(): total = lax.all_to_all(total, ('dp_0', 'dp_1'), 0, 0, tiled=True)  22.2 us
    ppermute x4, starting transfers between devices, flip(): return lax.ppermute(x, 'col', [(0, 1), (1, 0)])  9.84 us
    ppermute x4, waiting for transfers between devices, flip(): return lax.ppermute(x, ('row', 'col'), [(0, 3), (3, 0), (1, 2), (2, 1)])  8.79 us
    pallas_call x1, Pallas kernels, outer(): call(outer_parts, [jax.ShapeDtypeStruct(*s) for s in shapes], 1, 1, 2 * p...  8.68 us
    ppermute x4, waiting for transfers between devices, flip(): return lax.ppermute(x, 'col', [(0, 1), (1, 0)])  8.25 us
    pallas_call x1, Pallas kernels, inner(): call(inner_parts, [jax.ShapeDtypeStruct((pixels, width), BF), jax.ShapeDt...  6.14 us
    ppermute x4, starting transfers between devices, flip(): return lax.ppermute(x, ('row', 'col'), [(0, 3), (3, 0), (1, 2), (2, 1)])  4.53 us
    ppermute x4, waiting for transfers between devices, swap_core(): return lax.ppermute(x, 'dp_2', [(0, 1), (1, 0)])  3.18 us
  transfers between devices with their start and end apart: 16, of which 11 were waited for; matrix products, arithmetic and copies ran while one was open for 0% of the time, Pallas kernels for 24%

profile of v13, /device:TPU:0, one launch (start us, length us, event | category | flops | bytes accessed | tf_op | source)
XLA Modules:
  0.0 93.1 jit_solution(11152996527969570430)
XLA Ops:
  0.1 2.6 %pick.1 = (bf16[576,256]{1,0:T(8,128)(2,1)S(1)}, bf16[576,256]{1,0:T(8,128)(2,1)S(1)}, bf16[576,256]{1,0:T(8,128)(2,1)S(1)}, bf16[576,256]{1,0:T(8,128)(2,1)S(1)}) custom-call(s32[6]{0:T(128)S(1)} %stack.27.pos_ref, bf16[576,1024]{1,0:T(8,128)(2,1)} %bitcast.8), custom_call_target="tpu_custom_call" | custom-call | flops 603979776 | bytes 2359296 | tf_op jit(solution)/shard_map/pick/pallas_call | solution.py:204
  2.7 3.2 %collective-permute-start.3 = (bf16[576,256]{1,0:T(8,128)(2,1)S(1)}, bf16[576,256]{1,0:T(8,128)(2,1)S(1)}, u32[]{:S(2)}, u32[]{:S(2)}) collective-permute-start(bf16[576,256]{1,0:T(8,128)(2,1)S(1)} %get-tuple-element.70), channel_id=1, source_target_pairs={{0,32},{32,0},{1,33},{33,1},{2,34},{34,2},{3,35},{35,3},{4,36},{36... | collective-permute-start | bytes 884744 | tf_op jit(solution)/shard_map/ppermute | solution.py:23
  5.8 0.6 collective-permute-start.4
  6.4 0.6 collective-permute-start.5
  7.0 8.7 %outer.1 = (f32[3,576,256]{2,1,0:T(8,128)S(1)}, bf16[864,256]{1,0:T(8,128)(2,1)S(1)}, bf16[864,256]{1,0:T(8,128)(2,1)S(1)}, bf16[576,256]{1,0:T(8,128)(2,1)S(1)}) custom-call(s32[6]{0:T(128)S(1)} %stack.27.pos_ref, bf16[576,1024]{1,0:T(8,128)(2,1)S(1)} %bitcast.9, bf16[3,3,1024,256]{3,2,1,0:T(8,128)(2,1)} %wc_ref.3, bf16[3,3,1024,256]{3,2,1,0:T(8,128)(2,1)} %wb_ref.3, ...), custom_call_target="tpu_custom_call" | custom-call | flops 4227858432 | bytes 10485760 | tf_op jit(solution)/shard_map/outer/pallas_call | solution.py:473
  15.7 1.5 %collective-permute-start = (bf16[864,256]{1,0:T(8,128)(2,1)S(1)}, bf16[864,256]{1,0:T(8,128)(2,1)S(1)}, u32[]{:S(2)}, u32[]{:S(2)}) collective-permute-start(bf16[864,256]{1,0:T(8,128)(2,1)S(1)} %get-tuple-element.65), channel_id=1, source_target_pairs={{0,64},{64,0},{1,65},{65,1},{2,66},{66,2},{3,67},{67,3},{4,68},{68... | collective-permute-start | bytes 1327112 | tf_op jit(solution)/shard_map/ppermute | solution.py:25
  17.1 2.7 %collective-permute-start.1 = (bf16[864,256]{1,0:T(8,128)(2,1)S(1)}, bf16[864,256]{1,0:T(8,128)(2,1)S(1)}, u32[]{:S(2)}, u32[]{:S(2)}) collective-permute-start(bf16[864,256]{1,0:T(8,128)(2,1)S(1)} %get-tuple-element.66), channel_id=1, source_target_pairs={{0,32},{32,0},{1,33},{33,1},{2,34},{34,2},{3,35},{35,3},{4,36},{36... | collective-permute-start | bytes 1327112 | tf_op jit(solution)/shard_map/ppermute | solution.py:23
  19.9 0.6 collective-permute-start.2
  20.7 1.3 %turn.1 = (bf16[2,256,1152]{2,1,0:T(8,128)(2,1)S(1)}, bf16[2,256,384]{2,1,0:T(8,128)(2,1)S(1)}) custom-call(s32[6]{0:T(128)S(1)} %stack.27.pos_ref, bf16[576,256]{1,0:T(8,128)(2,1)S(1)} %get-tuple-element.76.x0, bf16[576,256]{1,0:T(8,128)(2,1)S(1)} %collective-permute-done.3.x1, bf16[576,256]{1,0:T(8,128)(2,1)S(1)} %collective-permute-done.4.x2, ...), custom_call_target="tpu_custom_call" | custom-call | flops 301989888 | bytes 2359296 | tf_op jit(solution)/shard_map/turn/pallas_call | solution.py:220
  22.0 6.1 %inner.1 = (bf16[576,256]{1,0:T(8,128)(2,1)S(1)}, f32[576,256]{1,0:T(8,128)S(1)}, f32[3,576,256]{2,1,0:T(8,128)S(1)}) custom-call(s32[6]{0:T(128)S(1)} %stack.27.pos_ref, bf16[576,1024]{1,0:T(8,128)(2,1)S(1)} %bitcast.10, f32[3,576,256]{2,1,0:T(8,128)S(1)} %get-tuple-element.73.part_ref, bf16[1024,256]{1,0:T(8,128)(2,1)S(1)} %copy-done.2, ...), custom_call_target="tpu_custom_call" | custom-call | flops 3019898880 | bytes 10485760 | tf_op jit(solution)/shard_map/inner/pallas_call | solution.py:496
  28.2 1.8 %collective-permute-done.2.diag_ref = bf16[576,256]{1,0:T(8,128)(2,1)S(1)} collective-permute-done((bf16[576,256]{1,0:T(8,128)(2,1)S(1)}, bf16[576,256]{1,0:T(8,128)(2,1)S(1)}, u32[]{:S(2)}, u32[]{:S(2)}) %collective-permute-start.2) | collective-permute-done | bytes 294944 | tf_op jit(solution)/shard_map/ppermute | solution.py:26
  30.1 8.2 %collective-permute-done.1.col_ref = bf16[864,256]{1,0:T(8,128)(2,1)S(1)} collective-permute-done((bf16[864,256]{1,0:T(8,128)(2,1)S(1)}, bf16[864,256]{1,0:T(8,128)(2,1)S(1)}, u32[]{:S(2)}, u32[]{:S(2)}) %collective-permute-start.1) | collective-permute-done | bytes 442400 | tf_op jit(solution)/shard_map/ppermute | solution.py:23
  38.4 2.1 %merge.1 = (bf16[576,1024]{1,0:T(8,128)(2,1)S(1)}, bf16[576,256]{1,0:T(8,128)(2,1)S(1)}, bf16[576,256]{1,0:T(8,128)(2,1)S(1)}) custom-call(s32[6]{0:T(128)S(1)} %stack.27.pos_ref, bf16[576,256]{1,0:T(8,128)(2,1)S(1)} %get-tuple-element.82.joined0_ref, f32[3,576,256]{2,1,0:T(8,128)S(1)} %get-tuple-element.83.own_ref, ...), custom_call_target="tpu_custom_call" | custom-call | flops 452984832 | bytes 6291456 | tf_op jit(solution)/shard_map/merge/pallas_call | solution.py:582
  40.5 2.9 %collective-permute-start.10 = (bf16[576,256]{1,0:T(8,128)(2,1)S(1)}, bf16[576,256]{1,0:T(8,128)(2,1)S(1)}, u32[]{:S(2)}, u32[]{:S(2)}) collective-permute-start(bf16[576,256]{1,0:T(8,128)(2,1)S(1)} %get-tuple-element.98.d0), channel_id=1, source_target_pairs={{0,96},{96,0},{32,64},{64,32},{1,97},{97,1},{33,65},{65,33},{2,98}... | collective-permute-start | bytes 884744 | tf_op jit(solution)/shard_map/ppermute | solution.py:26
  43.4 0.8 collective-permute-start.8
  44.2 0.5 collective-permute-start.9
  44.7 2.5 %pair.1 = (f32[1024,256]{1,0:T(8,128)S(1)}, bf16[512,256]{1,0:T(8,128)(2,1)S(1)}, bf16[512,256]{1,0:T(8,128)(2,1)S(1)}) custom-call(s32[6]{0:T(128)S(1)} %stack.27.pos_ref, bf16[576,1024]{1,0:T(8,128)(2,1)S(1)} %get-tuple-element.87.joined_ref, bf16[576,256]{1,0:T(8,128)(2,1)S(1)} %get-tuple-element.88.g_ref, bf16[576,1024]{1,0:T(8,128)(2,1)S(1)} %bitcast.11, ...), custom_call_target="tpu_custom_call" | custom-call | flops 603979776 | bytes 4194304 | tf_op jit(solution)/shard_map/pair/pallas_call | solution.py:636
  47.8 1.0 %collective-permute-done.6.got0 = bf16[512,256]{1,0:T(8,128)(2,1)S(1)} collective-permute-done((bf16[512,256]{1,0:T(8,128)(2,1)S(1)}, bf16[512,256]{1,0:T(8,128)(2,1)S(1)}, u32[]{:S(2)}, u32[]{:S(2)}) %collective-permute-start.6) | collective-permute-done | bytes 262176 | tf_op jit(solution)/shard_map/ppermute | solution.py:198
  49.2 0.7 rows.1
  49.9 5.9 %collective-permute-done.10.d3 = bf16[576,256]{1,0:T(8,128)(2,1)S(1)} collective-permute-done((bf16[576,256]{1,0:T(8,128)(2,1)S(1)}, bf16[576,256]{1,0:T(8,128)(2,1)S(1)}, u32[]{:S(2)}, u32[]{:S(2)}) %collective-permute-start.10) | collective-permute-done | bytes 294944 | tf_op jit(solution)/shard_map/ppermute | solution.py:26
  55.8 0.7 collective-permute-done.9.d2
  56.5 3.1 %collective-permute-start.11 = (bf16[16,16,256]{2,1,0:T(8,128)(2,1)S(1)}, bf16[16,16,256]{2,1,0:T(8,128)(2,1)S(1)}, u32[]{:S(2)}, u32[]{:S(2)}) collective-permute-start(bf16[16,16,256]{2,1,0:T(8,128)(2,1)S(1)} %get-tuple-element.107), channel_id=1, source_target_pairs={{0,32},{32,0},{1,33},{33,1},{2,34},{34,2},{3,35},{35,3},{4,36},{36... | collective-permute-start | bytes 393224 | tf_op jit(solution)/shard_map/ppermute | solution.py:23
  59.7 0.6 collective-permute-start.12
  60.3 0.5 collective-permute-start.13
  60.8 3.1 %taps.1 = (f32[96,16,256]{2,1,0:T(8,128)S(1)}, bf16[96,16,256]{2,1,0:T(8,128)(2,1)S(1)}) custom-call(s32[6]{0:T(128)S(1)} %stack.27.pos_ref, s32[176]{0:T(256)S(1)} %fusion.1.place_ref, bf16[576,256]{1,0:T(8,128)(2,1)S(1)} %get-tuple-element.98.d0, bf16[576,256]{1,0:T(8,128)(2,1)S(1)} %collective-permute-done.8.d1, ...), custom_call_target="tpu_custom_call" | custom-call | flops 2113929216 | bytes 8388608 | tf_op jit(solution)/shard_map/taps/pallas_call | solution.py:269
  63.9 1.5 %collective-permute-done.12 = bf16[16,16,256]{2,1,0:T(8,128)(2,1)S(1)} collective-permute-done((bf16[16,16,256]{2,1,0:T(8,128)(2,1)S(1)}, bf16[16,16,256]{2,1,0:T(8,128)(2,1)S(1)}, u32[]{:S(2)}, u32[]{:S(2)}) %collective-permute-start.12) | collective-permute-done | bytes 131104 | tf_op jit(solution)/shard_map/ppermute | solution.py:25
  65.4 1.1 %collective-permute-done.13 = bf16[16,16,256]{2,1,0:T(8,128)(2,1)S(1)} collective-permute-done((bf16[16,16,256]{2,1,0:T(8,128)(2,1)S(1)}, bf16[16,16,256]{2,1,0:T(8,128)(2,1)S(1)}, u32[]{:S(2)}, u32[]{:S(2)}) %collective-permute-start.13) | collective-permute-done | bytes 131104 | tf_op jit(solution)/shard_map/ppermute | solution.py:26
  66.5 0.6 collective-permute-start.15
  67.1 1.8 %collective-permute-done.15.other_ref = bf16[16,16,256]{2,1,0:T(8,128)(2,1)S(1)} collective-permute-done((bf16[16,16,256]{2,1,0:T(8,128)(2,1)S(1)}, bf16[16,16,256]{2,1,0:T(8,128)(2,1)S(1)}, u32[]{:S(2)}, u32[]{:S(2)}) %collective-permute-start.15) | collective-permute-done | bytes 131104 | tf_op jit(solution)/shard_map/ppermute | solution.py:198
  68.9 1.1 %owners.1 = bf16[16,96,256]{2,1,0:T(8,128)(2,1)S(1)} custom-call(s32[6]{0:T(128)S(1)} %stack.27.pos_ref, s32[176]{0:T(256)S(1)} %fusion.1.place_ref, f32[96,16,256]{2,1,0:T(8,128)S(1)} %get-tuple-element.104.keep_ref, bf16[96,16,256]{2,1,0:T(8,128)(2,1)S(1)} %collective-permute-done.14.got_ref, f32[16,16,256]{2,1,0:T(8,128)S(1)} %get-tuple-element.116.mine_ref, ...), custom_call_target="tpu_custom_call" | custom-call | flops 393216 | bytes 3145728 | tf_op jit(solution)/shard_map/owners/pallas_call | solution.py:291
  70.1 22.2 %all_to_all.5.r_ref = bf16[16,96,256]{2,1,0:T(8,128)(2,1)S(1)} all-to-all(bf16[16,96,256]{2,1,0:T(8,128)(2,1)S(1)} %owners.1), channel_id=1, replica_groups=mesh['row'=2,'col'=2,'dp_0'=4,'dp_1'=4,'dp_2'=2] {'dp_0','dp_1'}, dimensions={0} | all-to-all | bytes 1572864 | tf_op jit(solution)/shard_map/all_to_all | solution.py:301
  92.3 0.8 last.1
  (24 shorter events, 1.5 us)
Async XLA Ops:
  0.0 7.0 %copy-start = (bf16[1,24,24,1024]{3,2,1,0:T(8,128)(2,1)S(1)}, bf16[1,24,24,1024]{3,2,1,0:T(8,128)(2,1)}, u32[]{:S(2)}) copy-start(bf16[1,24,24,1024]{3,2,1,0:T(8,128)(2,1)} %param.8) | copy-start | bytes 3538948
  2.6 19.3 %copy-start.2 = (bf16[1024,256]{1,0:T(8,128)(2,1)S(1)}, bf16[1024,256]{1,0:T(8,128)(2,1)}, u32[]{:S(2)}) copy-start(bf16[1024,256]{1,0:T(8,128)(2,1)} %wp_ref.3) | copy-start | bytes 1572868
  2.7 17.2 %collective-permute-start.3 = (bf16[576,256]{1,0:T(8,128)(2,1)S(1)}, bf16[576,256]{1,0:T(8,128)(2,1)S(1)}, u32[]{:S(2)}, u32[]{:S(2)}) collective-permute-start(bf16[576,256]{1,0:T(8,128)(2,1)S(1)} %get-tuple-element.70), channel_id=1, source_target_pairs={{0,32},{32,0},{1,33},{33,1},{2,34},{34,2},{3,35},{35,3},{4,36},{36... | collective-permute-start | bytes 884744 | tf_op jit(solution)/shard_map/ppermute | solution.py:23
  5.8 14.8 %collective-permute-start.4 = (bf16[576,256]{1,0:T(8,128)(2,1)S(1)}, bf16[576,256]{1,0:T(8,128)(2,1)S(1)}, u32[]{:S(2)}, u32[]{:S(2)}) collective-permute-start(bf16[576,256]{1,0:T(8,128)(2,1)S(1)} %get-tuple-element.71), channel_id=1, source_target_pairs={{0,64},{64,0},{1,65},{65,1},{2,66},{66,2},{3,67},{67,3},{4,68},{68... | collective-permute-start | bytes 884744 | tf_op jit(solution)/shard_map/ppermute | solution.py:25
  6.4 14.2 %collective-permute-start.5 = (bf16[576,256]{1,0:T(8,128)(2,1)S(1)}, bf16[576,256]{1,0:T(8,128)(2,1)S(1)}, u32[]{:S(2)}, u32[]{:S(2)}) collective-permute-start(bf16[576,256]{1,0:T(8,128)(2,1)S(1)} %get-tuple-element.72), channel_id=1, source_target_pairs={{0,96},{96,0},{32,64},{64,32},{1,97},{97,1},{33,65},{65,33},{2,98}... | collective-permute-start | bytes 884744 | tf_op jit(solution)/shard_map/ppermute | solution.py:26
  15.7 14.5 %collective-permute-start = (bf16[864,256]{1,0:T(8,128)(2,1)S(1)}, bf16[864,256]{1,0:T(8,128)(2,1)S(1)}, u32[]{:S(2)}, u32[]{:S(2)}) collective-permute-start(bf16[864,256]{1,0:T(8,128)(2,1)S(1)} %get-tuple-element.65), channel_id=1, source_target_pairs={{0,64},{64,0},{1,65},{65,1},{2,66},{66,2},{3,67},{67,3},{4,68},{68... | collective-permute-start | bytes 1327112 | tf_op jit(solution)/shard_map/ppermute | solution.py:25
  17.1 21.2 %collective-permute-start.1 = (bf16[864,256]{1,0:T(8,128)(2,1)S(1)}, bf16[864,256]{1,0:T(8,128)(2,1)S(1)}, u32[]{:S(2)}, u32[]{:S(2)}) collective-permute-start(bf16[864,256]{1,0:T(8,128)(2,1)S(1)} %get-tuple-element.66), channel_id=1, source_target_pairs={{0,32},{32,0},{1,33},{33,1},{2,34},{34,2},{3,35},{35,3},{4,36},{36... | collective-permute-start | bytes 1327112 | tf_op jit(solution)/shard_map/ppermute | solution.py:23
  19.9 10.1 %collective-permute-start.2 = (bf16[576,256]{1,0:T(8,128)(2,1)S(1)}, bf16[576,256]{1,0:T(8,128)(2,1)S(1)}, u32[]{:S(2)}, u32[]{:S(2)}) collective-permute-start(bf16[576,256]{1,0:T(8,128)(2,1)S(1)} %get-tuple-element.67), channel_id=1, source_target_pairs={{0,96},{96,0},{32,64},{64,32},{1,97},{97,1},{33,65},{65,33},{2,98}... | collective-permute-start | bytes 884744 | tf_op jit(solution)/shard_map/ppermute | solution.py:26
  22.0 16.4 %copy-start.1 = (bf16[1024,256]{1,0:T(8,128)(2,1)S(1)}, bf16[1024,256]{1,0:T(8,128)(2,1)}, u32[]{:S(2)}) copy-start(bf16[1024,256]{1,0:T(8,128)(2,1)} %wp_ref.5) | copy-start | bytes 1572868
  22.0 16.4 %copy-start.3 = (bf16[1,24,24,256]{3,2,1,0:T(8,128)(2,1)S(1)}, bf16[1,24,24,256]{3,2,1,0:T(8,128)(2,1)}, u32[]{:S(2)}) copy-start(bf16[1,24,24,256]{3,2,1,0:T(8,128)(2,1)} %param.9) | copy-start | bytes 884740
  40.5 15.3 %collective-permute-start.10 = (bf16[576,256]{1,0:T(8,128)(2,1)S(1)}, bf16[576,256]{1,0:T(8,128)(2,1)S(1)}, u32[]{:S(2)}, u32[]{:S(2)}) collective-permute-start(bf16[576,256]{1,0:T(8,128)(2,1)S(1)} %get-tuple-element.98.d0), channel_id=1, source_target_pairs={{0,96},{96,0},{32,64},{64,32},{1,97},{97,1},{33,65},{65,33},{2,98}... | collective-permute-start | bytes 884744 | tf_op jit(solution)/shard_map/ppermute | solution.py:26
  43.4 12.5 %collective-permute-start.8 = (bf16[576,256]{1,0:T(8,128)(2,1)S(1)}, bf16[576,256]{1,0:T(8,128)(2,1)S(1)}, u32[]{:S(2)}, u32[]{:S(2)}) collective-permute-start(bf16[576,256]{1,0:T(8,128)(2,1)S(1)} %get-tuple-element.98.d0), channel_id=1, source_target_pairs={{0,32},{32,0},{1,33},{33,1},{2,34},{34,2},{3,35},{35,3},{4,36},{36... | collective-permute-start | bytes 884744 | tf_op jit(solution)/shard_map/ppermute | solution.py:23
  44.2 12.4 %collective-permute-start.9 = (bf16[576,256]{1,0:T(8,128)(2,1)S(1)}, bf16[576,256]{1,0:T(8,128)(2,1)S(1)}, u32[]{:S(2)}, u32[]{:S(2)}) collective-permute-start(bf16[576,256]{1,0:T(8,128)(2,1)S(1)} %get-tuple-element.98.d0), channel_id=1, source_target_pairs={{0,64},{64,0},{1,65},{65,1},{2,66},{66,2},{3,67},{67,3},{4,68},{68... | collective-permute-start | bytes 884744 | tf_op jit(solution)/shard_map/ppermute | solution.py:25
  44.7 3.1 %copy-start.4 = (s32[176]{0:T(256)S(1)}, s32[176]{0:T(256)}, u32[]{:S(2)}) copy-start(s32[176]{0:T(256)} %param.15) | copy-start | bytes 2116
  47.2 1.6 %collective-permute-start.6 = (bf16[512,256]{1,0:T(8,128)(2,1)S(1)}, bf16[512,256]{1,0:T(8,128)(2,1)S(1)}, u32[]{:S(2)}, u32[]{:S(2)}) collective-permute-start(bf16[512,256]{1,0:T(8,128)(2,1)S(1)} %get-tuple-element.91), channel_id=1, source_target_pairs={{0,1},{1,0},{2,3},{3,2},{4,5},{5,4},{6,7},{7,6},{8,9},{9,8},{10,11... | collective-permute-start | bytes 786440 | tf_op jit(solution)/shard_map/ppermute | solution.py:198
  47.3 1.9 %collective-permute-start.7 = (bf16[512,256]{1,0:T(8,128)(2,1)S(1)}, bf16[512,256]{1,0:T(8,128)(2,1)S(1)}, u32[]{:S(2)}, u32[]{:S(2)}) collective-permute-start(bf16[512,256]{1,0:T(8,128)(2,1)S(1)} %get-tuple-element.92), channel_id=1, source_target_pairs={{0,1},{1,0},{2,3},{3,2},{4,5},{5,4},{6,7},{7,6},{8,9},{9,8},{10,11... | collective-permute-start | bytes 786440 | tf_op jit(solution)/shard_map/ppermute | solution.py:198
  56.5 7.4 %collective-permute-start.11 = (bf16[16,16,256]{2,1,0:T(8,128)(2,1)S(1)}, bf16[16,16,256]{2,1,0:T(8,128)(2,1)S(1)}, u32[]{:S(2)}, u32[]{:S(2)}) collective-permute-start(bf16[16,16,256]{2,1,0:T(8,128)(2,1)S(1)} %get-tuple-element.107), channel_id=1, source_target_pairs={{0,32},{32,0},{1,33},{33,1},{2,34},{34,2},{3,35},{35,3},{4,36},{36... | collective-permute-start | bytes 393224 | tf_op jit(solution)/shard_map/ppermute | solution.py:23
  59.7 5.7 %collective-permute-start.12 = (bf16[16,16,256]{2,1,0:T(8,128)(2,1)S(1)}, bf16[16,16,256]{2,1,0:T(8,128)(2,1)S(1)}, u32[]{:S(2)}, u32[]{:S(2)}) collective-permute-start(bf16[16,16,256]{2,1,0:T(8,128)(2,1)S(1)} %get-tuple-element.108), channel_id=1, source_target_pairs={{0,64},{64,0},{1,65},{65,1},{2,66},{66,2},{3,67},{67,3},{4,68},{68... | collective-permute-start | bytes 393224 | tf_op jit(solution)/shard_map/ppermute | solution.py:25
  60.3 6.2 %collective-permute-start.13 = (bf16[16,16,256]{2,1,0:T(8,128)(2,1)S(1)}, bf16[16,16,256]{2,1,0:T(8,128)(2,1)S(1)}, u32[]{:S(2)}, u32[]{:S(2)}) collective-permute-start(bf16[16,16,256]{2,1,0:T(8,128)(2,1)S(1)} %get-tuple-element.109), channel_id=1, source_target_pairs={{0,96},{96,0},{32,64},{64,32},{1,97},{97,1},{33,65},{65,33},{2,98}... | collective-permute-start | bytes 393224 | tf_op jit(solution)/shard_map/ppermute | solution.py:26
  66.4 2.5 %collective-permute-start.14 = (bf16[96,16,256]{2,1,0:T(8,128)(2,1)S(1)}, bf16[96,16,256]{2,1,0:T(8,128)(2,1)S(1)}, u32[]{:S(2)}, u32[]{:S(2)}) collective-permute-start(bf16[96,16,256]{2,1,0:T(8,128)(2,1)S(1)} %get-tuple-element.110), channel_id=1, source_target_pairs={{0,1},{1,0},{2,3},{3,2},{4,5},{5,4},{6,7},{7,6},{8,9},{9,8},{10,11... | collective-permute-start | bytes 2359304 | tf_op jit(solution)/shard_map/ppermute | solution.py:198
  66.5 2.4 %collective-permute-start.15 = (bf16[16,16,256]{2,1,0:T(8,128)(2,1)S(1)}, bf16[16,16,256]{2,1,0:T(8,128)(2,1)S(1)}, u32[]{:S(2)}, u32[]{:S(2)}) collective-permute-start(bf16[16,16,256]{2,1,0:T(8,128)(2,1)S(1)} %get-tuple-element.115), channel_id=1, source_target_pairs={{0,1},{1,0},{2,3},{3,2},{4,5},{5,4},{6,7},{7,6},{8,9},{9,8},{10,11... | collective-permute-start | bytes 393224 | tf_op jit(solution)/shard_map/ppermute | solution.py:198

commit v14 on v12

--- a/solution.py
+++ b/solution.py
@@ -173,18 +173,18 @@
     send_ref[...] = buf[half:].astype(BF)
 
 
-def join_owners(pos_ref, place_ref, keep_ref, got_ref, mine_ref, other_ref, o_ref, total):
-    total[...] = keep_ref[...] + got_ref[...].astype(F32)
+def join_owners(pos_ref, place_ref, keep_ref, got_ref, mine_ref, other_ref, o_ref):
+    o_ref[...] = (keep_ref[...] + got_ref[...].astype(F32)).astype(BF).reshape(o_ref.shape)
+    each = o_ref.shape[1] // 16
     core = pos_ref[4]
     for n in range(mine_ref.shape[0]):
         for ref, first in ((mine_ref, 16 * core), (other_ref, 16 * (1 - core))):
             at = place_ref[first + n]
 
-            @pl.when(at < total.shape[0])
+            @pl.when(at < o_ref.shape[0] * each)
             def _(ref=ref, at=at, n=n):
-                total[at] = ref[n].astype(F32)
-
-    o_ref[...] = total[...].astype(BF).reshape(o_ref.shape)
+                rows = pl.ds(pl.multiple_of((at % each) * 16, 16), 16)
+                o_ref[at // each, rows, :] = ref[n].astype(BF)
 
 
 def fold_last(r_ref, o_ref, total):
@@ -308,8 +308,7 @@
         4,
         kept.size,
         8 * kept.size,
-        12,
-        [pltpu.VMEM((half, rows, width), F32)],
+        8,
         name="owners",
     )(pos, place, kept, swap_core(sent), mine, other)
     total = lax.all_to_all(total, ("dp_0", "dp_1"), 0, 0, tiled=True)

time: 93.2 us -> 93.3 us (level)
  no operation moved by 1% of the time
where the time goes in v14:
time: 93.3 us; the launch traced here: 93.1 us
  Pallas kernels  29.6 us (32%)
  blocking collectives  22.3 us (24%)
  waiting for transfers between devices  22.1 us (24%)
  starting transfers between devices  18.7 us (20%)
    all_to_all x1, blocking collectives, reduce_slots(): total = lax.all_to_all(total, ('dp_0', 'dp_1'), 0, 0, tiled=True)  22.3 us
    ppermute x4, starting transfers between devices, flip(): return lax.ppermute(x, 'col', [(0, 1), (1, 0)])  9.84 us
    pallas_call x1, Pallas kernels, outer(): call(outer_parts, [jax.ShapeDtypeStruct(*s) for s in shapes], 1, 1, 2 * p...  8.69 us
    ppermute x4, waiting for transfers between devices, flip(): return lax.ppermute(x, 'col', [(0, 1), (1, 0)])  8.28 us
    ppermute x4, waiting for transfers between devices, flip(): return lax.ppermute(x, ('row', 'col'), [(0, 3), (3, 0), (1, 2), (2, 1)])  8.22 us
    pallas_call x1, Pallas kernels, inner(): call(inner_parts, [jax.ShapeDtypeStruct((pixels, width), BF), jax.ShapeDt...  6.18 us
    ppermute x4, starting transfers between devices, flip(): return lax.ppermute(x, ('row', 'col'), [(0, 3), (3, 0), (1, 2), (2, 1)])  4.48 us
    ppermute x4, starting transfers between devices, flip(): return lax.ppermute(x, 'row', [(0, 1), (1, 0)])  3.24 us
  transfers between devices with their start and end apart: 16, of which 11 were waited for; matrix products, arithmetic and copies ran while one was open for 0% of the time, Pallas kernels for 25%

profile of v14, /device:TPU:0, one launch (start us, length us, event | category | flops | bytes accessed | tf_op | source)
XLA Modules:
  0.0 93.1 jit_solution(5711041340985164680)
XLA Ops:
  0.1 2.7 %pick.1 = (bf16[576,1024]{1,0:T(8,128)(2,1)S(1)}, bf16[576,256]{1,0:T(8,128)(2,1)S(1)}, bf16[576,256]{1,0:T(8,128)(2,1)S(1)}, bf16[576,256]{1,0:T(8,128)(2,1)S(1)}) custom-call(s32[6]{0:T(128)S(1)} %stack.27.pos_ref, bf16[576,1024]{1,0:T(8,128)(2,1)} %bitcast.9), custom_call_target="tpu_custom_call" | custom-call | flops 603979776 | bytes 2359296 | tf_op jit(solution)/shard_map/pick/pallas_call | solution.py:217
  2.8 3.2 %collective-permute-start.3 = (bf16[576,256]{1,0:T(8,128)(2,1)S(1)}, bf16[576,256]{1,0:T(8,128)(2,1)S(1)}, u32[]{:S(2)}, u32[]{:S(2)}) collective-permute-start(bf16[576,256]{1,0:T(8,128)(2,1)S(1)} %get-tuple-element.59), channel_id=1, source_target_pairs={{0,32},{32,0},{1,33},{33,1},{2,34},{34,2},{3,35},{35,3},{4,36},{36... | collective-permute-start | bytes 884744 | tf_op jit(solution)/shard_map/ppermute | solution.py:23
  5.9 0.6 collective-permute-start.4
  6.5 0.6 collective-permute-start.5
  7.1 8.7 %outer.1 = (f32[3,576,256]{2,1,0:T(8,128)S(1)}, bf16[864,256]{1,0:T(8,128)(2,1)S(1)}, bf16[864,256]{1,0:T(8,128)(2,1)S(1)}, bf16[576,256]{1,0:T(8,128)(2,1)S(1)}) custom-call(s32[6]{0:T(128)S(1)} %stack.27.pos_ref, bf16[576,1024]{1,0:T(8,128)(2,1)S(1)} %get-tuple-element.54.x_ref, bf16[3,3,1024,256]{3,2,1,0:T(8,128)(2,1)} %wc_ref.3, ...), custom_call_target="tpu_custom_call" | custom-call | flops 4227858432 | bytes 10485760 | tf_op jit(solution)/shard_map/outer/pallas_call | solution.py:486
  15.8 1.5 %collective-permute-start = (bf16[864,256]{1,0:T(8,128)(2,1)S(1)}, bf16[864,256]{1,0:T(8,128)(2,1)S(1)}, u32[]{:S(2)}, u32[]{:S(2)}) collective-permute-start(bf16[864,256]{1,0:T(8,128)(2,1)S(1)} %get-tuple-element.55), channel_id=1, source_target_pairs={{0,64},{64,0},{1,65},{65,1},{2,66},{66,2},{3,67},{67,3},{4,68},{68... | collective-permute-start | bytes 1327112 | tf_op jit(solution)/shard_map/ppermute | solution.py:25
  17.3 2.7 %collective-permute-start.1 = (bf16[864,256]{1,0:T(8,128)(2,1)S(1)}, bf16[864,256]{1,0:T(8,128)(2,1)S(1)}, u32[]{:S(2)}, u32[]{:S(2)}) collective-permute-start(bf16[864,256]{1,0:T(8,128)(2,1)S(1)} %get-tuple-element.56), channel_id=1, source_target_pairs={{0,32},{32,0},{1,33},{33,1},{2,34},{34,2},{3,35},{35,3},{4,36},{36... | collective-permute-start | bytes 1327112 | tf_op jit(solution)/shard_map/ppermute | solution.py:23
  20.0 0.6 collective-permute-start.2
  20.8 1.8 %turn.1 = (bf16[2,256,1152]{2,1,0:T(8,128)(2,1)S(1)}, bf16[2,256,384]{2,1,0:T(8,128)(2,1)S(1)}) custom-call(s32[6]{0:T(128)S(1)} %stack.27.pos_ref, bf16[576,1024]{1,0:T(8,128)(2,1)S(1)} %get-tuple-element.54.x_ref, bf16[576,256]{1,0:T(8,128)(2,1)S(1)} %collective-permute-done.3.x1, bf16[576,256]{1,0:T(8,128)(2,1)S(1)} %collective-permute-done.4.x2, ...), custom_call_target="tpu_custom_call" | custom-call | flops 301989888 | bytes 2359296 | tf_op jit(solution)/shard_map/turn/pallas_call | solution.py:233
  22.6 6.2 %inner.1 = (bf16[576,256]{1,0:T(8,128)(2,1)S(1)}, f32[576,256]{1,0:T(8,128)S(1)}, f32[3,576,256]{2,1,0:T(8,128)S(1)}) custom-call(s32[6]{0:T(128)S(1)} %stack.27.pos_ref, bf16[576,1024]{1,0:T(8,128)(2,1)S(1)} %get-tuple-element.54.x_ref, f32[3,576,256]{2,1,0:T(8,128)S(1)} %get-tuple-element.62.part_ref, bf16[1024,256]{1,0:T(8,128)(2,1)S(1)} %copy-done.1, ...), custom_call_target="tpu_custom_call" | custom-call | flops 3019898880 | bytes 10485760 | tf_op jit(solution)/shard_map/inner/pallas_call | solution.py:509
  28.8 1.3 %collective-permute-done.2.diag_ref = bf16[576,256]{1,0:T(8,128)(2,1)S(1)} collective-permute-done((bf16[576,256]{1,0:T(8,128)(2,1)S(1)}, bf16[576,256]{1,0:T(8,128)(2,1)S(1)}, u32[]{:S(2)}, u32[]{:S(2)}) %collective-permute-start.2) | collective-permute-done | bytes 294944 | tf_op jit(solution)/shard_map/ppermute | solution.py:26
  30.2 8.3 %collective-permute-done.1.col_ref = bf16[864,256]{1,0:T(8,128)(2,1)S(1)} collective-permute-done((bf16[864,256]{1,0:T(8,128)(2,1)S(1)}, bf16[864,256]{1,0:T(8,128)(2,1)S(1)}, u32[]{:S(2)}, u32[]{:S(2)}) %collective-permute-start.1) | collective-permute-done | bytes 442400 | tf_op jit(solution)/shard_map/ppermute | solution.py:23
  38.5 2.0 %merge.1 = (bf16[576,1024]{1,0:T(8,128)(2,1)S(1)}, bf16[576,256]{1,0:T(8,128)(2,1)S(1)}, bf16[576,256]{1,0:T(8,128)(2,1)S(1)}) custom-call(s32[6]{0:T(128)S(1)} %stack.27.pos_ref, bf16[576,256]{1,0:T(8,128)(2,1)S(1)} %get-tuple-element.70.joined0_ref, f32[3,576,256]{2,1,0:T(8,128)S(1)} %get-tuple-element.71.own_ref, ...), custom_call_target="tpu_custom_call" | custom-call | flops 452984832 | bytes 6291456 | tf_op jit(solution)/shard_map/merge/pallas_call | solution.py:594
  40.6 2.8 %collective-permute-start.10 = (bf16[576,256]{1,0:T(8,128)(2,1)S(1)}, bf16[576,256]{1,0:T(8,128)(2,1)S(1)}, u32[]{:S(2)}, u32[]{:S(2)}) collective-permute-start(bf16[576,256]{1,0:T(8,128)(2,1)S(1)} %get-tuple-element.86.d0), channel_id=1, source_target_pairs={{0,96},{96,0},{32,64},{64,32},{1,97},{97,1},{33,65},{65,33},{2,98}... | collective-permute-start | bytes 884744 | tf_op jit(solution)/shard_map/ppermute | solution.py:26
  43.4 0.8 collective-permute-start.8
  44.2 0.6 collective-permute-start.9
  44.7 2.5 %pair.1 = (f32[1024,256]{1,0:T(8,128)S(1)}, bf16[512,256]{1,0:T(8,128)(2,1)S(1)}, bf16[512,256]{1,0:T(8,128)(2,1)S(1)}) custom-call(s32[6]{0:T(128)S(1)} %stack.27.pos_ref, bf16[576,1024]{1,0:T(8,128)(2,1)S(1)} %get-tuple-element.75.joined_ref, bf16[576,256]{1,0:T(8,128)(2,1)S(1)} %get-tuple-element.76.g_ref, bf16[576,1024]{1,0:T(8,128)(2,1)S(1)} %get-tuple-element.54.x_ref, ...), custom_call_target="tpu_custom_call" | custom-call | flops 603979776 | bytes 4194304 | tf_op jit(solution)/shard_map/pair/pallas_call | solution.py:647
  47.9 1.0 %collective-permute-done.6.got0 = bf16[512,256]{1,0:T(8,128)(2,1)S(1)} collective-permute-done((bf16[512,256]{1,0:T(8,128)(2,1)S(1)}, bf16[512,256]{1,0:T(8,128)(2,1)S(1)}, u32[]{:S(2)}, u32[]{:S(2)}) %collective-permute-start.6) | collective-permute-done | bytes 262176 | tf_op jit(solution)/shard_map/ppermute | solution.py:211
  49.3 0.7 rows.1
  50.0 5.8 %collective-permute-done.10.d3 = bf16[576,256]{1,0:T(8,128)(2,1)S(1)} collective-permute-done((bf16[576,256]{1,0:T(8,128)(2,1)S(1)}, bf16[576,256]{1,0:T(8,128)(2,1)S(1)}, u32[]{:S(2)}, u32[]{:S(2)}) %collective-permute-start.10) | collective-permute-done | bytes 294944 | tf_op jit(solution)/shard_map/ppermute | solution.py:26
  55.8 0.7 collective-permute-done.9.d2
  56.5 3.1 %collective-permute-start.11 = (bf16[16,16,256]{2,1,0:T(8,128)(2,1)S(1)}, bf16[16,16,256]{2,1,0:T(8,128)(2,1)S(1)}, u32[]{:S(2)}, u32[]{:S(2)}) collective-permute-start(bf16[16,16,256]{2,1,0:T(8,128)(2,1)S(1)} %get-tuple-element.95), channel_id=1, source_target_pairs={{0,32},{32,0},{1,33},{33,1},{2,34},{34,2},{3,35},{35,3},{4,36},{36... | collective-permute-start | bytes 393224 | tf_op jit(solution)/shard_map/ppermute | solution.py:23
  59.7 0.6 collective-permute-start.12
  60.3 0.5 collective-permute-start.13
  60.8 3.1 %taps.1 = (f32[96,16,256]{2,1,0:T(8,128)S(1)}, bf16[96,16,256]{2,1,0:T(8,128)(2,1)S(1)}) custom-call(s32[6]{0:T(128)S(1)} %stack.27.pos_ref, s32[176]{0:T(256)S(1)} %fusion.1.place_ref, bf16[576,256]{1,0:T(8,128)(2,1)S(1)} %get-tuple-element.86.d0, bf16[576,256]{1,0:T(8,128)(2,1)S(1)} %collective-permute-done.8.d1, ...), custom_call_target="tpu_custom_call" | custom-call | flops 2113929216 | bytes 8388608 | tf_op jit(solution)/shard_map/taps/pallas_call | solution.py:282
  63.9 1.4 %collective-permute-done.12 = bf16[16,16,256]{2,1,0:T(8,128)(2,1)S(1)} collective-permute-done((bf16[16,16,256]{2,1,0:T(8,128)(2,1)S(1)}, bf16[16,16,256]{2,1,0:T(8,128)(2,1)S(1)}, u32[]{:S(2)}, u32[]{:S(2)}) %collective-permute-start.12) | collective-permute-done | bytes 131104 | tf_op jit(solution)/shard_map/ppermute | solution.py:25
  65.4 1.1 %collective-permute-done.13 = bf16[16,16,256]{2,1,0:T(8,128)(2,1)S(1)} collective-permute-done((bf16[16,16,256]{2,1,0:T(8,128)(2,1)S(1)}, bf16[16,16,256]{2,1,0:T(8,128)(2,1)S(1)}, u32[]{:S(2)}, u32[]{:S(2)}) %collective-permute-start.13) | collective-permute-done | bytes 131104 | tf_op jit(solution)/shard_map/ppermute | solution.py:26
  66.5 0.6 collective-permute-start.15
  67.1 1.8 %collective-permute-done.15.other_ref = bf16[16,16,256]{2,1,0:T(8,128)(2,1)S(1)} collective-permute-done((bf16[16,16,256]{2,1,0:T(8,128)(2,1)S(1)}, bf16[16,16,256]{2,1,0:T(8,128)(2,1)S(1)}, u32[]{:S(2)}, u32[]{:S(2)}) %collective-permute-start.15) | collective-permute-done | bytes 131104 | tf_op jit(solution)/shard_map/ppermute | solution.py:211
  68.9 1.1 %owners.1 = bf16[16,96,256]{2,1,0:T(8,128)(2,1)S(1)} custom-call(s32[6]{0:T(128)S(1)} %stack.27.pos_ref, s32[176]{0:T(256)S(1)} %fusion.1.place_ref, f32[96,16,256]{2,1,0:T(8,128)S(1)} %get-tuple-element.92.keep_ref, bf16[96,16,256]{2,1,0:T(8,128)(2,1)S(1)} %collective-permute-done.14.got_ref, f32[16,16,256]{2,1,0:T(8,128)S(1)} %get-tuple-element.104.mine_ref, ...), custom_call_target="tpu_custom_call" | custom-call | flops 393216 | bytes 3145728 | tf_op jit(solution)/shard_map/owners/pallas_call | solution.py:304
  70.1 22.3 %all_to_all.5.r_ref = bf16[16,96,256]{2,1,0:T(8,128)(2,1)S(1)} all-to-all(bf16[16,96,256]{2,1,0:T(8,128)(2,1)S(1)} %owners.1), channel_id=1, replica_groups=mesh['row'=2,'col'=2,'dp_0'=4,'dp_1'=4,'dp_2'=2] {'dp_0','dp_1'}, dimensions={0} | all-to-all | bytes 1572864 | tf_op jit(solution)/shard_map/all_to_all | solution.py:314
  92.3 0.8 last.1
  (22 shorter events, 1.5 us)
Async XLA Ops:
  2.8 17.2 %collective-permute-start.3 = (bf16[576,256]{1,0:T(8,128)(2,1)S(1)}, bf16[576,256]{1,0:T(8,128)(2,1)S(1)}, u32[]{:S(2)}, u32[]{:S(2)}) collective-permute-start(bf16[576,256]{1,0:T(8,128)(2,1)S(1)} %get-tuple-element.59), channel_id=1, source_target_pairs={{0,32},{32,0},{1,33},{33,1},{2,34},{34,2},{3,35},{35,3},{4,36},{36... | collective-permute-start | bytes 884744 | tf_op jit(solution)/shard_map/ppermute | solution.py:23
  5.9 14.8 %collective-permute-start.4 = (bf16[576,256]{1,0:T(8,128)(2,1)S(1)}, bf16[576,256]{1,0:T(8,128)(2,1)S(1)}, u32[]{:S(2)}, u32[]{:S(2)}) collective-permute-start(bf16[576,256]{1,0:T(8,128)(2,1)S(1)} %get-tuple-element.60), channel_id=1, source_target_pairs={{0,64},{64,0},{1,65},{65,1},{2,66},{66,2},{3,67},{67,3},{4,68},{68... | collective-permute-start | bytes 884744 | tf_op jit(solution)/shard_map/ppermute | solution.py:25
  6.5 14.2 %collective-permute-start.5 = (bf16[576,256]{1,0:T(8,128)(2,1)S(1)}, bf16[576,256]{1,0:T(8,128)(2,1)S(1)}, u32[]{:S(2)}, u32[]{:S(2)}) collective-permute-start(bf16[576,256]{1,0:T(8,128)(2,1)S(1)} %get-tuple-element.61), channel_id=1, source_target_pairs={{0,96},{96,0},{32,64},{64,32},{1,97},{97,1},{33,65},{65,33},{2,98}... | collective-permute-start | bytes 884744 | tf_op jit(solution)/shard_map/ppermute | solution.py:26
  15.8 6.8 %copy-start.1 = (bf16[1024,256]{1,0:T(8,128)(2,1)S(1)}, bf16[1024,256]{1,0:T(8,128)(2,1)}, u32[]{:S(2)}) copy-start(bf16[1024,256]{1,0:T(8,128)(2,1)} %wp_ref.3) | copy-start | bytes 1572868
  15.8 14.4 %collective-permute-start = (bf16[864,256]{1,0:T(8,128)(2,1)S(1)}, bf16[864,256]{1,0:T(8,128)(2,1)S(1)}, u32[]{:S(2)}, u32[]{:S(2)}) collective-permute-start(bf16[864,256]{1,0:T(8,128)(2,1)S(1)} %get-tuple-element.55), channel_id=1, source_target_pairs={{0,64},{64,0},{1,65},{65,1},{2,66},{66,2},{3,67},{67,3},{4,68},{68... | collective-permute-start | bytes 1327112 | tf_op jit(solution)/shard_map/ppermute | solution.py:25
  17.3 21.2 %collective-permute-start.1 = (bf16[864,256]{1,0:T(8,128)(2,1)S(1)}, bf16[864,256]{1,0:T(8,128)(2,1)S(1)}, u32[]{:S(2)}, u32[]{:S(2)}) collective-permute-start(bf16[864,256]{1,0:T(8,128)(2,1)S(1)} %get-tuple-element.56), channel_id=1, source_target_pairs={{0,32},{32,0},{1,33},{33,1},{2,34},{34,2},{3,35},{35,3},{4,36},{36... | collective-permute-start | bytes 1327112 | tf_op jit(solution)/shard_map/ppermute | solution.py:23
  20.0 10.1 %collective-permute-start.2 = (bf16[576,256]{1,0:T(8,128)(2,1)S(1)}, bf16[576,256]{1,0:T(8,128)(2,1)S(1)}, u32[]{:S(2)}, u32[]{:S(2)}) collective-permute-start(bf16[576,256]{1,0:T(8,128)(2,1)S(1)} %get-tuple-element.57), channel_id=1, source_target_pairs={{0,96},{96,0},{32,64},{64,32},{1,97},{97,1},{33,65},{65,33},{2,98}... | collective-permute-start | bytes 884744 | tf_op jit(solution)/shard_map/ppermute | solution.py:26
  22.6 15.9 %copy-start = (bf16[1024,256]{1,0:T(8,128)(2,1)S(1)}, bf16[1024,256]{1,0:T(8,128)(2,1)}, u32[]{:S(2)}) copy-start(bf16[1024,256]{1,0:T(8,128)(2,1)} %wp_ref.5) | copy-start | bytes 1572868
  22.6 15.9 %copy-start.2 = (bf16[1,24,24,256]{3,2,1,0:T(8,128)(2,1)S(1)}, bf16[1,24,24,256]{3,2,1,0:T(8,128)(2,1)}, u32[]{:S(2)}) copy-start(bf16[1,24,24,256]{3,2,1,0:T(8,128)(2,1)} %param.9) | copy-start | bytes 884740
  40.6 15.3 %collective-permute-start.10 = (bf16[576,256]{1,0:T(8,128)(2,1)S(1)}, bf16[576,256]{1,0:T(8,128)(2,1)S(1)}, u32[]{:S(2)}, u32[]{:S(2)}) collective-permute-start(bf16[576,256]{1,0:T(8,128)(2,1)S(1)} %get-tuple-element.86.d0), channel_id=1, source_target_pairs={{0,96},{96,0},{32,64},{64,32},{1,97},{97,1},{33,65},{65,33},{2,98}... | collective-permute-start | bytes 884744 | tf_op jit(solution)/shard_map/ppermute | solution.py:26
  43.4 12.5 %collective-permute-start.8 = (bf16[576,256]{1,0:T(8,128)(2,1)S(1)}, bf16[576,256]{1,0:T(8,128)(2,1)S(1)}, u32[]{:S(2)}, u32[]{:S(2)}) collective-permute-start(bf16[576,256]{1,0:T(8,128)(2,1)S(1)} %get-tuple-element.86.d0), channel_id=1, source_target_pairs={{0,32},{32,0},{1,33},{33,1},{2,34},{34,2},{3,35},{35,3},{4,36},{36... | collective-permute-start | bytes 884744 | tf_op jit(solution)/shard_map/ppermute | solution.py:23
  44.2 12.4 %collective-permute-start.9 = (bf16[576,256]{1,0:T(8,128)(2,1)S(1)}, bf16[576,256]{1,0:T(8,128)(2,1)S(1)}, u32[]{:S(2)}, u32[]{:S(2)}) collective-permute-start(bf16[576,256]{1,0:T(8,128)(2,1)S(1)} %get-tuple-element.86.d0), channel_id=1, source_target_pairs={{0,64},{64,0},{1,65},{65,1},{2,66},{66,2},{3,67},{67,3},{4,68},{68... | collective-permute-start | bytes 884744 | tf_op jit(solution)/shard_map/ppermute | solution.py:25
  44.7 3.1 %copy-start.3 = (s32[176]{0:T(256)S(1)}, s32[176]{0:T(256)}, u32[]{:S(2)}) copy-start(s32[176]{0:T(256)} %param.15) | copy-start | bytes 2116
  47.3 1.6 %collective-permute-start.6 = (bf16[512,256]{1,0:T(8,128)(2,1)S(1)}, bf16[512,256]{1,0:T(8,128)(2,1)S(1)}, u32[]{:S(2)}, u32[]{:S(2)}) collective-permute-start(bf16[512,256]{1,0:T(8,128)(2,1)S(1)} %get-tuple-element.79), channel_id=1, source_target_pairs={{0,1},{1,0},{2,3},{3,2},{4,5},{5,4},{6,7},{7,6},{8,9},{9,8},{10,11... | collective-permute-start | bytes 786440 | tf_op jit(solution)/shard_map/ppermute | solution.py:211
  47.4 1.9 %collective-permute-start.7 = (bf16[512,256]{1,0:T(8,128)(2,1)S(1)}, bf16[512,256]{1,0:T(8,128)(2,1)S(1)}, u32[]{:S(2)}, u32[]{:S(2)}) collective-permute-start(bf16[512,256]{1,0:T(8,128)(2,1)S(1)} %get-tuple-element.80), channel_id=1, source_target_pairs={{0,1},{1,0},{2,3},{3,2},{4,5},{5,4},{6,7},{7,6},{8,9},{9,8},{10,11... | collective-permute-start | bytes 786440 | tf_op jit(solution)/shard_map/ppermute | solution.py:211
  56.5 7.4 %collective-permute-start.11 = (bf16[16,16,256]{2,1,0:T(8,128)(2,1)S(1)}, bf16[16,16,256]{2,1,0:T(8,128)(2,1)S(1)}, u32[]{:S(2)}, u32[]{:S(2)}) collective-permute-start(bf16[16,16,256]{2,1,0:T(8,128)(2,1)S(1)} %get-tuple-element.95), channel_id=1, source_target_pairs={{0,32},{32,0},{1,33},{33,1},{2,34},{34,2},{3,35},{35,3},{4,36},{36... | collective-permute-start | bytes 393224 | tf_op jit(solution)/shard_map/ppermute | solution.py:23
  59.7 5.7 %collective-permute-start.12 = (bf16[16,16,256]{2,1,0:T(8,128)(2,1)S(1)}, bf16[16,16,256]{2,1,0:T(8,128)(2,1)S(1)}, u32[]{:S(2)}, u32[]{:S(2)}) collective-permute-start(bf16[16,16,256]{2,1,0:T(8,128)(2,1)S(1)} %get-tuple-element.96), channel_id=1, source_target_pairs={{0,64},{64,0},{1,65},{65,1},{2,66},{66,2},{3,67},{67,3},{4,68},{68... | collective-permute-start | bytes 393224 | tf_op jit(solution)/shard_map/ppermute | solution.py:25
  60.3 6.2 %collective-permute-start.13 = (bf16[16,16,256]{2,1,0:T(8,128)(2,1)S(1)}, bf16[16,16,256]{2,1,0:T(8,128)(2,1)S(1)}, u32[]{:S(2)}, u32[]{:S(2)}) collective-permute-start(bf16[16,16,256]{2,1,0:T(8,128)(2,1)S(1)} %get-tuple-element.97), channel_id=1, source_target_pairs={{0,96},{96,0},{32,64},{64,32},{1,97},{97,1},{33,65},{65,33},{2,98}... | collective-permute-start | bytes 393224 | tf_op jit(solution)/shard_map/ppermute | solution.py:26
  66.4 2.5 %collective-permute-start.14 = (bf16[96,16,256]{2,1,0:T(8,128)(2,1)S(1)}, bf16[96,16,256]{2,1,0:T(8,128)(2,1)S(1)}, u32[]{:S(2)}, u32[]{:S(2)}) collective-permute-start(bf16[96,16,256]{2,1,0:T(8,128)(2,1)S(1)} %get-tuple-element.98), channel_id=1, source_target_pairs={{0,1},{1,0},{2,3},{3,2},{4,5},{5,4},{6,7},{7,6},{8,9},{9,8},{10,11... | collective-permute-start | bytes 2359304 | tf_op jit(solution)/shard_map/ppermute | solution.py:211
  66.5 2.4 %collective-permute-start.15 = (bf16[16,16,256]{2,1,0:T(8,128)(2,1)S(1)}, bf16[16,16,256]{2,1,0:T(8,128)(2,1)S(1)}, u32[]{:S(2)}, u32[]{:S(2)}) collective-permute-start(bf16[16,16,256]{2,1,0:T(8,128)(2,1)S(1)} %get-tuple-element.103), channel_id=1, source_target_pairs={{0,1},{1,0},{2,3},{3,2},{4,5},{5,4},{6,7},{7,6},{8,9},{9,8},{10,11... | collective-permute-start | bytes 393224 | tf_op jit(solution)/shard_map/ppermute | solution.py:211
